TPU v7x, 256 devices: a whole 4x4x8 slice. The times are simulated.
256 devices in a mesh: ctx: 64 (over x, z, core), rep: 4 (over y).
Axes of the slice: x: 4, y: 4, z: 8, core: 2. Of those that a mesh axis runs over, the one named last changes fastest.
Arguments:
- latents: bfloat16 [1048576, 576], P(('ctx', 'rep')), may hold values from -6 to 6
- queries: bfloat16 [64, 73728], P('rep', 'ctx'), may hold values from -4000 to 4000, as said below
- hot_ids: int32 [128], P('ctx'), may hold values from 0 to 15, as said below
- lengths: int32 [64], P('rep'), may hold values from 524288 to 1048576
Outputs:
- attended: bfloat16 [64, 65536], P('rep', 'ctx')
Inputs may be any that keep to these rules, and one draw needn't show every extreme that they name: `queries`: query entries lie in the stated range. `hot_ids`: entries g * 2 to (g + 1) * 2 - 1 are distinct block numbers within group g.
All inputs are finite; a program needn't handle non-finite values.
Results may differ from a plain program's by a relative error of at most 0.0031.
Values may be sent and summed in bfloat16 or wider, within the bound.
No kernel may reach another device: no remote copies, remote signals or barrier semaphores. Data moves between devices by JAX's collectives and lax.ppermute only.
A program may use at most 128 MiB of HBM per device.

v0:
```python
import jax
import jax.numpy as jnp
from jax import lax
from jax.sharding import PartitionSpec as P

H = 128
LAT = 512
ROPE = 64
QK = 192
BLK = 1024
HOT_GRP = 2


def from_root(shard, axis, root):
    return lax.dynamic_index_in_dim(lax.all_gather(shard, axis), root, 0, keepdims=False)


def copy_for_each(shard, axis):
    count = lax.axis_size(axis)
    return lax.all_to_all(
        jnp.broadcast_to(shard[None], (count, *shard.shape)), axis, 0, 0, tiled=True
    )


def laid_out(pieces, dim):
    pieces = jnp.moveaxis(pieces, 0, dim)
    shape = pieces.shape
    return pieces.reshape(*shape[:dim], shape[dim] * shape[dim + 1], *shape[dim + 2 :])


def collect(shard, axis, dim):
    pieces = copy_for_each(shard, axis)
    return laid_out(pieces, dim)


def in_one_piece(arrays, axis, split_dim, concat_dim, along):
    columns = [a.reshape(*a.shape[:along], -1) for a in arrays]
    both = jnp.concatenate(columns, axis=along)
    out, at, finished = (
        lax.all_to_all(both, axis, split_axis=split_dim, concat_axis=concat_dim, tiled=True),
        0,
        [],
    )
    for a, column in zip(arrays, columns):
        section = out[..., at : at + column.shape[along]]
        finished.append(section.reshape(*section.shape[:along], *a.shape[along:]))
        at += column.shape[along]
    return tuple(finished)


def on_device(latents, queries, hot_ids, lengths):
    row_width = LAT + ROPE
    score_scale = QK ** (-0.5)
    rep_count = lax.axis_size("rep")
    group_index = lax.axis_index("ctx")
    per_device = latents.shape[0] // BLK
    blocks_held = []
    for slot_index in range(HOT_GRP):
        owner_index = hot_ids[slot_index] // per_device
        local_block = lax.dynamic_slice_in_dim(
            latents, hot_ids[slot_index] % per_device * BLK, BLK, 0
        )
        blocks_held.append(from_root(local_block, "rep", owner_index))
    key_rows = jnp.concatenate(blocks_held, axis=0)
    value_rows = key_rows[:, :LAT]
    offsets = jnp.arange(BLK, dtype=jnp.int32)
    row_index = (
        (group_index * (rep_count * per_device) + hot_ids)[:, None] * BLK + offsets[None, :]
    ).reshape(-1)
    all_heads = collect(queries, "ctx", 1)
    query_count = all_heads.shape[0]
    query_blocks = all_heads.reshape(query_count // 4, 4, H, row_width)
    span_blocks = lengths.reshape(query_count // 4, 4)

    def partial_value(item_pair):
        query_block, span_block = item_pair
        scores = (
            jnp.einsum("qhw,kw->qhk", query_block, key_rows, preferred_element_type=jnp.float32)
            * score_scale
        )
        visible = row_index[None, None, :] < span_block[:, None, None]
        peak_score = jnp.max(jnp.where(visible, scores, -1e30), axis=2)
        exponent = jnp.where(visible, scores - peak_score[:, :, None], -1e30)
        weights = jnp.exp(exponent).astype(jnp.bfloat16)
        totals = jnp.sum(weights, axis=2, dtype=jnp.float32)
        numerators = jnp.einsum(
            "qhk,kl->qhl", weights, value_rows, preferred_element_type=jnp.float32
        )
        return (numerators, peak_score, totals)

    numerators, peak_score, totals = lax.map(partial_value, (query_blocks, span_blocks))
    numerators = numerators.reshape(query_count, H, LAT)
    peak_score = peak_score.reshape(query_count, H)
    totals = totals.reshape(query_count, H)
    all_numer, all_peak, all_total = in_one_piece(
        (numerators[None], peak_score[None], totals[None]), "ctx", 2, 0, 3
    )
    overall = jnp.max(all_peak, axis=0)
    factor = jnp.exp(all_peak - overall[None])
    merged = jnp.sum(all_numer * factor[..., None], axis=0)
    weight_sum = jnp.sum(all_total * factor, axis=0)
    return (merged / weight_sum[..., None]).reshape(query_count, -1).astype(jnp.bfloat16)


def solution(mesh):
    placed = (P(("ctx", "rep"), None), P("rep", "ctx"), P("ctx"), P("rep"))
    return jax.shard_map(
        on_device, mesh=mesh, in_specs=placed, out_specs=P("rep", "ctx"), check_vma=False
    )
```

profile of v0, /device:TPU:6, one launch (start us, length us, event | category | flops | bytes accessed | tf_op | source)
XLA Modules:
  0.0 342.0 jit_solution(12186973133906544572)
XLA Ops:
  6.5 1.4 fusion.24
  11.7 3.3 constant_dynamic-slice_fusion.4
  15.7 1.6 broadcast_in_dim.44
  17.3 12.2 %all-to-all-start = ((bf16[64,16,1152]{2,1,0:T(8,128)(2,1)}), bf16[64,16,1152]{2,1,0:T(8,128)(2,1)S(1)}, u32[]{:S(2)}, u32[]{:S(2)}) async-start(bf16[64,16,1152]{2,1,0:T(8,128)(2,1)} %broadcast_in_dim.44), calls=%async_computation | async-start | bytes 4718592 | tf_op jit(solution)/shard_map/all_to_all | solution.py:20
  30.9 52.8 %all-to-all-done = bf16[64,16,1152]{2,1,0:T(8,128)(2,1)S(1)} async-done(((bf16[64,16,1152]{2,1,0:T(8,128)(2,1)}), bf16[64,16,1152]{2,1,0:T(8,128)(2,1)S(1)}, u32[]{:S(2)}, u32[]{:S(2)}) %all-to-all-start) | async-done | bytes 2359328 | tf_op jit(solution)/shard_map/all_to_all | solution.py:20
  83.7 1.9 copy.56
  85.6 4.3 %reshape_reshape.3 = bf16[4,4,128,576]{3,2,1,0:T(8,128)(2,1)S(1)} reshape(bf16[16,64,1152]{2,1,0:T(8,128)(2,1)} %copy.56) | data formatting | bytes 4718592 | tf_op jit(solution)/shard_map/reshape;reshape | solution.py:72
  89.9 2.6 copy.60
  92.5 8.8 %reshape.59 = bf16[4,1024,576]{1,0,2:T(4,128)(2,1)} reshape(bf16[4096,576]{0,1:T(8,128)(2,1)} %all-gather.7.cloned.1.call-done) | data formatting | bytes 9437184 | tf_op jit(solution)/shard_map/all_gather | solution.py:15
  101.3 4.8 %constant_dynamic-slice_fusion.1 = bf16[1,1024,576]{1,0,2:T(2,128)(2,1)S(1)} fusion(bf16[4,1024,576]{1,0,2:T(4,128)(2,1)} %reshape.59, s32[]{:T(128)S(6)} %select_n.45), kind=kLoop, calls=%fused_computation.40 | loop fusion | bytes 2359300 | tf_op jit(solution)/shard_map/jit(dynamic_index_in_dim)/dynamic_slice | solution.py:15
  106.1 24.5 %all-gather.5.cloned.1.call-done = bf16[4096,576]{0,1:T(8,128)(2,1)} async-done(((bf16[1024,576]{0,1:T(8,128)(2,1)}), bf16[4096,576]{0,1:T(8,128)(2,1)}) %all-gather.5.cloned.1.call-update) | async-done | bytes 4718608 | tf_op jit(solution)/shard_map/all_gather | solution.py:15
  130.6 8.9 %reshape.58 = bf16[4,1024,576]{1,0,2:T(4,128)(2,1)} reshape(bf16[4096,576]{0,1:T(8,128)(2,1)} %all-gather.5.cloned.1.call-done) | data formatting | bytes 9437184 | tf_op jit(solution)/shard_map/all_gather | solution.py:15
  139.5 4.8 %constant_dynamic-slice_fusion.3 = bf16[1,1024,576]{1,0,2:T(2,128)(2,1)S(1)} fusion(bf16[4,1024,576]{1,0,2:T(4,128)(2,1)} %reshape.58, s32[]{:T(128)S(6)} %select_n.41), kind=kLoop, calls=%fused_computation.42 | loop fusion | bytes 2359300 | tf_op jit(solution)/shard_map/jit(dynamic_index_in_dim)/dynamic_slice | solution.py:15
  145.2 1.5 fusion.19
  146.9 3.9 %copy.71 = bf16[2048,512]{1,0:T(8,128)(2,1)} copy(bf16[2048,512]{0,1:T(8,128)(2,1)} %fusion.19) | data formatting | bytes 4194304
  150.9 27.8 %while.15 = (s32[]{:T(128)}, f32[4,4,128,512]{3,2,1,0:T(8,128)}, f32[4,4,128]{2,1,0:T(4,128)S(1)}, f32[4,4,128]{2,1,0:T(4,128)S(1)}, s32[4,4]{1,0:T(4,128)S(1)},...) while((s32[]{:T(128)}, f32[4,4,128,512]{3,2,1,0:T(8,128)}, ...), condition=%wide.region_3.4_spmd.clone, body=%wide.region_0.3_spmd.clone.sunk | while | flops 2295342080 | bytes 27149504 | solution.py:91
  151.0 3.4 select_reduce_fusion.2
  154.4 1.1 convert_reduce_fusion.2
  155.5 2.3 fusion.30
  158.0 3.4 select_reduce_fusion.2
  161.3 1.1 convert_reduce_fusion.2
  162.5 2.3 fusion.30
  164.9 3.4 select_reduce_fusion.2
  169.4 2.3 fusion.30
  171.9 3.4 select_reduce_fusion.2
  175.2 1.1 convert_reduce_fusion.2
  176.4 2.3 fusion.30
  178.7 6.6 %copy.67 = f32[1,16,128,512]{3,1,0,2:T(8,128)} copy(f32[1,16,128,512]{3,2,1,0:T(8,128)} %bitcast.5) | data formatting | bytes 8388608 | tf_op jit(solution)/shard_map/broadcast_in_dim;reshape | solution.py:96
  186.3 3.0 pad_maximum_fusion
  189.3 127.7 %all_to_all.23 = f32[1,16,128,514]{3,1,0,2:T(8,128)} all-to-all(f32[1,16,128,514]{3,1,0,2:T(8,128)S(1)} %pad_maximum_fusion), channel_id=1, replica_groups=mesh['ctx'=64,'rep'=4] {'ctx'}, dimensions={2} | all-to-all | bytes 8421376 | tf_op jit(solution)/shard_map/all_to_all | solution.py:40
  317.0 9.1 %copy.64 = f32[1,16,64,2,514]{2,1,4,3,0:T(8,128)} copy(f32[1,16,64,2,514]{4,1,3,2,0:T(8,128)} %bitcast.87) | data formatting | bytes 8421376 | tf_op jit(solution)/shard_map/all_to_all | solution.py:40
  328.6 5.6 %fusion.18 = f32[16,2,512]{0,2,1:T(8,128)S(1)} fusion(f32[64,16,2,514]{0,1,3,2:T(8,128)} %bitcast.86, f32[64,16,2]{0,1,2:T(8,128)S(1)} %exponential_bitcast_fusion), kind=kLoop, calls=%fused_computation.23 | loop fusion | flops 2080768 | bytes 4268032 | tf_op jit(solution)/shard_map/reduce_sum | solution.py:100
  (55 shorter events, 8.2 us)
Async XLA Ops:
  6.5 9.2 %copy-start.1 = (bf16[16,1152]{1,0:T(8,128)(2,1)S(1)}, bf16[16,1152]{1,0:T(8,128)(2,1)}, u32[]{:S(2)}) copy-start(bf16[16,1152]{1,0:T(8,128)(2,1)} %param.7) | copy-start | bytes 110596
  6.5 85.9 %all-gather.7.cloned.1.call-start = ((), (), s32[]{:S(2)}) async-start(), calls=%async_computation.3 | async-start | bytes 5898240 | tf_op jit(solution)/shard_map/all_gather | solution.py:15
  14.9 15.8 %copy-start.3 = (s32[16]{0:T(128)S(1)}, s32[16]{0:T(128)}, u32[]{:S(2)}) copy-start(s32[16]{0:T(128)} %param.9) | copy-start | bytes 196
  15.0 15.9 %copy-start.2 = (s32[2]{0:T(128)S(1)}, s32[2]{0:T(128)}, u32[]{:S(2)}) copy-start(s32[2]{0:T(128)} %param.8) | copy-start | bytes 28
  15.0 115.7 %all-gather.5.cloned.1.call-start = ((), (), s32[]{:S(2)}) async-start(), calls=%async_computation.2 | async-start | bytes 5898240 | tf_op jit(solution)/shard_map/all_gather | solution.py:15
  17.3 66.4 %all-to-all-start = ((bf16[64,16,1152]{2,1,0:T(8,128)(2,1)}), bf16[64,16,1152]{2,1,0:T(8,128)(2,1)S(1)}, u32[]{:S(2)}, u32[]{:S(2)}) async-start(bf16[64,16,1152]{2,1,0:T(8,128)(2,1)} %broadcast_in_dim.44), calls=%async_computation | async-start | bytes 4718592 | tf_op jit(solution)/shard_map/all_to_all | solution.py:20
  151.0 4.5 %copy-start = (bf16[2048,512]{1,0:T(8,128)(2,1)S(1)}, bf16[2048,512]{1,0:T(8,128)(2,1)}, u32[]{:S(2)}) copy-start(bf16[2048,512]{1,0:T(8,128)(2,1)} %get-tuple-element.241) | copy-start | bytes 6291460 | tf_op jit(solution)/shard_map/while
  158.0 4.5 %copy-start = (bf16[2048,512]{1,0:T(8,128)(2,1)S(1)}, bf16[2048,512]{1,0:T(8,128)(2,1)}, u32[]{:S(2)}) copy-start(bf16[2048,512]{1,0:T(8,128)(2,1)} %get-tuple-element.241) | copy-start | bytes 6291460 | tf_op jit(solution)/shard_map/while
  164.9 4.5 %copy-start = (bf16[2048,512]{1,0:T(8,128)(2,1)S(1)}, bf16[2048,512]{1,0:T(8,128)(2,1)}, u32[]{:S(2)}) copy-start(bf16[2048,512]{1,0:T(8,128)(2,1)} %get-tuple-element.241) | copy-start | bytes 6291460 | tf_op jit(solution)/shard_map/while
  171.9 4.5 %copy-start = (bf16[2048,512]{1,0:T(8,128)(2,1)S(1)}, bf16[2048,512]{1,0:T(8,128)(2,1)}, u32[]{:S(2)}) copy-start(bf16[2048,512]{1,0:T(8,128)(2,1)} %get-tuple-element.241) | copy-start | bytes 6291460 | tf_op jit(solution)/shard_map/while
Sparse Core Ops, SparseCore 0:
  15.1 58.0 all-gather.6
  75.0 55.6 all-gather.4
where the time goes:
time: 346 us; the launch traced here: 342 us
  blocking collectives  128 us (37%)
  waiting for transfers between devices  78.1 us (23%)
  local copies, waits for them, and re-layouts  64.8 us (19%)
  matrix products  22.6 us (7%)
  between operations  18.6 us (5%)
  other arithmetic  17.9 us (5%)
  starting transfers between devices  12.2 us (4%)
    all_to_all x1, blocking collectives, in_one_piece(): lax.all_to_all(both, axis, split_axis=split_dim, concat_axis=concat_dim,...  128 us
    all_to_all x1, waiting for transfers between devices, copy_for_each(): lax.all_to_all(jnp.broadcast_to(shard[None], (count, *shard.shape)), axis...  52.8 us
    all_gather x2, waiting for transfers between devices, from_root(): lax.all_gather(shard, axis)  24.5 us
    all_gather x2, local copies, waits for them, and re-layouts, from_root(): lax.all_gather(shard, axis)  17.7 us
    dot_general x4, matrix products, partial_value(): jnp.einsum('qhw,kw->qhk', query_block, key_rows, preferred_element_type=j...  13.4 us
    all_to_all x1, starting transfers between devices, copy_for_each(): lax.all_to_all(jnp.broadcast_to(shard[None], (count, *shard.shape)), axis...  12.2 us
    dynamic_slice x2, local copies, waits for them, and re-layouts, from_root(): lax.dynamic_index_in_dim(lax.all_gather(shard, axis), root, 0, keepdims=F...  9.55 us
    dot_general x4, matrix products, partial_value(): jnp.einsum('qhk,kl->qhl', weights, value_rows, preferred_element_type=jnp...  9.22 us
  transfers between devices with their start and end apart: 3, of which 2 were waited for; matrix products, arithmetic and copies ran while one was open for 7% of the time, Pallas kernels for 0%

commit v1 on v0

v1 whole, which is shorter than its diff:
```python
import functools

import jax
import jax.numpy as jnp
from jax import lax
from jax.experimental import pallas as pl
from jax.experimental.pallas import tpu as pltpu
from jax.sharding import Mesh, PartitionSpec as P

H = 128
LAT = 512
ROPE = 64
QK = 192
BLK = 1024
HOT_GRP = 2
BPG = 16
WIDTH = LAT + ROPE
N_X = 4
N_Z = 8
N_C = 2
N_REP = 4
PER_DEV = BPG // N_REP
QUARTER = BLK // N_REP
HALF = QUARTER // 2
PAIR = HOT_GRP * HALF
CHUNK = 2 * PAIR
NEVER = -1e30
N_FAR = N_Z // 2
f32 = jnp.float32
bf16 = jnp.bfloat16

VMEM = pl.BlockSpec(memory_space=pltpu.VMEM)
SMEM = pl.BlockSpec(memory_space=pltpu.SMEM)
ANY = pl.BlockSpec(memory_space=pltpu.HBM)
PARAMS = pltpu.CompilerParams(vmem_limit_bytes=32 * 1024 * 1024)


def shift_rep(a, by):
    return lax.ppermute(a, "rep", [(i, (i + by) % N_REP) for i in range(N_REP)])


def swap_core(a):
    return lax.ppermute(a, "c", [(0, 1), (1, 0)])


def back_xz(a, hop, flip):
    pairs = []
    for x in range(N_X):
        for z in range(N_Z):
            pairs.append((x * N_Z + z, (x - hop) % N_X * N_Z + (z ^ flip)))
    return lax.ppermute(a, ("x", "z"), pairs)


def back_far(a, hop):
    pairs = [(z, (z - 2 * hop) % N_Z) for z in range(N_Z)]
    return lax.ppermute(a, "z", pairs)


def column(hot_ref, slot, rank, half):
    at = hot_ref[slot] % PER_DEV * BLK + rank * QUARTER + half * HALF
    return pl.ds(pl.multiple_of(at, HALF), HALF)


def run_copies(copies):
    for c in copies:
        c.start()
    for c in copies:
        c.wait()


def first_cut_kernel(hot_ref, lat_ref, up_ref, down_ref, sems):
    far = (lax.axis_index("rep") + 2) % N_REP
    copies = []
    for half, dst in enumerate((up_ref, down_ref)):
        for slot in range(HOT_GRP):
            copies.append(
                pltpu.make_async_copy(
                    lat_ref.at[:, column(hot_ref, slot, far, half)],
                    dst.at[:, pl.ds(slot * HALF, HALF)],
                    sems.at[len(copies)],
                )
            )
    run_copies(copies)


def own_cut_kernel(hot_ref, lat_ref, right_ref, left_ref, mine_ref, sems):
    rank = lax.axis_index("rep")
    copies = []
    for hop, dst in ((1, right_ref), (3, left_ref), (0, mine_ref)):
        for half in range(2):
            for slot in range(HOT_GRP):
                copies.append(
                    pltpu.make_async_copy(
                        lat_ref.at[:, column(hot_ref, slot, (rank + hop) % N_REP, half)],
                        dst.at[:, pl.ds(half * PAIR + slot * HALF, HALF)],
                        sems.at[len(copies)],
                    )
                )
    run_copies(copies)


def pass_on_kernel(hot_ref, from_left, from_right, right_in, left_in, right_ref, left_ref):
    rank = lax.axis_index("rep")
    for slot in range(HOT_GRP):
        a = slice(slot * HALF, (slot + 1) * HALF)
        b = slice(PAIR + slot * HALF, PAIR + (slot + 1) * HALF)

        @pl.when(hot_ref[slot] // PER_DEV != rank)
        def _():
            right_ref[:, a] = from_left[:, a]
            left_ref[:, b] = from_right[:, a]


def settle_kernel(hot_ref, from_left, from_right, mine_in, mine_ref):
    rank = lax.axis_index("rep")
    for slot in range(HOT_GRP):
        a = slice(slot * HALF, (slot + 1) * HALF)
        b = slice(PAIR + slot * HALF, PAIR + (slot + 1) * HALF)
        away = (hot_ref[slot] // PER_DEV - rank + N_REP) % N_REP

        @pl.when(away >= 2)
        def _():
            mine_ref[:, a] = from_left[:, a]

        @pl.when(away == 1)
        def _():
            mine_ref[:, a] = from_right[:, a]

        @pl.when(away == 3)
        def _():
            mine_ref[:, b] = from_left[:, b]

        @pl.when((away == 1) | (away == 2))
        def _():
            mine_ref[:, b] = from_right[:, b]


def three_terms(v):
    hi = v.astype(bf16)
    mid = (v - hi.astype(f32)).astype(bf16)
    low = (v - hi.astype(f32) - mid.astype(f32)).astype(bf16)
    return [hi, mid, low]


PLACES = ((0, 0, 2), (3, 0, 2), (1, 0, 2), (2, 0, 1), (2, 1, 1))


def attend_kernel(hop, q_ref, len_ref, hot_ref, hot_other_ref, *refs):
    n = len(PLACES)
    key_refs, outs = refs[: N_C * n], refs[N_C * n :]
    x, z, c = lax.axis_index("x"), lax.axis_index("z"), lax.axis_index("c")
    rank = lax.axis_index("rep")
    group = (x * N_Z + z) * N_C + c
    n_own = q_ref.shape[0] // (N_X * N_Z)
    first = (x - hop + N_X) % N_X * N_Z
    q = jnp.concatenate(
        [
            q_ref[
                pl.ds(pl.multiple_of((first + 2 * far + ((z + flip) & 1)) * n_own, n_own), n_own), :
            ]
            for flip in range(2)
            for far in range(N_FAR)
        ],
        axis=0,
    )
    lens = jnp.concatenate([len_ref[...]] * (q.shape[0] // len_ref.shape[0]), axis=0)
    lane = lax.broadcasted_iota(jnp.int32, (1, HALF), 1)
    parts = []
    for other in range(N_C):
        keys = key_refs[other * n : (other + 1) * n]
        hot = hot_other_ref if other else hot_ref
        own_group = group + other * (1 - 2 * c)
        scores = []
        for k_ref, (away, half, halves) in zip(keys, PLACES):
            at = (rank + away) % N_REP * QUARTER
            rows = jnp.concatenate(
                [
                    (own_group * BPG + hot[slot]) * BLK + at + h * HALF + lane
                    for h in range(half, half + halves)
                    for slot in range(HOT_GRP)
                ],
                axis=1,
            )
            s = jnp.dot(q, k_ref[...], preferred_element_type=f32) * (QK**-0.5)
            scores.append(jnp.where(rows < lens, s, NEVER))
        peak = scores[0].max(axis=1, keepdims=True)
        for s in scores[1:]:
            peak = jnp.maximum(peak, s.max(axis=1, keepdims=True))
        total = jnp.zeros_like(peak)
        numer = None
        for s, k_ref in zip(scores, keys):
            w = jnp.exp(s - peak).astype(bf16)
            total = total + jnp.sum(w.astype(f32), axis=1, keepdims=True)
            v = lax.dot_general(
                w, k_ref[:LAT, :], (((1,), (1,)), ((), ())), preferred_element_type=f32
            )
            numer = v if numer is None else numer + v
        parts.append((peak, total, numer))
    top = jnp.maximum(parts[0][0], parts[1][0])
    numer, total = 0.0, 0.0
    for peak, t, v in parts:
        f = jnp.where(peak > NEVER / 2, jnp.exp(peak - top), 0.0)
        numer = numer + v * f
        total = total + t * f
    o = (numer * (1.0 / jnp.maximum(total, 1.0))).astype(bf16)
    lanes = lax.broadcasted_iota(jnp.int32, (q.shape[0], 128), 1)
    stats = jnp.where(lanes == 0, top, total).T[:2, :]
    rows = o.shape[0] // 2
    for flip, o_ref in enumerate(outs):
        o_ref[:rows, :] = o[flip * rows : (flip + 1) * rows]
        mine = stats[:, flip * rows : (flip + 1) * rows]
        terms = three_terms(mine[0:1]) + three_terms(mine[1:2])
        terms = [t.astype(f32) for t in terms] + [jnp.zeros((10, rows), f32)]
        o_ref[rows:, :rows] = jnp.concatenate(terms, axis=0).astype(bf16)
        o_ref[rows:, rows:] = jnp.zeros((16, LAT - rows), bf16)


def merge_kernel(*refs):
    n_in = N_X * 2
    parts, sends, (own_ref, stat_ref), (acc_ref,) = (
        refs[:n_in],
        refs[n_in : n_in + N_FAR - 1],
        refs[n_in + N_FAR - 1 : n_in + N_FAR + 1],
        refs[n_in + N_FAR + 1 :],
    )
    rows = parts[0].shape[0] - 16
    tops, totals = [], []
    for p in parts:
        s = p[rows:, :rows].astype(f32)
        tops.append(s[0:1] + s[1:2] + s[2:3])
        totals.append(s[3:4] + s[4:5] + s[5:6])
    top = functools.reduce(jnp.maximum, tops)
    weights = [t * jnp.exp(m - top) for m, t in zip(tops, totals)]
    total = sum(weights)
    inv = 1.0 / jnp.maximum(total, 1.0)
    table = [w * inv for w in weights] + [top, total]
    table.append(jnp.zeros((128 - len(table), rows), f32))
    table = jnp.concatenate(table, axis=0).T
    acc = 0.0
    for i, p in enumerate(parts):
        acc = acc + p[:rows, :].astype(f32) * table[:, i : i + 1]
    acc_ref[:, :LAT] = acc
    acc_ref[:, LAT:] = table
    far = lax.axis_index("z") // 2
    n = rows // N_FAR

    def block(hop):
        return acc_ref[pl.ds(pl.multiple_of((far - hop + N_FAR) % N_FAR * n, n), n), :]

    lane = lax.broadcasted_iota(jnp.int32, (n, 128), 1)
    for hop, ref in enumerate(sends, 1):
        b = block(hop)
        ref[:, :LAT] = b[:, :LAT].astype(bf16)
        top, total = b[:, LAT + n_in : LAT + n_in + 1], b[:, LAT + n_in + 1 : LAT + n_in + 2]
        packed = jnp.zeros((n, 128), f32)
        for i, term in enumerate(three_terms(top) + three_terms(total)):
            packed = jnp.where(lane == i, term.astype(f32), packed)
        ref[:, LAT:] = packed.astype(bf16)
    b = block(0)
    own_ref[...] = b[:, :LAT]
    stat_ref[...] = b[:, LAT:]


def finish_kernel(own_ref, stat_ref, *refs):
    parts, out_ref = refs[:-1], refs[-1]
    n_in = N_X * 2
    tops, totals, values = [stat_ref[:, n_in : n_in + 1]], [stat_ref[:, n_in + 1 : n_in + 2]], [own_ref[...]]
    for p in parts:
        s = p[:, LAT:].astype(f32)
        tops.append(s[:, 0:1] + s[:, 1:2] + s[:, 2:3])
        totals.append(s[:, 3:4] + s[:, 4:5] + s[:, 5:6])
        values.append(p[:, :LAT].astype(f32))
    top = functools.reduce(jnp.maximum, tops)
    weights = [t * jnp.exp(m - top) for m, t in zip(tops, totals)]
    total = sum(weights)
    o = sum(v * w for v, w in zip(values, weights)) / total
    count = out_ref.shape[0]
    for head in range(o.shape[0] // count):
        out_ref[:, head * LAT : (head + 1) * LAT] = o[head * count : (head + 1) * count].astype(bf16)


def call(kernel, outs, in_specs, args, **more):
    return pl.pallas_call(
        kernel,
        out_shape=tuple(jax.ShapeDtypeStruct(*o) for o in outs),
        in_specs=in_specs,
        out_specs=(VMEM,) * len(outs),
        compiler_params=PARAMS,
        **more,
    )(*args)


def on_device(latents, queries, hot_ids, lengths):
    by_column = latents.T
    count = queries.shape[0]
    chunk, pair = ((WIDTH, CHUNK), bf16), ((WIDTH, PAIR), bf16)

    up, down = call(
        first_cut_kernel,
        [pair, pair],
        [SMEM, ANY],
        [hot_ids, by_column],
        scratch_shapes=[pltpu.SemaphoreType.DMA((4,))],
    )
    up, down = shift_rep(up, 1), shift_rep(down, -1)
    right, left, mine = call(
        own_cut_kernel,
        [chunk] * 3,
        [SMEM, ANY],
        [hot_ids, by_column],
        scratch_shapes=[pltpu.SemaphoreType.DMA((12,))],
    )
    right, left = call(
        pass_on_kernel,
        [chunk] * 2,
        [SMEM] + [VMEM] * 4,
        [hot_ids, up, down, right, left],
        input_output_aliases={3: 0, 4: 1},
    )
    from_left, from_right = shift_rep(right, 1), shift_rep(left, -1)
    (mine,) = call(
        settle_kernel,
        [chunk],
        [SMEM] + [VMEM] * 3,
        [hot_ids, from_left, from_right, mine],
        input_output_aliases={3: 0},
    )

    own = queries.reshape(count, -1, WIDTH).transpose(1, 0, 2).reshape(-1, WIDTH)
    asked = lax.all_gather(own, "z", tiled=True)
    asked = lax.all_gather(asked, "x", tiled=True)
    hot_other = swap_core(hot_ids)

    of_left, of_right = shift_rep(mine, 1), shift_rep(mine, -1)
    far_a, far_b = shift_rep(of_left[:, :PAIR], 1), shift_rep(of_right[:, PAIR:], -1)
    keys = [mine, of_left, of_right, far_a, far_b]
    keys = keys + [swap_core(k) for k in keys]

    rows = asked.shape[0] // N_X // 2
    part = ((rows + 16, LAT), bf16)
    lens = lengths[:, None]
    parts = []
    for hop in (2, 1, 3, 0):
        same, flipped = call(
            functools.partial(attend_kernel, hop),
            [part, part],
            [VMEM, VMEM, SMEM, SMEM] + [VMEM] * len(keys),
            [asked, lens, hot_ids, hot_other] + keys,
        )
        parts.append(back_xz(flipped, hop, 1))
        parts.append(back_xz(same, hop, 0) if hop else same)

    n = own.shape[0]
    message = ((n, LAT + 128), bf16)
    *sends, mine, stat = call(
        merge_kernel,
        [message] * (N_FAR - 1) + [((n, LAT), f32), ((n, 128), f32)],
        [VMEM] * len(parts),
        parts,
        scratch_shapes=[pltpu.VMEM((rows, LAT + 128), f32)],
    )
    sends = [back_far(s, hop) for hop, s in enumerate(sends, 1)]
    (out,) = call(
        finish_kernel,
        [((count, n // count * LAT), bf16)],
        [VMEM] * (2 + len(sends)),
        [mine, stat, *sends],
    )
    return out


def solution(mesh):
    assert dict(mesh.shape) == {"ctx": N_X * N_Z * N_C, "rep": N_REP}
    split = Mesh(mesh.devices.reshape(N_X, N_Z, N_C, N_REP), ("x", "z", "c", "rep"))
    ctx = ("x", "z", "c")
    placed = (P((*ctx, "rep"), None), P("rep", ctx), P(ctx), P("rep"))
    return jax.shard_map(
        on_device, mesh=split, in_specs=placed, out_specs=P("rep", ctx), check_vma=False
    )
```

time: 346 us -> 139 us (0.40)
  blocking collectives: 128 us -> 30.7 us
  local copies, waits for them, and re-layouts: 64.8 us -> 5.2 us
  waiting for transfers between devices: 78.1 us -> 32 us
  Pallas kernels: 0 us -> 24 us
  matrix products: 22.6 us -> 0 us
  starting transfers between devices: 12.2 us -> 32.2 us
  other arithmetic: 17.9 us -> 0 us
  between operations: 18.6 us -> 13.6 us
    all_to_all x1 -> x0, blocking collectives: 128 us -> none  [in_one_piece(): lax.all_to_all(both, axis, split_axis=split_dim, concat_axis=concat_dim,...]
    all_to_all x1 -> x0, waiting for transfers between devices: 52.8 us -> none  [copy_for_each(): lax.all_to_all(jnp.broadcast_to(shard[None], (count, *shard.shape)), axis...]
    ppermute x0 -> x24, starting transfers between devices: none -> 32.2 us  [the longest x8 13.3 us: shift_rep(): return lax.ppermute(a, 'rep', [(i, (i + by) % N_REP) for i in range(N_REP)])]
    ppermute x0 -> x24, waiting for transfers between devices: none -> 32 us  [the longest x8 20.2 us: shift_rep(): return lax.ppermute(a, 'rep', [(i, (i + by) % N_REP) for i in range(N_REP)])]
    all_gather x0 -> x1, blocking collectives: none -> 30.7 us  [on_device(): asked = lax.all_gather(own, 'z', tiled=True)]
    all_gather x2 -> x1, waiting for transfers between devices: 24.5 us -> 0.01 us  [on_device(): asked = lax.all_gather(asked, 'x', tiled=True)]
    pallas_call x0 -> x10, Pallas kernels: none -> 24 us  [call(): pl.pallas_call(kernel, out_shape=tuple((jax.ShapeDtypeStruct(*o) for o in...]
    dot_general x8 -> x0, matrix products: 22.6 us -> none  [the longest x4 13.4 us: partial_value(): jnp.einsum('qhw,kw->qhk', query_block, key_rows, preferred_element_type=j...]
  transfers between devices with their start and end apart: 3 -> 25, of which waited for: 2 -> 9; matrix products, arithmetic and copies ran while one was open for 7% -> 1% of each run, Pallas kernels for 0% -> 12%
where the time goes in v1:
time: 139 us; the launch traced here: 138 us
  starting transfers between devices  32.2 us (23%)
  waiting for transfers between devices  32 us (23%)
  blocking collectives  30.7 us (22%)
  Pallas kernels  24 us (17%)
  between operations  13.6 us (10%)
  local copies, waits for them, and re-layouts  5.2 us (4%)
    all_gather x1, blocking collectives, on_device(): asked = lax.all_gather(own, 'z', tiled=True)  30.7 us
    pallas_call x10, Pallas kernels, call(): pl.pallas_call(kernel, out_shape=tuple((jax.ShapeDtypeStruct(*o) for o in...  24 us
    ppermute x8, waiting for transfers between devices, shift_rep(): return lax.ppermute(a, 'rep', [(i, (i + by) % N_REP) for i in range(N_REP)])  20.2 us
    ppermute x8, starting transfers between devices, shift_rep(): return lax.ppermute(a, 'rep', [(i, (i + by) % N_REP) for i in range(N_REP)])  13.3 us
    ppermute x7, starting transfers between devices, back_xz(): return lax.ppermute(a, ('x', 'z'), pairs)  10.3 us
    ppermute x3, starting transfers between devices, back_far(): return lax.ppermute(a, 'z', pairs)  7.08 us
    ppermute x7, waiting for transfers between devices, back_xz(): return lax.ppermute(a, ('x', 'z'), pairs)  6.39 us
    unnamed x10, local copies, waits for them, and re-layouts  4.31 us
  transfers between devices with their start and end apart: 25, of which 9 were waited for; matrix products, arithmetic and copies ran while one was open for 1% of the time, Pallas kernels for 12%

profile of v1, /device:TPU:6, one launch (start us, length us, event | category | flops | bytes accessed | tf_op | source)
XLA Modules:
  0.0 137.6 jit_solution(5511022518155718693)
XLA Ops:
  6.5 2.3 %copy-done.1 = bf16[4096,576]{0,1:T(8,128)(2,1)S(1)} copy-done((bf16[4096,576]{0,1:T(8,128)(2,1)S(1)}, bf16[4096,576]{0,1:T(8,128)(2,1)}, u32[]{:S(2)}) %copy-start.1) | copy-done | bytes 4718616
  10.3 1.7 %collective-permute-start.1 = (bf16[576,256]{1,0:T(8,128)(2,1)S(1)}, bf16[576,256]{1,0:T(8,128)(2,1)S(1)}, u32[]{:S(2)}, u32[]{:S(2)}) collective-permute-start(bf16[576,256]{1,0:T(8,128)(2,1)S(1)} %get-tuple-element.25), channel_id=1, source_target_pairs={{0,1},{1,2},{2,3},{3,0},{4,5},{5,6},{6,7},{7,4},{8,9},{9,10},{10,1... | collective-permute-start | bytes 884744 | tf_op jit(solution)/shard_map/ppermute | solution.py:39
  12.0 1.7 %collective-permute-start.2 = (bf16[576,256]{1,0:T(8,128)(2,1)S(1)}, bf16[576,256]{1,0:T(8,128)(2,1)S(1)}, u32[]{:S(2)}, u32[]{:S(2)}) collective-permute-start(bf16[576,256]{1,0:T(8,128)(2,1)S(1)} %get-tuple-element.26), channel_id=1, source_target_pairs={{0,3},{1,0},{2,1},{3,2},{4,7},{5,4},{6,5},{7,6},{8,11},{9,8},{10,9... | collective-permute-start | bytes 884744 | tf_op jit(solution)/shard_map/ppermute | solution.py:39
  13.6 1.2 shard_map.47
  14.9 5.5 %collective-permute-done.1.from_left = bf16[576,256]{1,0:T(8,128)(2,1)S(1)} collective-permute-done((bf16[576,256]{1,0:T(8,128)(2,1)S(1)}, bf16[576,256]{1,0:T(8,128)(2,1)S(1)}, u32[]{:S(2)}, u32[]{:S(2)}) %collective-permute-start.1) | collective-permute-done | bytes 294944 | tf_op jit(solution)/shard_map/ppermute | solution.py:39
  21.1 1.6 %collective-permute-start.3 = (bf16[576,512]{1,0:T(8,128)(2,1)S(1)}, bf16[576,512]{1,0:T(8,128)(2,1)S(1)}, u32[]{:S(2)}, u32[]{:S(2)}) collective-permute-start(bf16[576,512]{1,0:T(8,128)(2,1)S(1)} %get-tuple-element.29), channel_id=1, source_target_pairs={{0,1},{1,2},{2,3},{3,0},{4,5},{5,6},{6,7},{7,4},{8,9},{9,10},{10,1... | collective-permute-start | bytes 1769480 | tf_op jit(solution)/shard_map/ppermute | solution.py:39
  22.7 1.7 %collective-permute-start.4 = (bf16[576,512]{1,0:T(8,128)(2,1)S(1)}, bf16[576,512]{1,0:T(8,128)(2,1)S(1)}, u32[]{:S(2)}, u32[]{:S(2)}) collective-permute-start(bf16[576,512]{1,0:T(8,128)(2,1)S(1)} %get-tuple-element.30), channel_id=1, source_target_pairs={{0,3},{1,0},{2,1},{3,2},{4,7},{5,4},{6,5},{7,6},{8,11},{9,8},{10,9... | collective-permute-start | bytes 1769480 | tf_op jit(solution)/shard_map/ppermute | solution.py:39
  24.4 30.7 %all_gather.6 = bf16[256,576]{1,0:T(8,128)(2,1)} all-gather(bf16[32,576]{1,0:T(8,128)(2,1)S(1)} %bitcast.7), channel_id=1, replica_groups=mesh['x'=4,'z'=8,'c'=2,'rep'=4] {'z'}, dimensions={0}, use_global_device_ids=true | all-gather | bytes 331776 | tf_op jit(solution)/shard_map/all_gather | solution.py:330
  56.1 3.1 %collective-permute-start.6 = (bf16[576,512]{1,0:T(8,128)(2,1)S(1)}, bf16[576,512]{1,0:T(8,128)(2,1)S(1)}, u32[]{:S(2)}, u32[]{:S(2)}) collective-permute-start(bf16[576,512]{1,0:T(8,128)(2,1)S(1)} %shard_map.49.refs_0_), channel_id=1, source_target_pairs={{0,3},{1,0},{2,1},{3,2},{4,7},{5,4},{6,5},{7,6},{8,11},{9,8},{10,9... | collective-permute-start | bytes 1769480 | tf_op jit(solution)/shard_map/ppermute | solution.py:39
  59.7 10.5 %collective-permute-done.5.refs_1_ = bf16[576,512]{1,0:T(8,128)(2,1)S(1)} collective-permute-done((bf16[576,512]{1,0:T(8,128)(2,1)S(1)}, bf16[576,512]{1,0:T(8,128)(2,1)S(1)}, u32[]{:S(2)}, u32[]{:S(2)}) %collective-permute-start.5) | collective-permute-done | bytes 589856 | tf_op jit(solution)/shard_map/ppermute | solution.py:39
  70.4 3.3 %collective-permute-start.8 = (bf16[576,256]{1,0:T(8,128)(2,1)S(1)}, bf16[576,256]{1,0:T(8,128)(2,1)}, u32[]{:S(2)}, u32[]{:S(2)}) collective-permute-start(bf16[576,256]{1,0:T(8,128)(2,1)S(1)} %slice.9), channel_id=1, source_target_pairs={{0,3},{1,0},{2,1},{3,2},{4,7},{5,4},{6,5},{7,6},{8,11},{9,8},{10,9... | collective-permute-start | bytes 884744 | tf_op jit(solution)/shard_map/ppermute | solution.py:39
  74.2 4.2 %collective-permute-done.7.refs_3_ = bf16[576,256]{1,0:T(8,128)(2,1)} collective-permute-done((bf16[576,256]{1,0:T(8,128)(2,1)S(1)}, bf16[576,256]{1,0:T(8,128)(2,1)}, u32[]{:S(2)}, u32[]{:S(2)}) %collective-permute-start.7) | collective-permute-done | bytes 294944 | tf_op jit(solution)/shard_map/ppermute | solution.py:39
  80.7 1.3 copy-done
  82.0 4.8 %shard_map.53 = (bf16[144,512]{1,0:T(8,128)(2,1)S(1)}, bf16[144,512]{1,0:T(8,128)(2,1)S(1)}) custom-call(bf16[1024,576]{1,0:T(8,128)(2,1)S(1)} %copy-done, s32[16,1]{1,0:T(8,128)S(1)} %copy.9.len_ref, s32[2]{0:T(128)S(1)} %copy-done.3, s32[2]{0:T(128)S(1)} %collective-permute-done.hot_other_ref, bf16[576,512]{1,0:T(8,128)(2,1)S(1)} %shard_map.49.refs_0_, ...), custom_call_target="tpu_custom_call" | custom-call | tf_op jit(solution)/shard_map/pallas_call | solution.py:283
  86.8 1.0 collective-permute-start.20
  87.8 4.8 %shard_map.52 = (bf16[144,512]{1,0:T(8,128)(2,1)S(1)}, bf16[144,512]{1,0:T(8,128)(2,1)S(1)}) custom-call(bf16[1024,576]{1,0:T(8,128)(2,1)S(1)} %copy-done, s32[16,1]{1,0:T(8,128)S(1)} %copy.9.len_ref, s32[2]{0:T(128)S(1)} %copy-done.3, s32[2]{0:T(128)S(1)} %collective-permute-done.hot_other_ref, bf16[576,512]{1,0:T(8,128)(2,1)S(1)} %shard_map.49.refs_0_, ...), custom_call_target="tpu_custom_call" | custom-call | tf_op jit(solution)/shard_map/pallas_call | solution.py:283
  92.6 1.0 collective-permute-start.18
  93.5 1.6 %collective-permute-start.19 = (bf16[144,512]{1,0:T(8,128)(2,1)S(1)}, bf16[144,512]{1,0:T(8,128)(2,1)S(1)}, u32[]{:S(2)}, u32[]{:S(2)}) collective-permute-start(bf16[144,512]{1,0:T(8,128)(2,1)S(1)} %get-tuple-element.37), channel_id=1, source_target_pairs={{0,64},{8,72},{16,80},{24,88},{32,96},{40,104},{48,112},{56,120},{... | collective-permute-start | bytes 442376 | tf_op jit(solution)/shard_map/ppermute | solution.py:51
  95.1 4.8 %shard_map.51 = (bf16[144,512]{1,0:T(8,128)(2,1)S(1)}, bf16[144,512]{1,0:T(8,128)(2,1)S(1)}) custom-call(bf16[1024,576]{1,0:T(8,128)(2,1)S(1)} %copy-done, s32[16,1]{1,0:T(8,128)S(1)} %copy.9.len_ref, s32[2]{0:T(128)S(1)} %copy-done.3, s32[2]{0:T(128)S(1)} %collective-permute-done.hot_other_ref, bf16[576,512]{1,0:T(8,128)(2,1)S(1)} %shard_map.49.refs_0_, ...), custom_call_target="tpu_custom_call" | custom-call | tf_op jit(solution)/shard_map/pallas_call | solution.py:283
  99.9 1.5 %collective-permute-start.16 = (bf16[144,512]{1,0:T(8,128)(2,1)S(1)}, bf16[144,512]{1,0:T(8,128)(2,1)S(1)}, u32[]{:S(2)}, u32[]{:S(2)}) collective-permute-start(bf16[144,512]{1,0:T(8,128)(2,1)S(1)} %get-tuple-element.34), channel_id=1, source_target_pairs={{0,200},{8,192},{16,216},{24,208},{32,232},{40,224},{48,248},{56,2... | collective-permute-start | bytes 442376 | tf_op jit(solution)/shard_map/ppermute | solution.py:51
  101.4 1.0 collective-permute-start.17
  102.4 4.8 %shard_map.50 = (bf16[144,512]{1,0:T(8,128)(2,1)S(1)}, bf16[144,512]{1,0:T(8,128)(2,1)S(1)}) custom-call(bf16[1024,576]{1,0:T(8,128)(2,1)S(1)} %copy-done, s32[16,1]{1,0:T(8,128)S(1)} %copy.9.len_ref, s32[2]{0:T(128)S(1)} %copy-done.3, s32[2]{0:T(128)S(1)} %collective-permute-done.hot_other_ref, bf16[576,512]{1,0:T(8,128)(2,1)S(1)} %shard_map.49.refs_0_, ...), custom_call_target="tpu_custom_call" | custom-call | tf_op jit(solution)/shard_map/pallas_call | solution.py:283
  107.2 3.2 %collective-permute-start.14 = (bf16[144,512]{1,0:T(8,128)(2,1)S(1)}, bf16[144,512]{1,0:T(8,128)(2,1)S(1)}, u32[]{:S(2)}, u32[]{:S(2)}) collective-permute-start(bf16[144,512]{1,0:T(8,128)(2,1)S(1)} %get-tuple-element.32), channel_id=1, source_target_pairs={{0,136},{8,128},{16,152},{24,144},{32,168},{40,160},{48,184},{56,1... | collective-permute-start | bytes 442376 | tf_op jit(solution)/shard_map/ppermute | solution.py:51
  110.4 0.9 collective-permute-start.15
  111.4 3.6 %collective-permute-done.14.refs_0_ = bf16[144,512]{1,0:T(8,128)(2,1)S(1)} collective-permute-done((bf16[144,512]{1,0:T(8,128)(2,1)S(1)}, bf16[144,512]{1,0:T(8,128)(2,1)S(1)}, u32[]{:S(2)}, u32[]{:S(2)}) %collective-permute-start.14) | collective-permute-done | bytes 147488 | tf_op jit(solution)/shard_map/ppermute | solution.py:51
  115.0 2.8 %collective-permute-done.15.refs_1_ = bf16[144,512]{1,0:T(8,128)(2,1)S(1)} collective-permute-done((bf16[144,512]{1,0:T(8,128)(2,1)S(1)}, bf16[144,512]{1,0:T(8,128)(2,1)S(1)}, u32[]{:S(2)}, u32[]{:S(2)}) %collective-permute-start.15) | collective-permute-done | bytes 147488 | tf_op jit(solution)/shard_map/ppermute | solution.py:51
  118.3 2.5 %collective-permute-start.21 = (bf16[32,640]{1,0:T(8,128)(2,1)S(1)}, bf16[32,640]{1,0:T(8,128)(2,1)S(1)}, u32[]{:S(2)}, u32[]{:S(2)}) collective-permute-start(bf16[32,640]{1,0:T(8,128)(2,1)S(1)} %get-tuple-element.42), channel_id=1, source_target_pairs={{0,48},{8,56},{16,0},{24,8},{32,16},{40,24},{48,32},{56,40},{1,49}... | collective-permute-start | bytes 122888 | tf_op jit(solution)/shard_map/ppermute | solution.py:56
  120.9 2.4 %collective-permute-start.22 = (bf16[32,640]{1,0:T(8,128)(2,1)S(1)}, bf16[32,640]{1,0:T(8,128)(2,1)S(1)}, u32[]{:S(2)}, u32[]{:S(2)}) collective-permute-start(bf16[32,640]{1,0:T(8,128)(2,1)S(1)} %get-tuple-element.43), channel_id=1, source_target_pairs={{0,32},{8,40},{16,48},{24,56},{32,0},{40,8},{48,16},{56,24},{1,33}... | collective-permute-start | bytes 122888 | tf_op jit(solution)/shard_map/ppermute | solution.py:56
  123.3 2.1 %collective-permute-start.23 = (bf16[32,640]{1,0:T(8,128)(2,1)S(1)}, bf16[32,640]{1,0:T(8,128)(2,1)S(1)}, u32[]{:S(2)}, u32[]{:S(2)}) collective-permute-start(bf16[32,640]{1,0:T(8,128)(2,1)S(1)} %get-tuple-element.44), channel_id=1, source_target_pairs={{0,16},{8,24},{16,32},{24,40},{32,48},{40,56},{48,0},{56,8},{1,17}... | collective-permute-start | bytes 122888 | tf_op jit(solution)/shard_map/ppermute | solution.py:56
  125.4 3.5 %collective-permute-done.22.refs_1_ = bf16[32,640]{1,0:T(8,128)(2,1)S(1)} collective-permute-done((bf16[32,640]{1,0:T(8,128)(2,1)S(1)}, bf16[32,640]{1,0:T(8,128)(2,1)S(1)}, u32[]{:S(2)}, u32[]{:S(2)}) %collective-permute-start.22) | collective-permute-done | bytes 40992 | tf_op jit(solution)/shard_map/ppermute | solution.py:56
  128.9 0.8 collective-permute-done.23.refs_2_
  129.7 1.1 shard_map.55
  (45 shorter events, 7.3 us)
Async XLA Ops:
  6.5 73.1 %all-gather.2.cloned.1.call-start = ((), (), s32[]{:S(2)}) async-start(), calls=%async_computation | async-start | bytes 1638400 | tf_op jit(solution)/shard_map/all_gather | solution.py:331
  6.5 2.3 %copy-start.1 = (bf16[4096,576]{0,1:T(8,128)(2,1)S(1)}, bf16[4096,576]{0,1:T(8,128)(2,1)}, u32[]{:S(2)}) copy-start(bf16[4096,576]{0,1:T(8,128)(2,1)} %param.4) | copy-start | bytes 14155780
  8.9 0.7 copy-start.2
  9.5 5.3 %copy-start.4 = (bf16[16,1152]{1,0:T(8,128)(2,1)S(1)}, bf16[16,1152]{1,0:T(8,128)(2,1)}, u32[]{:S(2)}) copy-start(bf16[16,1152]{1,0:T(8,128)(2,1)} %param.5) | copy-start | bytes 110596
  9.5 10.9 %copy-start.3 = (s32[2]{0:T(128)S(1)}, s32[2]{0:T(128)}, u32[]{:S(2)}) copy-start(s32[2]{0:T(128)} %hot_ref.15) | copy-start | bytes 28
  10.3 10.1 %collective-permute-start.1 = (bf16[576,256]{1,0:T(8,128)(2,1)S(1)}, bf16[576,256]{1,0:T(8,128)(2,1)S(1)}, u32[]{:S(2)}, u32[]{:S(2)}) collective-permute-start(bf16[576,256]{1,0:T(8,128)(2,1)S(1)} %get-tuple-element.25), channel_id=1, source_target_pairs={{0,1},{1,2},{2,3},{3,0},{4,5},{5,6},{6,7},{7,4},{8,9},{9,10},{10,1... | collective-permute-start | bytes 884744 | tf_op jit(solution)/shard_map/ppermute | solution.py:39
  12.0 8.5 %collective-permute-start.2 = (bf16[576,256]{1,0:T(8,128)(2,1)S(1)}, bf16[576,256]{1,0:T(8,128)(2,1)S(1)}, u32[]{:S(2)}, u32[]{:S(2)}) collective-permute-start(bf16[576,256]{1,0:T(8,128)(2,1)S(1)} %get-tuple-element.26), channel_id=1, source_target_pairs={{0,3},{1,0},{2,1},{3,2},{4,7},{5,4},{6,5},{7,6},{8,11},{9,8},{10,9... | collective-permute-start | bytes 884744 | tf_op jit(solution)/shard_map/ppermute | solution.py:39
  21.1 34.0 %collective-permute-start.3 = (bf16[576,512]{1,0:T(8,128)(2,1)S(1)}, bf16[576,512]{1,0:T(8,128)(2,1)S(1)}, u32[]{:S(2)}, u32[]{:S(2)}) collective-permute-start(bf16[576,512]{1,0:T(8,128)(2,1)S(1)} %get-tuple-element.29), channel_id=1, source_target_pairs={{0,1},{1,2},{2,3},{3,0},{4,5},{5,6},{6,7},{7,4},{8,9},{9,10},{10,1... | collective-permute-start | bytes 1769480 | tf_op jit(solution)/shard_map/ppermute | solution.py:39
  22.7 32.4 %collective-permute-start.4 = (bf16[576,512]{1,0:T(8,128)(2,1)S(1)}, bf16[576,512]{1,0:T(8,128)(2,1)S(1)}, u32[]{:S(2)}, u32[]{:S(2)}) collective-permute-start(bf16[576,512]{1,0:T(8,128)(2,1)S(1)} %get-tuple-element.30), channel_id=1, source_target_pairs={{0,3},{1,0},{2,1},{3,2},{4,7},{5,4},{6,5},{7,6},{8,11},{9,8},{10,9... | collective-permute-start | bytes 1769480 | tf_op jit(solution)/shard_map/ppermute | solution.py:39
  55.9 14.3 %collective-permute-start.5 = (bf16[576,512]{1,0:T(8,128)(2,1)S(1)}, bf16[576,512]{1,0:T(8,128)(2,1)S(1)}, u32[]{:S(2)}, u32[]{:S(2)}) collective-permute-start(bf16[576,512]{1,0:T(8,128)(2,1)S(1)} %shard_map.49.refs_0_), channel_id=1, source_target_pairs={{0,1},{1,2},{2,3},{3,0},{4,5},{5,6},{6,7},{7,4},{8,9},{9,10},{10,1... | collective-permute-start | bytes 1769480 | tf_op jit(solution)/shard_map/ppermute | solution.py:39
  56.1 14.2 %collective-permute-start.6 = (bf16[576,512]{1,0:T(8,128)(2,1)S(1)}, bf16[576,512]{1,0:T(8,128)(2,1)S(1)}, u32[]{:S(2)}, u32[]{:S(2)}) collective-permute-start(bf16[576,512]{1,0:T(8,128)(2,1)S(1)} %shard_map.49.refs_0_), channel_id=1, source_target_pairs={{0,3},{1,0},{2,1},{3,2},{4,7},{5,4},{6,5},{7,6},{8,11},{9,8},{10,9... | collective-permute-start | bytes 1769480 | tf_op jit(solution)/shard_map/ppermute | solution.py:39
  59.2 14.5 %collective-permute-start = (s32[2]{0:T(128)S(1)}, s32[2]{0:T(128)S(1)}, u32[]{:S(2)}, u32[]{:S(2)}) collective-permute-start(s32[2]{0:T(128)S(1)} %copy-done.3), channel_id=1, source_target_pairs={{0,4},{4,0},{1,5},{5,1},{2,6},{6,2},{3,7},{7,3},{8,12},{12,8},{9,1... | collective-permute-start | bytes 32 | tf_op jit(solution)/shard_map/ppermute | solution.py:43
  59.2 20.4 %collective-permute-start.9 = (bf16[576,512]{1,0:T(8,128)(2,1)S(1)}, bf16[576,512]{1,0:T(8,128)(2,1)S(1)}, u32[]{:S(2)}, u32[]{:S(2)}) collective-permute-start(bf16[576,512]{1,0:T(8,128)(2,1)S(1)} %shard_map.49.refs_0_), channel_id=1, source_target_pairs={{0,4},{4,0},{1,5},{5,1},{2,6},{6,2},{3,7},{7,3},{8,12},{12,8},{9,1... | collective-permute-start | bytes 1769480 | tf_op jit(solution)/shard_map/ppermute | solution.py:43
  70.2 8.1 %collective-permute-start.7 = (bf16[576,256]{1,0:T(8,128)(2,1)S(1)}, bf16[576,256]{1,0:T(8,128)(2,1)}, u32[]{:S(2)}, u32[]{:S(2)}) collective-permute-start(bf16[576,256]{1,0:T(8,128)(2,1)S(1)} %slice.8), channel_id=1, source_target_pairs={{0,1},{1,2},{2,3},{3,0},{4,5},{5,6},{6,7},{7,4},{8,9},{9,10},{10,1... | collective-permute-start | bytes 884744 | tf_op jit(solution)/shard_map/ppermute | solution.py:39
  70.4 8.0 %collective-permute-start.8 = (bf16[576,256]{1,0:T(8,128)(2,1)S(1)}, bf16[576,256]{1,0:T(8,128)(2,1)}, u32[]{:S(2)}, u32[]{:S(2)}) collective-permute-start(bf16[576,256]{1,0:T(8,128)(2,1)S(1)} %slice.9), channel_id=1, source_target_pairs={{0,3},{1,0},{2,1},{3,2},{4,7},{5,4},{6,5},{7,6},{8,11},{9,8},{10,9... | collective-permute-start | bytes 884744 | tf_op jit(solution)/shard_map/ppermute | solution.py:39
  73.6 7.0 %collective-permute-start.10 = (bf16[576,512]{1,0:T(8,128)(2,1)S(1)}, bf16[576,512]{1,0:T(8,128)(2,1)S(1)}, u32[]{:S(2)}, u32[]{:S(2)}) collective-permute-start(bf16[576,512]{1,0:T(8,128)(2,1)S(1)} %collective-permute-done.5.refs_1_), channel_id=1, source_target_pairs={{0,4},{4,0},{1,5},{5,1},{2,6},{6,2},{3,7},{7,3},{8,12},{12,8},{9,1... | collective-permute-start | bytes 1769480 | tf_op jit(solution)/shard_map/ppermute | solution.py:43
  73.6 7.0 %collective-permute-start.11 = (bf16[576,512]{1,0:T(8,128)(2,1)S(1)}, bf16[576,512]{1,0:T(8,128)(2,1)S(1)}, u32[]{:S(2)}, u32[]{:S(2)}) collective-permute-start(bf16[576,512]{1,0:T(8,128)(2,1)S(1)} %collective-permute-done.6.refs_2_), channel_id=1, source_target_pairs={{0,4},{4,0},{1,5},{5,1},{2,6},{6,2},{3,7},{7,3},{8,12},{12,8},{9,1... | collective-permute-start | bytes 1769480 | tf_op jit(solution)/shard_map/ppermute | solution.py:43
  78.3 1.9 %collective-permute-start.12 = (bf16[576,256]{1,0:T(8,128)(2,1)}, bf16[576,256]{1,0:T(8,128)(2,1)}, u32[]{:S(2)}, u32[]{:S(2)}) collective-permute-start(bf16[576,256]{1,0:T(8,128)(2,1)} %collective-permute-done.7.refs_3_), channel_id=1, source_target_pairs={{0,4},{4,0},{1,5},{5,1},{2,6},{6,2},{3,7},{7,3},{8,12},{12,8},{9,1... | collective-permute-start | bytes 884744 | tf_op jit(solution)/shard_map/ppermute | solution.py:43
  78.3 2.3 %collective-permute-start.13 = (bf16[576,256]{1,0:T(8,128)(2,1)}, bf16[576,256]{1,0:T(8,128)(2,1)}, u32[]{:S(2)}, u32[]{:S(2)}) collective-permute-start(bf16[576,256]{1,0:T(8,128)(2,1)} %collective-permute-done.8.refs_4_), channel_id=1, source_target_pairs={{0,4},{4,0},{1,5},{5,1},{2,6},{6,2},{3,7},{7,3},{8,12},{12,8},{9,1... | collective-permute-start | bytes 884744 | tf_op jit(solution)/shard_map/ppermute | solution.py:43
  80.7 1.3 copy-start
  86.8 20.4 %collective-permute-start.20 = (bf16[144,512]{1,0:T(8,128)(2,1)S(1)}, bf16[144,512]{1,0:T(8,128)(2,1)S(1)}, u32[]{:S(2)}, u32[]{:S(2)}) collective-permute-start(bf16[144,512]{1,0:T(8,128)(2,1)S(1)} %get-tuple-element.38), channel_id=1, source_target_pairs={{0,8},{8,0},{16,24},{24,16},{32,40},{40,32},{48,56},{56,48},{64,72... | collective-permute-start | bytes 442376 | tf_op jit(solution)/shard_map/ppermute | solution.py:51
  92.6 17.9 %collective-permute-start.18 = (bf16[144,512]{1,0:T(8,128)(2,1)S(1)}, bf16[144,512]{1,0:T(8,128)(2,1)S(1)}, u32[]{:S(2)}, u32[]{:S(2)}) collective-permute-start(bf16[144,512]{1,0:T(8,128)(2,1)S(1)} %get-tuple-element.36), channel_id=1, source_target_pairs={{0,72},{8,64},{16,88},{24,80},{32,104},{40,96},{48,120},{56,112},{... | collective-permute-start | bytes 442376 | tf_op jit(solution)/shard_map/ppermute | solution.py:51
  93.5 17.8 %collective-permute-start.19 = (bf16[144,512]{1,0:T(8,128)(2,1)S(1)}, bf16[144,512]{1,0:T(8,128)(2,1)S(1)}, u32[]{:S(2)}, u32[]{:S(2)}) collective-permute-start(bf16[144,512]{1,0:T(8,128)(2,1)S(1)} %get-tuple-element.37), channel_id=1, source_target_pairs={{0,64},{8,72},{16,80},{24,88},{32,96},{40,104},{48,112},{56,120},{... | collective-permute-start | bytes 442376 | tf_op jit(solution)/shard_map/ppermute | solution.py:51
  99.9 11.5 %collective-permute-start.16 = (bf16[144,512]{1,0:T(8,128)(2,1)S(1)}, bf16[144,512]{1,0:T(8,128)(2,1)S(1)}, u32[]{:S(2)}, u32[]{:S(2)}) collective-permute-start(bf16[144,512]{1,0:T(8,128)(2,1)S(1)} %get-tuple-element.34), channel_id=1, source_target_pairs={{0,200},{8,192},{16,216},{24,208},{32,232},{40,224},{48,248},{56,2... | collective-permute-start | bytes 442376 | tf_op jit(solution)/shard_map/ppermute | solution.py:51
  101.4 9.9 %collective-permute-start.17 = (bf16[144,512]{1,0:T(8,128)(2,1)S(1)}, bf16[144,512]{1,0:T(8,128)(2,1)S(1)}, u32[]{:S(2)}, u32[]{:S(2)}) collective-permute-start(bf16[144,512]{1,0:T(8,128)(2,1)S(1)} %get-tuple-element.35), channel_id=1, source_target_pairs={{0,192},{8,200},{16,208},{24,216},{32,224},{40,232},{48,240},{56,2... | collective-permute-start | bytes 442376 | tf_op jit(solution)/shard_map/ppermute | solution.py:51
  107.2 7.7 %collective-permute-start.14 = (bf16[144,512]{1,0:T(8,128)(2,1)S(1)}, bf16[144,512]{1,0:T(8,128)(2,1)S(1)}, u32[]{:S(2)}, u32[]{:S(2)}) collective-permute-start(bf16[144,512]{1,0:T(8,128)(2,1)S(1)} %get-tuple-element.32), channel_id=1, source_target_pairs={{0,136},{8,128},{16,152},{24,144},{32,168},{40,160},{48,184},{56,1... | collective-permute-start | bytes 442376 | tf_op jit(solution)/shard_map/ppermute | solution.py:51
  110.4 7.3 %collective-permute-start.15 = (bf16[144,512]{1,0:T(8,128)(2,1)S(1)}, bf16[144,512]{1,0:T(8,128)(2,1)S(1)}, u32[]{:S(2)}, u32[]{:S(2)}) collective-permute-start(bf16[144,512]{1,0:T(8,128)(2,1)S(1)} %get-tuple-element.33), channel_id=1, source_target_pairs={{0,128},{8,136},{16,144},{24,152},{32,160},{40,168},{48,176},{56,1... | collective-permute-start | bytes 442376 | tf_op jit(solution)/shard_map/ppermute | solution.py:51
  118.3 7.1 %collective-permute-start.21 = (bf16[32,640]{1,0:T(8,128)(2,1)S(1)}, bf16[32,640]{1,0:T(8,128)(2,1)S(1)}, u32[]{:S(2)}, u32[]{:S(2)}) collective-permute-start(bf16[32,640]{1,0:T(8,128)(2,1)S(1)} %get-tuple-element.42), channel_id=1, source_target_pairs={{0,48},{8,56},{16,0},{24,8},{32,16},{40,24},{48,32},{56,40},{1,49}... | collective-permute-start | bytes 122888 | tf_op jit(solution)/shard_map/ppermute | solution.py:56
  120.9 8.0 %collective-permute-start.22 = (bf16[32,640]{1,0:T(8,128)(2,1)S(1)}, bf16[32,640]{1,0:T(8,128)(2,1)S(1)}, u32[]{:S(2)}, u32[]{:S(2)}) collective-permute-start(bf16[32,640]{1,0:T(8,128)(2,1)S(1)} %get-tuple-element.43), channel_id=1, source_target_pairs={{0,32},{8,40},{16,48},{24,56},{32,0},{40,8},{48,16},{56,24},{1,33}... | collective-permute-start | bytes 122888 | tf_op jit(solution)/shard_map/ppermute | solution.py:56
  123.3 6.4 %collective-permute-start.23 = (bf16[32,640]{1,0:T(8,128)(2,1)S(1)}, bf16[32,640]{1,0:T(8,128)(2,1)S(1)}, u32[]{:S(2)}, u32[]{:S(2)}) collective-permute-start(bf16[32,640]{1,0:T(8,128)(2,1)S(1)} %get-tuple-element.44), channel_id=1, source_target_pairs={{0,16},{8,24},{16,32},{24,40},{32,48},{40,56},{48,0},{56,8},{1,17}... | collective-permute-start | bytes 122888 | tf_op jit(solution)/shard_map/ppermute | solution.py:56
Sparse Core Ops, SparseCore 0:
  55.3 24.2 all-gather.1

commit v2 on v1

--- a/solution.py
+++ b/solution.py
@@ -25,6 +25,8 @@
 PAIR = HOT_GRP * HALF
 CHUNK = 2 * PAIR
 NEVER = -1e30
+SCALE = QK**-0.5
+LOG2_E = 1.4426950408889634
 N_FAR = N_Z // 2
 f32 = jnp.float32
 bf16 = jnp.bfloat16
@@ -32,7 +34,7 @@
 VMEM = pl.BlockSpec(memory_space=pltpu.VMEM)
 SMEM = pl.BlockSpec(memory_space=pltpu.SMEM)
 ANY = pl.BlockSpec(memory_space=pltpu.HBM)
-PARAMS = pltpu.CompilerParams(vmem_limit_bytes=32 * 1024 * 1024)
+MIB = 1024 * 1024
 
 
 def shift_rep(a, by):
@@ -43,17 +45,20 @@
     return lax.ppermute(a, "c", [(0, 1), (1, 0)])
 
 
-def back_xz(a, hop, flip):
+def cross_x(a, bits):
+    return lax.ppermute(a, "x", [(i, i ^ bits) for i in range(N_X)])
+
+
+def cross_z(a, bits):
+    return lax.ppermute(a, "z", [(i, i ^ bits) for i in range(N_Z)])
+
+
+def cross_xz(a, bits_x, bits_z):
     pairs = []
     for x in range(N_X):
         for z in range(N_Z):
-            pairs.append((x * N_Z + z, (x - hop) % N_X * N_Z + (z ^ flip)))
+            pairs.append((x * N_Z + z, (x ^ bits_x) * N_Z + (z ^ bits_z)))
     return lax.ppermute(a, ("x", "z"), pairs)
-
-
-def back_far(a, hop):
-    pairs = [(z, (z - 2 * hop) % N_Z) for z in range(N_Z)]
-    return lax.ppermute(a, "z", pairs)
 
 
 def column(hot_ref, slot, rank, half):
@@ -101,11 +106,19 @@
 
 def pass_on_kernel(hot_ref, from_left, from_right, right_in, left_in, right_ref, left_ref):
     rank = lax.axis_index("rep")
+    right_ref[:, PAIR:] = right_in[:, PAIR:]
+    left_ref[:, :PAIR] = left_in[:, :PAIR]
     for slot in range(HOT_GRP):
         a = slice(slot * HALF, (slot + 1) * HALF)
         b = slice(PAIR + slot * HALF, PAIR + (slot + 1) * HALF)
-
-        @pl.when(hot_ref[slot] // PER_DEV != rank)
+        here = hot_ref[slot] // PER_DEV == rank
+
+        @pl.when(here)
+        def _():
+            right_ref[:, a] = right_in[:, a]
+            left_ref[:, b] = left_in[:, b]
+
+        @pl.when(jnp.logical_not(here))
         def _():
             right_ref[:, a] = from_left[:, a]
             left_ref[:, b] = from_right[:, a]
@@ -118,6 +131,11 @@
         b = slice(PAIR + slot * HALF, PAIR + (slot + 1) * HALF)
         away = (hot_ref[slot] // PER_DEV - rank + N_REP) % N_REP
 
+        @pl.when(away == 0)
+        def _():
+            mine_ref[:, a] = mine_in[:, a]
+            mine_ref[:, b] = mine_in[:, b]
+
         @pl.when(away >= 2)
         def _():
             mine_ref[:, a] = from_left[:, a]
@@ -145,25 +163,19 @@
 PLACES = ((0, 0, 2), (3, 0, 2), (1, 0, 2), (2, 0, 1), (2, 1, 1))
 
 
-def attend_kernel(hop, q_ref, len_ref, hot_ref, hot_other_ref, *refs):
+def attend_kernel(q_ref, len_ref, hot_ref, hot_other_ref, *refs):
     n = len(PLACES)
     key_refs, outs = refs[: N_C * n], refs[N_C * n :]
     x, z, c = lax.axis_index("x"), lax.axis_index("z"), lax.axis_index("c")
     rank = lax.axis_index("rep")
     group = (x * N_Z + z) * N_C + c
-    n_own = q_ref.shape[0] // (N_X * N_Z)
-    first = (x - hop + N_X) % N_X * N_Z
-    q = jnp.concatenate(
-        [
-            q_ref[
-                pl.ds(pl.multiple_of((first + 2 * far + ((z + flip) & 1)) * n_own, n_own), n_own), :
-            ]
-            for flip in range(2)
-            for far in range(N_FAR)
-        ],
-        axis=0,
-    )
-    lens = jnp.concatenate([len_ref[...]] * (q.shape[0] // len_ref.shape[0]), axis=0)
+    q = q_ref[...]
+    count = len_ref.shape[0]
+    line = lax.broadcasted_iota(jnp.int32, (count, 1), 0)
+    lens = jnp.zeros((count, 1), jnp.int32)
+    for i in range(count):
+        lens = jnp.where(line == i, len_ref[i], lens)
+    lens = jnp.concatenate([lens] * (q.shape[0] // count), axis=0)
     lane = lax.broadcasted_iota(jnp.int32, (1, HALF), 1)
     parts = []
     for other in range(N_C):
@@ -181,7 +193,7 @@
                 ],
                 axis=1,
             )
-            s = jnp.dot(q, k_ref[...], preferred_element_type=f32) * (QK**-0.5)
+            s = jnp.dot(q, k_ref[...], preferred_element_type=f32)
             scores.append(jnp.where(rows < lens, s, NEVER))
         peak = scores[0].max(axis=1, keepdims=True)
         for s in scores[1:]:
@@ -189,7 +201,7 @@
         total = jnp.zeros_like(peak)
         numer = None
         for s, k_ref in zip(scores, keys):
-            w = jnp.exp(s - peak).astype(bf16)
+            w = jnp.exp2((s - peak) * (SCALE * LOG2_E)).astype(bf16)
             total = total + jnp.sum(w.astype(f32), axis=1, keepdims=True)
             v = lax.dot_general(
                 w, k_ref[:LAT, :], (((1,), (1,)), ((), ())), preferred_element_type=f32
@@ -199,12 +211,12 @@
     top = jnp.maximum(parts[0][0], parts[1][0])
     numer, total = 0.0, 0.0
     for peak, t, v in parts:
-        f = jnp.where(peak > NEVER / 2, jnp.exp(peak - top), 0.0)
+        f = jnp.where(peak > NEVER / 2, jnp.exp((peak - top) * SCALE), 0.0)
         numer = numer + v * f
         total = total + t * f
     o = (numer * (1.0 / jnp.maximum(total, 1.0))).astype(bf16)
     lanes = lax.broadcasted_iota(jnp.int32, (q.shape[0], 128), 1)
-    stats = jnp.where(lanes == 0, top, total).T[:2, :]
+    stats = jnp.where(lanes == 0, top * SCALE, total).T[:2, :]
     rows = o.shape[0] // 2
     for flip, o_ref in enumerate(outs):
         o_ref[:rows, :] = o[flip * rows : (flip + 1) * rows]
@@ -217,11 +229,10 @@
 
 def merge_kernel(*refs):
     n_in = N_X * 2
-    parts, sends, (own_ref, stat_ref), (acc_ref,) = (
+    parts, sends, (own_ref, stat_ref) = (
         refs[:n_in],
         refs[n_in : n_in + N_FAR - 1],
-        refs[n_in + N_FAR - 1 : n_in + N_FAR + 1],
-        refs[n_in + N_FAR + 1 :],
+        refs[n_in + N_FAR - 1 :],
     )
     rows = parts[0].shape[0] - 16
     tops, totals = [], []
@@ -236,29 +247,25 @@
     table = [w * inv for w in weights] + [top, total]
     table.append(jnp.zeros((128 - len(table), rows), f32))
     table = jnp.concatenate(table, axis=0).T
-    acc = 0.0
-    for i, p in enumerate(parts):
-        acc = acc + p[:rows, :].astype(f32) * table[:, i : i + 1]
-    acc_ref[:, :LAT] = acc
-    acc_ref[:, LAT:] = table
-    far = lax.axis_index("z") // 2
     n = rows // N_FAR
-
-    def block(hop):
-        return acc_ref[pl.ds(pl.multiple_of((far - hop + N_FAR) % N_FAR * n, n), n), :]
-
     lane = lax.broadcasted_iota(jnp.int32, (n, 128), 1)
-    for hop, ref in enumerate(sends, 1):
-        b = block(hop)
-        ref[:, :LAT] = b[:, :LAT].astype(bf16)
-        top, total = b[:, LAT + n_in : LAT + n_in + 1], b[:, LAT + n_in + 1 : LAT + n_in + 2]
-        packed = jnp.zeros((n, 128), f32)
-        for i, term in enumerate(three_terms(top) + three_terms(total)):
-            packed = jnp.where(lane == i, term.astype(f32), packed)
-        ref[:, LAT:] = packed.astype(bf16)
-    b = block(0)
-    own_ref[...] = b[:, :LAT]
-    stat_ref[...] = b[:, LAT:]
+    for far in range(N_FAR):
+        at = slice(far * n, (far + 1) * n)
+        acc = 0.0
+        for i, p in enumerate(parts):
+            acc = acc + p[at, :].astype(f32) * table[at, i : i + 1]
+        if far:
+            ref = sends[far - 1]
+            ref[:, :LAT] = acc.astype(bf16)
+            packed = jnp.zeros((n, 128), f32)
+            terms = three_terms(table[at, n_in : n_in + 1])
+            terms += three_terms(table[at, n_in + 1 : n_in + 2])
+            for i, term in enumerate(terms):
+                packed = jnp.where(lane == i, term.astype(f32), packed)
+            ref[:, LAT:] = packed.astype(bf16)
+        else:
+            own_ref[...] = acc
+            stat_ref[...] = table[at]
 
 
 def finish_kernel(own_ref, stat_ref, *refs):
@@ -279,13 +286,13 @@
         out_ref[:, head * LAT : (head + 1) * LAT] = o[head * count : (head + 1) * count].astype(bf16)
 
 
-def call(kernel, outs, in_specs, args, **more):
+def call(kernel, outs, in_specs, args, mib=16, **more):
     return pl.pallas_call(
         kernel,
         out_shape=tuple(jax.ShapeDtypeStruct(*o) for o in outs),
         in_specs=in_specs,
         out_specs=(VMEM,) * len(outs),
-        compiler_params=PARAMS,
+        compiler_params=pltpu.CompilerParams(vmem_limit_bytes=mib * MIB),
         **more,
     )(*args)
 
@@ -300,6 +307,7 @@
         [pair, pair],
         [SMEM, ANY],
         [hot_ids, by_column],
+        mib=50,
         scratch_shapes=[pltpu.SemaphoreType.DMA((4,))],
     )
     up, down = shift_rep(up, 1), shift_rep(down, -1)
@@ -308,6 +316,7 @@
         [chunk] * 3,
         [SMEM, ANY],
         [hot_ids, by_column],
+        mib=50,
         scratch_shapes=[pltpu.SemaphoreType.DMA((12,))],
     )
     right, left = call(
@@ -315,7 +324,6 @@
         [chunk] * 2,
         [SMEM] + [VMEM] * 4,
         [hot_ids, up, down, right, left],
-        input_output_aliases={3: 0, 4: 1},
     )
     from_left, from_right = shift_rep(right, 1), shift_rep(left, -1)
     (mine,) = call(
@@ -323,12 +331,13 @@
         [chunk],
         [SMEM] + [VMEM] * 3,
         [hot_ids, from_left, from_right, mine],
-        input_output_aliases={3: 0},
     )
 
     own = queries.reshape(count, -1, WIDTH).transpose(1, 0, 2).reshape(-1, WIDTH)
-    asked = lax.all_gather(own, "z", tiled=True)
-    asked = lax.all_gather(asked, "x", tiled=True)
+    near = own
+    for bits in (2, 4, 1):
+        near = jnp.concatenate([near, cross_z(near, bits)], axis=0)
+    asked = [near] + [cross_x(near, bits) for bits in range(1, N_X)]
     hot_other = swap_core(hot_ids)
 
     of_left, of_right = shift_rep(mine, 1), shift_rep(mine, -1)
@@ -336,19 +345,19 @@
     keys = [mine, of_left, of_right, far_a, far_b]
     keys = keys + [swap_core(k) for k in keys]
 
-    rows = asked.shape[0] // N_X // 2
+    rows = near.shape[0] // 2
     part = ((rows + 16, LAT), bf16)
-    lens = lengths[:, None]
     parts = []
     for hop in (2, 1, 3, 0):
         same, flipped = call(
-            functools.partial(attend_kernel, hop),
+            attend_kernel,
             [part, part],
-            [VMEM, VMEM, SMEM, SMEM] + [VMEM] * len(keys),
-            [asked, lens, hot_ids, hot_other] + keys,
+            [VMEM, SMEM, SMEM, SMEM] + [VMEM] * len(keys),
+            [asked[hop], lengths, hot_ids, hot_other] + keys,
         )
-        parts.append(back_xz(flipped, hop, 1))
-        parts.append(back_xz(same, hop, 0) if hop else same)
+        lengths, same, flipped = lax.optimization_barrier((lengths, same, flipped))
+        parts.append(cross_xz(flipped, hop, 1))
+        parts.append(cross_xz(same, hop, 0) if hop else same)
 
     n = own.shape[0]
     message = ((n, LAT + 128), bf16)
@@ -357,9 +366,8 @@
         [message] * (N_FAR - 1) + [((n, LAT), f32), ((n, 128), f32)],
         [VMEM] * len(parts),
         parts,
-        scratch_shapes=[pltpu.VMEM((rows, LAT + 128), f32)],
-    )
-    sends = [back_far(s, hop) for hop, s in enumerate(sends, 1)]
+    )
+    sends = [cross_z(s, 2 * far) for far, s in enumerate(sends, 1)]
     (out,) = call(
         finish_kernel,
         [((count, n // count * LAT), bf16)],

time: 139 us -> 108 us (0.78)
  blocking collectives: 30.7 us -> 0 us
  starting transfers between devices: 32.2 us -> 50.1 us
  between operations: 13.6 us -> 0.18 us
  local copies, waits for them, and re-layouts: 5.2 us -> 0.82 us
    all_gather x1 -> x0, blocking collectives: 30.7 us -> none  [on_device(): asked = lax.all_gather(own, 'z', tiled=True)]
    ppermute x10 -> x16, starting transfers between devices: 17.4 us -> 36.3 us  [the longest x6 20.1 us: cross_z(): return lax.ppermute(a, 'z', [(i, i ^ bits) for i in range(N_Z)])]
    ppermute x10 -> x16, waiting for transfers between devices: 10.7 us -> 17.3 us  [the longest x6 11.7 us: cross_z(): return lax.ppermute(a, 'z', [(i, i ^ bits) for i in range(N_Z)])]
    ppermute x8, waiting for transfers between devices: 20.2 us -> 15 us  [shift_rep(): return lax.ppermute(a, 'rep', [(i, (i + by) % N_REP) for i in range(N_REP)])]
    unnamed x10 -> x8, local copies, waits for them, and re-layouts: 4.31 us -> 0.67 us
  transfers between devices with their start and end apart: 25 -> 30, of which waited for: 9 -> 11; matrix products, arithmetic and copies ran while one was open for 1% -> 0% of each run, Pallas kernels for 12% -> 18%
where the time goes in v2:
time: 108 us; the launch traced here: 107 us
  starting transfers between devices  50.1 us (46%)
  waiting for transfers between devices  32.3 us (30%)
  Pallas kernels  23.2 us (21%)
    pallas_call x10, Pallas kernels, call(): pl.pallas_call(kernel, out_shape=tuple((jax.ShapeDtypeStruct(*o) for o in...  23.2 us
    ppermute x6, starting transfers between devices, cross_z(): return lax.ppermute(a, 'z', [(i, i ^ bits) for i in range(N_Z)])  20.1 us
    ppermute x8, waiting for transfers between devices, shift_rep(): return lax.ppermute(a, 'rep', [(i, (i + by) % N_REP) for i in range(N_REP)])  15 us
    ppermute x8, starting transfers between devices, shift_rep(): return lax.ppermute(a, 'rep', [(i, (i + by) % N_REP) for i in range(N_REP)])  13.2 us
    ppermute x7, starting transfers between devices, cross_xz(): return lax.ppermute(a, ('x', 'z'), pairs)  12.6 us
    ppermute x6, waiting for transfers between devices, cross_z(): return lax.ppermute(a, 'z', [(i, i ^ bits) for i in range(N_Z)])  11.7 us
    ppermute x7, waiting for transfers between devices, cross_xz(): return lax.ppermute(a, ('x', 'z'), pairs)  5.02 us
    ppermute x3, starting transfers between devices, cross_x(): return lax.ppermute(a, 'x', [(i, i ^ bits) for i in range(N_X)])  3.53 us
  transfers between devices with their start and end apart: 30, of which 11 were waited for; matrix products, arithmetic and copies ran while one was open for 0% of the time, Pallas kernels for 18%

profile of v2, /device:TPU:6, one launch (start us, length us, event | category | flops | bytes accessed | tf_op | source)
XLA Modules:
  0.0 106.7 jit_solution(12966823125748114156)
XLA Ops:
  0.7 1.7 %shard_map.46 = (bf16[576,256]{1,0:T(8,128)(2,1)S(1)}, bf16[576,256]{1,0:T(8,128)(2,1)S(1)}) custom-call(s32[2]{0:T(128)S(1)} %copy-done, bf16[576,4096]{1,0:T(8,128)(2,1)} %bitcast.4), custom_call_target="tpu_custom_call" | custom-call | tf_op jit(solution)/shard_map/pallas_call | solution.py:290
  2.4 1.7 %collective-permute-start.5 = (bf16[576,256]{1,0:T(8,128)(2,1)S(1)}, bf16[576,256]{1,0:T(8,128)(2,1)S(1)}, u32[]{:S(2)}, u32[]{:S(2)}) collective-permute-start(bf16[576,256]{1,0:T(8,128)(2,1)S(1)} %get-tuple-element.36), channel_id=1, source_target_pairs={{0,1},{1,2},{2,3},{3,0},{4,5},{5,6},{6,7},{7,4},{8,9},{9,10},{10,1... | collective-permute-start | bytes 884744 | tf_op jit(solution)/shard_map/ppermute | solution.py:41
  4.1 1.7 %collective-permute-start.6 = (bf16[576,256]{1,0:T(8,128)(2,1)S(1)}, bf16[576,256]{1,0:T(8,128)(2,1)S(1)}, u32[]{:S(2)}, u32[]{:S(2)}) collective-permute-start(bf16[576,256]{1,0:T(8,128)(2,1)S(1)} %get-tuple-element.37), channel_id=1, source_target_pairs={{0,3},{1,0},{2,1},{3,2},{4,7},{5,4},{6,5},{7,6},{8,11},{9,8},{10,9... | collective-permute-start | bytes 884744 | tf_op jit(solution)/shard_map/ppermute | solution.py:41
  5.7 2.2 %shard_map.47 = (bf16[576,512]{1,0:T(8,128)(2,1)S(1)}, bf16[576,512]{1,0:T(8,128)(2,1)S(1)}, bf16[576,512]{1,0:T(8,128)(2,1)S(1)}) custom-call(s32[2]{0:T(128)S(1)} %copy-done, bf16[576,4096]{1,0:T(8,128)(2,1)} %bitcast.5), custom_call_target="tpu_custom_call" | custom-call | tf_op jit(solution)/shard_map/pallas_call | solution.py:290
  8.0 4.5 %collective-permute-done.5.from_left = bf16[576,256]{1,0:T(8,128)(2,1)S(1)} collective-permute-done((bf16[576,256]{1,0:T(8,128)(2,1)S(1)}, bf16[576,256]{1,0:T(8,128)(2,1)S(1)}, u32[]{:S(2)}, u32[]{:S(2)}) %collective-permute-start.5) | collective-permute-done | bytes 294944 | tf_op jit(solution)/shard_map/ppermute | solution.py:41
  13.2 1.7 %collective-permute-start.7 = (bf16[576,512]{1,0:T(8,128)(2,1)S(1)}, bf16[576,512]{1,0:T(8,128)(2,1)S(1)}, u32[]{:S(2)}, u32[]{:S(2)}) collective-permute-start(bf16[576,512]{1,0:T(8,128)(2,1)S(1)} %get-tuple-element.40), channel_id=1, source_target_pairs={{0,1},{1,2},{2,3},{3,0},{4,5},{5,6},{6,7},{7,4},{8,9},{9,10},{10,1... | collective-permute-start | bytes 1769480 | tf_op jit(solution)/shard_map/ppermute | solution.py:41
  14.9 1.7 %collective-permute-start.8 = (bf16[576,512]{1,0:T(8,128)(2,1)S(1)}, bf16[576,512]{1,0:T(8,128)(2,1)S(1)}, u32[]{:S(2)}, u32[]{:S(2)}) collective-permute-start(bf16[576,512]{1,0:T(8,128)(2,1)S(1)} %get-tuple-element.41), channel_id=1, source_target_pairs={{0,3},{1,0},{2,1},{3,2},{4,7},{5,4},{6,5},{7,6},{8,11},{9,8},{10,9... | collective-permute-start | bytes 1769480 | tf_op jit(solution)/shard_map/ppermute | solution.py:41
  16.7 3.4 %collective-permute-start = (bf16[32,576]{1,0:T(8,128)(2,1)S(1)}, bf16[32,576]{1,0:T(8,128)(2,1)S(1)}, u32[]{:S(2)}, u32[]{:S(2)}) collective-permute-start(bf16[32,576]{1,0:T(8,128)(2,1)S(1)} %bitcast.6), channel_id=1, source_target_pairs={{0,16},{8,24},{16,0},{24,8},{32,48},{40,56},{48,32},{56,40},{1,17}... | collective-permute-start | bytes 110600 | tf_op jit(solution)/shard_map/ppermute | solution.py:53
  20.0 2.0 %collective-permute-done = bf16[32,576]{1,0:T(8,128)(2,1)S(1)} collective-permute-done((bf16[32,576]{1,0:T(8,128)(2,1)S(1)}, bf16[32,576]{1,0:T(8,128)(2,1)S(1)}, u32[]{:S(2)}, u32[]{:S(2)}) %collective-permute-start) | collective-permute-done | bytes 36896 | tf_op jit(solution)/shard_map/ppermute | solution.py:53
  22.0 7.0 %collective-permute-start.1 = (bf16[64,576]{1,0:T(8,128)(2,1)S(1)}, bf16[64,576]{1,0:T(8,128)(2,1)S(1)}, u32[]{:S(2)}, u32[]{:S(2)}) collective-permute-start(bf16[64,576]{1,0:T(8,128)(2,1)S(1)} %pad_maximum_fusion.2), channel_id=1, source_target_pairs={{0,32},{8,40},{16,48},{24,56},{32,0},{40,8},{48,16},{56,24},{1,33}... | collective-permute-start | bytes 221192 | tf_op jit(solution)/shard_map/ppermute | solution.py:53
  30.6 2.5 %collective-permute-start.10 = (bf16[576,512]{1,0:T(8,128)(2,1)S(1)}, bf16[576,512]{1,0:T(8,128)(2,1)S(1)}, u32[]{:S(2)}, u32[]{:S(2)}) collective-permute-start(bf16[576,512]{1,0:T(8,128)(2,1)S(1)} %shard_map.49.refs_0_), channel_id=1, source_target_pairs={{0,3},{1,0},{2,1},{3,2},{4,7},{5,4},{6,5},{7,6},{8,11},{9,8},{10,9... | collective-permute-start | bytes 1769480 | tf_op jit(solution)/shard_map/ppermute | solution.py:41
  33.1 1.8 %collective-permute-start.2 = (bf16[128,576]{1,0:T(8,128)(2,1)S(1)}, bf16[128,576]{1,0:T(8,128)(2,1)S(1)}, u32[]{:S(2)}, u32[]{:S(2)}) collective-permute-start(bf16[128,576]{1,0:T(8,128)(2,1)S(1)} %pad_maximum_fusion.1), channel_id=1, source_target_pairs={{0,8},{8,0},{16,24},{24,16},{32,40},{40,32},{48,56},{56,48},{1,9},... | collective-permute-start | bytes 442376 | tf_op jit(solution)/shard_map/ppermute | solution.py:53
  34.8 3.6 %collective-permute-done.2 = bf16[128,576]{1,0:T(8,128)(2,1)S(1)} collective-permute-done((bf16[128,576]{1,0:T(8,128)(2,1)S(1)}, bf16[128,576]{1,0:T(8,128)(2,1)S(1)}, u32[]{:S(2)}, u32[]{:S(2)}) %collective-permute-start.2) | collective-permute-done | bytes 147488 | tf_op jit(solution)/shard_map/ppermute | solution.py:53
  38.5 1.6 %collective-permute-start.3 = (bf16[256,576]{1,0:T(8,128)(2,1)S(1)}, bf16[256,576]{1,0:T(8,128)(2,1)S(1)}, u32[]{:S(2)}, u32[]{:S(2)}) collective-permute-start(bf16[256,576]{1,0:T(8,128)(2,1)S(1)} %pad_maximum_fusion.q_ref), channel_id=1, source_target_pairs={{0,128},{64,192},{128,0},{192,64},{1,129},{65,193},{129,1},{193,65... | collective-permute-start | bytes 884744 | tf_op jit(solution)/shard_map/ppermute | solution.py:49
  40.1 4.0 %collective-permute-done.9.refs_1_ = bf16[576,512]{1,0:T(8,128)(2,1)S(1)} collective-permute-done((bf16[576,512]{1,0:T(8,128)(2,1)S(1)}, bf16[576,512]{1,0:T(8,128)(2,1)S(1)}, u32[]{:S(2)}, u32[]{:S(2)}) %collective-permute-start.9) | collective-permute-done | bytes 589856 | tf_op jit(solution)/shard_map/ppermute | solution.py:41
  44.3 3.2 %collective-permute-start.12 = (bf16[576,256]{1,0:T(8,128)(2,1)S(1)}, bf16[576,256]{1,0:T(8,128)(2,1)S(1)}, u32[]{:S(2)}, u32[]{:S(2)}) collective-permute-start(bf16[576,256]{1,0:T(8,128)(2,1)S(1)} %slice.9), channel_id=1, source_target_pairs={{0,3},{1,0},{2,1},{3,2},{4,7},{5,4},{6,5},{7,6},{8,11},{9,8},{10,9... | collective-permute-start | bytes 884744 | tf_op jit(solution)/shard_map/ppermute | solution.py:41
  48.1 4.1 %collective-permute-done.11.refs_3_ = bf16[576,256]{1,0:T(8,128)(2,1)S(1)} collective-permute-done((bf16[576,256]{1,0:T(8,128)(2,1)S(1)}, bf16[576,256]{1,0:T(8,128)(2,1)S(1)}, u32[]{:S(2)}, u32[]{:S(2)}) %collective-permute-start.11) | collective-permute-done | bytes 294944 | tf_op jit(solution)/shard_map/ppermute | solution.py:41
  52.1 2.3 %collective-permute-done.12.refs_4_ = bf16[576,256]{1,0:T(8,128)(2,1)S(1)} collective-permute-done((bf16[576,256]{1,0:T(8,128)(2,1)S(1)}, bf16[576,256]{1,0:T(8,128)(2,1)S(1)}, u32[]{:S(2)}, u32[]{:S(2)}) %collective-permute-start.12) | collective-permute-done | bytes 294944 | tf_op jit(solution)/shard_map/ppermute | solution.py:41
  56.5 4.1 %shard_map.50 = (bf16[144,512]{1,0:T(8,128)(2,1)S(1)}, bf16[144,512]{1,0:T(8,128)(2,1)S(1)}) custom-call(bf16[256,576]{1,0:T(8,128)(2,1)S(1)} %collective-permute-done.3.q_ref, s32[16]{0:T(128)S(1)} %copy-done.2, s32[2]{0:T(128)S(1)} %copy-done.1, s32[2]{0:T(128)S(1)} %collective-permute-done.4.hot_other_ref, bf16[576,512]{1,0:T(8,128)(2,1)S(1)} %shard_map.49.refs_0_, ...), custom_call_target="tpu_custom_call" | custom-call | tf_op jit(solution)/shard_map/pallas_call | solution.py:290
  60.6 3.6 %collective-permute-start.18 = (bf16[144,512]{1,0:T(8,128)(2,1)S(1)}, bf16[144,512]{1,0:T(8,128)(2,1)S(1)}, u32[]{:S(2)}, u32[]{:S(2)}) collective-permute-start(bf16[144,512]{1,0:T(8,128)(2,1)S(1)} %get-tuple-element.45), channel_id=1, source_target_pairs={{0,136},{8,128},{16,152},{24,144},{32,168},{40,160},{48,184},{56,1... | collective-permute-start | bytes 442376 | tf_op jit(solution)/shard_map/ppermute | solution.py:61
  64.1 1.4 %collective-permute-start.19 = (bf16[144,512]{1,0:T(8,128)(2,1)S(1)}, bf16[144,512]{1,0:T(8,128)(2,1)S(1)}, u32[]{:S(2)}, u32[]{:S(2)}) collective-permute-start(bf16[144,512]{1,0:T(8,128)(2,1)S(1)} %get-tuple-element.46), channel_id=1, source_target_pairs={{0,128},{8,136},{16,144},{24,152},{32,160},{40,168},{48,176},{56,1... | collective-permute-start | bytes 442376 | tf_op jit(solution)/shard_map/ppermute | solution.py:61
  65.5 4.1 %shard_map.51 = (bf16[144,512]{1,0:T(8,128)(2,1)S(1)}, bf16[144,512]{1,0:T(8,128)(2,1)S(1)}) custom-call(bf16[256,576]{1,0:T(8,128)(2,1)S(1)} %collective-permute-done.20.q_ref, s32[16]{0:T(128)S(1)} %copy-done.2, s32[2]{0:T(128)S(1)} %copy-done.1, s32[2]{0:T(128)S(1)} %collective-permute-done.4.hot_other_ref, bf16[576,512]{1,0:T(8,128)(2,1)S(1)} %shard_map.49.refs_0_, ...), custom_call_target="tpu_custom_call" | custom-call | tf_op jit(solution)/shard_map/pallas_call | solution.py:290
  69.6 1.3 %collective-permute-start.21 = (bf16[144,512]{1,0:T(8,128)(2,1)S(1)}, bf16[144,512]{1,0:T(8,128)(2,1)S(1)}, u32[]{:S(2)}, u32[]{:S(2)}) collective-permute-start(bf16[144,512]{1,0:T(8,128)(2,1)S(1)} %get-tuple-element.50), channel_id=1, source_target_pairs={{0,72},{8,64},{16,88},{24,80},{32,104},{40,96},{48,120},{56,112},{... | collective-permute-start | bytes 442376 | tf_op jit(solution)/shard_map/ppermute | solution.py:61
  72.7 4.1 %shard_map.52 = (bf16[144,512]{1,0:T(8,128)(2,1)S(1)}, bf16[144,512]{1,0:T(8,128)(2,1)S(1)}) custom-call(bf16[256,576]{1,0:T(8,128)(2,1)S(1)} %collective-permute-done.23.q_ref, s32[16]{0:T(128)S(1)} %copy-done.2, s32[2]{0:T(128)S(1)} %copy-done.1, s32[2]{0:T(128)S(1)} %collective-permute-done.4.hot_other_ref, bf16[576,512]{1,0:T(8,128)(2,1)S(1)} %shard_map.49.refs_0_, ...), custom_call_target="tpu_custom_call" | custom-call | tf_op jit(solution)/shard_map/pallas_call | solution.py:290
  76.8 2.8 %collective-permute-start.24 = (bf16[144,512]{1,0:T(8,128)(2,1)S(1)}, bf16[144,512]{1,0:T(8,128)(2,1)S(1)}, u32[]{:S(2)}, u32[]{:S(2)}) collective-permute-start(bf16[144,512]{1,0:T(8,128)(2,1)S(1)} %get-tuple-element.55), channel_id=1, source_target_pairs={{0,200},{8,192},{16,216},{24,208},{32,232},{40,224},{48,248},{56,2... | collective-permute-start | bytes 442376 | tf_op jit(solution)/shard_map/ppermute | solution.py:61
  79.6 4.1 %shard_map.53 = (bf16[144,512]{1,0:T(8,128)(2,1)S(1)}, bf16[144,512]{1,0:T(8,128)(2,1)S(1)}) custom-call(bf16[256,576]{1,0:T(8,128)(2,1)S(1)} %pad_maximum_fusion.q_ref, s32[16]{0:T(128)S(1)} %copy-done.2, s32[2]{0:T(128)S(1)} %copy-done.1, s32[2]{0:T(128)S(1)} %collective-permute-done.4.hot_other_ref, bf16[576,512]{1,0:T(8,128)(2,1)S(1)} %shard_map.49.refs_0_, ...), custom_call_target="tpu_custom_call" | custom-call | tf_op jit(solution)/shard_map/pallas_call | solution.py:290
  83.7 2.2 %collective-permute-start.25 = (bf16[144,512]{1,0:T(8,128)(2,1)S(1)}, bf16[144,512]{1,0:T(8,128)(2,1)S(1)}, u32[]{:S(2)}, u32[]{:S(2)}) collective-permute-start(bf16[144,512]{1,0:T(8,128)(2,1)S(1)} %get-tuple-element.56), channel_id=1, source_target_pairs={{0,192},{8,200},{16,208},{24,216},{32,224},{40,232},{48,240},{56,2... | collective-permute-start | bytes 442376 | tf_op jit(solution)/shard_map/ppermute | solution.py:61
  86.0 4.1 %collective-permute-done.25.refs_5_ = bf16[144,512]{1,0:T(8,128)(2,1)S(1)} collective-permute-done((bf16[144,512]{1,0:T(8,128)(2,1)S(1)}, bf16[144,512]{1,0:T(8,128)(2,1)S(1)}, u32[]{:S(2)}, u32[]{:S(2)}) %collective-permute-start.25) | collective-permute-done | bytes 147488 | tf_op jit(solution)/shard_map/ppermute | solution.py:61
  91.5 3.7 %collective-permute-start.27 = (bf16[32,640]{1,0:T(8,128)(2,1)S(1)}, bf16[32,640]{1,0:T(8,128)(2,1)S(1)}, u32[]{:S(2)}, u32[]{:S(2)}) collective-permute-start(bf16[32,640]{1,0:T(8,128)(2,1)S(1)} %get-tuple-element.64), channel_id=1, source_target_pairs={{0,16},{8,24},{16,0},{24,8},{32,48},{40,56},{48,32},{56,40},{1,17}... | collective-permute-start | bytes 122888 | tf_op jit(solution)/shard_map/ppermute | solution.py:53
  95.2 4.3 %collective-permute-start.28 = (bf16[32,640]{1,0:T(8,128)(2,1)S(1)}, bf16[32,640]{1,0:T(8,128)(2,1)S(1)}, u32[]{:S(2)}, u32[]{:S(2)}) collective-permute-start(bf16[32,640]{1,0:T(8,128)(2,1)S(1)} %get-tuple-element.65), channel_id=1, source_target_pairs={{0,32},{8,40},{16,48},{24,56},{32,0},{40,8},{48,16},{56,24},{1,33}... | collective-permute-start | bytes 122888 | tf_op jit(solution)/shard_map/ppermute | solution.py:53
  99.6 3.6 %collective-permute-done.28.refs_1_ = bf16[32,640]{1,0:T(8,128)(2,1)S(1)} collective-permute-done((bf16[32,640]{1,0:T(8,128)(2,1)S(1)}, bf16[32,640]{1,0:T(8,128)(2,1)S(1)}, u32[]{:S(2)}, u32[]{:S(2)}) %collective-permute-start.28) | collective-permute-done | bytes 40992 | tf_op jit(solution)/shard_map/ppermute | solution.py:53
  103.1 2.5 %collective-permute-done.29.refs_2_ = bf16[32,640]{1,0:T(8,128)(2,1)S(1)} collective-permute-done((bf16[32,640]{1,0:T(8,128)(2,1)S(1)}, bf16[32,640]{1,0:T(8,128)(2,1)S(1)}, u32[]{:S(2)}, u32[]{:S(2)}) %collective-permute-start.29) | collective-permute-done | bytes 40992 | tf_op jit(solution)/shard_map/ppermute | solution.py:53
  (53 shorter events, 10.2 us)
Async XLA Ops:
  0.7 28.3 %copy-start.1 = (s32[2]{0:T(128)S(1)}, s32[2]{0:T(128)}, u32[]{:S(2)}) copy-start(s32[2]{0:T(128)} %hot_ref.15) | copy-start | bytes 28
  2.4 10.1 %collective-permute-start.5 = (bf16[576,256]{1,0:T(8,128)(2,1)S(1)}, bf16[576,256]{1,0:T(8,128)(2,1)S(1)}, u32[]{:S(2)}, u32[]{:S(2)}) collective-permute-start(bf16[576,256]{1,0:T(8,128)(2,1)S(1)} %get-tuple-element.36), channel_id=1, source_target_pairs={{0,1},{1,2},{2,3},{3,0},{4,5},{5,6},{6,7},{7,4},{8,9},{9,10},{10,1... | collective-permute-start | bytes 884744 | tf_op jit(solution)/shard_map/ppermute | solution.py:41
  4.0 52.4 %copy-start.2 = (s32[16]{0:T(128)S(1)}, s32[16]{0:T(128)}, u32[]{:S(2)}) copy-start(s32[16]{0:T(128)} %len_ref.4) | copy-start | bytes 196
  4.1 8.5 %collective-permute-start.6 = (bf16[576,256]{1,0:T(8,128)(2,1)S(1)}, bf16[576,256]{1,0:T(8,128)(2,1)S(1)}, u32[]{:S(2)}, u32[]{:S(2)}) collective-permute-start(bf16[576,256]{1,0:T(8,128)(2,1)S(1)} %get-tuple-element.37), channel_id=1, source_target_pairs={{0,3},{1,0},{2,1},{3,2},{4,7},{5,4},{6,5},{7,6},{8,11},{9,8},{10,9... | collective-permute-start | bytes 884744 | tf_op jit(solution)/shard_map/ppermute | solution.py:41
  13.2 15.8 %collective-permute-start.7 = (bf16[576,512]{1,0:T(8,128)(2,1)S(1)}, bf16[576,512]{1,0:T(8,128)(2,1)S(1)}, u32[]{:S(2)}, u32[]{:S(2)}) collective-permute-start(bf16[576,512]{1,0:T(8,128)(2,1)S(1)} %get-tuple-element.40), channel_id=1, source_target_pairs={{0,1},{1,2},{2,3},{3,0},{4,5},{5,6},{6,7},{7,4},{8,9},{9,10},{10,1... | collective-permute-start | bytes 1769480 | tf_op jit(solution)/shard_map/ppermute | solution.py:41
  14.9 14.1 %collective-permute-start.8 = (bf16[576,512]{1,0:T(8,128)(2,1)S(1)}, bf16[576,512]{1,0:T(8,128)(2,1)S(1)}, u32[]{:S(2)}, u32[]{:S(2)}) collective-permute-start(bf16[576,512]{1,0:T(8,128)(2,1)S(1)} %get-tuple-element.41), channel_id=1, source_target_pairs={{0,3},{1,0},{2,1},{3,2},{4,7},{5,4},{6,5},{7,6},{8,11},{9,8},{10,9... | collective-permute-start | bytes 1769480 | tf_op jit(solution)/shard_map/ppermute | solution.py:41
  16.7 5.3 %collective-permute-start = (bf16[32,576]{1,0:T(8,128)(2,1)S(1)}, bf16[32,576]{1,0:T(8,128)(2,1)S(1)}, u32[]{:S(2)}, u32[]{:S(2)}) collective-permute-start(bf16[32,576]{1,0:T(8,128)(2,1)S(1)} %bitcast.6), channel_id=1, source_target_pairs={{0,16},{8,24},{16,0},{24,8},{32,48},{40,56},{48,32},{56,40},{1,17}... | collective-permute-start | bytes 110600 | tf_op jit(solution)/shard_map/ppermute | solution.py:53
  22.0 11.0 %collective-permute-start.1 = (bf16[64,576]{1,0:T(8,128)(2,1)S(1)}, bf16[64,576]{1,0:T(8,128)(2,1)S(1)}, u32[]{:S(2)}, u32[]{:S(2)}) collective-permute-start(bf16[64,576]{1,0:T(8,128)(2,1)S(1)} %pad_maximum_fusion.2), channel_id=1, source_target_pairs={{0,32},{8,40},{16,48},{24,56},{32,0},{40,8},{48,16},{56,24},{1,33}... | collective-permute-start | bytes 221192 | tf_op jit(solution)/shard_map/ppermute | solution.py:53
  29.7 14.4 %collective-permute-start.9 = (bf16[576,512]{1,0:T(8,128)(2,1)S(1)}, bf16[576,512]{1,0:T(8,128)(2,1)S(1)}, u32[]{:S(2)}, u32[]{:S(2)}) collective-permute-start(bf16[576,512]{1,0:T(8,128)(2,1)S(1)} %shard_map.49.refs_0_), channel_id=1, source_target_pairs={{0,1},{1,2},{2,3},{3,0},{4,5},{5,6},{6,7},{7,4},{8,9},{9,10},{10,1... | collective-permute-start | bytes 1769480 | tf_op jit(solution)/shard_map/ppermute | solution.py:41
  30.6 13.7 %collective-permute-start.10 = (bf16[576,512]{1,0:T(8,128)(2,1)S(1)}, bf16[576,512]{1,0:T(8,128)(2,1)S(1)}, u32[]{:S(2)}, u32[]{:S(2)}) collective-permute-start(bf16[576,512]{1,0:T(8,128)(2,1)S(1)} %shard_map.49.refs_0_), channel_id=1, source_target_pairs={{0,3},{1,0},{2,1},{3,2},{4,7},{5,4},{6,5},{7,6},{8,11},{9,8},{10,9... | collective-permute-start | bytes 1769480 | tf_op jit(solution)/shard_map/ppermute | solution.py:41
  33.1 5.4 %collective-permute-start.2 = (bf16[128,576]{1,0:T(8,128)(2,1)S(1)}, bf16[128,576]{1,0:T(8,128)(2,1)S(1)}, u32[]{:S(2)}, u32[]{:S(2)}) collective-permute-start(bf16[128,576]{1,0:T(8,128)(2,1)S(1)} %pad_maximum_fusion.1), channel_id=1, source_target_pairs={{0,8},{8,0},{16,24},{24,16},{32,40},{40,32},{48,56},{56,48},{1,9},... | collective-permute-start | bytes 442376 | tf_op jit(solution)/shard_map/ppermute | solution.py:53
  38.5 9.3 %collective-permute-start.3 = (bf16[256,576]{1,0:T(8,128)(2,1)S(1)}, bf16[256,576]{1,0:T(8,128)(2,1)S(1)}, u32[]{:S(2)}, u32[]{:S(2)}) collective-permute-start(bf16[256,576]{1,0:T(8,128)(2,1)S(1)} %pad_maximum_fusion.q_ref), channel_id=1, source_target_pairs={{0,128},{64,192},{128,0},{192,64},{1,129},{65,193},{129,1},{193,65... | collective-permute-start | bytes 884744 | tf_op jit(solution)/shard_map/ppermute | solution.py:49
  40.1 14.4 %collective-permute-start.13 = (bf16[576,512]{1,0:T(8,128)(2,1)S(1)}, bf16[576,512]{1,0:T(8,128)(2,1)S(1)}, u32[]{:S(2)}, u32[]{:S(2)}) collective-permute-start(bf16[576,512]{1,0:T(8,128)(2,1)S(1)} %shard_map.49.refs_0_), channel_id=1, source_target_pairs={{0,4},{4,0},{1,5},{5,1},{2,6},{6,2},{3,7},{7,3},{8,12},{12,8},{9,1... | collective-permute-start | bytes 1769480 | tf_op jit(solution)/shard_map/ppermute | solution.py:45
  44.1 8.0 %collective-permute-start.11 = (bf16[576,256]{1,0:T(8,128)(2,1)S(1)}, bf16[576,256]{1,0:T(8,128)(2,1)S(1)}, u32[]{:S(2)}, u32[]{:S(2)}) collective-permute-start(bf16[576,256]{1,0:T(8,128)(2,1)S(1)} %slice.8), channel_id=1, source_target_pairs={{0,1},{1,2},{2,3},{3,0},{4,5},{5,6},{6,7},{7,4},{8,9},{9,10},{10,1... | collective-permute-start | bytes 884744 | tf_op jit(solution)/shard_map/ppermute | solution.py:41
  44.2 3.3 %collective-permute-start.4 = (s32[2]{0:T(128)S(1)}, s32[2]{0:T(128)S(1)}, u32[]{:S(2)}, u32[]{:S(2)}) collective-permute-start(s32[2]{0:T(128)S(1)} %copy-done.1), channel_id=1, source_target_pairs={{0,4},{4,0},{1,5},{5,1},{2,6},{6,2},{3,7},{7,3},{8,12},{12,8},{9,1... | collective-permute-start | bytes 32 | tf_op jit(solution)/shard_map/ppermute | solution.py:45
  44.3 10.1 %collective-permute-start.12 = (bf16[576,256]{1,0:T(8,128)(2,1)S(1)}, bf16[576,256]{1,0:T(8,128)(2,1)S(1)}, u32[]{:S(2)}, u32[]{:S(2)}) collective-permute-start(bf16[576,256]{1,0:T(8,128)(2,1)S(1)} %slice.9), channel_id=1, source_target_pairs={{0,3},{1,0},{2,1},{3,2},{4,7},{5,4},{6,5},{7,6},{8,11},{9,8},{10,9... | collective-permute-start | bytes 884744 | tf_op jit(solution)/shard_map/ppermute | solution.py:41
  47.5 8.9 %collective-permute-start.14 = (bf16[576,512]{1,0:T(8,128)(2,1)S(1)}, bf16[576,512]{1,0:T(8,128)(2,1)S(1)}, u32[]{:S(2)}, u32[]{:S(2)}) collective-permute-start(bf16[576,512]{1,0:T(8,128)(2,1)S(1)} %collective-permute-done.9.refs_1_), channel_id=1, source_target_pairs={{0,4},{4,0},{1,5},{5,1},{2,6},{6,2},{3,7},{7,3},{8,12},{12,8},{9,1... | collective-permute-start | bytes 1769480 | tf_op jit(solution)/shard_map/ppermute | solution.py:45
  47.8 8.7 %collective-permute-start.15 = (bf16[576,512]{1,0:T(8,128)(2,1)S(1)}, bf16[576,512]{1,0:T(8,128)(2,1)S(1)}, u32[]{:S(2)}, u32[]{:S(2)}) collective-permute-start(bf16[576,512]{1,0:T(8,128)(2,1)S(1)} %collective-permute-done.10.refs_2_), channel_id=1, source_target_pairs={{0,4},{4,0},{1,5},{5,1},{2,6},{6,2},{3,7},{7,3},{8,12},{12,8},{9,1... | collective-permute-start | bytes 1769480 | tf_op jit(solution)/shard_map/ppermute | solution.py:45
  52.1 3.2 %collective-permute-start.16 = (bf16[576,256]{1,0:T(8,128)(2,1)S(1)}, bf16[576,256]{1,0:T(8,128)(2,1)S(1)}, u32[]{:S(2)}, u32[]{:S(2)}) collective-permute-start(bf16[576,256]{1,0:T(8,128)(2,1)S(1)} %collective-permute-done.11.refs_3_), channel_id=1, source_target_pairs={{0,4},{4,0},{1,5},{5,1},{2,6},{6,2},{3,7},{7,3},{8,12},{12,8},{9,1... | collective-permute-start | bytes 884744 | tf_op jit(solution)/shard_map/ppermute | solution.py:45
  54.5 2.0 %collective-permute-start.17 = (bf16[576,256]{1,0:T(8,128)(2,1)S(1)}, bf16[576,256]{1,0:T(8,128)(2,1)S(1)}, u32[]{:S(2)}, u32[]{:S(2)}) collective-permute-start(bf16[576,256]{1,0:T(8,128)(2,1)S(1)} %collective-permute-done.12.refs_4_), channel_id=1, source_target_pairs={{0,4},{4,0},{1,5},{5,1},{2,6},{6,2},{3,7},{7,3},{8,12},{12,8},{9,1... | collective-permute-start | bytes 884744 | tf_op jit(solution)/shard_map/ppermute | solution.py:45
  54.5 11.1 %collective-permute-start.20 = (bf16[256,576]{1,0:T(8,128)(2,1)S(1)}, bf16[256,576]{1,0:T(8,128)(2,1)S(1)}, u32[]{:S(2)}, u32[]{:S(2)}) collective-permute-start(bf16[256,576]{1,0:T(8,128)(2,1)S(1)} %pad_maximum_fusion.q_ref), channel_id=1, source_target_pairs={{0,64},{64,0},{128,192},{192,128},{1,65},{65,1},{129,193},{193,129... | collective-permute-start | bytes 884744 | tf_op jit(solution)/shard_map/ppermute | solution.py:49
  55.3 17.4 %collective-permute-start.23 = (bf16[256,576]{1,0:T(8,128)(2,1)S(1)}, bf16[256,576]{1,0:T(8,128)(2,1)S(1)}, u32[]{:S(2)}, u32[]{:S(2)}) collective-permute-start(bf16[256,576]{1,0:T(8,128)(2,1)S(1)} %pad_maximum_fusion.q_ref), channel_id=1, source_target_pairs={{0,192},{64,128},{128,64},{192,0},{1,193},{65,129},{129,65},{193,1... | collective-permute-start | bytes 884744 | tf_op jit(solution)/shard_map/ppermute | solution.py:49
  60.6 23.1 %collective-permute-start.18 = (bf16[144,512]{1,0:T(8,128)(2,1)S(1)}, bf16[144,512]{1,0:T(8,128)(2,1)S(1)}, u32[]{:S(2)}, u32[]{:S(2)}) collective-permute-start(bf16[144,512]{1,0:T(8,128)(2,1)S(1)} %get-tuple-element.45), channel_id=1, source_target_pairs={{0,136},{8,128},{16,152},{24,144},{32,168},{40,160},{48,184},{56,1... | collective-permute-start | bytes 442376 | tf_op jit(solution)/shard_map/ppermute | solution.py:61
  64.1 21.7 %collective-permute-start.19 = (bf16[144,512]{1,0:T(8,128)(2,1)S(1)}, bf16[144,512]{1,0:T(8,128)(2,1)S(1)}, u32[]{:S(2)}, u32[]{:S(2)}) collective-permute-start(bf16[144,512]{1,0:T(8,128)(2,1)S(1)} %get-tuple-element.46), channel_id=1, source_target_pairs={{0,128},{8,136},{16,144},{24,152},{32,160},{40,168},{48,176},{56,1... | collective-permute-start | bytes 442376 | tf_op jit(solution)/shard_map/ppermute | solution.py:61
  69.6 16.3 %collective-permute-start.21 = (bf16[144,512]{1,0:T(8,128)(2,1)S(1)}, bf16[144,512]{1,0:T(8,128)(2,1)S(1)}, u32[]{:S(2)}, u32[]{:S(2)}) collective-permute-start(bf16[144,512]{1,0:T(8,128)(2,1)S(1)} %get-tuple-element.50), channel_id=1, source_target_pairs={{0,72},{8,64},{16,88},{24,80},{32,104},{40,96},{48,120},{56,112},{... | collective-permute-start | bytes 442376 | tf_op jit(solution)/shard_map/ppermute | solution.py:61
  71.0 15.0 %collective-permute-start.22 = (bf16[144,512]{1,0:T(8,128)(2,1)S(1)}, bf16[144,512]{1,0:T(8,128)(2,1)S(1)}, u32[]{:S(2)}, u32[]{:S(2)}) collective-permute-start(bf16[144,512]{1,0:T(8,128)(2,1)S(1)} %get-tuple-element.51), channel_id=1, source_target_pairs={{0,64},{8,72},{16,80},{24,88},{32,96},{40,104},{48,112},{56,120},{... | collective-permute-start | bytes 442376 | tf_op jit(solution)/shard_map/ppermute | solution.py:61
  76.8 9.2 %collective-permute-start.24 = (bf16[144,512]{1,0:T(8,128)(2,1)S(1)}, bf16[144,512]{1,0:T(8,128)(2,1)S(1)}, u32[]{:S(2)}, u32[]{:S(2)}) collective-permute-start(bf16[144,512]{1,0:T(8,128)(2,1)S(1)} %get-tuple-element.55), channel_id=1, source_target_pairs={{0,200},{8,192},{16,216},{24,208},{32,232},{40,224},{48,248},{56,2... | collective-permute-start | bytes 442376 | tf_op jit(solution)/shard_map/ppermute | solution.py:61
  83.7 6.4 %collective-permute-start.25 = (bf16[144,512]{1,0:T(8,128)(2,1)S(1)}, bf16[144,512]{1,0:T(8,128)(2,1)S(1)}, u32[]{:S(2)}, u32[]{:S(2)}) collective-permute-start(bf16[144,512]{1,0:T(8,128)(2,1)S(1)} %get-tuple-element.56), channel_id=1, source_target_pairs={{0,192},{8,200},{16,208},{24,216},{32,224},{40,232},{48,240},{56,2... | collective-permute-start | bytes 442376 | tf_op jit(solution)/shard_map/ppermute | solution.py:61
  85.9 5.1 %collective-permute-start.26 = (bf16[144,512]{1,0:T(8,128)(2,1)S(1)}, bf16[144,512]{1,0:T(8,128)(2,1)S(1)}, u32[]{:S(2)}, u32[]{:S(2)}) collective-permute-start(bf16[144,512]{1,0:T(8,128)(2,1)S(1)} %get-tuple-element.60), channel_id=1, source_target_pairs={{0,8},{8,0},{16,24},{24,16},{32,40},{40,32},{48,56},{56,48},{64,72... | collective-permute-start | bytes 442376 | tf_op jit(solution)/shard_map/ppermute | solution.py:61
  91.5 8.1 %collective-permute-start.27 = (bf16[32,640]{1,0:T(8,128)(2,1)S(1)}, bf16[32,640]{1,0:T(8,128)(2,1)S(1)}, u32[]{:S(2)}, u32[]{:S(2)}) collective-permute-start(bf16[32,640]{1,0:T(8,128)(2,1)S(1)} %get-tuple-element.64), channel_id=1, source_target_pairs={{0,16},{8,24},{16,0},{24,8},{32,48},{40,56},{48,32},{56,40},{1,17}... | collective-permute-start | bytes 122888 | tf_op jit(solution)/shard_map/ppermute | solution.py:53
  95.2 7.9 %collective-permute-start.28 = (bf16[32,640]{1,0:T(8,128)(2,1)S(1)}, bf16[32,640]{1,0:T(8,128)(2,1)S(1)}, u32[]{:S(2)}, u32[]{:S(2)}) collective-permute-start(bf16[32,640]{1,0:T(8,128)(2,1)S(1)} %get-tuple-element.65), channel_id=1, source_target_pairs={{0,32},{8,40},{16,48},{24,56},{32,0},{40,8},{48,16},{56,24},{1,33}... | collective-permute-start | bytes 122888 | tf_op jit(solution)/shard_map/ppermute | solution.py:53
  99.5 6.1 %collective-permute-start.29 = (bf16[32,640]{1,0:T(8,128)(2,1)S(1)}, bf16[32,640]{1,0:T(8,128)(2,1)S(1)}, u32[]{:S(2)}, u32[]{:S(2)}) collective-permute-start(bf16[32,640]{1,0:T(8,128)(2,1)S(1)} %get-tuple-element.66), channel_id=1, source_target_pairs={{0,48},{8,56},{16,32},{24,40},{32,16},{40,24},{48,0},{56,8},{1,49}... | collective-permute-start | bytes 122888 | tf_op jit(solution)/shard_map/ppermute | solution.py:53
  (2 other events, 16.5 us)

commit v3 on v2

--- a/solution.py
+++ b/solution.py
@@ -25,6 +25,7 @@
 PAIR = HOT_GRP * HALF
 CHUNK = 2 * PAIR
 NEVER = -1e30
+STAT_ROWS = 8
 SCALE = QK**-0.5
 LOG2_E = 1.4426950408889634
 N_FAR = N_Z // 2
@@ -160,54 +161,87 @@
     return [hi, mid, low]
 
 
-PLACES = ((0, 0, 2), (3, 0, 2), (1, 0, 2), (2, 0, 1), (2, 1, 1))
-
-
-def attend_kernel(q_ref, len_ref, hot_ref, hot_other_ref, *refs):
-    n = len(PLACES)
-    key_refs, outs = refs[: N_C * n], refs[N_C * n :]
-    x, z, c = lax.axis_index("x"), lax.axis_index("z"), lax.axis_index("c")
-    rank = lax.axis_index("rep")
-    group = (x * N_Z + z) * N_C + c
-    q = q_ref[...]
+def visible_lengths(len_ref, rows):
     count = len_ref.shape[0]
     line = lax.broadcasted_iota(jnp.int32, (count, 1), 0)
     lens = jnp.zeros((count, 1), jnp.int32)
     for i in range(count):
         lens = jnp.where(line == i, len_ref[i], lens)
-    lens = jnp.concatenate([lens] * (q.shape[0] // count), axis=0)
+    return jnp.concatenate([lens] * (rows // count), axis=0)
+
+
+def row_numbers(hot_ref, other, away, half, halves):
+    x, z, c = lax.axis_index("x"), lax.axis_index("z"), lax.axis_index("c")
+    group = (x * N_Z + z) * N_C + c + other * (1 - 2 * c)
+    at = (lax.axis_index("rep") + away) % N_REP * QUARTER
     lane = lax.broadcasted_iota(jnp.int32, (1, HALF), 1)
+    return jnp.concatenate(
+        [
+            (group * BPG + hot_ref[slot]) * BLK + at + h * HALF + lane
+            for h in range(half, half + halves)
+            for slot in range(HOT_GRP)
+        ],
+        axis=1,
+    )
+
+
+NEAR = (0, 3, 1)
+FAR = 2
+
+
+def fold(op, s):
+    return functools.reduce(op, [s[:, i : i + 128] for i in range(0, s.shape[1], 128)])
+
+
+def score_kernel(other, len_ref, hot_ref, *refs):
+    q_refs, key_refs, outs = refs[:N_X], refs[N_X : N_X + len(NEAR)], refs[N_X + len(NEAR) :]
+    lens = visible_lengths(len_ref, q_refs[0].shape[0])
+    rows = [row_numbers(hot_ref, other, away, 0, 2) for away in NEAR]
+    for i, q_ref in enumerate(q_refs):
+        s_ref, peak_ref = outs[2 * i : 2 * i + 2]
+        q = q_ref[...]
+        peaks = []
+        for j, k_ref in enumerate(key_refs):
+            s = jnp.dot(q, k_ref[...], preferred_element_type=f32)
+            s = jnp.where(rows[j] < lens, s, NEVER)
+            s_ref[:, j * CHUNK : (j + 1) * CHUNK] = s
+            peaks.append(fold(jnp.maximum, s))
+        peak_ref[...] = functools.reduce(jnp.maximum, peaks)
+
+
+def attend_kernel(q_ref, *refs):
+    n = len(NEAR)
+    (s_refs, peak_refs), refs = (refs[0:4:2], refs[1:4:2]), refs[4:]
+    (len_ref, *hot_refs), refs = refs[:3], refs[3:]
+    key_refs, outs = refs[: N_C * (n + 2)], refs[N_C * (n + 2) :]
+    q = q_ref[...]
+    lens = visible_lengths(len_ref, q.shape[0])
+    last = []
+    for other in range(N_C):
+        for half in range(2):
+            k_ref = key_refs[other * (n + 2) + n + half]
+            rows = row_numbers(hot_refs[other], other, FAR, half, 1)
+            s = jnp.dot(q, k_ref[...], preferred_element_type=f32)
+            last.append(jnp.where(rows < lens, s, NEVER))
     parts = []
     for other in range(N_C):
-        keys = key_refs[other * n : (other + 1) * n]
-        hot = hot_other_ref if other else hot_ref
-        own_group = group + other * (1 - 2 * c)
-        scores = []
-        for k_ref, (away, half, halves) in zip(keys, PLACES):
-            at = (rank + away) % N_REP * QUARTER
-            rows = jnp.concatenate(
-                [
-                    (own_group * BPG + hot[slot]) * BLK + at + h * HALF + lane
-                    for h in range(half, half + halves)
-                    for slot in range(HOT_GRP)
-                ],
-                axis=1,
-            )
-            s = jnp.dot(q, k_ref[...], preferred_element_type=f32)
-            scores.append(jnp.where(rows < lens, s, NEVER))
-        peak = scores[0].max(axis=1, keepdims=True)
-        for s in scores[1:]:
-            peak = jnp.maximum(peak, s.max(axis=1, keepdims=True))
-        total = jnp.zeros_like(peak)
+        keys = key_refs[other * (n + 2) : (other + 1) * (n + 2)]
+        scores = [s_refs[other][:, i * CHUNK : (i + 1) * CHUNK] for i in range(n)]
+        scores += last[other * 2 : other * 2 + 2]
+        peak = peak_refs[other][...]
+        for s in last[other * 2 : other * 2 + 2]:
+            peak = jnp.maximum(peak, fold(jnp.maximum, s))
+        peak = peak.max(axis=1, keepdims=True)
+        total = 0.0
         numer = None
         for s, k_ref in zip(scores, keys):
             w = jnp.exp2((s - peak) * (SCALE * LOG2_E)).astype(bf16)
-            total = total + jnp.sum(w.astype(f32), axis=1, keepdims=True)
+            total = total + fold(jnp.add, w.astype(f32))
             v = lax.dot_general(
                 w, k_ref[:LAT, :], (((1,), (1,)), ((), ())), preferred_element_type=f32
             )
             numer = v if numer is None else numer + v
-        parts.append((peak, total, numer))
+        parts.append((peak, total.sum(axis=1, keepdims=True), numer))
     top = jnp.maximum(parts[0][0], parts[1][0])
     numer, total = 0.0, 0.0
     for peak, t, v in parts:
@@ -222,9 +256,9 @@
         o_ref[:rows, :] = o[flip * rows : (flip + 1) * rows]
         mine = stats[:, flip * rows : (flip + 1) * rows]
         terms = three_terms(mine[0:1]) + three_terms(mine[1:2])
-        terms = [t.astype(f32) for t in terms] + [jnp.zeros((10, rows), f32)]
+        terms = [t.astype(f32) for t in terms] + [jnp.zeros((STAT_ROWS - 6, rows), f32)]
         o_ref[rows:, :rows] = jnp.concatenate(terms, axis=0).astype(bf16)
-        o_ref[rows:, rows:] = jnp.zeros((16, LAT - rows), bf16)
+        o_ref[rows:, rows:] = jnp.zeros((STAT_ROWS, LAT - rows), bf16)
 
 
 def merge_kernel(*refs):
@@ -234,7 +268,7 @@
         refs[n_in : n_in + N_FAR - 1],
         refs[n_in + N_FAR - 1 :],
     )
-    rows = parts[0].shape[0] - 16
+    rows = parts[0].shape[0] - STAT_ROWS
     tops, totals = [], []
     for p in parts:
         s = p[rows:, :rows].astype(f32)
@@ -286,7 +320,11 @@
         out_ref[:, head * LAT : (head + 1) * LAT] = o[head * count : (head + 1) * count].astype(bf16)
 
 
-def call(kernel, outs, in_specs, args, mib=16, **more):
+def call(kernel, outs, in_specs, args, mib=16, flops=0, **more):
+    if flops:
+        more["cost_estimate"] = pl.CostEstimate(
+            flops=flops, bytes_accessed=8 * MIB, transcendentals=0
+        )
     return pl.pallas_call(
         kernel,
         out_shape=tuple(jax.ShapeDtypeStruct(*o) for o in outs),
@@ -311,6 +349,8 @@
         scratch_shapes=[pltpu.SemaphoreType.DMA((4,))],
     )
     up, down = shift_rep(up, 1), shift_rep(down, -1)
+    own = queries.reshape(count, -1, WIDTH).transpose(1, 0, 2).reshape(-1, WIDTH)
+    near = jnp.concatenate([own, cross_z(own, 2)], axis=0)
     right, left, mine = call(
         own_cut_kernel,
         [chunk] * 3,
@@ -319,6 +359,7 @@
         mib=50,
         scratch_shapes=[pltpu.SemaphoreType.DMA((12,))],
     )
+    up, down, near = lax.optimization_barrier((up, down, near))
     right, left = call(
         pass_on_kernel,
         [chunk] * 2,
@@ -326,34 +367,52 @@
         [hot_ids, up, down, right, left],
     )
     from_left, from_right = shift_rep(right, 1), shift_rep(left, -1)
+    for bits in (4, 1):
+        near = jnp.concatenate([near, cross_z(near, bits)], axis=0)
+    from_left, from_right, near = lax.optimization_barrier((from_left, from_right, near))
     (mine,) = call(
         settle_kernel,
         [chunk],
         [SMEM] + [VMEM] * 3,
         [hot_ids, from_left, from_right, mine],
     )
-
-    own = queries.reshape(count, -1, WIDTH).transpose(1, 0, 2).reshape(-1, WIDTH)
-    near = own
-    for bits in (2, 4, 1):
-        near = jnp.concatenate([near, cross_z(near, bits)], axis=0)
     asked = [near] + [cross_x(near, bits) for bits in range(1, N_X)]
     hot_other = swap_core(hot_ids)
 
     of_left, of_right = shift_rep(mine, 1), shift_rep(mine, -1)
+    of_left, of_right, *asked = lax.optimization_barrier((of_left, of_right, *asked))
     far_a, far_b = shift_rep(of_left[:, :PAIR], 1), shift_rep(of_right[:, PAIR:], -1)
-    keys = [mine, of_left, of_right, far_a, far_b]
-    keys = keys + [swap_core(k) for k in keys]
-
-    rows = near.shape[0] // 2
-    part = ((rows + 16, LAT), bf16)
+    keys = [mine, of_left, of_right]
+    swapped = [swap_core(k) for k in keys]
+
+    rows = near.shape[0]
+    scores = []
+    for other, (hot, some) in enumerate(((hot_ids, keys), (hot_other, swapped))):
+        found = call(
+            functools.partial(score_kernel, other),
+            [((rows, len(NEAR) * CHUNK), f32), ((rows, 128), f32)] * N_X,
+            [SMEM, SMEM] + [VMEM] * (N_X + len(NEAR)),
+            [lengths, hot, *asked, *some],
+            flops=2 * N_X * rows * WIDTH * len(NEAR) * CHUNK,
+        )
+        scores.append([found[2 * hop : 2 * hop + 2] for hop in range(N_X)])
+    scores, far_a, far_b = lax.optimization_barrier((scores, far_a, far_b))
+    keys += [far_a, far_b]
+    swapped += [swap_core(far_a), swap_core(far_b)]
+
+    rows = rows // 2
+    part = ((rows + STAT_ROWS, LAT), bf16)
     parts = []
-    for hop in (2, 1, 3, 0):
+    for i, hop in enumerate((2, 1, 3, 0)):
+        if i > 1:
+            lengths, *sent = lax.optimization_barrier((lengths, *parts[2 * i - 4 : 2 * i - 2]))
+            parts[2 * i - 4 : 2 * i - 2] = sent
         same, flipped = call(
             attend_kernel,
             [part, part],
-            [VMEM, SMEM, SMEM, SMEM] + [VMEM] * len(keys),
-            [asked[hop], lengths, hot_ids, hot_other] + keys,
+            [VMEM] * 5 + [SMEM] * 3 + [VMEM] * (N_C * len(keys)),
+            [asked[hop], *scores[0][hop], *scores[1][hop], lengths, hot_ids, hot_other, *keys, *swapped],
+            flops=4 * rows * (LAT + WIDTH // 4) * N_C * N_REP * CHUNK,
         )
         lengths, same, flipped = lax.optimization_barrier((lengths, same, flipped))
         parts.append(cross_xz(flipped, hop, 1))

time: 108 us -> 116 us (1.074)
  waiting for transfers between devices: 32.3 us -> 42.5 us
  starting transfers between devices: 50.1 us -> 47 us
  Pallas kernels: 23.2 us -> 24.5 us
    ppermute x3, waiting for transfers between devices: 0.53 us -> 11.5 us  [cross_x(): return lax.ppermute(a, 'x', [(i, i ^ bits) for i in range(N_X)])]
    ppermute x8, waiting for transfers between devices: 15 us -> 4.71 us  [shift_rep(): return lax.ppermute(a, 'rep', [(i, (i + by) % N_REP) for i in range(N_REP)])]
    ppermute x7, waiting for transfers between devices: 5.02 us -> 11.3 us  [cross_xz(): return lax.ppermute(a, ('x', 'z'), pairs)]
    ppermute x6, waiting for transfers between devices: 11.7 us -> 13.5 us  [cross_z(): return lax.ppermute(a, 'z', [(i, i ^ bits) for i in range(N_Z)])]
    ppermute x6, starting transfers between devices: 20.1 us -> 18.6 us  [cross_z(): return lax.ppermute(a, 'z', [(i, i ^ bits) for i in range(N_Z)])]
    ppermute x6, waiting for transfers between devices: 0.02 us -> 1.5 us  [swap_core(): return lax.ppermute(a, 'c', [(0, 1), (1, 0)])]
    ppermute x8, starting transfers between devices: 13.2 us -> 11.8 us  [shift_rep(): return lax.ppermute(a, 'rep', [(i, (i + by) % N_REP) for i in range(N_REP)])]
    pallas_call x10 -> x12, Pallas kernels: 23.2 us -> 24.5 us  [call(): pl.pallas_call(kernel, out_shape=tuple((jax.ShapeDtypeStruct(*o) for o in...]
  transfers between devices with their start and end apart: 30 -> 30, of which waited for: 11 -> 16; matrix products, arithmetic and copies ran while one was open for 0% -> 0% of each run, Pallas kernels for 18% -> 12%
where the time goes in v3:
time: 116 us; the launch traced here: 115 us
  starting transfers between devices  47 us (41%)
  waiting for transfers between devices  42.5 us (37%)
  Pallas kernels  24.5 us (21%)
    pallas_call x12, Pallas kernels, call(): pl.pallas_call(kernel, out_shape=tuple((jax.ShapeDtypeStruct(*o) for o in...  24.5 us
    ppermute x6, starting transfers between devices, cross_z(): return lax.ppermute(a, 'z', [(i, i ^ bits) for i in range(N_Z)])  18.6 us
    ppermute x6, waiting for transfers between devices, cross_z(): return lax.ppermute(a, 'z', [(i, i ^ bits) for i in range(N_Z)])  13.5 us
    ppermute x8, starting transfers between devices, shift_rep(): return lax.ppermute(a, 'rep', [(i, (i + by) % N_REP) for i in range(N_REP)])  11.8 us
    ppermute x3, waiting for transfers between devices, cross_x(): return lax.ppermute(a, 'x', [(i, i ^ bits) for i in range(N_X)])  11.5 us
    ppermute x7, starting transfers between devices, cross_xz(): return lax.ppermute(a, ('x', 'z'), pairs)  11.4 us
    ppermute x7, waiting for transfers between devices, cross_xz(): return lax.ppermute(a, ('x', 'z'), pairs)  11.3 us
    ppermute x8, waiting for transfers between devices, shift_rep(): return lax.ppermute(a, 'rep', [(i, (i + by) % N_REP) for i in range(N_REP)])  4.71 us
  transfers between devices with their start and end apart: 30, of which 16 were waited for; matrix products, arithmetic and copies ran while one was open for 0% of the time, Pallas kernels for 12%

profile of v3, /device:TPU:6, one launch (start us, length us, event | category | flops | bytes accessed | tf_op | source)
XLA Modules:
  0.0 115.0 jit_solution(12174372200878985336)
XLA Ops:
  0.7 1.7 %shard_map.46 = (bf16[576,256]{1,0:T(8,128)(2,1)S(1)}, bf16[576,256]{1,0:T(8,128)(2,1)S(1)}) custom-call(s32[2]{0:T(128)S(1)} %copy-done, bf16[576,4096]{1,0:T(8,128)(2,1)} %bitcast.4), custom_call_target="tpu_custom_call" | custom-call | tf_op jit(solution)/shard_map/pallas_call | solution.py:328
  2.4 1.7 %collective-permute-start = (bf16[576,256]{1,0:T(8,128)(2,1)S(1)}, bf16[576,256]{1,0:T(8,128)(2,1)S(1)}, u32[]{:S(2)}, u32[]{:S(2)}) collective-permute-start(bf16[576,256]{1,0:T(8,128)(2,1)S(1)} %get-tuple-element.88), channel_id=1, source_target_pairs={{0,1},{1,2},{2,3},{3,0},{4,5},{5,6},{6,7},{7,4},{8,9},{9,10},{10,1... | collective-permute-start | bytes 884744 | tf_op jit(solution)/shard_map/ppermute | solution.py:42
  4.0 1.7 %collective-permute-start.1 = (bf16[576,256]{1,0:T(8,128)(2,1)S(1)}, bf16[576,256]{1,0:T(8,128)(2,1)S(1)}, u32[]{:S(2)}, u32[]{:S(2)}) collective-permute-start(bf16[576,256]{1,0:T(8,128)(2,1)S(1)} %get-tuple-element.89), channel_id=1, source_target_pairs={{0,3},{1,0},{2,1},{3,2},{4,7},{5,4},{6,5},{7,6},{8,11},{9,8},{10,9... | collective-permute-start | bytes 884744 | tf_op jit(solution)/shard_map/ppermute | solution.py:42
  5.8 3.4 %collective-permute-start.2 = (bf16[32,576]{1,0:T(8,128)(2,1)S(1)}, bf16[32,576]{1,0:T(8,128)(2,1)S(1)}, u32[]{:S(2)}, u32[]{:S(2)}) collective-permute-start(bf16[32,576]{1,0:T(8,128)(2,1)S(1)} %bitcast.6), channel_id=1, source_target_pairs={{0,16},{8,24},{16,0},{24,8},{32,48},{40,56},{48,32},{56,40},{1,17}... | collective-permute-start | bytes 110600 | tf_op jit(solution)/shard_map/ppermute | solution.py:54
  9.2 2.2 %shard_map.47 = (bf16[576,512]{1,0:T(8,128)(2,1)S(1)}, bf16[576,512]{1,0:T(8,128)(2,1)S(1)}, bf16[576,512]{1,0:T(8,128)(2,1)S(1)}) custom-call(s32[2]{0:T(128)S(1)} %copy-done.1, bf16[576,4096]{1,0:T(8,128)(2,1)} %bitcast.5), custom_call_target="tpu_custom_call" | custom-call | tf_op jit(solution)/shard_map/pallas_call | solution.py:328
  13.2 1.7 %collective-permute-start.3 = (bf16[576,512]{1,0:T(8,128)(2,1)S(1)}, bf16[576,512]{1,0:T(8,128)(2,1)S(1)}, u32[]{:S(2)}, u32[]{:S(2)}) collective-permute-start(bf16[576,512]{1,0:T(8,128)(2,1)S(1)} %get-tuple-element.94), channel_id=1, source_target_pairs={{0,1},{1,2},{2,3},{3,0},{4,5},{5,6},{6,7},{7,4},{8,9},{9,10},{10,1... | collective-permute-start | bytes 1769480 | tf_op jit(solution)/shard_map/ppermute | solution.py:42
  14.9 1.7 %collective-permute-start.4 = (bf16[576,512]{1,0:T(8,128)(2,1)S(1)}, bf16[576,512]{1,0:T(8,128)(2,1)S(1)}, u32[]{:S(2)}, u32[]{:S(2)}) collective-permute-start(bf16[576,512]{1,0:T(8,128)(2,1)S(1)} %get-tuple-element.95), channel_id=1, source_target_pairs={{0,3},{1,0},{2,1},{3,2},{4,7},{5,4},{6,5},{7,6},{8,11},{9,8},{10,9... | collective-permute-start | bytes 1769480 | tf_op jit(solution)/shard_map/ppermute | solution.py:42
  16.5 7.2 %collective-permute-start.5 = (bf16[64,576]{1,0:T(8,128)(2,1)S(1)}, bf16[64,576]{1,0:T(8,128)(2,1)S(1)}, u32[]{:S(2)}, u32[]{:S(2)}) collective-permute-start(bf16[64,576]{1,0:T(8,128)(2,1)S(1)} %pad_maximum_fusion.2), channel_id=1, source_target_pairs={{0,32},{8,40},{16,48},{24,56},{32,0},{40,8},{48,16},{56,24},{1,33}... | collective-permute-start | bytes 221192 | tf_op jit(solution)/shard_map/ppermute | solution.py:54
  23.7 3.1 %collective-permute-done.5 = bf16[64,576]{1,0:T(8,128)(2,1)S(1)} collective-permute-done((bf16[64,576]{1,0:T(8,128)(2,1)S(1)}, bf16[64,576]{1,0:T(8,128)(2,1)S(1)}, u32[]{:S(2)}, u32[]{:S(2)}) %collective-permute-start.5) | collective-permute-done | bytes 73760 | tf_op jit(solution)/shard_map/ppermute | solution.py:54
  28.2 4.1 %collective-permute-done.6 = bf16[128,576]{1,0:T(8,128)(2,1)S(1)} collective-permute-done((bf16[128,576]{1,0:T(8,128)(2,1)S(1)}, bf16[128,576]{1,0:T(8,128)(2,1)S(1)}, u32[]{:S(2)}, u32[]{:S(2)}) %collective-permute-start.6) | collective-permute-done | bytes 147488 | tf_op jit(solution)/shard_map/ppermute | solution.py:54
  33.0 2.0 %collective-permute-start.8 = (bf16[576,512]{1,0:T(8,128)(2,1)S(1)}, bf16[576,512]{1,0:T(8,128)(2,1)S(1)}, u32[]{:S(2)}, u32[]{:S(2)}) collective-permute-start(bf16[576,512]{1,0:T(8,128)(2,1)S(1)} %shard_map.49.refs_4_.refs_7_), channel_id=1, source_target_pairs={{0,3},{1,0},{2,1},{3,2},{4,7},{5,4},{6,5},{7,6},{8,11},{9,8},{10,9... | collective-permute-start | bytes 1769480 | tf_op jit(solution)/shard_map/ppermute | solution.py:42
  35.6 2.4 %collective-permute-start.10 = (bf16[256,576]{1,0:T(8,128)(2,1)S(1)}, bf16[256,576]{1,0:T(8,128)(2,1)S(1)}, u32[]{:S(2)}, u32[]{:S(2)}) collective-permute-start(bf16[256,576]{1,0:T(8,128)(2,1)S(1)} %pad_maximum_fusion.refs_0_.q_ref), channel_id=1, source_target_pairs={{0,128},{64,192},{128,0},{192,64},{1,129},{65,193},{129,1},{193,65... | collective-permute-start | bytes 884744 | tf_op jit(solution)/shard_map/ppermute | solution.py:50
  39.2 10.9 %collective-permute-done.11.refs_3_.q_ref = bf16[256,576]{1,0:T(8,128)(2,1)S(1)} collective-permute-done((bf16[256,576]{1,0:T(8,128)(2,1)S(1)}, bf16[256,576]{1,0:T(8,128)(2,1)S(1)}, u32[]{:S(2)}, u32[]{:S(2)}) %collective-permute-start.11) | collective-permute-done | bytes 294944 | tf_op jit(solution)/shard_map/ppermute | solution.py:50
  51.4 3.0 %collective-permute-start.17 = (bf16[576,256]{1,0:T(8,128)(2,1)S(1)}, bf16[576,256]{1,0:T(8,128)(2,1)S(1)}, u32[]{:S(2)}, u32[]{:S(2)}) collective-permute-start(bf16[576,256]{1,0:T(8,128)(2,1)S(1)} %slice.7), channel_id=1, source_target_pairs={{0,3},{1,0},{2,1},{3,2},{4,7},{5,4},{6,5},{7,6},{8,11},{9,8},{10,9... | collective-permute-start | bytes 884744 | tf_op jit(solution)/shard_map/ppermute | solution.py:42
  54.5 3.2 %shard_map.50 = (f32[256,1536]{1,0:T(8,128)S(1)}, f32[256,128]{1,0:T(8,128)S(1)}, f32[256,1536]{1,0:T(8,128)S(1)}, f32[256,128]{1,0:T(8,128)S(1)}, f32[256,1536]...) custom-call(s32[16]{0:T(128)S(1)} %copy-done.2, s32[2]{0:T(128)S(1)} %copy-done.1, ...), custom_call_target="tpu_custom_call" | custom-call | flops 1811939328 | bytes 8388608 | tf_op jit(solution)/shard_map/pallas_call | solution.py:328
  57.7 3.2 %shard_map.51 = (f32[256,1536]{1,0:T(8,128)S(1)}, f32[256,128]{1,0:T(8,128)S(1)}, f32[256,1536]{1,0:T(8,128)S(1)}, f32[256,128]{1,0:T(8,128)S(1)}, f32[256,1536]...) custom-call(s32[16]{0:T(128)S(1)} %copy-done.2, ...), custom_call_target="tpu_custom_call" | custom-call | flops 1811939328 | bytes 8388608 | tf_op jit(solution)/shard_map/pallas_call | solution.py:328
  61.3 3.4 %collective-permute-done.16.refs_10_ = bf16[576,256]{1,0:T(8,128)(2,1)S(1)} collective-permute-done((bf16[576,256]{1,0:T(8,128)(2,1)S(1)}, bf16[576,256]{1,0:T(8,128)(2,1)S(1)}, u32[]{:S(2)}, u32[]{:S(2)}) %collective-permute-start.16) | collective-permute-done | bytes 294944 | tf_op jit(solution)/shard_map/ppermute | solution.py:42
  66.8 2.8 %shard_map.52 = (bf16[136,512]{1,0:T(8,128)(2,1)S(1)}, bf16[136,512]{1,0:T(8,128)(2,1)S(1)}) custom-call(bf16[256,576]{1,0:T(8,128)(2,1)S(1)} %collective-permute-done.10.refs_2_.q_ref, f32[256,1536]{1,0:T(8,128)S(1)} %get-tuple-element.123.refs_0_, f32[256,128]{1,0:T(8,128)S(1)} %get-tuple-element.124.refs_1_, f32[256,1536]{1,0:T(8,128)S(1)} %get-tuple-element.125.refs_2_, ...), custom_call_target="tpu_custom_call" | custom-call | flops 1375731712 | bytes 8388608 | tf_op jit(solution)/shard_map/pallas_call | solution.py:328
  71.0 2.1 %collective-permute-start.21 = (bf16[136,512]{1,0:T(8,128)(2,1)S(1)}, bf16[136,512]{1,0:T(8,128)(2,1)S(1)}, u32[]{:S(2)}, u32[]{:S(2)}) collective-permute-start(bf16[136,512]{1,0:T(8,128)(2,1)S(1)} %get-tuple-element.140), channel_id=1, source_target_pairs={{0,128},{8,136},{16,144},{24,152},{32,160},{40,168},{48,176},{56,1... | collective-permute-start | bytes 417800 | tf_op jit(solution)/shard_map/ppermute | solution.py:62
  73.2 2.8 %shard_map.53 = (bf16[136,512]{1,0:T(8,128)(2,1)S(1)}, bf16[136,512]{1,0:T(8,128)(2,1)S(1)}) custom-call(bf16[256,576]{1,0:T(8,128)(2,1)S(1)} %collective-permute-done.9.refs_1_.q_ref, f32[256,1536]{1,0:T(8,128)S(1)} %get-tuple-element.132.refs_0_, f32[256,128]{1,0:T(8,128)S(1)} %get-tuple-element.133.refs_1_, f32[256,1536]{1,0:T(8,128)S(1)} %get-tuple-element.134.refs_2_, ...), custom_call_target="tpu_custom_call" | custom-call | flops 1375731712 | bytes 8388608 | tf_op jit(solution)/shard_map/pallas_call | solution.py:328
  76.0 1.8 %collective-permute-start.22 = (bf16[136,512]{1,0:T(8,128)(2,1)S(1)}, bf16[136,512]{1,0:T(8,128)(2,1)S(1)}, u32[]{:S(2)}, u32[]{:S(2)}) collective-permute-start(bf16[136,512]{1,0:T(8,128)(2,1)S(1)} %get-tuple-element.151), channel_id=1, source_target_pairs={{0,72},{8,64},{16,88},{24,80},{32,104},{40,96},{48,120},{56,112},{... | collective-permute-start | bytes 417800 | tf_op jit(solution)/shard_map/ppermute | solution.py:62
  79.0 4.8 %collective-permute-done.21.refs_1_ = bf16[136,512]{1,0:T(8,128)(2,1)S(1)} collective-permute-done((bf16[136,512]{1,0:T(8,128)(2,1)S(1)}, bf16[136,512]{1,0:T(8,128)(2,1)S(1)}, u32[]{:S(2)}, u32[]{:S(2)}) %collective-permute-start.21) | collective-permute-done | bytes 139296 | tf_op jit(solution)/shard_map/ppermute | solution.py:62
  83.8 2.8 %shard_map.54 = (bf16[136,512]{1,0:T(8,128)(2,1)S(1)}, bf16[136,512]{1,0:T(8,128)(2,1)S(1)}) custom-call(bf16[256,576]{1,0:T(8,128)(2,1)S(1)} %collective-permute-done.11.refs_3_.q_ref, f32[256,1536]{1,0:T(8,128)S(1)} %get-tuple-element.144.refs_0_, f32[256,128]{1,0:T(8,128)S(1)} %get-tuple-element.145.refs_1_, f32[256,1536]{1,0:T(8,128)S(1)} %get-tuple-element.146.refs_2_, ...), custom_call_target="tpu_custom_call" | custom-call | flops 1375731712 | bytes 8388608 | tf_op jit(solution)/shard_map/pallas_call | solution.py:328
  86.6 2.8 %shard_map.55 = (bf16[136,512]{1,0:T(8,128)(2,1)S(1)}, bf16[136,512]{1,0:T(8,128)(2,1)S(1)}) custom-call(bf16[256,576]{1,0:T(8,128)(2,1)S(1)} %pad_maximum_fusion.refs_0_.q_ref, f32[256,1536]{1,0:T(8,128)S(1)} %get-tuple-element.158.refs_0_, f32[256,128]{1,0:T(8,128)S(1)} %get-tuple-element.159.refs_1_, f32[256,1536]{1,0:T(8,128)S(1)} %get-tuple-element.160.refs_2_, ...), custom_call_target="tpu_custom_call" | custom-call | flops 1375731712 | bytes 8388608 | tf_op jit(solution)/shard_map/pallas_call | solution.py:328
  90.1 1.5 %collective-permute-start.24 = (bf16[136,512]{1,0:T(8,128)(2,1)S(1)}, bf16[136,512]{1,0:T(8,128)(2,1)S(1)}, u32[]{:S(2)}, u32[]{:S(2)}) collective-permute-start(bf16[136,512]{1,0:T(8,128)(2,1)S(1)} %get-tuple-element.155), channel_id=1, source_target_pairs={{0,200},{8,192},{16,216},{24,208},{32,232},{40,224},{48,248},{56,2... | collective-permute-start | bytes 417800 | tf_op jit(solution)/shard_map/ppermute | solution.py:62
  91.6 2.6 %collective-permute-start.25 = (bf16[136,512]{1,0:T(8,128)(2,1)S(1)}, bf16[136,512]{1,0:T(8,128)(2,1)S(1)}, u32[]{:S(2)}, u32[]{:S(2)}) collective-permute-start(bf16[136,512]{1,0:T(8,128)(2,1)S(1)} %get-tuple-element.156), channel_id=1, source_target_pairs={{0,192},{8,200},{16,208},{24,216},{32,224},{40,232},{48,240},{56,2... | collective-permute-start | bytes 417800 | tf_op jit(solution)/shard_map/ppermute | solution.py:62
  94.2 1.8 %collective-permute-done.26.refs_6_ = bf16[136,512]{1,0:T(8,128)(2,1)S(1)} collective-permute-done((bf16[136,512]{1,0:T(8,128)(2,1)S(1)}, bf16[136,512]{1,0:T(8,128)(2,1)S(1)}, u32[]{:S(2)}, u32[]{:S(2)}) %collective-permute-start.26) | collective-permute-done | bytes 139296 | tf_op jit(solution)/shard_map/ppermute | solution.py:62
  96.1 2.2 %collective-permute-done.24.refs_4_ = bf16[136,512]{1,0:T(8,128)(2,1)S(1)} collective-permute-done((bf16[136,512]{1,0:T(8,128)(2,1)S(1)}, bf16[136,512]{1,0:T(8,128)(2,1)S(1)}, u32[]{:S(2)}, u32[]{:S(2)}) %collective-permute-start.24) | collective-permute-done | bytes 139296 | tf_op jit(solution)/shard_map/ppermute | solution.py:62
  98.3 2.4 %collective-permute-done.25.refs_5_ = bf16[136,512]{1,0:T(8,128)(2,1)S(1)} collective-permute-done((bf16[136,512]{1,0:T(8,128)(2,1)S(1)}, bf16[136,512]{1,0:T(8,128)(2,1)S(1)}, u32[]{:S(2)}, u32[]{:S(2)}) %collective-permute-start.25) | collective-permute-done | bytes 139296 | tf_op jit(solution)/shard_map/ppermute | solution.py:62
  102.4 5.4 %collective-permute-start.28 = (bf16[32,640]{1,0:T(8,128)(2,1)S(1)}, bf16[32,640]{1,0:T(8,128)(2,1)S(1)}, u32[]{:S(2)}, u32[]{:S(2)}) collective-permute-start(bf16[32,640]{1,0:T(8,128)(2,1)S(1)} %get-tuple-element.169), channel_id=1, source_target_pairs={{0,32},{8,40},{16,48},{24,56},{32,0},{40,8},{48,16},{56,24},{1,33}... | collective-permute-start | bytes 122888 | tf_op jit(solution)/shard_map/ppermute | solution.py:54
  107.8 2.5 %collective-permute-done.28.refs_1_ = bf16[32,640]{1,0:T(8,128)(2,1)S(1)} collective-permute-done((bf16[32,640]{1,0:T(8,128)(2,1)S(1)}, bf16[32,640]{1,0:T(8,128)(2,1)S(1)}, u32[]{:S(2)}, u32[]{:S(2)}) %collective-permute-start.28) | collective-permute-done | bytes 40992 | tf_op jit(solution)/shard_map/ppermute | solution.py:54
  110.4 3.6 %collective-permute-done.29.refs_2_ = bf16[32,640]{1,0:T(8,128)(2,1)S(1)} collective-permute-done((bf16[32,640]{1,0:T(8,128)(2,1)S(1)}, bf16[32,640]{1,0:T(8,128)(2,1)S(1)}, u32[]{:S(2)}, u32[]{:S(2)}) %collective-permute-start.29) | collective-permute-done | bytes 40992 | tf_op jit(solution)/shard_map/ppermute | solution.py:54
  (55 shorter events, 16.3 us)
Async XLA Ops:
  0.7 8.6 %copy-start.1 = (s32[2]{0:T(128)S(1)}, s32[2]{0:T(128)}, u32[]{:S(2)}) copy-start(s32[2]{0:T(128)} %refs_5_.7) | copy-start | bytes 28
  2.4 10.1 %collective-permute-start = (bf16[576,256]{1,0:T(8,128)(2,1)S(1)}, bf16[576,256]{1,0:T(8,128)(2,1)S(1)}, u32[]{:S(2)}, u32[]{:S(2)}) collective-permute-start(bf16[576,256]{1,0:T(8,128)(2,1)S(1)} %get-tuple-element.88), channel_id=1, source_target_pairs={{0,1},{1,2},{2,3},{3,0},{4,5},{5,6},{6,7},{7,4},{8,9},{9,10},{10,1... | collective-permute-start | bytes 884744 | tf_op jit(solution)/shard_map/ppermute | solution.py:42
  4.0 8.5 %collective-permute-start.1 = (bf16[576,256]{1,0:T(8,128)(2,1)S(1)}, bf16[576,256]{1,0:T(8,128)(2,1)S(1)}, u32[]{:S(2)}, u32[]{:S(2)}) collective-permute-start(bf16[576,256]{1,0:T(8,128)(2,1)S(1)} %get-tuple-element.89), channel_id=1, source_target_pairs={{0,3},{1,0},{2,1},{3,2},{4,7},{5,4},{6,5},{7,6},{8,11},{9,8},{10,9... | collective-permute-start | bytes 884744 | tf_op jit(solution)/shard_map/ppermute | solution.py:42
  5.8 5.8 %collective-permute-start.2 = (bf16[32,576]{1,0:T(8,128)(2,1)S(1)}, bf16[32,576]{1,0:T(8,128)(2,1)S(1)}, u32[]{:S(2)}, u32[]{:S(2)}) collective-permute-start(bf16[32,576]{1,0:T(8,128)(2,1)S(1)} %bitcast.6), channel_id=1, source_target_pairs={{0,16},{8,24},{16,0},{24,8},{32,48},{40,56},{48,32},{56,40},{1,17}... | collective-permute-start | bytes 110600 | tf_op jit(solution)/shard_map/ppermute | solution.py:54
  13.2 19.1 %collective-permute-start.3 = (bf16[576,512]{1,0:T(8,128)(2,1)S(1)}, bf16[576,512]{1,0:T(8,128)(2,1)S(1)}, u32[]{:S(2)}, u32[]{:S(2)}) collective-permute-start(bf16[576,512]{1,0:T(8,128)(2,1)S(1)} %get-tuple-element.94), channel_id=1, source_target_pairs={{0,1},{1,2},{2,3},{3,0},{4,5},{5,6},{6,7},{7,4},{8,9},{9,10},{10,1... | collective-permute-start | bytes 1769480 | tf_op jit(solution)/shard_map/ppermute | solution.py:42
  14.9 17.4 %collective-permute-start.4 = (bf16[576,512]{1,0:T(8,128)(2,1)S(1)}, bf16[576,512]{1,0:T(8,128)(2,1)S(1)}, u32[]{:S(2)}, u32[]{:S(2)}) collective-permute-start(bf16[576,512]{1,0:T(8,128)(2,1)S(1)} %get-tuple-element.95), channel_id=1, source_target_pairs={{0,3},{1,0},{2,1},{3,2},{4,7},{5,4},{6,5},{7,6},{8,11},{9,8},{10,9... | collective-permute-start | bytes 1769480 | tf_op jit(solution)/shard_map/ppermute | solution.py:42
  16.5 10.3 %collective-permute-start.5 = (bf16[64,576]{1,0:T(8,128)(2,1)S(1)}, bf16[64,576]{1,0:T(8,128)(2,1)S(1)}, u32[]{:S(2)}, u32[]{:S(2)}) collective-permute-start(bf16[64,576]{1,0:T(8,128)(2,1)S(1)} %pad_maximum_fusion.2), channel_id=1, source_target_pairs={{0,32},{8,40},{16,48},{24,56},{32,0},{40,8},{48,16},{56,24},{1,33}... | collective-permute-start | bytes 221192 | tf_op jit(solution)/shard_map/ppermute | solution.py:54
  26.9 5.4 %collective-permute-start.6 = (bf16[128,576]{1,0:T(8,128)(2,1)S(1)}, bf16[128,576]{1,0:T(8,128)(2,1)S(1)}, u32[]{:S(2)}, u32[]{:S(2)}) collective-permute-start(bf16[128,576]{1,0:T(8,128)(2,1)S(1)} %pad_maximum_fusion.1), channel_id=1, source_target_pairs={{0,8},{8,0},{16,24},{24,16},{32,40},{40,32},{48,56},{56,48},{1,9},... | collective-permute-start | bytes 442376 | tf_op jit(solution)/shard_map/ppermute | solution.py:54
  32.3 22.2 %copy-start.2 = (s32[16]{0:T(128)S(1)}, s32[16]{0:T(128)}, u32[]{:S(2)}) copy-start(s32[16]{0:T(128)} %refs_4_.4) | copy-start | bytes 196
  33.0 17.7 %collective-permute-start.8 = (bf16[576,512]{1,0:T(8,128)(2,1)S(1)}, bf16[576,512]{1,0:T(8,128)(2,1)S(1)}, u32[]{:S(2)}, u32[]{:S(2)}) collective-permute-start(bf16[576,512]{1,0:T(8,128)(2,1)S(1)} %shard_map.49.refs_4_.refs_7_), channel_id=1, source_target_pairs={{0,3},{1,0},{2,1},{3,2},{4,7},{5,4},{6,5},{7,6},{8,11},{9,8},{10,9... | collective-permute-start | bytes 1769480 | tf_op jit(solution)/shard_map/ppermute | solution.py:42
  35.1 15.7 %collective-permute-start.7 = (bf16[576,512]{1,0:T(8,128)(2,1)S(1)}, bf16[576,512]{1,0:T(8,128)(2,1)S(1)}, u32[]{:S(2)}, u32[]{:S(2)}) collective-permute-start(bf16[576,512]{1,0:T(8,128)(2,1)S(1)} %shard_map.49.refs_4_.refs_7_), channel_id=1, source_target_pairs={{0,1},{1,2},{2,3},{3,0},{4,5},{5,6},{6,7},{7,4},{8,9},{9,10},{10,1... | collective-permute-start | bytes 1769480 | tf_op jit(solution)/shard_map/ppermute | solution.py:42
  35.2 15.0 %collective-permute-start.11 = (bf16[256,576]{1,0:T(8,128)(2,1)S(1)}, bf16[256,576]{1,0:T(8,128)(2,1)S(1)}, u32[]{:S(2)}, u32[]{:S(2)}) collective-permute-start(bf16[256,576]{1,0:T(8,128)(2,1)S(1)} %pad_maximum_fusion.refs_0_.q_ref), channel_id=1, source_target_pairs={{0,192},{64,128},{128,64},{192,0},{1,193},{65,129},{129,65},{193,1... | collective-permute-start | bytes 884744 | tf_op jit(solution)/shard_map/ppermute | solution.py:50
  35.6 14.5 %collective-permute-start.10 = (bf16[256,576]{1,0:T(8,128)(2,1)S(1)}, bf16[256,576]{1,0:T(8,128)(2,1)S(1)}, u32[]{:S(2)}, u32[]{:S(2)}) collective-permute-start(bf16[256,576]{1,0:T(8,128)(2,1)S(1)} %pad_maximum_fusion.refs_0_.q_ref), channel_id=1, source_target_pairs={{0,128},{64,192},{128,0},{192,64},{1,129},{65,193},{129,1},{193,65... | collective-permute-start | bytes 884744 | tf_op jit(solution)/shard_map/ppermute | solution.py:50
  38.0 12.7 %collective-permute-start.9 = (bf16[256,576]{1,0:T(8,128)(2,1)S(1)}, bf16[256,576]{1,0:T(8,128)(2,1)S(1)}, u32[]{:S(2)}, u32[]{:S(2)}) collective-permute-start(bf16[256,576]{1,0:T(8,128)(2,1)S(1)} %pad_maximum_fusion.refs_0_.q_ref), channel_id=1, source_target_pairs={{0,64},{64,0},{128,192},{192,128},{1,65},{65,1},{129,193},{193,129... | collective-permute-start | bytes 884744 | tf_op jit(solution)/shard_map/ppermute | solution.py:50
  50.2 7.5 %collective-permute-start.13 = (bf16[576,512]{1,0:T(8,128)(2,1)S(1)}, bf16[576,512]{1,0:T(8,128)(2,1)S(1)}, u32[]{:S(2)}, u32[]{:S(2)}) collective-permute-start(bf16[576,512]{1,0:T(8,128)(2,1)S(1)} %shard_map.49.refs_4_.refs_7_), channel_id=1, source_target_pairs={{0,4},{4,0},{1,5},{5,1},{2,6},{6,2},{3,7},{7,3},{8,12},{12,8},{9,1... | collective-permute-start | bytes 1769480 | tf_op jit(solution)/shard_map/ppermute | solution.py:46
  50.8 6.9 %collective-permute-start.14 = (bf16[576,512]{1,0:T(8,128)(2,1)S(1)}, bf16[576,512]{1,0:T(8,128)(2,1)S(1)}, u32[]{:S(2)}, u32[]{:S(2)}) collective-permute-start(bf16[576,512]{1,0:T(8,128)(2,1)S(1)} %collective-permute-done.7.refs_5_.refs_8_), channel_id=1, source_target_pairs={{0,4},{4,0},{1,5},{5,1},{2,6},{6,2},{3,7},{7,3},{8,12},{12,8},{9,1... | collective-permute-start | bytes 1769480 | tf_op jit(solution)/shard_map/ppermute | solution.py:46
  50.8 6.9 %collective-permute-start.15 = (bf16[576,512]{1,0:T(8,128)(2,1)S(1)}, bf16[576,512]{1,0:T(8,128)(2,1)S(1)}, u32[]{:S(2)}, u32[]{:S(2)}) collective-permute-start(bf16[576,512]{1,0:T(8,128)(2,1)S(1)} %collective-permute-done.8.refs_6_.refs_9_), channel_id=1, source_target_pairs={{0,4},{4,0},{1,5},{5,1},{2,6},{6,2},{3,7},{7,3},{8,12},{12,8},{9,1... | collective-permute-start | bytes 1769480 | tf_op jit(solution)/shard_map/ppermute | solution.py:46
  51.3 3.2 %collective-permute-start.12 = (s32[2]{0:T(128)S(1)}, s32[2]{0:T(128)S(1)}, u32[]{:S(2)}, u32[]{:S(2)}) collective-permute-start(s32[2]{0:T(128)S(1)} %copy-done.1), channel_id=1, source_target_pairs={{0,4},{4,0},{1,5},{5,1},{2,6},{6,2},{3,7},{7,3},{8,12},{12,8},{9,1... | collective-permute-start | bytes 32 | tf_op jit(solution)/shard_map/ppermute | solution.py:46
  51.4 9.9 %collective-permute-start.17 = (bf16[576,256]{1,0:T(8,128)(2,1)S(1)}, bf16[576,256]{1,0:T(8,128)(2,1)S(1)}, u32[]{:S(2)}, u32[]{:S(2)}) collective-permute-start(bf16[576,256]{1,0:T(8,128)(2,1)S(1)} %slice.7), channel_id=1, source_target_pairs={{0,3},{1,0},{2,1},{3,2},{4,7},{5,4},{6,5},{7,6},{8,11},{9,8},{10,9... | collective-permute-start | bytes 884744 | tf_op jit(solution)/shard_map/ppermute | solution.py:42
  54.5 10.3 %collective-permute-start.16 = (bf16[576,256]{1,0:T(8,128)(2,1)S(1)}, bf16[576,256]{1,0:T(8,128)(2,1)S(1)}, u32[]{:S(2)}, u32[]{:S(2)}) collective-permute-start(bf16[576,256]{1,0:T(8,128)(2,1)S(1)} %slice.6), channel_id=1, source_target_pairs={{0,1},{1,2},{2,3},{3,0},{4,5},{5,6},{6,7},{7,4},{8,9},{9,10},{10,1... | collective-permute-start | bytes 884744 | tf_op jit(solution)/shard_map/ppermute | solution.py:42
  64.7 1.6 %collective-permute-start.18 = (bf16[576,256]{1,0:T(8,128)(2,1)S(1)}, bf16[576,256]{1,0:T(8,128)(2,1)S(1)}, u32[]{:S(2)}, u32[]{:S(2)}) collective-permute-start(bf16[576,256]{1,0:T(8,128)(2,1)S(1)} %collective-permute-done.16.refs_10_), channel_id=1, source_target_pairs={{0,4},{4,0},{1,5},{5,1},{2,6},{6,2},{3,7},{7,3},{8,12},{12,8},{9,1... | collective-permute-start | bytes 884744 | tf_op jit(solution)/shard_map/ppermute | solution.py:46
  64.8 2.0 %collective-permute-start.19 = (bf16[576,256]{1,0:T(8,128)(2,1)S(1)}, bf16[576,256]{1,0:T(8,128)(2,1)S(1)}, u32[]{:S(2)}, u32[]{:S(2)}) collective-permute-start(bf16[576,256]{1,0:T(8,128)(2,1)S(1)} %collective-permute-done.17.refs_11_), channel_id=1, source_target_pairs={{0,4},{4,0},{1,5},{5,1},{2,6},{6,2},{3,7},{7,3},{8,12},{12,8},{9,1... | collective-permute-start | bytes 884744 | tf_op jit(solution)/shard_map/ppermute | solution.py:46
  69.6 9.4 %collective-permute-start.20 = (bf16[136,512]{1,0:T(8,128)(2,1)S(1)}, bf16[136,512]{1,0:T(8,128)(2,1)S(1)}, u32[]{:S(2)}, u32[]{:S(2)}) collective-permute-start(bf16[136,512]{1,0:T(8,128)(2,1)S(1)} %get-tuple-element.139), channel_id=1, source_target_pairs={{0,136},{8,128},{16,152},{24,144},{32,168},{40,160},{48,184},{56,1... | collective-permute-start | bytes 417800 | tf_op jit(solution)/shard_map/ppermute | solution.py:62
  71.0 12.8 %collective-permute-start.21 = (bf16[136,512]{1,0:T(8,128)(2,1)S(1)}, bf16[136,512]{1,0:T(8,128)(2,1)S(1)}, u32[]{:S(2)}, u32[]{:S(2)}) collective-permute-start(bf16[136,512]{1,0:T(8,128)(2,1)S(1)} %get-tuple-element.140), channel_id=1, source_target_pairs={{0,128},{8,136},{16,144},{24,152},{32,160},{40,168},{48,176},{56,1... | collective-permute-start | bytes 417800 | tf_op jit(solution)/shard_map/ppermute | solution.py:62
  76.0 10.7 %collective-permute-start.22 = (bf16[136,512]{1,0:T(8,128)(2,1)S(1)}, bf16[136,512]{1,0:T(8,128)(2,1)S(1)}, u32[]{:S(2)}, u32[]{:S(2)}) collective-permute-start(bf16[136,512]{1,0:T(8,128)(2,1)S(1)} %get-tuple-element.151), channel_id=1, source_target_pairs={{0,72},{8,64},{16,88},{24,80},{32,104},{40,96},{48,120},{56,112},{... | collective-permute-start | bytes 417800 | tf_op jit(solution)/shard_map/ppermute | solution.py:62
  77.8 8.8 %collective-permute-start.23 = (bf16[136,512]{1,0:T(8,128)(2,1)S(1)}, bf16[136,512]{1,0:T(8,128)(2,1)S(1)}, u32[]{:S(2)}, u32[]{:S(2)}) collective-permute-start(bf16[136,512]{1,0:T(8,128)(2,1)S(1)} %get-tuple-element.152), channel_id=1, source_target_pairs={{0,64},{8,72},{16,80},{24,88},{32,96},{40,104},{48,112},{56,120},{... | collective-permute-start | bytes 417800 | tf_op jit(solution)/shard_map/ppermute | solution.py:62
  89.4 6.6 %collective-permute-start.26 = (bf16[136,512]{1,0:T(8,128)(2,1)S(1)}, bf16[136,512]{1,0:T(8,128)(2,1)S(1)}, u32[]{:S(2)}, u32[]{:S(2)}) collective-permute-start(bf16[136,512]{1,0:T(8,128)(2,1)S(1)} %get-tuple-element.164), channel_id=1, source_target_pairs={{0,8},{8,0},{16,24},{24,16},{32,40},{40,32},{48,56},{56,48},{64,72... | collective-permute-start | bytes 417800 | tf_op jit(solution)/shard_map/ppermute | solution.py:62
  90.1 8.2 %collective-permute-start.24 = (bf16[136,512]{1,0:T(8,128)(2,1)S(1)}, bf16[136,512]{1,0:T(8,128)(2,1)S(1)}, u32[]{:S(2)}, u32[]{:S(2)}) collective-permute-start(bf16[136,512]{1,0:T(8,128)(2,1)S(1)} %get-tuple-element.155), channel_id=1, source_target_pairs={{0,200},{8,192},{16,216},{24,208},{32,232},{40,224},{48,248},{56,2... | collective-permute-start | bytes 417800 | tf_op jit(solution)/shard_map/ppermute | solution.py:62
  91.6 9.0 %collective-permute-start.25 = (bf16[136,512]{1,0:T(8,128)(2,1)S(1)}, bf16[136,512]{1,0:T(8,128)(2,1)S(1)}, u32[]{:S(2)}, u32[]{:S(2)}) collective-permute-start(bf16[136,512]{1,0:T(8,128)(2,1)S(1)} %get-tuple-element.156), channel_id=1, source_target_pairs={{0,192},{8,200},{16,208},{24,216},{32,224},{40,232},{48,240},{56,2... | collective-permute-start | bytes 417800 | tf_op jit(solution)/shard_map/ppermute | solution.py:62
  101.1 6.7 %collective-permute-start.27 = (bf16[32,640]{1,0:T(8,128)(2,1)S(1)}, bf16[32,640]{1,0:T(8,128)(2,1)S(1)}, u32[]{:S(2)}, u32[]{:S(2)}) collective-permute-start(bf16[32,640]{1,0:T(8,128)(2,1)S(1)} %get-tuple-element.168), channel_id=1, source_target_pairs={{0,16},{8,24},{16,0},{24,8},{32,48},{40,56},{48,32},{56,40},{1,17}... | collective-permute-start | bytes 122888 | tf_op jit(solution)/shard_map/ppermute | solution.py:54
  102.4 7.9 %collective-permute-start.28 = (bf16[32,640]{1,0:T(8,128)(2,1)S(1)}, bf16[32,640]{1,0:T(8,128)(2,1)S(1)}, u32[]{:S(2)}, u32[]{:S(2)}) collective-permute-start(bf16[32,640]{1,0:T(8,128)(2,1)S(1)} %get-tuple-element.169), channel_id=1, source_target_pairs={{0,32},{8,40},{16,48},{24,56},{32,0},{40,8},{48,16},{56,24},{1,33}... | collective-permute-start | bytes 122888 | tf_op jit(solution)/shard_map/ppermute | solution.py:54
  107.8 6.1 %collective-permute-start.29 = (bf16[32,640]{1,0:T(8,128)(2,1)S(1)}, bf16[32,640]{1,0:T(8,128)(2,1)S(1)}, u32[]{:S(2)}, u32[]{:S(2)}) collective-permute-start(bf16[32,640]{1,0:T(8,128)(2,1)S(1)} %get-tuple-element.170), channel_id=1, source_target_pairs={{0,48},{8,56},{16,32},{24,40},{32,16},{40,24},{48,0},{56,8},{1,49}... | collective-permute-start | bytes 122888 | tf_op jit(solution)/shard_map/ppermute | solution.py:54
  (2 other events, 5.7 us)

commit v4 on v3

--- a/solution.py
+++ b/solution.py
@@ -26,6 +26,7 @@
 CHUNK = 2 * PAIR
 NEVER = -1e30
 STAT_ROWS = 8
+Z_ORDER = (0, 4, 2, 6)
 SCALE = QK**-0.5
 LOG2_E = 1.4426950408889634
 N_FAR = N_Z // 2
@@ -51,7 +52,7 @@
 
 
 def cross_z(a, bits):
-    return lax.ppermute(a, "z", [(i, i ^ bits) for i in range(N_Z)])
+    return lax.ppermute(a, ("zf", "zp"), [(i, i ^ bits) for i in range(N_Z)])
 
 
 def cross_xz(a, bits_x, bits_z):
@@ -59,7 +60,7 @@
     for x in range(N_X):
         for z in range(N_Z):
             pairs.append((x * N_Z + z, (x ^ bits_x) * N_Z + (z ^ bits_z)))
-    return lax.ppermute(a, ("x", "z"), pairs)
+    return lax.ppermute(a, ("x", "zf", "zp"), pairs)
 
 
 def column(hot_ref, slot, rank, half):
@@ -171,7 +172,8 @@
 
 
 def row_numbers(hot_ref, other, away, half, halves):
-    x, z, c = lax.axis_index("x"), lax.axis_index("z"), lax.axis_index("c")
+    x, c = lax.axis_index("x"), lax.axis_index("c")
+    z = lax.axis_index("zf") * 2 + lax.axis_index("zp")
     group = (x * N_Z + z) * N_C + c + other * (1 - 2 * c)
     at = (lax.axis_index("rep") + away) % N_REP * QUARTER
     lane = lax.broadcasted_iota(jnp.int32, (1, HALF), 1)
@@ -209,12 +211,18 @@
         peak_ref[...] = functools.reduce(jnp.maximum, peaks)
 
 
-def attend_kernel(q_ref, *refs):
+def attend_kernel(halves, *refs):
     n = len(NEAR)
-    (s_refs, peak_refs), refs = (refs[0:4:2], refs[1:4:2]), refs[4:]
+    q_refs, s_refs, refs = refs[:2], refs[2:10], refs[10:]
     (len_ref, *hot_refs), refs = refs[:3], refs[3:]
     key_refs, outs = refs[: N_C * (n + 2)], refs[N_C * (n + 2) :]
-    q = q_ref[...]
+    span = q_refs[0].shape[0] // 2
+    cuts = [slice(half * span, (half + 1) * span) for half in halves]
+
+    def two(a_ref, b_ref, columns=slice(None)):
+        return jnp.concatenate([a_ref[cuts[0], columns], b_ref[cuts[1], columns]], axis=0)
+
+    q = two(*q_refs)
     lens = visible_lengths(len_ref, q.shape[0])
     last = []
     for other in range(N_C):
@@ -226,9 +234,10 @@
     parts = []
     for other in range(N_C):
         keys = key_refs[other * (n + 2) : (other + 1) * (n + 2)]
-        scores = [s_refs[other][:, i * CHUNK : (i + 1) * CHUNK] for i in range(n)]
+        s_pair = s_refs[other * 4 : other * 4 + 4 : 2]
+        scores = [two(*s_pair, slice(i * CHUNK, (i + 1) * CHUNK)) for i in range(n)]
         scores += last[other * 2 : other * 2 + 2]
-        peak = peak_refs[other][...]
+        peak = two(*s_refs[other * 4 + 1 : other * 4 + 4 : 2])
         for s in last[other * 2 : other * 2 + 2]:
             peak = jnp.maximum(peak, fold(jnp.maximum, s))
         peak = peak.max(axis=1, keepdims=True)
@@ -251,23 +260,18 @@
     o = (numer * (1.0 / jnp.maximum(total, 1.0))).astype(bf16)
     lanes = lax.broadcasted_iota(jnp.int32, (q.shape[0], 128), 1)
     stats = jnp.where(lanes == 0, top * SCALE, total).T[:2, :]
-    rows = o.shape[0] // 2
     for flip, o_ref in enumerate(outs):
-        o_ref[:rows, :] = o[flip * rows : (flip + 1) * rows]
-        mine = stats[:, flip * rows : (flip + 1) * rows]
+        o_ref[:span, :] = o[flip * span : (flip + 1) * span]
+        mine = stats[:, flip * span : (flip + 1) * span]
         terms = three_terms(mine[0:1]) + three_terms(mine[1:2])
-        terms = [t.astype(f32) for t in terms] + [jnp.zeros((STAT_ROWS - 6, rows), f32)]
-        o_ref[rows:, :rows] = jnp.concatenate(terms, axis=0).astype(bf16)
-        o_ref[rows:, rows:] = jnp.zeros((STAT_ROWS, LAT - rows), bf16)
+        terms = [t.astype(f32) for t in terms] + [jnp.zeros((STAT_ROWS - 6, span), f32)]
+        o_ref[span:, :span] = jnp.concatenate(terms, axis=0).astype(bf16)
+        o_ref[span:, span:] = jnp.zeros((STAT_ROWS, LAT - span), bf16)
 
 
 def merge_kernel(*refs):
-    n_in = N_X * 2
-    parts, sends, (own_ref, stat_ref) = (
-        refs[:n_in],
-        refs[n_in : n_in + N_FAR - 1],
-        refs[n_in + N_FAR - 1 :],
-    )
+    parts, out_ref = refs[:-1], refs[-1]
+    n_in = len(parts)
     rows = parts[0].shape[0] - STAT_ROWS
     tops, totals = [], []
     for p in parts:
@@ -283,40 +287,34 @@
     table = jnp.concatenate(table, axis=0).T
     n = rows // N_FAR
     lane = lax.broadcasted_iota(jnp.int32, (n, 128), 1)
-    for far in range(N_FAR):
-        at = slice(far * n, (far + 1) * n)
+    for i, bits in enumerate(Z_ORDER):
+        at = slice(i * n, (i + 1) * n)
         acc = 0.0
-        for i, p in enumerate(parts):
-            acc = acc + p[at, :].astype(f32) * table[at, i : i + 1]
-        if far:
-            ref = sends[far - 1]
-            ref[:, :LAT] = acc.astype(bf16)
-            packed = jnp.zeros((n, 128), f32)
-            terms = three_terms(table[at, n_in : n_in + 1])
-            terms += three_terms(table[at, n_in + 1 : n_in + 2])
-            for i, term in enumerate(terms):
-                packed = jnp.where(lane == i, term.astype(f32), packed)
-            ref[:, LAT:] = packed.astype(bf16)
-        else:
-            own_ref[...] = acc
-            stat_ref[...] = table[at]
-
-
-def finish_kernel(own_ref, stat_ref, *refs):
-    parts, out_ref = refs[:-1], refs[-1]
-    n_in = N_X * 2
-    tops, totals, values = [stat_ref[:, n_in : n_in + 1]], [stat_ref[:, n_in + 1 : n_in + 2]], [own_ref[...]]
+        for j, p in enumerate(parts):
+            acc = acc + p[at, :].astype(f32) * table[at, j : j + 1]
+        to = pl.ds(pl.multiple_of((lax.axis_index("zf") ^ (bits // 2)) * n, n), n)
+        out_ref[to, :LAT] = acc.astype(bf16)
+        packed = jnp.zeros((n, 128), f32)
+        terms = three_terms(table[at, n_in : n_in + 1])
+        terms += three_terms(table[at, n_in + 1 : n_in + 2])
+        for j, term in enumerate(terms):
+            packed = jnp.where(lane == j, term.astype(f32), packed)
+        out_ref[to, LAT:] = packed.astype(bf16)
+
+
+def finish_kernel(in_ref, out_ref):
+    n = in_ref.shape[0] // N_FAR
+    parts = [in_ref[i * n : (i + 1) * n, :].astype(f32) for i in range(N_FAR)]
+    tops, totals = [], []
     for p in parts:
-        s = p[:, LAT:].astype(f32)
+        s = p[:, LAT:]
         tops.append(s[:, 0:1] + s[:, 1:2] + s[:, 2:3])
         totals.append(s[:, 3:4] + s[:, 4:5] + s[:, 5:6])
-        values.append(p[:, :LAT].astype(f32))
     top = functools.reduce(jnp.maximum, tops)
     weights = [t * jnp.exp(m - top) for m, t in zip(tops, totals)]
-    total = sum(weights)
-    o = sum(v * w for v, w in zip(values, weights)) / total
+    o = sum(p[:, :LAT] * w for p, w in zip(parts, weights)) / sum(weights)
     count = out_ref.shape[0]
-    for head in range(o.shape[0] // count):
+    for head in range(n // count):
         out_ref[:, head * LAT : (head + 1) * LAT] = o[head * count : (head + 1) * count].astype(bf16)
 
 
@@ -350,7 +348,7 @@
     )
     up, down = shift_rep(up, 1), shift_rep(down, -1)
     own = queries.reshape(count, -1, WIDTH).transpose(1, 0, 2).reshape(-1, WIDTH)
-    near = jnp.concatenate([own, cross_z(own, 2)], axis=0)
+    near = jnp.concatenate([own, cross_z(own, 4)], axis=0)
     right, left, mine = call(
         own_cut_kernel,
         [chunk] * 3,
@@ -367,9 +365,8 @@
         [hot_ids, up, down, right, left],
     )
     from_left, from_right = shift_rep(right, 1), shift_rep(left, -1)
-    for bits in (4, 1):
+    for bits in (2, 1):
         near = jnp.concatenate([near, cross_z(near, bits)], axis=0)
-    from_left, from_right, near = lax.optimization_barrier((from_left, from_right, near))
     (mine,) = call(
         settle_kernel,
         [chunk],
@@ -403,43 +400,41 @@
     rows = rows // 2
     part = ((rows + STAT_ROWS, LAT), bf16)
     parts = []
-    for i, hop in enumerate((2, 1, 3, 0)):
+    for i, pair_of in enumerate((((2, 0), (2, 1)), ((1, 0), (3, 0)), ((1, 1), (3, 1)), ((0, 1), (0, 0)))):
         if i > 1:
             lengths, *sent = lax.optimization_barrier((lengths, *parts[2 * i - 4 : 2 * i - 2]))
             parts[2 * i - 4 : 2 * i - 2] = sent
-        same, flipped = call(
-            attend_kernel,
+        (hop_a, half_a), (hop_b, half_b) = pair_of
+        found = [a for group in scores for hop in (hop_a, hop_b) for a in group[hop]]
+        first, second = call(
+            functools.partial(attend_kernel, (half_a, half_b)),
             [part, part],
-            [VMEM] * 5 + [SMEM] * 3 + [VMEM] * (N_C * len(keys)),
-            [asked[hop], *scores[0][hop], *scores[1][hop], lengths, hot_ids, hot_other, *keys, *swapped],
+            [VMEM] * 10 + [SMEM] * 3 + [VMEM] * (N_C * len(keys)),
+            [asked[hop_a], asked[hop_b], *found, lengths, hot_ids, hot_other, *keys, *swapped],
             flops=4 * rows * (LAT + WIDTH // 4) * N_C * N_REP * CHUNK,
         )
-        lengths, same, flipped = lax.optimization_barrier((lengths, same, flipped))
-        parts.append(cross_xz(flipped, hop, 1))
-        parts.append(cross_xz(same, hop, 0) if hop else same)
-
-    n = own.shape[0]
-    message = ((n, LAT + 128), bf16)
-    *sends, mine, stat = call(
-        merge_kernel,
-        [message] * (N_FAR - 1) + [((n, LAT), f32), ((n, 128), f32)],
-        [VMEM] * len(parts),
-        parts,
-    )
-    sends = [cross_z(s, 2 * far) for far, s in enumerate(sends, 1)]
+        lengths, first, second = lax.optimization_barrier((lengths, first, second))
+        if hop_b == 0:
+            first, *sent = lax.optimization_barrier((first, *parts[2 * i - 2 :]))
+            parts[2 * i - 2 :] = sent
+        for value, (hop, half) in zip((first, second), pair_of):
+            parts.append(cross_xz(value, hop, half) if hop or half else value)
+
+    message = ((rows, LAT + 128), bf16)
+    (merged,) = call(merge_kernel, [message], [VMEM] * len(parts), parts)
+    merged = lax.all_to_all(merged, "zf", 0, 0, tiled=True)
     (out,) = call(
-        finish_kernel,
-        [((count, n // count * LAT), bf16)],
-        [VMEM] * (2 + len(sends)),
-        [mine, stat, *sends],
+        finish_kernel, [((count, own.shape[0] // count * LAT), bf16)], [VMEM], [merged]
     )
     return out
 
 
 def solution(mesh):
     assert dict(mesh.shape) == {"ctx": N_X * N_Z * N_C, "rep": N_REP}
-    split = Mesh(mesh.devices.reshape(N_X, N_Z, N_C, N_REP), ("x", "z", "c", "rep"))
-    ctx = ("x", "z", "c")
+    split = Mesh(
+        mesh.devices.reshape(N_X, N_FAR, 2, N_C, N_REP), ("x", "zf", "zp", "c", "rep")
+    )
+    ctx = ("x", "zf", "zp", "c")
     placed = (P((*ctx, "rep"), None), P("rep", ctx), P(ctx), P("rep"))
     return jax.shard_map(
         on_device, mesh=split, in_specs=placed, out_specs=P("rep", ctx), check_vma=False

time: 116 us -> 114 us (0.983)
  blocking collectives: 0 us -> 13.6 us
  starting transfers between devices: 47 us -> 36.6 us
  waiting for transfers between devices: 42.5 us -> 37.3 us
    all_to_all x0 -> x1, blocking collectives: none -> 13.6 us  [on_device(): merged = lax.all_to_all(merged, 'zf', 0, 0, tiled=True)]
    ppermute x13 -> x10, starting transfers between devices: 30 us -> 18.7 us  [the longest x3 9.35 us: cross_z(): return lax.ppermute(a, ('zf', 'zp'), [(i, i ^ bits) for i in range(N_Z)])]
    ppermute x13 -> x10, waiting for transfers between devices: 24.7 us -> 14.2 us  [the longest x7 9.71 us: cross_xz(): return lax.ppermute(a, ('x', 'zf', 'zp'), pairs)]
    ppermute x8, waiting for transfers between devices: 4.71 us -> 9.59 us  [shift_rep(): return lax.ppermute(a, 'rep', [(i, (i + by) % N_REP) for i in range(N_REP)])]
  transfers between devices with their start and end apart: 30 -> 27, of which waited for: 16 -> 12; matrix products, arithmetic and copies ran while one was open for 0% -> 0% of each run, Pallas kernels for 12% -> 16%
where the time goes in v4:
time: 114 us; the launch traced here: 113 us
  waiting for transfers between devices  37.3 us (33%)
  starting transfers between devices  36.6 us (32%)
  Pallas kernels  24.5 us (21%)
  blocking collectives  13.6 us (12%)
    pallas_call x12, Pallas kernels, call(): pl.pallas_call(kernel, out_shape=tuple((jax.ShapeDtypeStruct(*o) for o in...  24.5 us
    all_to_all x1, blocking collectives, on_device(): merged = lax.all_to_all(merged, 'zf', 0, 0, tiled=True)  13.6 us
    ppermute x8, starting transfers between devices, shift_rep(): return lax.ppermute(a, 'rep', [(i, (i + by) % N_REP) for i in range(N_REP)])  12.7 us
    ppermute x3, waiting for transfers between devices, cross_x(): return lax.ppermute(a, 'x', [(i, i ^ bits) for i in range(N_X)])  12 us
    ppermute x7, waiting for transfers between devices, cross_xz(): return lax.ppermute(a, ('x', 'zf', 'zp'), pairs)  9.71 us
    ppermute x8, waiting for transfers between devices, shift_rep(): return lax.ppermute(a, 'rep', [(i, (i + by) % N_REP) for i in range(N_REP)])  9.59 us
    ppermute x3, starting transfers between devices, cross_z(): return lax.ppermute(a, ('zf', 'zp'), [(i, i ^ bits) for i in range(N_Z)])  9.35 us
    ppermute x7, starting transfers between devices, cross_xz(): return lax.ppermute(a, ('x', 'zf', 'zp'), pairs)  9.3 us
  transfers between devices with their start and end apart: 27, of which 12 were waited for; matrix products, arithmetic and copies ran while one was open for 0% of the time, Pallas kernels for 16%

profile of v4, /device:TPU:6, one launch (start us, length us, event | category | flops | bytes accessed | tf_op | source)
XLA Modules:
  0.0 113.1 jit_solution(18343258213880545425)
XLA Ops:
  0.7 1.7 %shard_map.46 = (bf16[576,256]{1,0:T(8,128)(2,1)S(1)}, bf16[576,256]{1,0:T(8,128)(2,1)S(1)}) custom-call(s32[2]{0:T(128)S(1)} %copy-done, bf16[576,4096]{1,0:T(8,128)(2,1)} %bitcast.8), custom_call_target="tpu_custom_call" | custom-call | tf_op jit(solution)/shard_map/pallas_call | solution.py:326
  2.4 1.7 %collective-permute-start = (bf16[576,256]{1,0:T(8,128)(2,1)S(1)}, bf16[576,256]{1,0:T(8,128)(2,1)S(1)}, u32[]{:S(2)}, u32[]{:S(2)}) collective-permute-start(bf16[576,256]{1,0:T(8,128)(2,1)S(1)} %get-tuple-element.83), channel_id=1, source_target_pairs={{0,1},{1,2},{2,3},{3,0},{4,5},{5,6},{6,7},{7,4},{8,9},{9,10},{10,1... | collective-permute-start | bytes 884744 | tf_op jit(solution)/shard_map/ppermute | solution.py:43
  4.0 1.7 %collective-permute-start.1 = (bf16[576,256]{1,0:T(8,128)(2,1)S(1)}, bf16[576,256]{1,0:T(8,128)(2,1)S(1)}, u32[]{:S(2)}, u32[]{:S(2)}) collective-permute-start(bf16[576,256]{1,0:T(8,128)(2,1)S(1)} %get-tuple-element.84), channel_id=1, source_target_pairs={{0,3},{1,0},{2,1},{3,2},{4,7},{5,4},{6,5},{7,6},{8,11},{9,8},{10,9... | collective-permute-start | bytes 884744 | tf_op jit(solution)/shard_map/ppermute | solution.py:43
  5.8 7.3 %collective-permute-start.2 = (bf16[32,576]{1,0:T(8,128)(2,1)S(1)}, bf16[32,576]{1,0:T(8,128)(2,1)S(1)}, u32[]{:S(2)}, u32[]{:S(2)}) collective-permute-start(bf16[32,576]{1,0:T(8,128)(2,1)S(1)} %bitcast.10), channel_id=1, source_target_pairs={{0,32},{8,40},{16,48},{24,56},{32,0},{40,8},{48,16},{56,24},{1,33}... | collective-permute-start | bytes 110600 | tf_op jit(solution)/shard_map/ppermute | solution.py:55
  13.1 2.2 %shard_map.47 = (bf16[576,512]{1,0:T(8,128)(2,1)S(1)}, bf16[576,512]{1,0:T(8,128)(2,1)S(1)}, bf16[576,512]{1,0:T(8,128)(2,1)S(1)}) custom-call(s32[2]{0:T(128)S(1)} %copy-done.1, bf16[576,4096]{1,0:T(8,128)(2,1)} %bitcast.9), custom_call_target="tpu_custom_call" | custom-call | tf_op jit(solution)/shard_map/pallas_call | solution.py:326
  16.6 2.9 %collective-permute-start.4 = (bf16[576,512]{1,0:T(8,128)(2,1)S(1)}, bf16[576,512]{1,0:T(8,128)(2,1)S(1)}, u32[]{:S(2)}, u32[]{:S(2)}) collective-permute-start(bf16[576,512]{1,0:T(8,128)(2,1)S(1)} %get-tuple-element.90), channel_id=1, source_target_pairs={{0,3},{1,0},{2,1},{3,2},{4,7},{5,4},{6,5},{7,6},{8,11},{9,8},{10,9... | collective-permute-start | bytes 1769480 | tf_op jit(solution)/shard_map/ppermute | solution.py:43
  19.4 1.7 %collective-permute-start.7 = (bf16[64,576]{1,0:T(8,128)(2,1)S(1)}, bf16[64,576]{1,0:T(8,128)(2,1)S(1)}, u32[]{:S(2)}, u32[]{:S(2)}) collective-permute-start(bf16[64,576]{1,0:T(8,128)(2,1)S(1)} %pad_maximum_fusion.1), channel_id=1, source_target_pairs={{0,16},{8,24},{16,0},{24,8},{32,48},{40,56},{48,32},{56,40},{1,17}... | collective-permute-start | bytes 221192 | tf_op jit(solution)/shard_map/ppermute | solution.py:55
  21.2 4.5 %collective-permute-done.7 = bf16[64,576]{1,0:T(8,128)(2,1)S(1)} collective-permute-done((bf16[64,576]{1,0:T(8,128)(2,1)S(1)}, bf16[64,576]{1,0:T(8,128)(2,1)S(1)}, u32[]{:S(2)}, u32[]{:S(2)}) %collective-permute-start.7) | collective-permute-done | bytes 73760 | tf_op jit(solution)/shard_map/ppermute | solution.py:55
  26.0 5.8 %collective-permute-done.3.from_left = bf16[576,512]{1,0:T(8,128)(2,1)S(1)} collective-permute-done((bf16[576,512]{1,0:T(8,128)(2,1)S(1)}, bf16[576,512]{1,0:T(8,128)(2,1)S(1)}, u32[]{:S(2)}, u32[]{:S(2)}) %collective-permute-start.3) | collective-permute-done | bytes 589856 | tf_op jit(solution)/shard_map/ppermute | solution.py:43
  32.5 3.0 %collective-permute-start.6 = (bf16[576,512]{1,0:T(8,128)(2,1)S(1)}, bf16[576,512]{1,0:T(8,128)(2,1)S(1)}, u32[]{:S(2)}, u32[]{:S(2)}) collective-permute-start(bf16[576,512]{1,0:T(8,128)(2,1)S(1)} %shard_map.49.refs_4_.refs_13_), channel_id=1, source_target_pairs={{0,3},{1,0},{2,1},{3,2},{4,7},{5,4},{6,5},{7,6},{8,11},{9,8},{10,9... | collective-permute-start | bytes 1769480 | tf_op jit(solution)/shard_map/ppermute | solution.py:43
  36.2 2.4 %collective-permute-start.10 = (bf16[256,576]{1,0:T(8,128)(2,1)S(1)}, bf16[256,576]{1,0:T(8,128)(2,1)S(1)}, u32[]{:S(2)}, u32[]{:S(2)}) collective-permute-start(bf16[256,576]{1,0:T(8,128)(2,1)S(1)} %constant_dynamic-update-slice_fusion.refs_0_.refs_1_), channel_id=1, source_target_pairs={{0,128},{64,192},{128,0},{192,64},{1,129},{65,193},{129,1},{193,65... | collective-permute-start | bytes 884744 | tf_op jit(solution)/shard_map/ppermute | solution.py:51
  38.6 1.2 %collective-permute-start.9 = (bf16[256,576]{1,0:T(8,128)(2,1)S(1)}, bf16[256,576]{1,0:T(8,128)(2,1)S(1)}, u32[]{:S(2)}, u32[]{:S(2)}) collective-permute-start(bf16[256,576]{1,0:T(8,128)(2,1)S(1)} %constant_dynamic-update-slice_fusion.refs_0_.refs_1_), channel_id=1, source_target_pairs={{0,64},{64,0},{128,192},{192,128},{1,65},{65,1},{129,193},{193,129... | collective-permute-start | bytes 884744 | tf_op jit(solution)/shard_map/ppermute | solution.py:51
  39.8 11.4 %collective-permute-done.11.refs_3_.refs_1_ = bf16[256,576]{1,0:T(8,128)(2,1)S(1)} collective-permute-done((bf16[256,576]{1,0:T(8,128)(2,1)S(1)}, bf16[256,576]{1,0:T(8,128)(2,1)S(1)}, u32[]{:S(2)}, u32[]{:S(2)}) %collective-permute-start.11) | collective-permute-done | bytes 294944 | tf_op jit(solution)/shard_map/ppermute | solution.py:51
  52.5 3.0 %collective-permute-start.17 = (bf16[576,256]{1,0:T(8,128)(2,1)S(1)}, bf16[576,256]{1,0:T(8,128)(2,1)S(1)}, u32[]{:S(2)}, u32[]{:S(2)}) collective-permute-start(bf16[576,256]{1,0:T(8,128)(2,1)S(1)} %slice.7), channel_id=1, source_target_pairs={{0,3},{1,0},{2,1},{3,2},{4,7},{5,4},{6,5},{7,6},{8,11},{9,8},{10,9... | collective-permute-start | bytes 884744 | tf_op jit(solution)/shard_map/ppermute | solution.py:43
  55.5 3.2 %shard_map.50 = (f32[256,1536]{1,0:T(8,128)S(1)}, f32[256,128]{1,0:T(8,128)S(1)}, f32[256,1536]{1,0:T(8,128)S(1)}, f32[256,128]{1,0:T(8,128)S(1)}, f32[256,1536]...) custom-call(s32[16]{0:T(128)S(1)} %copy-done.2, s32[2]{0:T(128)S(1)} %copy-done.1, ...), custom_call_target="tpu_custom_call" | custom-call | flops 1811939328 | bytes 8388608 | tf_op jit(solution)/shard_map/pallas_call | solution.py:326
  58.8 3.2 %shard_map.51 = (f32[256,1536]{1,0:T(8,128)S(1)}, f32[256,128]{1,0:T(8,128)S(1)}, f32[256,1536]{1,0:T(8,128)S(1)}, f32[256,128]{1,0:T(8,128)S(1)}, f32[256,1536]...) custom-call(s32[16]{0:T(128)S(1)} %copy-done.2, ...), custom_call_target="tpu_custom_call" | custom-call | flops 1811939328 | bytes 8388608 | tf_op jit(solution)/shard_map/pallas_call | solution.py:326
  62.4 3.4 %collective-permute-done.16.refs_16_ = bf16[576,256]{1,0:T(8,128)(2,1)S(1)} collective-permute-done((bf16[576,256]{1,0:T(8,128)(2,1)S(1)}, bf16[576,256]{1,0:T(8,128)(2,1)S(1)}, u32[]{:S(2)}, u32[]{:S(2)}) %collective-permute-start.16) | collective-permute-done | bytes 294944 | tf_op jit(solution)/shard_map/ppermute | solution.py:43
  66.3 1.1 collective-permute-done.18.refs_21_
  67.8 2.9 %shard_map.52 = (bf16[136,512]{1,0:T(8,128)(2,1)S(1)}, bf16[136,512]{1,0:T(8,128)(2,1)S(1)}) custom-call(bf16[256,576]{1,0:T(8,128)(2,1)S(1)} %collective-permute-done.10.refs_2_.refs_0_.refs_1_, bf16[256,576]{1,0:T(8,128)(2,1)S(1)} %collective-permute-done.10.refs_2_.refs_0_.refs_1_, f32[256,1536]{1,0:T(8,128)S(1)} %get-tuple-element.115.refs_2_.refs_4_, ...), custom_call_target="tpu_custom_call" | custom-call | flops 1375731712 | bytes 8388608 | tf_op jit(solution)/shard_map/pallas_call | solution.py:326
  70.7 1.5 %collective-permute-start.20 = (bf16[136,512]{1,0:T(8,128)(2,1)S(1)}, bf16[136,512]{1,0:T(8,128)(2,1)S(1)}, u32[]{:S(2)}, u32[]{:S(2)}) collective-permute-start(bf16[136,512]{1,0:T(8,128)(2,1)S(1)} %get-tuple-element.135), channel_id=1, source_target_pairs={{0,128},{8,136},{16,144},{24,152},{32,160},{40,168},{48,176},{56,1... | collective-permute-start | bytes 417800 | tf_op jit(solution)/shard_map/ppermute | solution.py:63
  72.2 2.6 %collective-permute-start.21 = (bf16[136,512]{1,0:T(8,128)(2,1)S(1)}, bf16[136,512]{1,0:T(8,128)(2,1)S(1)}, u32[]{:S(2)}, u32[]{:S(2)}) collective-permute-start(bf16[136,512]{1,0:T(8,128)(2,1)S(1)} %get-tuple-element.136), channel_id=1, source_target_pairs={{0,136},{8,128},{16,152},{24,144},{32,168},{40,160},{48,184},{56,1... | collective-permute-start | bytes 417800 | tf_op jit(solution)/shard_map/ppermute | solution.py:63
  74.7 2.8 %shard_map.53 = (bf16[136,512]{1,0:T(8,128)(2,1)S(1)}, bf16[136,512]{1,0:T(8,128)(2,1)S(1)}) custom-call(bf16[256,576]{1,0:T(8,128)(2,1)S(1)} %collective-permute-done.9.refs_1_.refs_0_, bf16[256,576]{1,0:T(8,128)(2,1)S(1)} %collective-permute-done.11.refs_3_.refs_1_, f32[256,1536]{1,0:T(8,128)S(1)} %get-tuple-element.124.refs_2_, ...), custom_call_target="tpu_custom_call" | custom-call | flops 1375731712 | bytes 8388608 | tf_op jit(solution)/shard_map/pallas_call | solution.py:326
  77.6 0.9 collective-permute-start.22
  78.5 1.1 %collective-permute-start.23 = (bf16[136,512]{1,0:T(8,128)(2,1)S(1)}, bf16[136,512]{1,0:T(8,128)(2,1)S(1)}, u32[]{:S(2)}, u32[]{:S(2)}) collective-permute-start(bf16[136,512]{1,0:T(8,128)(2,1)S(1)} %get-tuple-element.144), channel_id=1, source_target_pairs={{0,192},{8,200},{16,208},{24,216},{32,224},{40,232},{48,240},{56,2... | collective-permute-start | bytes 417800 | tf_op jit(solution)/shard_map/ppermute | solution.py:63
  79.6 2.1 %collective-permute-done.20.refs_0_ = bf16[136,512]{1,0:T(8,128)(2,1)S(1)} collective-permute-done((bf16[136,512]{1,0:T(8,128)(2,1)S(1)}, bf16[136,512]{1,0:T(8,128)(2,1)S(1)}, u32[]{:S(2)}, u32[]{:S(2)}) %collective-permute-start.20) | collective-permute-done | bytes 139296 | tf_op jit(solution)/shard_map/ppermute | solution.py:63
  81.8 2.8 %shard_map.54 = (bf16[136,512]{1,0:T(8,128)(2,1)S(1)}, bf16[136,512]{1,0:T(8,128)(2,1)S(1)}) custom-call(bf16[256,576]{1,0:T(8,128)(2,1)S(1)} %collective-permute-done.9.refs_1_.refs_0_, bf16[256,576]{1,0:T(8,128)(2,1)S(1)} %collective-permute-done.11.refs_3_.refs_1_, f32[256,1536]{1,0:T(8,128)S(1)} %get-tuple-element.124.refs_2_, ...), custom_call_target="tpu_custom_call" | custom-call | flops 1375731712 | bytes 8388608 | tf_op jit(solution)/shard_map/pallas_call | solution.py:326
  84.6 1.4 %collective-permute-start.24 = (bf16[136,512]{1,0:T(8,128)(2,1)S(1)}, bf16[136,512]{1,0:T(8,128)(2,1)S(1)}, u32[]{:S(2)}, u32[]{:S(2)}) collective-permute-start(bf16[136,512]{1,0:T(8,128)(2,1)S(1)} %get-tuple-element.155), channel_id=1, source_target_pairs={{0,72},{8,64},{16,88},{24,80},{32,104},{40,96},{48,120},{56,112},{... | collective-permute-start | bytes 417800 | tf_op jit(solution)/shard_map/ppermute | solution.py:63
  86.9 2.8 %shard_map.55 = (bf16[136,512]{1,0:T(8,128)(2,1)S(1)}, bf16[136,512]{1,0:T(8,128)(2,1)S(1)}) custom-call(bf16[256,576]{1,0:T(8,128)(2,1)S(1)} %constant_dynamic-update-slice_fusion.refs_0_.refs_1_, bf16[256,576]{1,0:T(8,128)(2,1)S(1)} %constant_dynamic-update-slice_fusion.refs_0_.refs_1_, f32[256,1536]{1,0:T(8,128)S(1)} %get-tuple-element.148.refs_2_.refs_4_, ...), custom_call_target="tpu_custom_call" | custom-call | flops 1375731712 | bytes 8388608 | tf_op jit(solution)/shard_map/pallas_call | solution.py:326
  89.7 1.5 %collective-permute-done.24.refs_4_ = bf16[136,512]{1,0:T(8,128)(2,1)S(1)} collective-permute-done((bf16[136,512]{1,0:T(8,128)(2,1)S(1)}, bf16[136,512]{1,0:T(8,128)(2,1)S(1)}, u32[]{:S(2)}, u32[]{:S(2)}) %collective-permute-start.24) | collective-permute-done | bytes 139296 | tf_op jit(solution)/shard_map/ppermute | solution.py:63
  91.2 2.0 %collective-permute-done.25.refs_5_ = bf16[136,512]{1,0:T(8,128)(2,1)S(1)} collective-permute-done((bf16[136,512]{1,0:T(8,128)(2,1)S(1)}, bf16[136,512]{1,0:T(8,128)(2,1)S(1)}, u32[]{:S(2)}, u32[]{:S(2)}) %collective-permute-start.25) | collective-permute-done | bytes 139296 | tf_op jit(solution)/shard_map/ppermute | solution.py:63
  94.1 4.1 %collective-permute-done.26.refs_6_ = bf16[136,512]{1,0:T(8,128)(2,1)S(1)} collective-permute-done((bf16[136,512]{1,0:T(8,128)(2,1)S(1)}, bf16[136,512]{1,0:T(8,128)(2,1)S(1)}, u32[]{:S(2)}, u32[]{:S(2)}) %collective-permute-start.26) | collective-permute-done | bytes 139296 | tf_op jit(solution)/shard_map/ppermute | solution.py:63
  98.7 13.6 %all_to_all.11 = bf16[4,32,640]{2,1,0:T(8,128)(2,1)S(1)} all-to-all(bf16[4,32,640]{2,1,0:T(8,128)(2,1)S(1)} %bitcast.6), channel_id=1, replica_groups=mesh['x'=4,'zf'=4,'zp'=2,'c'=2,'rep'=4] {'zf'}, dimensions={0} | all-to-all | bytes 327680 | tf_op jit(solution)/shard_map/all_to_all | solution.py:425
  (52 shorter events, 9.4 us)
Async XLA Ops:
  0.0 0.7 copy-start
  0.7 5.1 %copy-start.3 = (bf16[16,1152]{1,0:T(8,128)(2,1)S(1)}, bf16[16,1152]{1,0:T(8,128)(2,1)}, u32[]{:S(2)}) copy-start(bf16[16,1152]{1,0:T(8,128)(2,1)} %param.5) | copy-start | bytes 110596
  0.7 12.5 %copy-start.1 = (s32[2]{0:T(128)S(1)}, s32[2]{0:T(128)}, u32[]{:S(2)}) copy-start(s32[2]{0:T(128)} %refs_11_.7) | copy-start | bytes 28
  2.4 13.0 %collective-permute-start = (bf16[576,256]{1,0:T(8,128)(2,1)S(1)}, bf16[576,256]{1,0:T(8,128)(2,1)S(1)}, u32[]{:S(2)}, u32[]{:S(2)}) collective-permute-start(bf16[576,256]{1,0:T(8,128)(2,1)S(1)} %get-tuple-element.83), channel_id=1, source_target_pairs={{0,1},{1,2},{2,3},{3,0},{4,5},{5,6},{6,7},{7,4},{8,9},{9,10},{10,1... | collective-permute-start | bytes 884744 | tf_op jit(solution)/shard_map/ppermute | solution.py:43
  4.0 11.3 %collective-permute-start.1 = (bf16[576,256]{1,0:T(8,128)(2,1)S(1)}, bf16[576,256]{1,0:T(8,128)(2,1)S(1)}, u32[]{:S(2)}, u32[]{:S(2)}) collective-permute-start(bf16[576,256]{1,0:T(8,128)(2,1)S(1)} %get-tuple-element.84), channel_id=1, source_target_pairs={{0,3},{1,0},{2,1},{3,2},{4,7},{5,4},{6,5},{7,6},{8,11},{9,8},{10,9... | collective-permute-start | bytes 884744 | tf_op jit(solution)/shard_map/ppermute | solution.py:43
  5.8 9.5 %collective-permute-start.2 = (bf16[32,576]{1,0:T(8,128)(2,1)S(1)}, bf16[32,576]{1,0:T(8,128)(2,1)S(1)}, u32[]{:S(2)}, u32[]{:S(2)}) collective-permute-start(bf16[32,576]{1,0:T(8,128)(2,1)S(1)} %bitcast.10), channel_id=1, source_target_pairs={{0,32},{8,40},{16,48},{24,56},{32,0},{40,8},{48,16},{56,24},{1,33}... | collective-permute-start | bytes 110600 | tf_op jit(solution)/shard_map/ppermute | solution.py:55
  16.1 15.7 %collective-permute-start.3 = (bf16[576,512]{1,0:T(8,128)(2,1)S(1)}, bf16[576,512]{1,0:T(8,128)(2,1)S(1)}, u32[]{:S(2)}, u32[]{:S(2)}) collective-permute-start(bf16[576,512]{1,0:T(8,128)(2,1)S(1)} %get-tuple-element.89), channel_id=1, source_target_pairs={{0,1},{1,2},{2,3},{3,0},{4,5},{5,6},{6,7},{7,4},{8,9},{9,10},{10,1... | collective-permute-start | bytes 1769480 | tf_op jit(solution)/shard_map/ppermute | solution.py:43
  16.6 15.2 %collective-permute-start.4 = (bf16[576,512]{1,0:T(8,128)(2,1)S(1)}, bf16[576,512]{1,0:T(8,128)(2,1)S(1)}, u32[]{:S(2)}, u32[]{:S(2)}) collective-permute-start(bf16[576,512]{1,0:T(8,128)(2,1)S(1)} %get-tuple-element.90), channel_id=1, source_target_pairs={{0,3},{1,0},{2,1},{3,2},{4,7},{5,4},{6,5},{7,6},{8,11},{9,8},{10,9... | collective-permute-start | bytes 1769480 | tf_op jit(solution)/shard_map/ppermute | solution.py:43
  19.4 6.2 %collective-permute-start.7 = (bf16[64,576]{1,0:T(8,128)(2,1)S(1)}, bf16[64,576]{1,0:T(8,128)(2,1)S(1)}, u32[]{:S(2)}, u32[]{:S(2)}) collective-permute-start(bf16[64,576]{1,0:T(8,128)(2,1)S(1)} %pad_maximum_fusion.1), channel_id=1, source_target_pairs={{0,16},{8,24},{16,0},{24,8},{32,48},{40,56},{48,32},{56,40},{1,17}... | collective-permute-start | bytes 221192 | tf_op jit(solution)/shard_map/ppermute | solution.py:55
  25.7 9.9 %collective-permute-start.8 = (bf16[128,576]{1,0:T(8,128)(2,1)S(1)}, bf16[128,576]{1,0:T(8,128)(2,1)S(1)}, u32[]{:S(2)}, u32[]{:S(2)}) collective-permute-start(bf16[128,576]{1,0:T(8,128)(2,1)S(1)} %pad_maximum_fusion), channel_id=1, source_target_pairs={{0,8},{8,0},{16,24},{24,16},{32,40},{40,32},{48,56},{56,48},{1,9},... | collective-permute-start | bytes 442376 | tf_op jit(solution)/shard_map/ppermute | solution.py:55
  31.8 23.7 %copy-start.2 = (s32[16]{0:T(128)S(1)}, s32[16]{0:T(128)}, u32[]{:S(2)}) copy-start(s32[16]{0:T(128)} %refs_10_.4) | copy-start | bytes 196
  32.5 19.3 %collective-permute-start.6 = (bf16[576,512]{1,0:T(8,128)(2,1)S(1)}, bf16[576,512]{1,0:T(8,128)(2,1)S(1)}, u32[]{:S(2)}, u32[]{:S(2)}) collective-permute-start(bf16[576,512]{1,0:T(8,128)(2,1)S(1)} %shard_map.49.refs_4_.refs_13_), channel_id=1, source_target_pairs={{0,3},{1,0},{2,1},{3,2},{4,7},{5,4},{6,5},{7,6},{8,11},{9,8},{10,9... | collective-permute-start | bytes 1769480 | tf_op jit(solution)/shard_map/ppermute | solution.py:43
  35.5 16.3 %collective-permute-start.5 = (bf16[576,512]{1,0:T(8,128)(2,1)S(1)}, bf16[576,512]{1,0:T(8,128)(2,1)S(1)}, u32[]{:S(2)}, u32[]{:S(2)}) collective-permute-start(bf16[576,512]{1,0:T(8,128)(2,1)S(1)} %shard_map.49.refs_4_.refs_13_), channel_id=1, source_target_pairs={{0,1},{1,2},{2,3},{3,0},{4,5},{5,6},{6,7},{7,4},{8,9},{9,10},{10,1... | collective-permute-start | bytes 1769480 | tf_op jit(solution)/shard_map/ppermute | solution.py:43
  35.6 15.6 %collective-permute-start.11 = (bf16[256,576]{1,0:T(8,128)(2,1)S(1)}, bf16[256,576]{1,0:T(8,128)(2,1)S(1)}, u32[]{:S(2)}, u32[]{:S(2)}) collective-permute-start(bf16[256,576]{1,0:T(8,128)(2,1)S(1)} %constant_dynamic-update-slice_fusion.refs_0_.refs_1_), channel_id=1, source_target_pairs={{0,192},{64,128},{128,64},{192,0},{1,193},{65,129},{129,65},{193,1... | collective-permute-start | bytes 884744 | tf_op jit(solution)/shard_map/ppermute | solution.py:51
  36.2 15.0 %collective-permute-start.10 = (bf16[256,576]{1,0:T(8,128)(2,1)S(1)}, bf16[256,576]{1,0:T(8,128)(2,1)S(1)}, u32[]{:S(2)}, u32[]{:S(2)}) collective-permute-start(bf16[256,576]{1,0:T(8,128)(2,1)S(1)} %constant_dynamic-update-slice_fusion.refs_0_.refs_1_), channel_id=1, source_target_pairs={{0,128},{64,192},{128,0},{192,64},{1,129},{65,193},{129,1},{193,65... | collective-permute-start | bytes 884744 | tf_op jit(solution)/shard_map/ppermute | solution.py:51
  38.6 13.2 %collective-permute-start.9 = (bf16[256,576]{1,0:T(8,128)(2,1)S(1)}, bf16[256,576]{1,0:T(8,128)(2,1)S(1)}, u32[]{:S(2)}, u32[]{:S(2)}) collective-permute-start(bf16[256,576]{1,0:T(8,128)(2,1)S(1)} %constant_dynamic-update-slice_fusion.refs_0_.refs_1_), channel_id=1, source_target_pairs={{0,64},{64,0},{128,192},{192,128},{1,65},{65,1},{129,193},{193,129... | collective-permute-start | bytes 884744 | tf_op jit(solution)/shard_map/ppermute | solution.py:51
  51.2 7.6 %collective-permute-start.13 = (bf16[576,512]{1,0:T(8,128)(2,1)S(1)}, bf16[576,512]{1,0:T(8,128)(2,1)S(1)}, u32[]{:S(2)}, u32[]{:S(2)}) collective-permute-start(bf16[576,512]{1,0:T(8,128)(2,1)S(1)} %shard_map.49.refs_4_.refs_13_), channel_id=1, source_target_pairs={{0,4},{4,0},{1,5},{5,1},{2,6},{6,2},{3,7},{7,3},{8,12},{12,8},{9,1... | collective-permute-start | bytes 1769480 | tf_op jit(solution)/shard_map/ppermute | solution.py:47
  51.8 6.9 %collective-permute-start.14 = (bf16[576,512]{1,0:T(8,128)(2,1)S(1)}, bf16[576,512]{1,0:T(8,128)(2,1)S(1)}, u32[]{:S(2)}, u32[]{:S(2)}) collective-permute-start(bf16[576,512]{1,0:T(8,128)(2,1)S(1)} %collective-permute-done.5.refs_5_.refs_14_), channel_id=1, source_target_pairs={{0,4},{4,0},{1,5},{5,1},{2,6},{6,2},{3,7},{7,3},{8,12},{12,8},{9,1... | collective-permute-start | bytes 1769480 | tf_op jit(solution)/shard_map/ppermute | solution.py:47
  51.8 6.9 %collective-permute-start.15 = (bf16[576,512]{1,0:T(8,128)(2,1)S(1)}, bf16[576,512]{1,0:T(8,128)(2,1)S(1)}, u32[]{:S(2)}, u32[]{:S(2)}) collective-permute-start(bf16[576,512]{1,0:T(8,128)(2,1)S(1)} %collective-permute-done.6.refs_6_.refs_15_), channel_id=1, source_target_pairs={{0,4},{4,0},{1,5},{5,1},{2,6},{6,2},{3,7},{7,3},{8,12},{12,8},{9,1... | collective-permute-start | bytes 1769480 | tf_op jit(solution)/shard_map/ppermute | solution.py:47
  52.3 3.2 %collective-permute-start.12 = (s32[2]{0:T(128)S(1)}, s32[2]{0:T(128)S(1)}, u32[]{:S(2)}, u32[]{:S(2)}) collective-permute-start(s32[2]{0:T(128)S(1)} %copy-done.1), channel_id=1, source_target_pairs={{0,4},{4,0},{1,5},{5,1},{2,6},{6,2},{3,7},{7,3},{8,12},{12,8},{9,1... | collective-permute-start | bytes 32 | tf_op jit(solution)/shard_map/ppermute | solution.py:47
  52.5 9.9 %collective-permute-start.17 = (bf16[576,256]{1,0:T(8,128)(2,1)S(1)}, bf16[576,256]{1,0:T(8,128)(2,1)S(1)}, u32[]{:S(2)}, u32[]{:S(2)}) collective-permute-start(bf16[576,256]{1,0:T(8,128)(2,1)S(1)} %slice.7), channel_id=1, source_target_pairs={{0,3},{1,0},{2,1},{3,2},{4,7},{5,4},{6,5},{7,6},{8,11},{9,8},{10,9... | collective-permute-start | bytes 884744 | tf_op jit(solution)/shard_map/ppermute | solution.py:43
  55.5 10.3 %collective-permute-start.16 = (bf16[576,256]{1,0:T(8,128)(2,1)S(1)}, bf16[576,256]{1,0:T(8,128)(2,1)S(1)}, u32[]{:S(2)}, u32[]{:S(2)}) collective-permute-start(bf16[576,256]{1,0:T(8,128)(2,1)S(1)} %slice.6), channel_id=1, source_target_pairs={{0,1},{1,2},{2,3},{3,0},{4,5},{5,6},{6,7},{7,4},{8,9},{9,10},{10,1... | collective-permute-start | bytes 884744 | tf_op jit(solution)/shard_map/ppermute | solution.py:43
  65.8 1.6 %collective-permute-start.18 = (bf16[576,256]{1,0:T(8,128)(2,1)S(1)}, bf16[576,256]{1,0:T(8,128)(2,1)S(1)}, u32[]{:S(2)}, u32[]{:S(2)}) collective-permute-start(bf16[576,256]{1,0:T(8,128)(2,1)S(1)} %collective-permute-done.16.refs_16_), channel_id=1, source_target_pairs={{0,4},{4,0},{1,5},{5,1},{2,6},{6,2},{3,7},{7,3},{8,12},{12,8},{9,1... | collective-permute-start | bytes 884744 | tf_op jit(solution)/shard_map/ppermute | solution.py:47
  65.8 2.0 %collective-permute-start.19 = (bf16[576,256]{1,0:T(8,128)(2,1)S(1)}, bf16[576,256]{1,0:T(8,128)(2,1)S(1)}, u32[]{:S(2)}, u32[]{:S(2)}) collective-permute-start(bf16[576,256]{1,0:T(8,128)(2,1)S(1)} %collective-permute-done.17.refs_17_), channel_id=1, source_target_pairs={{0,4},{4,0},{1,5},{5,1},{2,6},{6,2},{3,7},{7,3},{8,12},{12,8},{9,1... | collective-permute-start | bytes 884744 | tf_op jit(solution)/shard_map/ppermute | solution.py:47
  70.7 11.1 %collective-permute-start.20 = (bf16[136,512]{1,0:T(8,128)(2,1)S(1)}, bf16[136,512]{1,0:T(8,128)(2,1)S(1)}, u32[]{:S(2)}, u32[]{:S(2)}) collective-permute-start(bf16[136,512]{1,0:T(8,128)(2,1)S(1)} %get-tuple-element.135), channel_id=1, source_target_pairs={{0,128},{8,136},{16,144},{24,152},{32,160},{40,168},{48,176},{56,1... | collective-permute-start | bytes 417800 | tf_op jit(solution)/shard_map/ppermute | solution.py:63
  72.2 9.6 %collective-permute-start.21 = (bf16[136,512]{1,0:T(8,128)(2,1)S(1)}, bf16[136,512]{1,0:T(8,128)(2,1)S(1)}, u32[]{:S(2)}, u32[]{:S(2)}) collective-permute-start(bf16[136,512]{1,0:T(8,128)(2,1)S(1)} %get-tuple-element.136), channel_id=1, source_target_pairs={{0,136},{8,128},{16,152},{24,144},{32,168},{40,160},{48,184},{56,1... | collective-permute-start | bytes 417800 | tf_op jit(solution)/shard_map/ppermute | solution.py:63
  77.6 9.3 %collective-permute-start.22 = (bf16[136,512]{1,0:T(8,128)(2,1)S(1)}, bf16[136,512]{1,0:T(8,128)(2,1)S(1)}, u32[]{:S(2)}, u32[]{:S(2)}) collective-permute-start(bf16[136,512]{1,0:T(8,128)(2,1)S(1)} %get-tuple-element.143), channel_id=1, source_target_pairs={{0,64},{8,72},{16,80},{24,88},{32,96},{40,104},{48,112},{56,120},{... | collective-permute-start | bytes 417800 | tf_op jit(solution)/shard_map/ppermute | solution.py:63
  78.5 8.4 %collective-permute-start.23 = (bf16[136,512]{1,0:T(8,128)(2,1)S(1)}, bf16[136,512]{1,0:T(8,128)(2,1)S(1)}, u32[]{:S(2)}, u32[]{:S(2)}) collective-permute-start(bf16[136,512]{1,0:T(8,128)(2,1)S(1)} %get-tuple-element.144), channel_id=1, source_target_pairs={{0,192},{8,200},{16,208},{24,216},{32,224},{40,232},{48,240},{56,2... | collective-permute-start | bytes 417800 | tf_op jit(solution)/shard_map/ppermute | solution.py:63
  84.6 6.6 %collective-permute-start.24 = (bf16[136,512]{1,0:T(8,128)(2,1)S(1)}, bf16[136,512]{1,0:T(8,128)(2,1)S(1)}, u32[]{:S(2)}, u32[]{:S(2)}) collective-permute-start(bf16[136,512]{1,0:T(8,128)(2,1)S(1)} %get-tuple-element.155), channel_id=1, source_target_pairs={{0,72},{8,64},{16,88},{24,80},{32,104},{40,96},{48,120},{56,112},{... | collective-permute-start | bytes 417800 | tf_op jit(solution)/shard_map/ppermute | solution.py:63
  86.0 7.2 %collective-permute-start.25 = (bf16[136,512]{1,0:T(8,128)(2,1)S(1)}, bf16[136,512]{1,0:T(8,128)(2,1)S(1)}, u32[]{:S(2)}, u32[]{:S(2)}) collective-permute-start(bf16[136,512]{1,0:T(8,128)(2,1)S(1)} %get-tuple-element.156), channel_id=1, source_target_pairs={{0,200},{8,192},{16,216},{24,208},{32,232},{40,224},{48,248},{56,2... | collective-permute-start | bytes 417800 | tf_op jit(solution)/shard_map/ppermute | solution.py:63
  93.1 5.1 %collective-permute-start.26 = (bf16[136,512]{1,0:T(8,128)(2,1)S(1)}, bf16[136,512]{1,0:T(8,128)(2,1)S(1)}, u32[]{:S(2)}, u32[]{:S(2)}) collective-permute-start(bf16[136,512]{1,0:T(8,128)(2,1)S(1)} %get-tuple-element.159), channel_id=1, source_target_pairs={{0,8},{8,0},{16,24},{24,16},{32,40},{40,32},{48,56},{56,48},{64,72... | collective-permute-start | bytes 417800 | tf_op jit(solution)/shard_map/ppermute | solution.py:63

commit v5 on v2

--- a/solution.py
+++ b/solution.py
@@ -25,6 +25,8 @@
 PAIR = HOT_GRP * HALF
 CHUNK = 2 * PAIR
 NEVER = -1e30
+STAT_ROWS = 8
+Z_ORDER = (0, 4, 2, 6, 1, 5, 3, 7)
 SCALE = QK**-0.5
 LOG2_E = 1.4426950408889634
 N_FAR = N_Z // 2
@@ -51,14 +53,6 @@
 
 def cross_z(a, bits):
     return lax.ppermute(a, "z", [(i, i ^ bits) for i in range(N_Z)])
-
-
-def cross_xz(a, bits_x, bits_z):
-    pairs = []
-    for x in range(N_X):
-        for z in range(N_Z):
-            pairs.append((x * N_Z + z, (x ^ bits_x) * N_Z + (z ^ bits_z)))
-    return lax.ppermute(a, ("x", "z"), pairs)
 
 
 def column(hot_ref, slot, rank, half):
@@ -160,54 +154,62 @@
     return [hi, mid, low]
 
 
-PLACES = ((0, 0, 2), (3, 0, 2), (1, 0, 2), (2, 0, 1), (2, 1, 1))
-
-
-def attend_kernel(q_ref, len_ref, hot_ref, hot_other_ref, *refs):
-    n = len(PLACES)
-    key_refs, outs = refs[: N_C * n], refs[N_C * n :]
-    x, z, c = lax.axis_index("x"), lax.axis_index("z"), lax.axis_index("c")
-    rank = lax.axis_index("rep")
-    group = (x * N_Z + z) * N_C + c
-    q = q_ref[...]
+def visible_lengths(len_ref, rows):
     count = len_ref.shape[0]
     line = lax.broadcasted_iota(jnp.int32, (count, 1), 0)
     lens = jnp.zeros((count, 1), jnp.int32)
     for i in range(count):
         lens = jnp.where(line == i, len_ref[i], lens)
-    lens = jnp.concatenate([lens] * (q.shape[0] // count), axis=0)
+    return jnp.concatenate([lens] * (rows // count), axis=0)
+
+
+def row_numbers(hot_ref, other, away, half, halves):
+    x, z, c = lax.axis_index("x"), lax.axis_index("z"), lax.axis_index("c")
+    group = (x * N_Z + z) * N_C + c + other * (1 - 2 * c)
+    at = (lax.axis_index("rep") + away) % N_REP * QUARTER
     lane = lax.broadcasted_iota(jnp.int32, (1, HALF), 1)
+    return jnp.concatenate(
+        [
+            (group * BPG + hot_ref[slot]) * BLK + at + h * HALF + lane
+            for h in range(half, half + halves)
+            for slot in range(HOT_GRP)
+        ],
+        axis=1,
+    )
+
+
+PLACES = ((0, 0, 2), (3, 0, 2), (1, 0, 2), (2, 0, 1), (2, 1, 1))
+
+
+def fold(op, s):
+    return functools.reduce(op, [s[:, i : i + 128] for i in range(0, s.shape[1], 128)])
+
+
+def attend_kernel(q_ref, len_ref, hot_ref, hot_other_ref, *refs):
+    n = len(PLACES)
+    key_refs, o_ref = refs[:-1], refs[-1]
+    q = q_ref[...]
+    lens = visible_lengths(len_ref, q.shape[0])
     parts = []
-    for other in range(N_C):
+    for other, hot in enumerate((hot_ref, hot_other_ref)):
         keys = key_refs[other * n : (other + 1) * n]
-        hot = hot_other_ref if other else hot_ref
-        own_group = group + other * (1 - 2 * c)
         scores = []
-        for k_ref, (away, half, halves) in zip(keys, PLACES):
-            at = (rank + away) % N_REP * QUARTER
-            rows = jnp.concatenate(
-                [
-                    (own_group * BPG + hot[slot]) * BLK + at + h * HALF + lane
-                    for h in range(half, half + halves)
-                    for slot in range(HOT_GRP)
-                ],
-                axis=1,
-            )
+        for k_ref, place in zip(keys, PLACES):
+            numbers = row_numbers(hot, other, *place)
             s = jnp.dot(q, k_ref[...], preferred_element_type=f32)
-            scores.append(jnp.where(rows < lens, s, NEVER))
-        peak = scores[0].max(axis=1, keepdims=True)
-        for s in scores[1:]:
-            peak = jnp.maximum(peak, s.max(axis=1, keepdims=True))
-        total = jnp.zeros_like(peak)
+            scores.append(jnp.where(numbers < lens, s, NEVER))
+        peak = functools.reduce(jnp.maximum, [fold(jnp.maximum, s) for s in scores])
+        peak = peak.max(axis=1, keepdims=True)
+        total = 0.0
         numer = None
         for s, k_ref in zip(scores, keys):
             w = jnp.exp2((s - peak) * (SCALE * LOG2_E)).astype(bf16)
-            total = total + jnp.sum(w.astype(f32), axis=1, keepdims=True)
+            total = total + fold(jnp.add, w.astype(f32))
             v = lax.dot_general(
                 w, k_ref[:LAT, :], (((1,), (1,)), ((), ())), preferred_element_type=f32
             )
             numer = v if numer is None else numer + v
-        parts.append((peak, total, numer))
+        parts.append((peak, total.sum(axis=1, keepdims=True), numer))
     top = jnp.maximum(parts[0][0], parts[1][0])
     numer, total = 0.0, 0.0
     for peak, t, v in parts:
@@ -215,26 +217,19 @@
         numer = numer + v * f
         total = total + t * f
     o = (numer * (1.0 / jnp.maximum(total, 1.0))).astype(bf16)
-    lanes = lax.broadcasted_iota(jnp.int32, (q.shape[0], 128), 1)
+    rows = q.shape[0]
+    lanes = lax.broadcasted_iota(jnp.int32, (rows, 128), 1)
     stats = jnp.where(lanes == 0, top * SCALE, total).T[:2, :]
-    rows = o.shape[0] // 2
-    for flip, o_ref in enumerate(outs):
-        o_ref[:rows, :] = o[flip * rows : (flip + 1) * rows]
-        mine = stats[:, flip * rows : (flip + 1) * rows]
-        terms = three_terms(mine[0:1]) + three_terms(mine[1:2])
-        terms = [t.astype(f32) for t in terms] + [jnp.zeros((10, rows), f32)]
-        o_ref[rows:, :rows] = jnp.concatenate(terms, axis=0).astype(bf16)
-        o_ref[rows:, rows:] = jnp.zeros((16, LAT - rows), bf16)
+    terms = three_terms(stats[0:1]) + three_terms(stats[1:2])
+    terms = [t.astype(f32) for t in terms] + [jnp.zeros((STAT_ROWS - 6, rows), f32)]
+    o_ref[:rows, :] = o
+    o_ref[rows:, :rows] = jnp.concatenate(terms, axis=0).astype(bf16)
+    o_ref[rows:, rows:] = jnp.zeros((STAT_ROWS, LAT - rows), bf16)
 
 
 def merge_kernel(*refs):
-    n_in = N_X * 2
-    parts, sends, (own_ref, stat_ref) = (
-        refs[:n_in],
-        refs[n_in : n_in + N_FAR - 1],
-        refs[n_in + N_FAR - 1 :],
-    )
-    rows = parts[0].shape[0] - 16
+    parts, outs = refs[:N_X], refs[N_X:]
+    rows = parts[0].shape[0] - STAT_ROWS
     tops, totals = [], []
     for p in parts:
         s = p[rows:, :rows].astype(f32)
@@ -247,40 +242,32 @@
     table = [w * inv for w in weights] + [top, total]
     table.append(jnp.zeros((128 - len(table), rows), f32))
     table = jnp.concatenate(table, axis=0).T
-    n = rows // N_FAR
+    n = rows // N_Z
     lane = lax.broadcasted_iota(jnp.int32, (n, 128), 1)
-    for far in range(N_FAR):
-        at = slice(far * n, (far + 1) * n)
+    for i, ref in enumerate(outs):
+        at = slice(i * n, (i + 1) * n)
         acc = 0.0
-        for i, p in enumerate(parts):
-            acc = acc + p[at, :].astype(f32) * table[at, i : i + 1]
-        if far:
-            ref = sends[far - 1]
-            ref[:, :LAT] = acc.astype(bf16)
-            packed = jnp.zeros((n, 128), f32)
-            terms = three_terms(table[at, n_in : n_in + 1])
-            terms += three_terms(table[at, n_in + 1 : n_in + 2])
-            for i, term in enumerate(terms):
-                packed = jnp.where(lane == i, term.astype(f32), packed)
-            ref[:, LAT:] = packed.astype(bf16)
-        else:
-            own_ref[...] = acc
-            stat_ref[...] = table[at]
-
-
-def finish_kernel(own_ref, stat_ref, *refs):
-    parts, out_ref = refs[:-1], refs[-1]
-    n_in = N_X * 2
-    tops, totals, values = [stat_ref[:, n_in : n_in + 1]], [stat_ref[:, n_in + 1 : n_in + 2]], [own_ref[...]]
+        for j, p in enumerate(parts):
+            acc = acc + p[at, :].astype(f32) * table[at, j : j + 1]
+        ref[:, :LAT] = acc.astype(ref.dtype)
+        packed = jnp.zeros((n, 128), f32)
+        terms = three_terms(table[at, N_X : N_X + 1])
+        terms += three_terms(table[at, N_X + 1 : N_X + 2])
+        for j, term in enumerate(terms):
+            packed = jnp.where(lane == j, term.astype(f32), packed)
+        ref[:, LAT:] = packed.astype(ref.dtype)
+
+
+def finish_kernel(*refs):
+    parts, out_ref = [r[...].astype(f32) for r in refs[:-1]], refs[-1]
+    tops, totals = [], []
     for p in parts:
-        s = p[:, LAT:].astype(f32)
+        s = p[:, LAT:]
         tops.append(s[:, 0:1] + s[:, 1:2] + s[:, 2:3])
         totals.append(s[:, 3:4] + s[:, 4:5] + s[:, 5:6])
-        values.append(p[:, :LAT].astype(f32))
     top = functools.reduce(jnp.maximum, tops)
     weights = [t * jnp.exp(m - top) for m, t in zip(tops, totals)]
-    total = sum(weights)
-    o = sum(v * w for v, w in zip(values, weights)) / total
+    o = sum(p[:, :LAT] * w for p, w in zip(parts, weights)) / sum(weights)
     count = out_ref.shape[0]
     for head in range(o.shape[0] // count):
         out_ref[:, head * LAT : (head + 1) * LAT] = o[head * count : (head + 1) * count].astype(bf16)
@@ -311,6 +298,8 @@
         scratch_shapes=[pltpu.SemaphoreType.DMA((4,))],
     )
     up, down = shift_rep(up, 1), shift_rep(down, -1)
+    own = queries.reshape(count, -1, WIDTH).transpose(1, 0, 2).reshape(-1, WIDTH)
+    near = jnp.concatenate([own, cross_z(own, 4)], axis=0)
     right, left, mine = call(
         own_cut_kernel,
         [chunk] * 3,
@@ -319,6 +308,7 @@
         mib=50,
         scratch_shapes=[pltpu.SemaphoreType.DMA((12,))],
     )
+    up, down, near = lax.optimization_barrier((up, down, near))
     right, left = call(
         pass_on_kernel,
         [chunk] * 2,
@@ -326,53 +316,50 @@
         [hot_ids, up, down, right, left],
     )
     from_left, from_right = shift_rep(right, 1), shift_rep(left, -1)
+    for bits in (2, 1):
+        near = jnp.concatenate([near, cross_z(near, bits)], axis=0)
     (mine,) = call(
         settle_kernel,
         [chunk],
         [SMEM] + [VMEM] * 3,
         [hot_ids, from_left, from_right, mine],
     )
-
-    own = queries.reshape(count, -1, WIDTH).transpose(1, 0, 2).reshape(-1, WIDTH)
-    near = own
-    for bits in (2, 4, 1):
-        near = jnp.concatenate([near, cross_z(near, bits)], axis=0)
     asked = [near] + [cross_x(near, bits) for bits in range(1, N_X)]
     hot_other = swap_core(hot_ids)
 
     of_left, of_right = shift_rep(mine, 1), shift_rep(mine, -1)
     far_a, far_b = shift_rep(of_left[:, :PAIR], 1), shift_rep(of_right[:, PAIR:], -1)
+    far_a, far_b, *asked = lax.optimization_barrier((far_a, far_b, *asked))
     keys = [mine, of_left, of_right, far_a, far_b]
     keys = keys + [swap_core(k) for k in keys]
 
-    rows = near.shape[0] // 2
-    part = ((rows + 16, LAT), bf16)
+    rows = near.shape[0]
     parts = []
-    for hop in (2, 1, 3, 0):
-        same, flipped = call(
+    for i, hop in enumerate((2, 1, 3, 0)):
+        if i > 1:
+            lengths, parts[i - 2] = lax.optimization_barrier((lengths, parts[i - 2]))
+        (o,) = call(
             attend_kernel,
-            [part, part],
+            [((rows + STAT_ROWS, LAT), bf16)],
             [VMEM, SMEM, SMEM, SMEM] + [VMEM] * len(keys),
-            [asked[hop], lengths, hot_ids, hot_other] + keys,
+            [asked[hop], lengths, hot_ids, hot_other, *keys],
         )
-        lengths, same, flipped = lax.optimization_barrier((lengths, same, flipped))
-        parts.append(cross_xz(flipped, hop, 1))
-        parts.append(cross_xz(same, hop, 0) if hop else same)
+        lengths, o = lax.optimization_barrier((lengths, o))
+        parts.append(cross_x(o, hop) if hop else o)
 
     n = own.shape[0]
-    message = ((n, LAT + 128), bf16)
-    *sends, mine, stat = call(
+    ours, *sends = call(
         merge_kernel,
-        [message] * (N_FAR - 1) + [((n, LAT), f32), ((n, 128), f32)],
-        [VMEM] * len(parts),
+        [((n, LAT + 128), f32 if i == 0 else bf16) for i in range(N_Z)],
+        [VMEM] * N_X,
         parts,
     )
-    sends = [cross_z(s, 2 * far) for far, s in enumerate(sends, 1)]
+    sends = [cross_z(s, bits) for s, bits in zip(sends, Z_ORDER[1:])]
     (out,) = call(
         finish_kernel,
         [((count, n // count * LAT), bf16)],
-        [VMEM] * (2 + len(sends)),
-        [mine, stat, *sends],
+        [VMEM] * N_Z,
+        [ours, *sends],
     )
     return out
 

time: 108 us -> 109 us (level)
  waiting for transfers between devices: 32.3 us -> 39.2 us
  starting transfers between devices: 50.1 us -> 44.2 us
    ppermute x7 -> x0, starting transfers between devices: 12.6 us -> none  [cross_xz(): return lax.ppermute(a, ('x', 'z'), pairs)]
    ppermute x3 -> x6, waiting for transfers between devices: 0.53 us -> 9.57 us  [cross_x(): return lax.ppermute(a, 'x', [(i, i ^ bits) for i in range(N_X)])]
    ppermute x7 -> x0, waiting for transfers between devices: 5.02 us -> none  [cross_xz(): return lax.ppermute(a, ('x', 'z'), pairs)]
    ppermute x8, waiting for transfers between devices: 15 us -> 18.3 us  [shift_rep(): return lax.ppermute(a, 'rep', [(i, (i + by) % N_REP) for i in range(N_REP)])]
    ppermute x3 -> x6, starting transfers between devices: 3.53 us -> 6.54 us  [cross_x(): return lax.ppermute(a, 'x', [(i, i ^ bits) for i in range(N_X)])]
    ppermute x6 -> x10, starting transfers between devices: 20.1 us -> 23.2 us  [cross_z(): return lax.ppermute(a, 'z', [(i, i ^ bits) for i in range(N_Z)])]
    ppermute x6 -> x10, waiting for transfers between devices: 11.7 us -> 9.78 us  [cross_z(): return lax.ppermute(a, 'z', [(i, i ^ bits) for i in range(N_Z)])]
    ppermute x6, waiting for transfers between devices: 0.02 us -> 1.5 us  [swap_core(): return lax.ppermute(a, 'c', [(0, 1), (1, 0)])]
  transfers between devices with their start and end apart: 30 -> 30, of which waited for: 11 -> 14; matrix products, arithmetic and copies ran while one was open for 0% -> 0% of each run, Pallas kernels for 18% -> 15%
where the time goes in v5:
time: 109 us
  starting transfers between devices  44.2 us (41%)
  waiting for transfers between devices  39.2 us (36%)
  Pallas kernels  24 us (22%)
    pallas_call x10, Pallas kernels, call(): pl.pallas_call(kernel, out_shape=tuple((jax.ShapeDtypeStruct(*o) for o in...  24 us
    ppermute x10, starting transfers between devices, cross_z(): return lax.ppermute(a, 'z', [(i, i ^ bits) for i in range(N_Z)])  23.2 us
    ppermute x8, waiting for transfers between devices, shift_rep(): return lax.ppermute(a, 'rep', [(i, (i + by) % N_REP) for i in range(N_REP)])  18.3 us
    ppermute x8, starting transfers between devices, shift_rep(): return lax.ppermute(a, 'rep', [(i, (i + by) % N_REP) for i in range(N_REP)])  13.5 us
    ppermute x10, waiting for transfers between devices, cross_z(): return lax.ppermute(a, 'z', [(i, i ^ bits) for i in range(N_Z)])  9.78 us
    ppermute x6, waiting for transfers between devices, cross_x(): return lax.ppermute(a, 'x', [(i, i ^ bits) for i in range(N_X)])  9.57 us
    ppermute x6, starting transfers between devices, cross_x(): return lax.ppermute(a, 'x', [(i, i ^ bits) for i in range(N_X)])  6.54 us
  transfers between devices with their start and end apart: 30, of which 14 were waited for; matrix products, arithmetic and copies ran while one was open for 0% of the time, Pallas kernels for 15%

profile of v5, /device:TPU:6, one launch (start us, length us, event | category | flops | bytes accessed | tf_op | source)
XLA Modules:
  0.0 108.6 jit_solution(4904235217108389344)
XLA Ops:
  0.7 1.7 %shard_map.46 = (bf16[576,256]{1,0:T(8,128)(2,1)S(1)}, bf16[576,256]{1,0:T(8,128)(2,1)S(1)}) custom-call(s32[2]{0:T(128)S(1)} %copy-done, bf16[576,4096]{1,0:T(8,128)(2,1)} %bitcast.4), custom_call_target="tpu_custom_call" | custom-call | tf_op jit(solution)/shard_map/pallas_call | solution.py:277
  2.5 1.6 %collective-permute-start = (bf16[576,256]{1,0:T(8,128)(2,1)S(1)}, bf16[576,256]{1,0:T(8,128)(2,1)S(1)}, u32[]{:S(2)}, u32[]{:S(2)}) collective-permute-start(bf16[576,256]{1,0:T(8,128)(2,1)S(1)} %get-tuple-element.40), channel_id=1, source_target_pairs={{0,1},{1,2},{2,3},{3,0},{4,5},{5,6},{6,7},{7,4},{8,9},{9,10},{10,1... | collective-permute-start | bytes 884744 | tf_op jit(solution)/shard_map/ppermute | solution.py:43
  4.1 1.7 %collective-permute-start.1 = (bf16[576,256]{1,0:T(8,128)(2,1)S(1)}, bf16[576,256]{1,0:T(8,128)(2,1)S(1)}, u32[]{:S(2)}, u32[]{:S(2)}) collective-permute-start(bf16[576,256]{1,0:T(8,128)(2,1)S(1)} %get-tuple-element.41), channel_id=1, source_target_pairs={{0,3},{1,0},{2,1},{3,2},{4,7},{5,4},{6,5},{7,6},{8,11},{9,8},{10,9... | collective-permute-start | bytes 884744 | tf_op jit(solution)/shard_map/ppermute | solution.py:43
  5.9 7.3 %collective-permute-start.2 = (bf16[32,576]{1,0:T(8,128)(2,1)S(1)}, bf16[32,576]{1,0:T(8,128)(2,1)S(1)}, u32[]{:S(2)}, u32[]{:S(2)}) collective-permute-start(bf16[32,576]{1,0:T(8,128)(2,1)S(1)} %bitcast.6), channel_id=1, source_target_pairs={{0,32},{8,40},{16,48},{24,56},{32,0},{40,8},{48,16},{56,24},{1,33}... | collective-permute-start | bytes 110600 | tf_op jit(solution)/shard_map/ppermute | solution.py:55
  13.2 2.3 %shard_map.47 = (bf16[576,512]{1,0:T(8,128)(2,1)S(1)}, bf16[576,512]{1,0:T(8,128)(2,1)S(1)}, bf16[576,512]{1,0:T(8,128)(2,1)S(1)}) custom-call(s32[2]{0:T(128)S(1)} %copy-done.1, bf16[576,4096]{1,0:T(8,128)(2,1)} %bitcast.5), custom_call_target="tpu_custom_call" | custom-call | tf_op jit(solution)/shard_map/pallas_call | solution.py:277
  16.6 3.0 %collective-permute-start.4 = (bf16[576,512]{1,0:T(8,128)(2,1)S(1)}, bf16[576,512]{1,0:T(8,128)(2,1)S(1)}, u32[]{:S(2)}, u32[]{:S(2)}) collective-permute-start(bf16[576,512]{1,0:T(8,128)(2,1)S(1)} %get-tuple-element.47), channel_id=1, source_target_pairs={{0,3},{1,0},{2,1},{3,2},{4,7},{5,4},{6,5},{7,6},{8,11},{9,8},{10,9... | collective-permute-start | bytes 1769480 | tf_op jit(solution)/shard_map/ppermute | solution.py:43
  19.6 1.7 %collective-permute-start.9 = (bf16[64,576]{1,0:T(8,128)(2,1)S(1)}, bf16[64,576]{1,0:T(8,128)(2,1)S(1)}, u32[]{:S(2)}, u32[]{:S(2)}) collective-permute-start(bf16[64,576]{1,0:T(8,128)(2,1)S(1)} %pad_maximum_fusion.1), channel_id=1, source_target_pairs={{0,16},{8,24},{16,0},{24,8},{32,48},{40,56},{48,32},{56,40},{1,17}... | collective-permute-start | bytes 221192 | tf_op jit(solution)/shard_map/ppermute | solution.py:55
  21.3 4.6 %collective-permute-done.9 = bf16[64,576]{1,0:T(8,128)(2,1)S(1)} collective-permute-done((bf16[64,576]{1,0:T(8,128)(2,1)S(1)}, bf16[64,576]{1,0:T(8,128)(2,1)S(1)}, u32[]{:S(2)}, u32[]{:S(2)}) %collective-permute-start.9) | collective-permute-done | bytes 73760 | tf_op jit(solution)/shard_map/ppermute | solution.py:55
  26.1 5.8 %collective-permute-done.3.from_left = bf16[576,512]{1,0:T(8,128)(2,1)S(1)} collective-permute-done((bf16[576,512]{1,0:T(8,128)(2,1)S(1)}, bf16[576,512]{1,0:T(8,128)(2,1)S(1)}, u32[]{:S(2)}, u32[]{:S(2)}) %collective-permute-start.3) | collective-permute-done | bytes 589856 | tf_op jit(solution)/shard_map/ppermute | solution.py:43
  32.6 3.0 %collective-permute-start.7 = (bf16[576,512]{1,0:T(8,128)(2,1)S(1)}, bf16[576,512]{1,0:T(8,128)(2,1)S(1)}, u32[]{:S(2)}, u32[]{:S(2)}) collective-permute-start(bf16[576,512]{1,0:T(8,128)(2,1)S(1)} %shard_map.49.refs_0_), channel_id=1, source_target_pairs={{0,3},{1,0},{2,1},{3,2},{4,7},{5,4},{6,5},{7,6},{8,11},{9,8},{10,9... | collective-permute-start | bytes 1769480 | tf_op jit(solution)/shard_map/ppermute | solution.py:43
  36.3 2.4 %collective-permute-start.12 = (bf16[256,576]{1,0:T(8,128)(2,1)S(1)}, bf16[256,576]{1,0:T(8,128)(2,1)S(1)}, u32[]{:S(2)}, u32[]{:S(2)}) collective-permute-start(bf16[256,576]{1,0:T(8,128)(2,1)S(1)} %constant_dynamic-update-slice_fusion.q_ref), channel_id=1, source_target_pairs={{0,128},{64,192},{128,0},{192,64},{1,129},{65,193},{129,1},{193,65... | collective-permute-start | bytes 884744 | tf_op jit(solution)/shard_map/ppermute | solution.py:51
  38.7 1.2 %collective-permute-start.11 = (bf16[256,576]{1,0:T(8,128)(2,1)S(1)}, bf16[256,576]{1,0:T(8,128)(2,1)S(1)}, u32[]{:S(2)}, u32[]{:S(2)}) collective-permute-start(bf16[256,576]{1,0:T(8,128)(2,1)S(1)} %constant_dynamic-update-slice_fusion.q_ref), channel_id=1, source_target_pairs={{0,64},{64,0},{128,192},{192,128},{1,65},{65,1},{129,193},{193,129... | collective-permute-start | bytes 884744 | tf_op jit(solution)/shard_map/ppermute | solution.py:51
  39.9 6.3 %collective-permute-done.7.refs_2_ = bf16[576,512]{1,0:T(8,128)(2,1)S(1)} collective-permute-done((bf16[576,512]{1,0:T(8,128)(2,1)S(1)}, bf16[576,512]{1,0:T(8,128)(2,1)S(1)}, u32[]{:S(2)}, u32[]{:S(2)}) %collective-permute-start.7) | collective-permute-done | bytes 589856 | tf_op jit(solution)/shard_map/ppermute | solution.py:43
  46.2 3.8 %collective-permute-start.8 = (bf16[576,256]{1,0:T(8,128)(2,1)S(1)}, bf16[576,256]{1,0:T(8,128)(2,1)S(1)}, u32[]{:S(2)}, u32[]{:S(2)}) collective-permute-start(bf16[576,256]{1,0:T(8,128)(2,1)S(1)} %slice.9), channel_id=1, source_target_pairs={{0,3},{1,0},{2,1},{3,2},{4,7},{5,4},{6,5},{7,6},{8,11},{9,8},{10,9... | collective-permute-start | bytes 884744 | tf_op jit(solution)/shard_map/ppermute | solution.py:43
  50.1 1.1 collective-permute-done.13.q_ref
  51.8 2.4 %collective-permute-done.8.refs_4_ = bf16[576,256]{1,0:T(8,128)(2,1)S(1)} collective-permute-done((bf16[576,256]{1,0:T(8,128)(2,1)S(1)}, bf16[576,256]{1,0:T(8,128)(2,1)S(1)}, u32[]{:S(2)}, u32[]{:S(2)}) %collective-permute-start.8) | collective-permute-done | bytes 294944 | tf_op jit(solution)/shard_map/ppermute | solution.py:43
  54.2 3.8 %collective-permute-done.6.refs_3_ = bf16[576,256]{1,0:T(8,128)(2,1)S(1)} collective-permute-done((bf16[576,256]{1,0:T(8,128)(2,1)S(1)}, bf16[576,256]{1,0:T(8,128)(2,1)S(1)}, u32[]{:S(2)}, u32[]{:S(2)}) %collective-permute-start.6) | collective-permute-done | bytes 294944 | tf_op jit(solution)/shard_map/ppermute | solution.py:43
  58.6 1.1 collective-permute-done.18.refs_8_
  60.1 4.3 %shard_map.50 = bf16[264,512]{1,0:T(8,128)(2,1)S(1)} custom-call(bf16[256,576]{1,0:T(8,128)(2,1)S(1)} %collective-permute-done.12.q_ref, s32[16]{0:T(128)S(1)} %copy-done.2, s32[2]{0:T(128)S(1)} %copy-done.1, s32[2]{0:T(128)S(1)} %collective-permute-done.14.hot_other_ref, bf16[576,512]{1,0:T(8,128)(2,1)S(1)} %shard_map.49.refs_0_, ...), custom_call_target="tpu_custom_call" | custom-call | tf_op jit(solution)/shard_map/pallas_call | solution.py:277
  64.3 1.7 %collective-permute-start.20 = (bf16[264,512]{1,0:T(8,128)(2,1)S(1)}, bf16[264,512]{1,0:T(8,128)(2,1)S(1)}, u32[]{:S(2)}, u32[]{:S(2)}) collective-permute-start(bf16[264,512]{1,0:T(8,128)(2,1)S(1)} %shard_map.50), channel_id=1, source_target_pairs={{0,128},{64,192},{128,0},{192,64},{1,129},{65,193},{129,1},{193,65... | collective-permute-start | bytes 811016 | tf_op jit(solution)/shard_map/ppermute | solution.py:51
  66.0 4.3 %shard_map.51 = bf16[264,512]{1,0:T(8,128)(2,1)S(1)} custom-call(bf16[256,576]{1,0:T(8,128)(2,1)S(1)} %collective-permute-done.11.q_ref, s32[16]{0:T(128)S(1)} %copy-done.2, s32[2]{0:T(128)S(1)} %copy-done.1, s32[2]{0:T(128)S(1)} %collective-permute-done.14.hot_other_ref, bf16[576,512]{1,0:T(8,128)(2,1)S(1)} %shard_map.49.refs_0_, ...), custom_call_target="tpu_custom_call" | custom-call | tf_op jit(solution)/shard_map/pallas_call | solution.py:277
  70.4 4.2 %collective-permute-done.20.refs_0_ = bf16[264,512]{1,0:T(8,128)(2,1)S(1)} collective-permute-done((bf16[264,512]{1,0:T(8,128)(2,1)S(1)}, bf16[264,512]{1,0:T(8,128)(2,1)S(1)}, u32[]{:S(2)}, u32[]{:S(2)}) %collective-permute-start.20) | collective-permute-done | bytes 270368 | tf_op jit(solution)/shard_map/ppermute | solution.py:51
  74.6 4.3 %shard_map.52 = bf16[264,512]{1,0:T(8,128)(2,1)S(1)} custom-call(bf16[256,576]{1,0:T(8,128)(2,1)S(1)} %collective-permute-done.13.q_ref, s32[16]{0:T(128)S(1)} %copy-done.2, s32[2]{0:T(128)S(1)} %copy-done.1, s32[2]{0:T(128)S(1)} %collective-permute-done.14.hot_other_ref, bf16[576,512]{1,0:T(8,128)(2,1)S(1)} %shard_map.49.refs_0_, ...), custom_call_target="tpu_custom_call" | custom-call | tf_op jit(solution)/shard_map/pallas_call | solution.py:277
  79.5 4.3 %shard_map.53.refs_3_ = bf16[264,512]{1,0:T(8,128)(2,1)S(1)} custom-call(bf16[256,576]{1,0:T(8,128)(2,1)S(1)} %constant_dynamic-update-slice_fusion.q_ref, s32[16]{0:T(128)S(1)} %copy-done.2, s32[2]{0:T(128)S(1)} %copy-done.1, s32[2]{0:T(128)S(1)} %collective-permute-done.14.hot_other_ref, bf16[576,512]{1,0:T(8,128)(2,1)S(1)} %shard_map.49.refs_0_, ...), custom_call_target="tpu_custom_call" | custom-call | tf_op jit(solution)/shard_map/pallas_call | solution.py:277
  83.7 4.2 %collective-permute-done.22.refs_2_ = bf16[264,512]{1,0:T(8,128)(2,1)S(1)} collective-permute-done((bf16[264,512]{1,0:T(8,128)(2,1)S(1)}, bf16[264,512]{1,0:T(8,128)(2,1)S(1)}, u32[]{:S(2)}, u32[]{:S(2)}) %collective-permute-start.22) | collective-permute-done | bytes 270368 | tf_op jit(solution)/shard_map/ppermute | solution.py:51
  88.5 4.1 %collective-permute-start.23 = (bf16[32,640]{1,0:T(8,128)(2,1)S(1)}, bf16[32,640]{1,0:T(8,128)(2,1)S(1)}, u32[]{:S(2)}, u32[]{:S(2)}) collective-permute-start(bf16[32,640]{1,0:T(8,128)(2,1)S(1)} %get-tuple-element.68), channel_id=1, source_target_pairs={{0,32},{8,40},{16,48},{24,56},{32,0},{40,8},{48,16},{56,24},{1,33}... | collective-permute-start | bytes 122888 | tf_op jit(solution)/shard_map/ppermute | solution.py:55
  92.6 1.5 %collective-permute-start.24 = (bf16[32,640]{1,0:T(8,128)(2,1)S(1)}, bf16[32,640]{1,0:T(8,128)(2,1)S(1)}, u32[]{:S(2)}, u32[]{:S(2)}) collective-permute-start(bf16[32,640]{1,0:T(8,128)(2,1)S(1)} %get-tuple-element.69), channel_id=1, source_target_pairs={{0,16},{8,24},{16,0},{24,8},{32,48},{40,56},{48,32},{56,40},{1,17}... | collective-permute-start | bytes 122888 | tf_op jit(solution)/shard_map/ppermute | solution.py:55
  95.1 1.2 %collective-permute-start.26 = (bf16[32,640]{1,0:T(8,128)(2,1)S(1)}, bf16[32,640]{1,0:T(8,128)(2,1)S(1)}, u32[]{:S(2)}, u32[]{:S(2)}) collective-permute-start(bf16[32,640]{1,0:T(8,128)(2,1)S(1)} %get-tuple-element.71), channel_id=1, source_target_pairs={{0,8},{8,0},{16,24},{24,16},{32,40},{40,32},{48,56},{56,48},{1,9},... | collective-permute-start | bytes 122888 | tf_op jit(solution)/shard_map/ppermute | solution.py:55
  96.3 3.4 %collective-permute-start.27 = (bf16[32,640]{1,0:T(8,128)(2,1)S(1)}, bf16[32,640]{1,0:T(8,128)(2,1)S(1)}, u32[]{:S(2)}, u32[]{:S(2)}) collective-permute-start(bf16[32,640]{1,0:T(8,128)(2,1)S(1)} %get-tuple-element.72), channel_id=1, source_target_pairs={{0,40},{8,32},{16,56},{24,48},{32,8},{40,0},{48,24},{56,16},{1,41}... | collective-permute-start | bytes 122888 | tf_op jit(solution)/shard_map/ppermute | solution.py:55
  99.7 2.8 %collective-permute-start.28 = (bf16[32,640]{1,0:T(8,128)(2,1)S(1)}, bf16[32,640]{1,0:T(8,128)(2,1)S(1)}, u32[]{:S(2)}, u32[]{:S(2)}) collective-permute-start(bf16[32,640]{1,0:T(8,128)(2,1)S(1)} %get-tuple-element.73), channel_id=1, source_target_pairs={{0,24},{8,16},{16,8},{24,0},{32,56},{40,48},{48,40},{56,32},{1,25}... | collective-permute-start | bytes 122888 | tf_op jit(solution)/shard_map/ppermute | solution.py:55
  103.5 2.1 %collective-permute-done.28.refs_6_ = bf16[32,640]{1,0:T(8,128)(2,1)S(1)} collective-permute-done((bf16[32,640]{1,0:T(8,128)(2,1)S(1)}, bf16[32,640]{1,0:T(8,128)(2,1)S(1)}, u32[]{:S(2)}, u32[]{:S(2)}) %collective-permute-start.28) | collective-permute-done | bytes 40992 | tf_op jit(solution)/shard_map/ppermute | solution.py:55
  105.6 2.1 %collective-permute-done.29.refs_7_ = bf16[32,640]{1,0:T(8,128)(2,1)S(1)} collective-permute-done((bf16[32,640]{1,0:T(8,128)(2,1)S(1)}, bf16[32,640]{1,0:T(8,128)(2,1)S(1)}, u32[]{:S(2)}, u32[]{:S(2)}) %collective-permute-start.29) | collective-permute-done | bytes 40992 | tf_op jit(solution)/shard_map/ppermute | solution.py:55
  (55 shorter events, 9.3 us)
Async XLA Ops:
  0.0 13.2 %copy-start.1 = (s32[2]{0:T(128)S(1)}, s32[2]{0:T(128)}, u32[]{:S(2)}) copy-start(s32[2]{0:T(128)} %hot_ref.15) | copy-start | bytes 28
  2.5 13.1 %collective-permute-start = (bf16[576,256]{1,0:T(8,128)(2,1)S(1)}, bf16[576,256]{1,0:T(8,128)(2,1)S(1)}, u32[]{:S(2)}, u32[]{:S(2)}) collective-permute-start(bf16[576,256]{1,0:T(8,128)(2,1)S(1)} %get-tuple-element.40), channel_id=1, source_target_pairs={{0,1},{1,2},{2,3},{3,0},{4,5},{5,6},{6,7},{7,4},{8,9},{9,10},{10,1... | collective-permute-start | bytes 884744 | tf_op jit(solution)/shard_map/ppermute | solution.py:43
  4.1 11.4 %collective-permute-start.1 = (bf16[576,256]{1,0:T(8,128)(2,1)S(1)}, bf16[576,256]{1,0:T(8,128)(2,1)S(1)}, u32[]{:S(2)}, u32[]{:S(2)}) collective-permute-start(bf16[576,256]{1,0:T(8,128)(2,1)S(1)} %get-tuple-element.41), channel_id=1, source_target_pairs={{0,3},{1,0},{2,1},{3,2},{4,7},{5,4},{6,5},{7,6},{8,11},{9,8},{10,9... | collective-permute-start | bytes 884744 | tf_op jit(solution)/shard_map/ppermute | solution.py:43
  5.9 54.1 %copy-start.2 = (s32[16]{0:T(128)S(1)}, s32[16]{0:T(128)}, u32[]{:S(2)}) copy-start(s32[16]{0:T(128)} %len_ref.4) | copy-start | bytes 196
  5.9 9.6 %collective-permute-start.2 = (bf16[32,576]{1,0:T(8,128)(2,1)S(1)}, bf16[32,576]{1,0:T(8,128)(2,1)S(1)}, u32[]{:S(2)}, u32[]{:S(2)}) collective-permute-start(bf16[32,576]{1,0:T(8,128)(2,1)S(1)} %bitcast.6), channel_id=1, source_target_pairs={{0,32},{8,40},{16,48},{24,56},{32,0},{40,8},{48,16},{56,24},{1,33}... | collective-permute-start | bytes 110600 | tf_op jit(solution)/shard_map/ppermute | solution.py:55
  16.3 15.6 %collective-permute-start.3 = (bf16[576,512]{1,0:T(8,128)(2,1)S(1)}, bf16[576,512]{1,0:T(8,128)(2,1)S(1)}, u32[]{:S(2)}, u32[]{:S(2)}) collective-permute-start(bf16[576,512]{1,0:T(8,128)(2,1)S(1)} %get-tuple-element.46), channel_id=1, source_target_pairs={{0,1},{1,2},{2,3},{3,0},{4,5},{5,6},{6,7},{7,4},{8,9},{9,10},{10,1... | collective-permute-start | bytes 1769480 | tf_op jit(solution)/shard_map/ppermute | solution.py:43
  16.6 15.2 %collective-permute-start.4 = (bf16[576,512]{1,0:T(8,128)(2,1)S(1)}, bf16[576,512]{1,0:T(8,128)(2,1)S(1)}, u32[]{:S(2)}, u32[]{:S(2)}) collective-permute-start(bf16[576,512]{1,0:T(8,128)(2,1)S(1)} %get-tuple-element.47), channel_id=1, source_target_pairs={{0,3},{1,0},{2,1},{3,2},{4,7},{5,4},{6,5},{7,6},{8,11},{9,8},{10,9... | collective-permute-start | bytes 1769480 | tf_op jit(solution)/shard_map/ppermute | solution.py:43
  19.6 6.2 %collective-permute-start.9 = (bf16[64,576]{1,0:T(8,128)(2,1)S(1)}, bf16[64,576]{1,0:T(8,128)(2,1)S(1)}, u32[]{:S(2)}, u32[]{:S(2)}) collective-permute-start(bf16[64,576]{1,0:T(8,128)(2,1)S(1)} %pad_maximum_fusion.1), channel_id=1, source_target_pairs={{0,16},{8,24},{16,0},{24,8},{32,48},{40,56},{48,32},{56,40},{1,17}... | collective-permute-start | bytes 221192 | tf_op jit(solution)/shard_map/ppermute | solution.py:55
  25.8 9.8 %collective-permute-start.10 = (bf16[128,576]{1,0:T(8,128)(2,1)S(1)}, bf16[128,576]{1,0:T(8,128)(2,1)S(1)}, u32[]{:S(2)}, u32[]{:S(2)}) collective-permute-start(bf16[128,576]{1,0:T(8,128)(2,1)S(1)} %pad_maximum_fusion), channel_id=1, source_target_pairs={{0,8},{8,0},{16,24},{24,16},{32,40},{40,32},{48,56},{56,48},{1,9},... | collective-permute-start | bytes 442376 | tf_op jit(solution)/shard_map/ppermute | solution.py:55
  32.6 13.6 %collective-permute-start.7 = (bf16[576,512]{1,0:T(8,128)(2,1)S(1)}, bf16[576,512]{1,0:T(8,128)(2,1)S(1)}, u32[]{:S(2)}, u32[]{:S(2)}) collective-permute-start(bf16[576,512]{1,0:T(8,128)(2,1)S(1)} %shard_map.49.refs_0_), channel_id=1, source_target_pairs={{0,3},{1,0},{2,1},{3,2},{4,7},{5,4},{6,5},{7,6},{8,11},{9,8},{10,9... | collective-permute-start | bytes 1769480 | tf_op jit(solution)/shard_map/ppermute | solution.py:43
  35.6 14.4 %collective-permute-start.5 = (bf16[576,512]{1,0:T(8,128)(2,1)S(1)}, bf16[576,512]{1,0:T(8,128)(2,1)S(1)}, u32[]{:S(2)}, u32[]{:S(2)}) collective-permute-start(bf16[576,512]{1,0:T(8,128)(2,1)S(1)} %shard_map.49.refs_0_), channel_id=1, source_target_pairs={{0,1},{1,2},{2,3},{3,0},{4,5},{5,6},{6,7},{7,4},{8,9},{9,10},{10,1... | collective-permute-start | bytes 1769480 | tf_op jit(solution)/shard_map/ppermute | solution.py:43
  35.7 15.5 %collective-permute-start.13 = (bf16[256,576]{1,0:T(8,128)(2,1)S(1)}, bf16[256,576]{1,0:T(8,128)(2,1)S(1)}, u32[]{:S(2)}, u32[]{:S(2)}) collective-permute-start(bf16[256,576]{1,0:T(8,128)(2,1)S(1)} %constant_dynamic-update-slice_fusion.q_ref), channel_id=1, source_target_pairs={{0,192},{64,128},{128,64},{192,0},{1,193},{65,129},{129,65},{193,1... | collective-permute-start | bytes 884744 | tf_op jit(solution)/shard_map/ppermute | solution.py:51
  36.3 14.9 %collective-permute-start.12 = (bf16[256,576]{1,0:T(8,128)(2,1)S(1)}, bf16[256,576]{1,0:T(8,128)(2,1)S(1)}, u32[]{:S(2)}, u32[]{:S(2)}) collective-permute-start(bf16[256,576]{1,0:T(8,128)(2,1)S(1)} %constant_dynamic-update-slice_fusion.q_ref), channel_id=1, source_target_pairs={{0,128},{64,192},{128,0},{192,64},{1,129},{65,193},{129,1},{193,65... | collective-permute-start | bytes 884744 | tf_op jit(solution)/shard_map/ppermute | solution.py:51
  38.7 13.1 %collective-permute-start.11 = (bf16[256,576]{1,0:T(8,128)(2,1)S(1)}, bf16[256,576]{1,0:T(8,128)(2,1)S(1)}, u32[]{:S(2)}, u32[]{:S(2)}) collective-permute-start(bf16[256,576]{1,0:T(8,128)(2,1)S(1)} %constant_dynamic-update-slice_fusion.q_ref), channel_id=1, source_target_pairs={{0,64},{64,0},{128,192},{192,128},{1,65},{65,1},{129,193},{193,129... | collective-permute-start | bytes 884744 | tf_op jit(solution)/shard_map/ppermute | solution.py:51
  46.2 8.0 %collective-permute-start.8 = (bf16[576,256]{1,0:T(8,128)(2,1)S(1)}, bf16[576,256]{1,0:T(8,128)(2,1)S(1)}, u32[]{:S(2)}, u32[]{:S(2)}) collective-permute-start(bf16[576,256]{1,0:T(8,128)(2,1)S(1)} %slice.9), channel_id=1, source_target_pairs={{0,3},{1,0},{2,1},{3,2},{4,7},{5,4},{6,5},{7,6},{8,11},{9,8},{10,9... | collective-permute-start | bytes 884744 | tf_op jit(solution)/shard_map/ppermute | solution.py:43
  50.0 8.0 %collective-permute-start.6 = (bf16[576,256]{1,0:T(8,128)(2,1)S(1)}, bf16[576,256]{1,0:T(8,128)(2,1)S(1)}, u32[]{:S(2)}, u32[]{:S(2)}) collective-permute-start(bf16[576,256]{1,0:T(8,128)(2,1)S(1)} %slice.8), channel_id=1, source_target_pairs={{0,1},{1,2},{2,3},{3,0},{4,5},{5,6},{6,7},{7,4},{8,9},{9,10},{10,1... | collective-permute-start | bytes 884744 | tf_op jit(solution)/shard_map/ppermute | solution.py:43
  51.2 7.4 %collective-permute-start.15 = (bf16[576,512]{1,0:T(8,128)(2,1)S(1)}, bf16[576,512]{1,0:T(8,128)(2,1)S(1)}, u32[]{:S(2)}, u32[]{:S(2)}) collective-permute-start(bf16[576,512]{1,0:T(8,128)(2,1)S(1)} %shard_map.49.refs_0_), channel_id=1, source_target_pairs={{0,4},{4,0},{1,5},{5,1},{2,6},{6,2},{3,7},{7,3},{8,12},{12,8},{9,1... | collective-permute-start | bytes 1769480 | tf_op jit(solution)/shard_map/ppermute | solution.py:47
  51.2 8.9 %collective-permute-start.17 = (bf16[576,512]{1,0:T(8,128)(2,1)S(1)}, bf16[576,512]{1,0:T(8,128)(2,1)S(1)}, u32[]{:S(2)}, u32[]{:S(2)}) collective-permute-start(bf16[576,512]{1,0:T(8,128)(2,1)S(1)} %collective-permute-done.7.refs_2_), channel_id=1, source_target_pairs={{0,4},{4,0},{1,5},{5,1},{2,6},{6,2},{3,7},{7,3},{8,12},{12,8},{9,1... | collective-permute-start | bytes 1769480 | tf_op jit(solution)/shard_map/ppermute | solution.py:47
  51.8 8.2 %collective-permute-start.16 = (bf16[576,512]{1,0:T(8,128)(2,1)S(1)}, bf16[576,512]{1,0:T(8,128)(2,1)S(1)}, u32[]{:S(2)}, u32[]{:S(2)}) collective-permute-start(bf16[576,512]{1,0:T(8,128)(2,1)S(1)} %collective-permute-done.5.refs_1_), channel_id=1, source_target_pairs={{0,4},{4,0},{1,5},{5,1},{2,6},{6,2},{3,7},{7,3},{8,12},{12,8},{9,1... | collective-permute-start | bytes 1769480 | tf_op jit(solution)/shard_map/ppermute | solution.py:47
  54.2 3.8 %collective-permute-start.14 = (s32[2]{0:T(128)S(1)}, s32[2]{0:T(128)S(1)}, u32[]{:S(2)}, u32[]{:S(2)}) collective-permute-start(s32[2]{0:T(128)S(1)} %copy-done.1), channel_id=1, source_target_pairs={{0,4},{4,0},{1,5},{5,1},{2,6},{6,2},{3,7},{7,3},{8,12},{12,8},{9,1... | collective-permute-start | bytes 32 | tf_op jit(solution)/shard_map/ppermute | solution.py:47
  58.0 1.6 %collective-permute-start.18 = (bf16[576,256]{1,0:T(8,128)(2,1)S(1)}, bf16[576,256]{1,0:T(8,128)(2,1)S(1)}, u32[]{:S(2)}, u32[]{:S(2)}) collective-permute-start(bf16[576,256]{1,0:T(8,128)(2,1)S(1)} %collective-permute-done.6.refs_3_), channel_id=1, source_target_pairs={{0,4},{4,0},{1,5},{5,1},{2,6},{6,2},{3,7},{7,3},{8,12},{12,8},{9,1... | collective-permute-start | bytes 884744 | tf_op jit(solution)/shard_map/ppermute | solution.py:47
  58.0 2.0 %collective-permute-start.19 = (bf16[576,256]{1,0:T(8,128)(2,1)S(1)}, bf16[576,256]{1,0:T(8,128)(2,1)S(1)}, u32[]{:S(2)}, u32[]{:S(2)}) collective-permute-start(bf16[576,256]{1,0:T(8,128)(2,1)S(1)} %collective-permute-done.8.refs_4_), channel_id=1, source_target_pairs={{0,4},{4,0},{1,5},{5,1},{2,6},{6,2},{3,7},{7,3},{8,12},{12,8},{9,1... | collective-permute-start | bytes 884744 | tf_op jit(solution)/shard_map/ppermute | solution.py:47
  64.3 10.2 %collective-permute-start.20 = (bf16[264,512]{1,0:T(8,128)(2,1)S(1)}, bf16[264,512]{1,0:T(8,128)(2,1)S(1)}, u32[]{:S(2)}, u32[]{:S(2)}) collective-permute-start(bf16[264,512]{1,0:T(8,128)(2,1)S(1)} %shard_map.50), channel_id=1, source_target_pairs={{0,128},{64,192},{128,0},{192,64},{1,129},{65,193},{129,1},{193,65... | collective-permute-start | bytes 811016 | tf_op jit(solution)/shard_map/ppermute | solution.py:51
  70.3 9.2 %collective-permute-start.21 = (bf16[264,512]{1,0:T(8,128)(2,1)S(1)}, bf16[264,512]{1,0:T(8,128)(2,1)S(1)}, u32[]{:S(2)}, u32[]{:S(2)}) collective-permute-start(bf16[264,512]{1,0:T(8,128)(2,1)S(1)} %shard_map.51), channel_id=1, source_target_pairs={{0,64},{64,0},{128,192},{192,128},{1,65},{65,1},{129,193},{193,129... | collective-permute-start | bytes 811016 | tf_op jit(solution)/shard_map/ppermute | solution.py:51
  78.8 9.1 %collective-permute-start.22 = (bf16[264,512]{1,0:T(8,128)(2,1)S(1)}, bf16[264,512]{1,0:T(8,128)(2,1)S(1)}, u32[]{:S(2)}, u32[]{:S(2)}) collective-permute-start(bf16[264,512]{1,0:T(8,128)(2,1)S(1)} %shard_map.52), channel_id=1, source_target_pairs={{0,192},{64,128},{128,64},{192,0},{1,193},{65,129},{129,65},{193,1... | collective-permute-start | bytes 811016 | tf_op jit(solution)/shard_map/ppermute | solution.py:51
  88.5 11.2 %collective-permute-start.23 = (bf16[32,640]{1,0:T(8,128)(2,1)S(1)}, bf16[32,640]{1,0:T(8,128)(2,1)S(1)}, u32[]{:S(2)}, u32[]{:S(2)}) collective-permute-start(bf16[32,640]{1,0:T(8,128)(2,1)S(1)} %get-tuple-element.68), channel_id=1, source_target_pairs={{0,32},{8,40},{16,48},{24,56},{32,0},{40,8},{48,16},{56,24},{1,33}... | collective-permute-start | bytes 122888 | tf_op jit(solution)/shard_map/ppermute | solution.py:55
  92.6 9.9 %collective-permute-start.24 = (bf16[32,640]{1,0:T(8,128)(2,1)S(1)}, bf16[32,640]{1,0:T(8,128)(2,1)S(1)}, u32[]{:S(2)}, u32[]{:S(2)}) collective-permute-start(bf16[32,640]{1,0:T(8,128)(2,1)S(1)} %get-tuple-element.69), channel_id=1, source_target_pairs={{0,16},{8,24},{16,0},{24,8},{32,48},{40,56},{48,32},{56,40},{1,17}... | collective-permute-start | bytes 122888 | tf_op jit(solution)/shard_map/ppermute | solution.py:55
  94.1 8.4 %collective-permute-start.25 = (bf16[32,640]{1,0:T(8,128)(2,1)S(1)}, bf16[32,640]{1,0:T(8,128)(2,1)S(1)}, u32[]{:S(2)}, u32[]{:S(2)}) collective-permute-start(bf16[32,640]{1,0:T(8,128)(2,1)S(1)} %get-tuple-element.70), channel_id=1, source_target_pairs={{0,48},{8,56},{16,32},{24,40},{32,16},{40,24},{48,0},{56,8},{1,49}... | collective-permute-start | bytes 122888 | tf_op jit(solution)/shard_map/ppermute | solution.py:55
  95.1 7.4 %collective-permute-start.26 = (bf16[32,640]{1,0:T(8,128)(2,1)S(1)}, bf16[32,640]{1,0:T(8,128)(2,1)S(1)}, u32[]{:S(2)}, u32[]{:S(2)}) collective-permute-start(bf16[32,640]{1,0:T(8,128)(2,1)S(1)} %get-tuple-element.71), channel_id=1, source_target_pairs={{0,8},{8,0},{16,24},{24,16},{32,40},{40,32},{48,56},{56,48},{1,9},... | collective-permute-start | bytes 122888 | tf_op jit(solution)/shard_map/ppermute | solution.py:55
  96.3 7.2 %collective-permute-start.27 = (bf16[32,640]{1,0:T(8,128)(2,1)S(1)}, bf16[32,640]{1,0:T(8,128)(2,1)S(1)}, u32[]{:S(2)}, u32[]{:S(2)}) collective-permute-start(bf16[32,640]{1,0:T(8,128)(2,1)S(1)} %get-tuple-element.72), channel_id=1, source_target_pairs={{0,40},{8,32},{16,56},{24,48},{32,8},{40,0},{48,24},{56,16},{1,41}... | collective-permute-start | bytes 122888 | tf_op jit(solution)/shard_map/ppermute | solution.py:55
  99.7 5.9 %collective-permute-start.28 = (bf16[32,640]{1,0:T(8,128)(2,1)S(1)}, bf16[32,640]{1,0:T(8,128)(2,1)S(1)}, u32[]{:S(2)}, u32[]{:S(2)}) collective-permute-start(bf16[32,640]{1,0:T(8,128)(2,1)S(1)} %get-tuple-element.73), channel_id=1, source_target_pairs={{0,24},{8,16},{16,8},{24,0},{32,56},{40,48},{48,40},{56,32},{1,25}... | collective-permute-start | bytes 122888 | tf_op jit(solution)/shard_map/ppermute | solution.py:55
  102.5 5.2 %collective-permute-start.29 = (bf16[32,640]{1,0:T(8,128)(2,1)S(1)}, bf16[32,640]{1,0:T(8,128)(2,1)S(1)}, u32[]{:S(2)}, u32[]{:S(2)}) collective-permute-start(bf16[32,640]{1,0:T(8,128)(2,1)S(1)} %get-tuple-element.74), channel_id=1, source_target_pairs={{0,56},{8,48},{16,40},{24,32},{32,24},{40,16},{48,8},{56,0},{1,57}... | collective-permute-start | bytes 122888 | tf_op jit(solution)/shard_map/ppermute | solution.py:55
  (2 other events, 5.8 us)

commit v6 on v5

--- a/solution.py
+++ b/solution.py
@@ -29,7 +29,6 @@
 Z_ORDER = (0, 4, 2, 6, 1, 5, 3, 7)
 SCALE = QK**-0.5
 LOG2_E = 1.4426950408889634
-N_FAR = N_Z // 2
 f32 = jnp.float32
 bf16 = jnp.bfloat16
 
@@ -178,27 +177,52 @@
     )
 
 
-PLACES = ((0, 0, 2), (3, 0, 2), (1, 0, 2), (2, 0, 1), (2, 1, 1))
+NEAR = (0, 3, 1)
+FAR = 2
 
 
 def fold(op, s):
     return functools.reduce(op, [s[:, i : i + 128] for i in range(0, s.shape[1], 128)])
 
 
-def attend_kernel(q_ref, len_ref, hot_ref, hot_other_ref, *refs):
-    n = len(PLACES)
+def score_kernel(other, len_ref, hot_ref, *refs):
+    q_refs, key_refs, outs = refs[:N_X], refs[N_X : N_X + len(NEAR)], refs[N_X + len(NEAR) :]
+    lens = visible_lengths(len_ref, q_refs[0].shape[0])
+    rows = [row_numbers(hot_ref, other, away, 0, 2) for away in NEAR]
+    for i, q_ref in enumerate(q_refs):
+        s_ref, peak_ref = outs[2 * i : 2 * i + 2]
+        q = q_ref[...]
+        peaks = []
+        for j, k_ref in enumerate(key_refs):
+            s = jnp.dot(q, k_ref[...], preferred_element_type=f32)
+            s = jnp.where(rows[j] < lens, s, NEVER)
+            s_ref[:, j * CHUNK : (j + 1) * CHUNK] = s
+            peaks.append(fold(jnp.maximum, s))
+        peak_ref[...] = functools.reduce(jnp.maximum, peaks)
+
+
+def attend_kernel(q_ref, *refs):
+    n = len(NEAR)
+    (s_refs, peak_refs), refs = (refs[0:4:2], refs[1:4:2]), refs[4:]
+    (len_ref, *hot_refs), refs = refs[:3], refs[3:]
     key_refs, o_ref = refs[:-1], refs[-1]
     q = q_ref[...]
     lens = visible_lengths(len_ref, q.shape[0])
+    last = []
+    for other in range(N_C):
+        for half in range(2):
+            k_ref = key_refs[other * (n + 2) + n + half]
+            rows = row_numbers(hot_refs[other], other, FAR, half, 1)
+            s = jnp.dot(q, k_ref[...], preferred_element_type=f32)
+            last.append(jnp.where(rows < lens, s, NEVER))
     parts = []
-    for other, hot in enumerate((hot_ref, hot_other_ref)):
-        keys = key_refs[other * n : (other + 1) * n]
-        scores = []
-        for k_ref, place in zip(keys, PLACES):
-            numbers = row_numbers(hot, other, *place)
-            s = jnp.dot(q, k_ref[...], preferred_element_type=f32)
-            scores.append(jnp.where(numbers < lens, s, NEVER))
-        peak = functools.reduce(jnp.maximum, [fold(jnp.maximum, s) for s in scores])
+    for other in range(N_C):
+        keys = key_refs[other * (n + 2) : (other + 1) * (n + 2)]
+        scores = [s_refs[other][:, i * CHUNK : (i + 1) * CHUNK] for i in range(n)]
+        scores += last[other * 2 : other * 2 + 2]
+        peak = peak_refs[other][...]
+        for s in last[other * 2 : other * 2 + 2]:
+            peak = jnp.maximum(peak, fold(jnp.maximum, s))
         peak = peak.max(axis=1, keepdims=True)
         total = 0.0
         numer = None
@@ -297,9 +321,11 @@
         mib=50,
         scratch_shapes=[pltpu.SemaphoreType.DMA((4,))],
     )
-    up, down = shift_rep(up, 1), shift_rep(down, -1)
     own = queries.reshape(count, -1, WIDTH).transpose(1, 0, 2).reshape(-1, WIDTH)
     near = jnp.concatenate([own, cross_z(own, 4)], axis=0)
+    up, down, near = lax.optimization_barrier((up, down, near))
+    up, down = shift_rep(up, 1), shift_rep(down, -1)
+    near = jnp.concatenate([near, cross_z(near, 2)], axis=0)
     right, left, mine = call(
         own_cut_kernel,
         [chunk] * 3,
@@ -316,33 +342,49 @@
         [hot_ids, up, down, right, left],
     )
     from_left, from_right = shift_rep(right, 1), shift_rep(left, -1)
-    for bits in (2, 1):
-        near = jnp.concatenate([near, cross_z(near, bits)], axis=0)
+    near = jnp.concatenate([near, cross_z(near, 1)], axis=0)
+    asked = [near] + [cross_x(near, bits) for bits in range(1, N_X)]
+    from_left, from_right, asked[1], asked[3] = lax.optimization_barrier(
+        (from_left, from_right, asked[1], asked[3])
+    )
     (mine,) = call(
         settle_kernel,
         [chunk],
         [SMEM] + [VMEM] * 3,
         [hot_ids, from_left, from_right, mine],
     )
-    asked = [near] + [cross_x(near, bits) for bits in range(1, N_X)]
     hot_other = swap_core(hot_ids)
 
     of_left, of_right = shift_rep(mine, 1), shift_rep(mine, -1)
+    of_left, of_right, asked[2] = lax.optimization_barrier((of_left, of_right, asked[2]))
     far_a, far_b = shift_rep(of_left[:, :PAIR], 1), shift_rep(of_right[:, PAIR:], -1)
-    far_a, far_b, *asked = lax.optimization_barrier((far_a, far_b, *asked))
-    keys = [mine, of_left, of_right, far_a, far_b]
-    keys = keys + [swap_core(k) for k in keys]
+    keys = [mine, of_left, of_right]
+    swapped = [swap_core(k) for k in keys]
+    asked, swapped = lax.optimization_barrier((asked, swapped))
 
     rows = near.shape[0]
+    scores = []
+    for other, (hot, some) in enumerate(((hot_ids, keys), (hot_other, swapped))):
+        found = call(
+            functools.partial(score_kernel, other),
+            [((rows, len(NEAR) * CHUNK), f32), ((rows, 128), f32)] * N_X,
+            [SMEM, SMEM] + [VMEM] * (N_X + len(NEAR)),
+            [lengths, hot, *asked, *some],
+        )
+        scores.append([found[2 * hop : 2 * hop + 2] for hop in range(N_X)])
+    scores, far_a, far_b = lax.optimization_barrier((scores, far_a, far_b))
+    keys += [far_a, far_b]
+    swapped += [swap_core(far_a), swap_core(far_b)]
+
     parts = []
-    for i, hop in enumerate((2, 1, 3, 0)):
+    for i, hop in enumerate((1, 3, 2, 0)):
         if i > 1:
             lengths, parts[i - 2] = lax.optimization_barrier((lengths, parts[i - 2]))
         (o,) = call(
             attend_kernel,
             [((rows + STAT_ROWS, LAT), bf16)],
-            [VMEM, SMEM, SMEM, SMEM] + [VMEM] * len(keys),
-            [asked[hop], lengths, hot_ids, hot_other, *keys],
+            [VMEM] * 5 + [SMEM] * 3 + [VMEM] * (N_C * len(keys)),
+            [asked[hop], *scores[0][hop], *scores[1][hop], lengths, hot_ids, hot_other, *keys, *swapped],
         )
         lengths, o = lax.optimization_barrier((lengths, o))
         parts.append(cross_x(o, hop) if hop else o)

time: 109 us -> 111 us (1.018)
  waiting for transfers between devices: 39.2 us -> 41 us
  starting transfers between devices: 44.2 us -> 42.5 us
    ppermute x6, waiting for transfers between devices: 9.57 us -> 22.6 us  [cross_x(): return lax.ppermute(a, 'x', [(i, i ^ bits) for i in range(N_X)])]
    ppermute x8, waiting for transfers between devices: 18.3 us -> 6.18 us  [shift_rep(): return lax.ppermute(a, 'rep', [(i, (i + by) % N_REP) for i in range(N_REP)])]
    ppermute x8, starting transfers between devices: 13.5 us -> 10.8 us  [shift_rep(): return lax.ppermute(a, 'rep', [(i, (i + by) % N_REP) for i in range(N_REP)])]
    pallas_call x10 -> x12, Pallas kernels: 24 us -> 24.4 us  [call(): pl.pallas_call(kernel, out_shape=tuple((jax.ShapeDtypeStruct(*o) for o in...]
  transfers between devices with their start and end apart: 30 -> 30, of which waited for: 14 -> 18; matrix products, arithmetic and copies ran while one was open for 0% -> 0% of each run, Pallas kernels for 15% -> 17%
where the time goes in v6:
time: 111 us; the launch traced here: 110 us
  starting transfers between devices  42.5 us (38%)
  waiting for transfers between devices  41 us (37%)
  Pallas kernels  24.4 us (22%)
  local copies, waits for them, and re-layouts  1.62 us (1%)
    pallas_call x12, Pallas kernels, call(): pl.pallas_call(kernel, out_shape=tuple((jax.ShapeDtypeStruct(*o) for o in...  24.4 us
    ppermute x10, starting transfers between devices, cross_z(): return lax.ppermute(a, 'z', [(i, i ^ bits) for i in range(N_Z)])  23.9 us
    ppermute x6, waiting for transfers between devices, cross_x(): return lax.ppermute(a, 'x', [(i, i ^ bits) for i in range(N_X)])  22.6 us
    ppermute x8, starting transfers between devices, shift_rep(): return lax.ppermute(a, 'rep', [(i, (i + by) % N_REP) for i in range(N_REP)])  10.8 us
    ppermute x10, waiting for transfers between devices, cross_z(): return lax.ppermute(a, 'z', [(i, i ^ bits) for i in range(N_Z)])  10.6 us
    ppermute x6, starting transfers between devices, cross_x(): return lax.ppermute(a, 'x', [(i, i ^ bits) for i in range(N_X)])  6.68 us
    ppermute x8, waiting for transfers between devices, shift_rep(): return lax.ppermute(a, 'rep', [(i, (i + by) % N_REP) for i in range(N_REP)])  6.18 us
  transfers between devices with their start and end apart: 30, of which 18 were waited for; matrix products, arithmetic and copies ran while one was open for 0% of the time, Pallas kernels for 17%

profile of v6, /device:TPU:6, one launch (start us, length us, event | category | flops | bytes accessed | tf_op | source)
XLA Modules:
  0.0 109.7 jit_solution(5614233861964586391)
XLA Ops:
  0.9 7.3 %collective-permute-start = (bf16[32,576]{1,0:T(8,128)(2,1)S(1)}, bf16[32,576]{1,0:T(8,128)(2,1)S(1)}, u32[]{:S(2)}, u32[]{:S(2)}) collective-permute-start(bf16[32,576]{1,0:T(8,128)(2,1)S(1)} %bitcast.6), channel_id=1, source_target_pairs={{0,32},{8,40},{16,48},{24,56},{32,0},{40,8},{48,16},{56,24},{1,33}... | collective-permute-start | bytes 110600 | tf_op jit(solution)/shard_map/ppermute | solution.py:54
  8.8 1.7 %shard_map.46 = (bf16[576,256]{1,0:T(8,128)(2,1)S(1)}, bf16[576,256]{1,0:T(8,128)(2,1)S(1)}) custom-call(s32[2]{0:T(128)S(1)} %copy-done, bf16[576,4096]{1,0:T(8,128)(2,1)} %bitcast.4), custom_call_target="tpu_custom_call" | custom-call | tf_op jit(solution)/shard_map/pallas_call | solution.py:301
  10.6 1.7 %collective-permute-start.1 = (bf16[576,256]{1,0:T(8,128)(2,1)S(1)}, bf16[576,256]{1,0:T(8,128)(2,1)S(1)}, u32[]{:S(2)}, u32[]{:S(2)}) collective-permute-start(bf16[576,256]{1,0:T(8,128)(2,1)S(1)} %get-tuple-element.87), channel_id=1, source_target_pairs={{0,1},{1,2},{2,3},{3,0},{4,5},{5,6},{6,7},{7,4},{8,9},{9,10},{10,1... | collective-permute-start | bytes 884744 | tf_op jit(solution)/shard_map/ppermute | solution.py:42
  12.2 1.7 %collective-permute-start.2 = (bf16[576,256]{1,0:T(8,128)(2,1)S(1)}, bf16[576,256]{1,0:T(8,128)(2,1)S(1)}, u32[]{:S(2)}, u32[]{:S(2)}) collective-permute-start(bf16[576,256]{1,0:T(8,128)(2,1)S(1)} %get-tuple-element.88), channel_id=1, source_target_pairs={{0,3},{1,0},{2,1},{3,2},{4,7},{5,4},{6,5},{7,6},{8,11},{9,8},{10,9... | collective-permute-start | bytes 884744 | tf_op jit(solution)/shard_map/ppermute | solution.py:42
  13.9 1.7 %collective-permute-start.3 = (bf16[64,576]{1,0:T(8,128)(2,1)S(1)}, bf16[64,576]{1,0:T(8,128)(2,1)S(1)}, u32[]{:S(2)}, u32[]{:S(2)}) collective-permute-start(bf16[64,576]{1,0:T(8,128)(2,1)S(1)} %pad_maximum_fusion.1), channel_id=1, source_target_pairs={{0,16},{8,24},{16,0},{24,8},{32,48},{40,56},{48,32},{56,40},{1,17}... | collective-permute-start | bytes 221192 | tf_op jit(solution)/shard_map/ppermute | solution.py:54
  15.6 2.2 %shard_map.47 = (bf16[576,512]{1,0:T(8,128)(2,1)S(1)}, bf16[576,512]{1,0:T(8,128)(2,1)S(1)}, bf16[576,512]{1,0:T(8,128)(2,1)S(1)}) custom-call(s32[2]{0:T(128)S(1)} %copy-done, bf16[576,4096]{1,0:T(8,128)(2,1)} %bitcast.5), custom_call_target="tpu_custom_call" | custom-call | tf_op jit(solution)/shard_map/pallas_call | solution.py:301
  17.8 2.3 %collective-permute-done.3 = bf16[64,576]{1,0:T(8,128)(2,1)S(1)} collective-permute-done((bf16[64,576]{1,0:T(8,128)(2,1)S(1)}, bf16[64,576]{1,0:T(8,128)(2,1)S(1)}, u32[]{:S(2)}, u32[]{:S(2)}) %collective-permute-start.3) | collective-permute-done | bytes 73760 | tf_op jit(solution)/shard_map/ppermute | solution.py:54
  21.2 1.6 %collective-permute-start.5 = (bf16[576,512]{1,0:T(8,128)(2,1)S(1)}, bf16[576,512]{1,0:T(8,128)(2,1)S(1)}, u32[]{:S(2)}, u32[]{:S(2)}) collective-permute-start(bf16[576,512]{1,0:T(8,128)(2,1)S(1)} %get-tuple-element.95), channel_id=1, source_target_pairs={{0,1},{1,2},{2,3},{3,0},{4,5},{5,6},{6,7},{7,4},{8,9},{9,10},{10,1... | collective-permute-start | bytes 1769480 | tf_op jit(solution)/shard_map/ppermute | solution.py:42
  22.8 1.7 %collective-permute-start.6 = (bf16[576,512]{1,0:T(8,128)(2,1)S(1)}, bf16[576,512]{1,0:T(8,128)(2,1)S(1)}, u32[]{:S(2)}, u32[]{:S(2)}) collective-permute-start(bf16[576,512]{1,0:T(8,128)(2,1)S(1)} %get-tuple-element.96), channel_id=1, source_target_pairs={{0,3},{1,0},{2,1},{3,2},{4,7},{5,4},{6,5},{7,6},{8,11},{9,8},{10,9... | collective-permute-start | bytes 1769480 | tf_op jit(solution)/shard_map/ppermute | solution.py:42
  25.5 4.3 %collective-permute-done.4 = bf16[128,576]{1,0:T(8,128)(2,1)S(1)} collective-permute-done((bf16[128,576]{1,0:T(8,128)(2,1)S(1)}, bf16[128,576]{1,0:T(8,128)(2,1)S(1)}, u32[]{:S(2)}, u32[]{:S(2)}) %collective-permute-start.4) | collective-permute-done | bytes 147488 | tf_op jit(solution)/shard_map/ppermute | solution.py:54
  31.2 6.9 %collective-permute-done.8.refs_3_.q_ref = bf16[256,576]{1,0:T(8,128)(2,1)S(1)} collective-permute-done((bf16[256,576]{1,0:T(8,128)(2,1)S(1)}, bf16[256,576]{1,0:T(8,128)(2,1)S(1)}, u32[]{:S(2)}, u32[]{:S(2)}) %collective-permute-start.8) | collective-permute-done | bytes 294944 | tf_op jit(solution)/shard_map/ppermute | solution.py:50
  38.9 1.9 %collective-permute-start.10 = (bf16[576,512]{1,0:T(8,128)(2,1)S(1)}, bf16[576,512]{1,0:T(8,128)(2,1)S(1)}, u32[]{:S(2)}, u32[]{:S(2)}) collective-permute-start(bf16[576,512]{1,0:T(8,128)(2,1)S(1)} %shard_map.49.refs_4_.refs_7_), channel_id=1, source_target_pairs={{0,3},{1,0},{2,1},{3,2},{4,7},{5,4},{6,5},{7,6},{8,11},{9,8},{10,9... | collective-permute-start | bytes 1769480 | tf_op jit(solution)/shard_map/ppermute | solution.py:42
  41.0 1.7 %collective-permute-start.11 = (bf16[256,576]{1,0:T(8,128)(2,1)S(1)}, bf16[256,576]{1,0:T(8,128)(2,1)S(1)}, u32[]{:S(2)}, u32[]{:S(2)}) collective-permute-start(bf16[256,576]{1,0:T(8,128)(2,1)S(1)} %constant_dynamic-update-slice_fusion.refs_0_.q_ref), channel_id=1, source_target_pairs={{0,128},{64,192},{128,0},{192,64},{1,129},{65,193},{129,1},{193,65... | collective-permute-start | bytes 884744 | tf_op jit(solution)/shard_map/ppermute | solution.py:50
  42.7 6.9 %collective-permute-done.11.refs_2_.q_ref = bf16[256,576]{1,0:T(8,128)(2,1)S(1)} collective-permute-done((bf16[256,576]{1,0:T(8,128)(2,1)S(1)}, bf16[256,576]{1,0:T(8,128)(2,1)S(1)}, u32[]{:S(2)}, u32[]{:S(2)}) %collective-permute-start.11) | collective-permute-done | bytes 294944 | tf_op jit(solution)/shard_map/ppermute | solution.py:50
  50.7 3.2 %collective-permute-done.9.refs_5_.refs_8_ = bf16[576,512]{1,0:T(8,128)(2,1)S(1)} collective-permute-done((bf16[576,512]{1,0:T(8,128)(2,1)S(1)}, bf16[576,512]{1,0:T(8,128)(2,1)S(1)}, u32[]{:S(2)}, u32[]{:S(2)}) %collective-permute-start.9) | collective-permute-done | bytes 589856 | tf_op jit(solution)/shard_map/ppermute | solution.py:42
  54.8 1.7 %collective-permute-start.16 = (bf16[576,256]{1,0:T(8,128)(2,1)S(1)}, bf16[576,256]{1,0:T(8,128)(2,1)S(1)}, u32[]{:S(2)}, u32[]{:S(2)}) collective-permute-start(bf16[576,256]{1,0:T(8,128)(2,1)S(1)} %slice.6), channel_id=1, source_target_pairs={{0,1},{1,2},{2,3},{3,0},{4,5},{5,6},{6,7},{7,4},{8,9},{9,10},{10,1... | collective-permute-start | bytes 884744 | tf_op jit(solution)/shard_map/ppermute | solution.py:42
  56.7 3.2 %shard_map.50 = (f32[256,1536]{1,0:T(8,128)S(1)}, f32[256,128]{1,0:T(8,128)S(1)}, f32[256,1536]{1,0:T(8,128)S(1)}, f32[256,128]{1,0:T(8,128)S(1)}, f32[256,1536]...) custom-call(s32[16]{0:T(128)S(1)} %copy-done.1, s32[2]{0:T(128)S(1)} %copy-done, ...), custom_call_target="tpu_custom_call" | custom-call | tf_op jit(solution)/shard_map/pallas_call | solution.py:301
  59.9 3.2 %shard_map.51 = (f32[256,1536]{1,0:T(8,128)S(1)}, f32[256,128]{1,0:T(8,128)S(1)}, f32[256,1536]{1,0:T(8,128)S(1)}, f32[256,128]{1,0:T(8,128)S(1)}, f32[256,1536]...) custom-call(s32[16]{0:T(128)S(1)} %copy-done.1, ...), custom_call_target="tpu_custom_call" | custom-call | tf_op jit(solution)/shard_map/pallas_call | solution.py:301
  63.4 1.3 %collective-permute-done.16.refs_10_ = bf16[576,256]{1,0:T(8,128)(2,1)S(1)} collective-permute-done((bf16[576,256]{1,0:T(8,128)(2,1)S(1)}, bf16[576,256]{1,0:T(8,128)(2,1)S(1)}, u32[]{:S(2)}, u32[]{:S(2)}) %collective-permute-start.16) | collective-permute-done | bytes 294944 | tf_op jit(solution)/shard_map/ppermute | solution.py:42
  66.7 2.8 %shard_map.52 = bf16[264,512]{1,0:T(8,128)(2,1)S(1)} custom-call(bf16[256,576]{1,0:T(8,128)(2,1)S(1)} %collective-permute-done.7.refs_1_.q_ref, f32[256,1536]{1,0:T(8,128)S(1)} %get-tuple-element.128.refs_0_, f32[256,128]{1,0:T(8,128)S(1)} %get-tuple-element.129.refs_1_, f32[256,1536]{1,0:T(8,128)S(1)} %get-tuple-element.130.refs_2_, ...), custom_call_target="tpu_custom_call" | custom-call | tf_op jit(solution)/shard_map/pallas_call | solution.py:301
  70.3 2.8 %shard_map.53 = bf16[264,512]{1,0:T(8,128)(2,1)S(1)} custom-call(bf16[256,576]{1,0:T(8,128)(2,1)S(1)} %collective-permute-done.8.refs_3_.q_ref, f32[256,1536]{1,0:T(8,128)S(1)} %get-tuple-element.135.refs_0_, f32[256,128]{1,0:T(8,128)S(1)} %get-tuple-element.136.refs_1_, f32[256,1536]{1,0:T(8,128)S(1)} %get-tuple-element.137.refs_2_, ...), custom_call_target="tpu_custom_call" | custom-call | tf_op jit(solution)/shard_map/pallas_call | solution.py:301
  73.1 1.4 %collective-permute-start.21 = (bf16[264,512]{1,0:T(8,128)(2,1)S(1)}, bf16[264,512]{1,0:T(8,128)(2,1)S(1)}, u32[]{:S(2)}, u32[]{:S(2)}) collective-permute-start(bf16[264,512]{1,0:T(8,128)(2,1)S(1)} %shard_map.53), channel_id=1, source_target_pairs={{0,192},{64,128},{128,64},{192,0},{1,193},{65,129},{129,65},{193,1... | collective-permute-start | bytes 811016 | tf_op jit(solution)/shard_map/ppermute | solution.py:50
  74.6 3.6 %collective-permute-done.20.refs_0_ = bf16[264,512]{1,0:T(8,128)(2,1)S(1)} collective-permute-done((bf16[264,512]{1,0:T(8,128)(2,1)S(1)}, bf16[264,512]{1,0:T(8,128)(2,1)S(1)}, u32[]{:S(2)}, u32[]{:S(2)}) %collective-permute-start.20) | collective-permute-done | bytes 270368 | tf_op jit(solution)/shard_map/ppermute | solution.py:50
  78.2 2.8 %shard_map.54 = bf16[264,512]{1,0:T(8,128)(2,1)S(1)} custom-call(bf16[256,576]{1,0:T(8,128)(2,1)S(1)} %collective-permute-done.11.refs_2_.q_ref, f32[256,1536]{1,0:T(8,128)S(1)} %get-tuple-element.143.refs_0_, f32[256,128]{1,0:T(8,128)S(1)} %get-tuple-element.144.refs_1_, f32[256,1536]{1,0:T(8,128)S(1)} %get-tuple-element.145.refs_2_, ...), custom_call_target="tpu_custom_call" | custom-call | tf_op jit(solution)/shard_map/pallas_call | solution.py:301
  81.0 1.4 %collective-permute-start.22 = (bf16[264,512]{1,0:T(8,128)(2,1)S(1)}, bf16[264,512]{1,0:T(8,128)(2,1)S(1)}, u32[]{:S(2)}, u32[]{:S(2)}) collective-permute-start(bf16[264,512]{1,0:T(8,128)(2,1)S(1)} %shard_map.54), channel_id=1, source_target_pairs={{0,128},{64,192},{128,0},{192,64},{1,129},{65,193},{129,1},{193,65... | collective-permute-start | bytes 811016 | tf_op jit(solution)/shard_map/ppermute | solution.py:50
  82.9 2.8 %shard_map.55.refs_3_ = bf16[264,512]{1,0:T(8,128)(2,1)S(1)} custom-call(bf16[256,576]{1,0:T(8,128)(2,1)S(1)} %constant_dynamic-update-slice_fusion.refs_0_.q_ref, f32[256,1536]{1,0:T(8,128)S(1)} %get-tuple-element.152.refs_0_, f32[256,128]{1,0:T(8,128)S(1)} %get-tuple-element.153.refs_1_, f32[256,1536]{1,0:T(8,128)S(1)} %get-tuple-element.154.refs_2_, ...), custom_call_target="tpu_custom_call" | custom-call | tf_op jit(solution)/shard_map/pallas_call | solution.py:301
  85.7 4.6 %collective-permute-done.22.refs_2_ = bf16[264,512]{1,0:T(8,128)(2,1)S(1)} collective-permute-done((bf16[264,512]{1,0:T(8,128)(2,1)S(1)}, bf16[264,512]{1,0:T(8,128)(2,1)S(1)}, u32[]{:S(2)}, u32[]{:S(2)}) %collective-permute-start.22) | collective-permute-done | bytes 270368 | tf_op jit(solution)/shard_map/ppermute | solution.py:50
  90.8 4.1 %collective-permute-start.23 = (bf16[32,640]{1,0:T(8,128)(2,1)S(1)}, bf16[32,640]{1,0:T(8,128)(2,1)S(1)}, u32[]{:S(2)}, u32[]{:S(2)}) collective-permute-start(bf16[32,640]{1,0:T(8,128)(2,1)S(1)} %get-tuple-element.158), channel_id=1, source_target_pairs={{0,32},{8,40},{16,48},{24,56},{32,0},{40,8},{48,16},{56,24},{1,33}... | collective-permute-start | bytes 122888 | tf_op jit(solution)/shard_map/ppermute | solution.py:54
  95.5 1.9 %collective-permute-start.25 = (bf16[32,640]{1,0:T(8,128)(2,1)S(1)}, bf16[32,640]{1,0:T(8,128)(2,1)S(1)}, u32[]{:S(2)}, u32[]{:S(2)}) collective-permute-start(bf16[32,640]{1,0:T(8,128)(2,1)S(1)} %get-tuple-element.160), channel_id=1, source_target_pairs={{0,48},{8,56},{16,32},{24,40},{32,16},{40,24},{48,0},{56,8},{1,49}... | collective-permute-start | bytes 122888 | tf_op jit(solution)/shard_map/ppermute | solution.py:54
  98.3 3.7 %collective-permute-start.27 = (bf16[32,640]{1,0:T(8,128)(2,1)S(1)}, bf16[32,640]{1,0:T(8,128)(2,1)S(1)}, u32[]{:S(2)}, u32[]{:S(2)}) collective-permute-start(bf16[32,640]{1,0:T(8,128)(2,1)S(1)} %get-tuple-element.162), channel_id=1, source_target_pairs={{0,40},{8,32},{16,56},{24,48},{32,8},{40,0},{48,24},{56,16},{1,41}... | collective-permute-start | bytes 122888 | tf_op jit(solution)/shard_map/ppermute | solution.py:54
  103.1 1.7 %collective-permute-start.29 = (bf16[32,640]{1,0:T(8,128)(2,1)S(1)}, bf16[32,640]{1,0:T(8,128)(2,1)S(1)}, u32[]{:S(2)}, u32[]{:S(2)}) collective-permute-start(bf16[32,640]{1,0:T(8,128)(2,1)S(1)} %get-tuple-element.164), channel_id=1, source_target_pairs={{0,56},{8,48},{16,40},{24,32},{32,24},{40,16},{48,8},{56,0},{1,57}... | collective-permute-start | bytes 122888 | tf_op jit(solution)/shard_map/ppermute | solution.py:54
  105.3 2.5 %collective-permute-done.28.refs_6_ = bf16[32,640]{1,0:T(8,128)(2,1)S(1)} collective-permute-done((bf16[32,640]{1,0:T(8,128)(2,1)S(1)}, bf16[32,640]{1,0:T(8,128)(2,1)S(1)}, u32[]{:S(2)}, u32[]{:S(2)}) %collective-permute-start.28) | collective-permute-done | bytes 40992 | tf_op jit(solution)/shard_map/ppermute | solution.py:54
  (52 shorter events, 17.2 us)
Async XLA Ops:
  0.9 9.7 %collective-permute-start = (bf16[32,576]{1,0:T(8,128)(2,1)S(1)}, bf16[32,576]{1,0:T(8,128)(2,1)S(1)}, u32[]{:S(2)}, u32[]{:S(2)}) collective-permute-start(bf16[32,576]{1,0:T(8,128)(2,1)S(1)} %bitcast.6), channel_id=1, source_target_pairs={{0,32},{8,40},{16,48},{24,56},{32,0},{40,8},{48,16},{56,24},{1,33}... | collective-permute-start | bytes 110600 | tf_op jit(solution)/shard_map/ppermute | solution.py:54
  8.2 0.7 copy-start
  10.6 9.9 %collective-permute-start.1 = (bf16[576,256]{1,0:T(8,128)(2,1)S(1)}, bf16[576,256]{1,0:T(8,128)(2,1)S(1)}, u32[]{:S(2)}, u32[]{:S(2)}) collective-permute-start(bf16[576,256]{1,0:T(8,128)(2,1)S(1)} %get-tuple-element.87), channel_id=1, source_target_pairs={{0,1},{1,2},{2,3},{3,0},{4,5},{5,6},{6,7},{7,4},{8,9},{9,10},{10,1... | collective-permute-start | bytes 884744 | tf_op jit(solution)/shard_map/ppermute | solution.py:42
  12.2 8.2 %collective-permute-start.2 = (bf16[576,256]{1,0:T(8,128)(2,1)S(1)}, bf16[576,256]{1,0:T(8,128)(2,1)S(1)}, u32[]{:S(2)}, u32[]{:S(2)}) collective-permute-start(bf16[576,256]{1,0:T(8,128)(2,1)S(1)} %get-tuple-element.88), channel_id=1, source_target_pairs={{0,3},{1,0},{2,1},{3,2},{4,7},{5,4},{6,5},{7,6},{8,11},{9,8},{10,9... | collective-permute-start | bytes 884744 | tf_op jit(solution)/shard_map/ppermute | solution.py:42
  13.9 6.2 %collective-permute-start.3 = (bf16[64,576]{1,0:T(8,128)(2,1)S(1)}, bf16[64,576]{1,0:T(8,128)(2,1)S(1)}, u32[]{:S(2)}, u32[]{:S(2)}) collective-permute-start(bf16[64,576]{1,0:T(8,128)(2,1)S(1)} %pad_maximum_fusion.1), channel_id=1, source_target_pairs={{0,16},{8,24},{16,0},{24,8},{32,48},{40,56},{48,32},{56,40},{1,17}... | collective-permute-start | bytes 221192 | tf_op jit(solution)/shard_map/ppermute | solution.py:54
  21.2 17.0 %collective-permute-start.5 = (bf16[576,512]{1,0:T(8,128)(2,1)S(1)}, bf16[576,512]{1,0:T(8,128)(2,1)S(1)}, u32[]{:S(2)}, u32[]{:S(2)}) collective-permute-start(bf16[576,512]{1,0:T(8,128)(2,1)S(1)} %get-tuple-element.95), channel_id=1, source_target_pairs={{0,1},{1,2},{2,3},{3,0},{4,5},{5,6},{6,7},{7,4},{8,9},{9,10},{10,1... | collective-permute-start | bytes 1769480 | tf_op jit(solution)/shard_map/ppermute | solution.py:42
  22.8 15.4 %collective-permute-start.6 = (bf16[576,512]{1,0:T(8,128)(2,1)S(1)}, bf16[576,512]{1,0:T(8,128)(2,1)S(1)}, u32[]{:S(2)}, u32[]{:S(2)}) collective-permute-start(bf16[576,512]{1,0:T(8,128)(2,1)S(1)} %get-tuple-element.96), channel_id=1, source_target_pairs={{0,3},{1,0},{2,1},{3,2},{4,7},{5,4},{6,5},{7,6},{8,11},{9,8},{10,9... | collective-permute-start | bytes 1769480 | tf_op jit(solution)/shard_map/ppermute | solution.py:42
  24.5 5.3 %collective-permute-start.4 = (bf16[128,576]{1,0:T(8,128)(2,1)S(1)}, bf16[128,576]{1,0:T(8,128)(2,1)S(1)}, u32[]{:S(2)}, u32[]{:S(2)}) collective-permute-start(bf16[128,576]{1,0:T(8,128)(2,1)S(1)} %pad_maximum_fusion), channel_id=1, source_target_pairs={{0,8},{8,0},{16,24},{24,16},{32,40},{40,32},{48,56},{56,48},{1,9},... | collective-permute-start | bytes 442376 | tf_op jit(solution)/shard_map/ppermute | solution.py:54
  29.8 8.4 %collective-permute-start.8 = (bf16[256,576]{1,0:T(8,128)(2,1)S(1)}, bf16[256,576]{1,0:T(8,128)(2,1)S(1)}, u32[]{:S(2)}, u32[]{:S(2)}) collective-permute-start(bf16[256,576]{1,0:T(8,128)(2,1)S(1)} %constant_dynamic-update-slice_fusion.refs_0_.q_ref), channel_id=1, source_target_pairs={{0,192},{64,128},{128,64},{192,0},{1,193},{65,129},{129,65},{193,1... | collective-permute-start | bytes 884744 | tf_op jit(solution)/shard_map/ppermute | solution.py:50
  30.4 7.8 %collective-permute-start.7 = (bf16[256,576]{1,0:T(8,128)(2,1)S(1)}, bf16[256,576]{1,0:T(8,128)(2,1)S(1)}, u32[]{:S(2)}, u32[]{:S(2)}) collective-permute-start(bf16[256,576]{1,0:T(8,128)(2,1)S(1)} %constant_dynamic-update-slice_fusion.refs_0_.q_ref), channel_id=1, source_target_pairs={{0,64},{64,0},{128,192},{192,128},{1,65},{65,1},{129,193},{193,129... | collective-permute-start | bytes 884744 | tf_op jit(solution)/shard_map/ppermute | solution.py:50
  38.2 18.5 %copy-start.1 = (s32[16]{0:T(128)S(1)}, s32[16]{0:T(128)}, u32[]{:S(2)}) copy-start(s32[16]{0:T(128)} %refs_4_.4) | copy-start | bytes 196
  38.9 11.8 %collective-permute-start.10 = (bf16[576,512]{1,0:T(8,128)(2,1)S(1)}, bf16[576,512]{1,0:T(8,128)(2,1)S(1)}, u32[]{:S(2)}, u32[]{:S(2)}) collective-permute-start(bf16[576,512]{1,0:T(8,128)(2,1)S(1)} %shard_map.49.refs_4_.refs_7_), channel_id=1, source_target_pairs={{0,3},{1,0},{2,1},{3,2},{4,7},{5,4},{6,5},{7,6},{8,11},{9,8},{10,9... | collective-permute-start | bytes 1769480 | tf_op jit(solution)/shard_map/ppermute | solution.py:42
  40.8 13.1 %collective-permute-start.9 = (bf16[576,512]{1,0:T(8,128)(2,1)S(1)}, bf16[576,512]{1,0:T(8,128)(2,1)S(1)}, u32[]{:S(2)}, u32[]{:S(2)}) collective-permute-start(bf16[576,512]{1,0:T(8,128)(2,1)S(1)} %shard_map.49.refs_4_.refs_7_), channel_id=1, source_target_pairs={{0,1},{1,2},{2,3},{3,0},{4,5},{5,6},{6,7},{7,4},{8,9},{9,10},{10,1... | collective-permute-start | bytes 1769480 | tf_op jit(solution)/shard_map/ppermute | solution.py:42
  41.0 8.6 %collective-permute-start.11 = (bf16[256,576]{1,0:T(8,128)(2,1)S(1)}, bf16[256,576]{1,0:T(8,128)(2,1)S(1)}, u32[]{:S(2)}, u32[]{:S(2)}) collective-permute-start(bf16[256,576]{1,0:T(8,128)(2,1)S(1)} %constant_dynamic-update-slice_fusion.refs_0_.q_ref), channel_id=1, source_target_pairs={{0,128},{64,192},{128,0},{192,64},{1,129},{65,193},{129,1},{193,65... | collective-permute-start | bytes 884744 | tf_op jit(solution)/shard_map/ppermute | solution.py:50
  42.7 13.9 %collective-permute-start.12 = (bf16[576,512]{1,0:T(8,128)(2,1)S(1)}, bf16[576,512]{1,0:T(8,128)(2,1)S(1)}, u32[]{:S(2)}, u32[]{:S(2)}) collective-permute-start(bf16[576,512]{1,0:T(8,128)(2,1)S(1)} %shard_map.49.refs_4_.refs_7_), channel_id=1, source_target_pairs={{0,4},{4,0},{1,5},{5,1},{2,6},{6,2},{3,7},{7,3},{8,12},{12,8},{9,1... | collective-permute-start | bytes 1769480 | tf_op jit(solution)/shard_map/ppermute | solution.py:46
  53.9 2.7 %collective-permute-start.13 = (bf16[576,512]{1,0:T(8,128)(2,1)S(1)}, bf16[576,512]{1,0:T(8,128)(2,1)S(1)}, u32[]{:S(2)}, u32[]{:S(2)}) collective-permute-start(bf16[576,512]{1,0:T(8,128)(2,1)S(1)} %collective-permute-done.9.refs_5_.refs_8_), channel_id=1, source_target_pairs={{0,4},{4,0},{1,5},{5,1},{2,6},{6,2},{3,7},{7,3},{8,12},{12,8},{9,1... | collective-permute-start | bytes 1769480 | tf_op jit(solution)/shard_map/ppermute | solution.py:46
  53.9 2.8 %collective-permute-start.14 = (bf16[576,512]{1,0:T(8,128)(2,1)S(1)}, bf16[576,512]{1,0:T(8,128)(2,1)S(1)}, u32[]{:S(2)}, u32[]{:S(2)}) collective-permute-start(bf16[576,512]{1,0:T(8,128)(2,1)S(1)} %collective-permute-done.10.refs_6_.refs_9_), channel_id=1, source_target_pairs={{0,4},{4,0},{1,5},{5,1},{2,6},{6,2},{3,7},{7,3},{8,12},{12,8},{9,1... | collective-permute-start | bytes 1769480 | tf_op jit(solution)/shard_map/ppermute | solution.py:46
  54.4 9.0 %collective-permute-start.17 = (bf16[576,256]{1,0:T(8,128)(2,1)S(1)}, bf16[576,256]{1,0:T(8,128)(2,1)S(1)}, u32[]{:S(2)}, u32[]{:S(2)}) collective-permute-start(bf16[576,256]{1,0:T(8,128)(2,1)S(1)} %slice.7), channel_id=1, source_target_pairs={{0,3},{1,0},{2,1},{3,2},{4,7},{5,4},{6,5},{7,6},{8,11},{9,8},{10,9... | collective-permute-start | bytes 884744 | tf_op jit(solution)/shard_map/ppermute | solution.py:42
  54.8 9.9 %collective-permute-start.16 = (bf16[576,256]{1,0:T(8,128)(2,1)S(1)}, bf16[576,256]{1,0:T(8,128)(2,1)S(1)}, u32[]{:S(2)}, u32[]{:S(2)}) collective-permute-start(bf16[576,256]{1,0:T(8,128)(2,1)S(1)} %slice.6), channel_id=1, source_target_pairs={{0,1},{1,2},{2,3},{3,0},{4,5},{5,6},{6,7},{7,4},{8,9},{9,10},{10,1... | collective-permute-start | bytes 884744 | tf_op jit(solution)/shard_map/ppermute | solution.py:42
  56.6 3.4 %collective-permute-start.15 = (s32[2]{0:T(128)S(1)}, s32[2]{0:T(128)S(1)}, u32[]{:S(2)}, u32[]{:S(2)}) collective-permute-start(s32[2]{0:T(128)S(1)} %copy-done), channel_id=1, source_target_pairs={{0,4},{4,0},{1,5},{5,1},{2,6},{6,2},{3,7},{7,3},{8,12},{12,8},{9,1... | collective-permute-start | bytes 32 | tf_op jit(solution)/shard_map/ppermute | solution.py:46
  64.7 1.6 %collective-permute-start.18 = (bf16[576,256]{1,0:T(8,128)(2,1)S(1)}, bf16[576,256]{1,0:T(8,128)(2,1)S(1)}, u32[]{:S(2)}, u32[]{:S(2)}) collective-permute-start(bf16[576,256]{1,0:T(8,128)(2,1)S(1)} %collective-permute-done.16.refs_10_), channel_id=1, source_target_pairs={{0,4},{4,0},{1,5},{5,1},{2,6},{6,2},{3,7},{7,3},{8,12},{12,8},{9,1... | collective-permute-start | bytes 884744 | tf_op jit(solution)/shard_map/ppermute | solution.py:46
  64.7 2.0 %collective-permute-start.19 = (bf16[576,256]{1,0:T(8,128)(2,1)S(1)}, bf16[576,256]{1,0:T(8,128)(2,1)S(1)}, u32[]{:S(2)}, u32[]{:S(2)}) collective-permute-start(bf16[576,256]{1,0:T(8,128)(2,1)S(1)} %collective-permute-done.17.refs_11_), channel_id=1, source_target_pairs={{0,4},{4,0},{1,5},{5,1},{2,6},{6,2},{3,7},{7,3},{8,12},{12,8},{9,1... | collective-permute-start | bytes 884744 | tf_op jit(solution)/shard_map/ppermute | solution.py:46
  69.6 8.6 %collective-permute-start.20 = (bf16[264,512]{1,0:T(8,128)(2,1)S(1)}, bf16[264,512]{1,0:T(8,128)(2,1)S(1)}, u32[]{:S(2)}, u32[]{:S(2)}) collective-permute-start(bf16[264,512]{1,0:T(8,128)(2,1)S(1)} %shard_map.52), channel_id=1, source_target_pairs={{0,64},{64,0},{128,192},{192,128},{1,65},{65,1},{129,193},{193,129... | collective-permute-start | bytes 811016 | tf_op jit(solution)/shard_map/ppermute | solution.py:50
  73.1 9.8 %collective-permute-start.21 = (bf16[264,512]{1,0:T(8,128)(2,1)S(1)}, bf16[264,512]{1,0:T(8,128)(2,1)S(1)}, u32[]{:S(2)}, u32[]{:S(2)}) collective-permute-start(bf16[264,512]{1,0:T(8,128)(2,1)S(1)} %shard_map.53), channel_id=1, source_target_pairs={{0,192},{64,128},{128,64},{192,0},{1,193},{65,129},{129,65},{193,1... | collective-permute-start | bytes 811016 | tf_op jit(solution)/shard_map/ppermute | solution.py:50
  81.0 9.3 %collective-permute-start.22 = (bf16[264,512]{1,0:T(8,128)(2,1)S(1)}, bf16[264,512]{1,0:T(8,128)(2,1)S(1)}, u32[]{:S(2)}, u32[]{:S(2)}) collective-permute-start(bf16[264,512]{1,0:T(8,128)(2,1)S(1)} %shard_map.54), channel_id=1, source_target_pairs={{0,128},{64,192},{128,0},{192,64},{1,129},{65,193},{129,1},{193,65... | collective-permute-start | bytes 811016 | tf_op jit(solution)/shard_map/ppermute | solution.py:50
  90.8 11.2 %collective-permute-start.23 = (bf16[32,640]{1,0:T(8,128)(2,1)S(1)}, bf16[32,640]{1,0:T(8,128)(2,1)S(1)}, u32[]{:S(2)}, u32[]{:S(2)}) collective-permute-start(bf16[32,640]{1,0:T(8,128)(2,1)S(1)} %get-tuple-element.158), channel_id=1, source_target_pairs={{0,32},{8,40},{16,48},{24,56},{32,0},{40,8},{48,16},{56,24},{1,33}... | collective-permute-start | bytes 122888 | tf_op jit(solution)/shard_map/ppermute | solution.py:54
  95.0 8.2 %collective-permute-start.24 = (bf16[32,640]{1,0:T(8,128)(2,1)S(1)}, bf16[32,640]{1,0:T(8,128)(2,1)S(1)}, u32[]{:S(2)}, u32[]{:S(2)}) collective-permute-start(bf16[32,640]{1,0:T(8,128)(2,1)S(1)} %get-tuple-element.159), channel_id=1, source_target_pairs={{0,16},{8,24},{16,0},{24,8},{32,48},{40,56},{48,32},{56,40},{1,17}... | collective-permute-start | bytes 122888 | tf_op jit(solution)/shard_map/ppermute | solution.py:54
  95.5 9.4 %collective-permute-start.25 = (bf16[32,640]{1,0:T(8,128)(2,1)S(1)}, bf16[32,640]{1,0:T(8,128)(2,1)S(1)}, u32[]{:S(2)}, u32[]{:S(2)}) collective-permute-start(bf16[32,640]{1,0:T(8,128)(2,1)S(1)} %get-tuple-element.160), channel_id=1, source_target_pairs={{0,48},{8,56},{16,32},{24,40},{32,16},{40,24},{48,0},{56,8},{1,49}... | collective-permute-start | bytes 122888 | tf_op jit(solution)/shard_map/ppermute | solution.py:54
  97.4 7.4 %collective-permute-start.26 = (bf16[32,640]{1,0:T(8,128)(2,1)S(1)}, bf16[32,640]{1,0:T(8,128)(2,1)S(1)}, u32[]{:S(2)}, u32[]{:S(2)}) collective-permute-start(bf16[32,640]{1,0:T(8,128)(2,1)S(1)} %get-tuple-element.161), channel_id=1, source_target_pairs={{0,8},{8,0},{16,24},{24,16},{32,40},{40,32},{48,56},{56,48},{1,9},... | collective-permute-start | bytes 122888 | tf_op jit(solution)/shard_map/ppermute | solution.py:54
  98.3 7.0 %collective-permute-start.27 = (bf16[32,640]{1,0:T(8,128)(2,1)S(1)}, bf16[32,640]{1,0:T(8,128)(2,1)S(1)}, u32[]{:S(2)}, u32[]{:S(2)}) collective-permute-start(bf16[32,640]{1,0:T(8,128)(2,1)S(1)} %get-tuple-element.162), channel_id=1, source_target_pairs={{0,40},{8,32},{16,56},{24,48},{32,8},{40,0},{48,24},{56,16},{1,41}... | collective-permute-start | bytes 122888 | tf_op jit(solution)/shard_map/ppermute | solution.py:54
  102.0 5.8 %collective-permute-start.28 = (bf16[32,640]{1,0:T(8,128)(2,1)S(1)}, bf16[32,640]{1,0:T(8,128)(2,1)S(1)}, u32[]{:S(2)}, u32[]{:S(2)}) collective-permute-start(bf16[32,640]{1,0:T(8,128)(2,1)S(1)} %get-tuple-element.163), channel_id=1, source_target_pairs={{0,24},{8,16},{16,8},{24,0},{32,56},{40,48},{48,40},{56,32},{1,25}... | collective-permute-start | bytes 122888 | tf_op jit(solution)/shard_map/ppermute | solution.py:54
  103.1 5.7 %collective-permute-start.29 = (bf16[32,640]{1,0:T(8,128)(2,1)S(1)}, bf16[32,640]{1,0:T(8,128)(2,1)S(1)}, u32[]{:S(2)}, u32[]{:S(2)}) collective-permute-start(bf16[32,640]{1,0:T(8,128)(2,1)S(1)} %get-tuple-element.164), channel_id=1, source_target_pairs={{0,56},{8,48},{16,40},{24,32},{32,24},{40,16},{48,8},{56,0},{1,57}... | collective-permute-start | bytes 122888 | tf_op jit(solution)/shard_map/ppermute | solution.py:54

commit v7 on v5

--- a/solution.py
+++ b/solution.py
@@ -82,16 +82,17 @@
     run_copies(copies)
 
 
-def own_cut_kernel(hot_ref, lat_ref, right_ref, left_ref, mine_ref, sems):
+def own_cut_kernel(hot_ref, lat_ref, right_a, right_b, left_a, left_b, mine_ref, sems):
     rank = lax.axis_index("rep")
     copies = []
-    for hop, dst in ((1, right_ref), (3, left_ref), (0, mine_ref)):
-        for half in range(2):
+    for hop, halves in ((1, (right_a, right_b)), (3, (left_a, left_b)), (0, (mine_ref, mine_ref))):
+        for half, dst in enumerate(halves):
             for slot in range(HOT_GRP):
+                to = slot * HALF + (half * PAIR if hop == 0 else 0)
                 copies.append(
                     pltpu.make_async_copy(
                         lat_ref.at[:, column(hot_ref, slot, (rank + hop) % N_REP, half)],
-                        dst.at[:, pl.ds(half * PAIR + slot * HALF, HALF)],
+                        dst.at[:, pl.ds(to, HALF)],
                         sems.at[len(copies)],
                     )
                 )
@@ -100,25 +101,22 @@
 
 def pass_on_kernel(hot_ref, from_left, from_right, right_in, left_in, right_ref, left_ref):
     rank = lax.axis_index("rep")
-    right_ref[:, PAIR:] = right_in[:, PAIR:]
-    left_ref[:, :PAIR] = left_in[:, :PAIR]
     for slot in range(HOT_GRP):
         a = slice(slot * HALF, (slot + 1) * HALF)
-        b = slice(PAIR + slot * HALF, PAIR + (slot + 1) * HALF)
         here = hot_ref[slot] // PER_DEV == rank
 
         @pl.when(here)
         def _():
             right_ref[:, a] = right_in[:, a]
-            left_ref[:, b] = left_in[:, b]
+            left_ref[:, a] = left_in[:, a]
 
         @pl.when(jnp.logical_not(here))
         def _():
             right_ref[:, a] = from_left[:, a]
-            left_ref[:, b] = from_right[:, a]
-
-
-def settle_kernel(hot_ref, from_left, from_right, mine_in, mine_ref):
+            left_ref[:, a] = from_right[:, a]
+
+
+def settle_kernel(hot_ref, left_a, left_b, right_a, right_b, mine_in, mine_ref):
     rank = lax.axis_index("rep")
     for slot in range(HOT_GRP):
         a = slice(slot * HALF, (slot + 1) * HALF)
@@ -132,19 +130,19 @@
 
         @pl.when(away >= 2)
         def _():
-            mine_ref[:, a] = from_left[:, a]
+            mine_ref[:, a] = left_a[:, a]
 
         @pl.when(away == 1)
         def _():
-            mine_ref[:, a] = from_right[:, a]
+            mine_ref[:, a] = right_a[:, a]
 
         @pl.when(away == 3)
         def _():
-            mine_ref[:, b] = from_left[:, b]
+            mine_ref[:, b] = left_b[:, a]
 
         @pl.when((away == 1) | (away == 2))
         def _():
-            mine_ref[:, b] = from_right[:, b]
+            mine_ref[:, b] = right_b[:, a]
 
 
 def three_terms(v):
@@ -300,38 +298,41 @@
     up, down = shift_rep(up, 1), shift_rep(down, -1)
     own = queries.reshape(count, -1, WIDTH).transpose(1, 0, 2).reshape(-1, WIDTH)
     near = jnp.concatenate([own, cross_z(own, 4)], axis=0)
-    right, left, mine = call(
+    hot_other = swap_core(hot_ids)
+    right_a, right_b, left_a, left_b, mine = call(
         own_cut_kernel,
-        [chunk] * 3,
+        [pair] * 4 + [chunk],
         [SMEM, ANY],
         [hot_ids, by_column],
         mib=50,
         scratch_shapes=[pltpu.SemaphoreType.DMA((12,))],
     )
-    up, down, near = lax.optimization_barrier((up, down, near))
-    right, left = call(
+    from_left_b, from_right_a = shift_rep(right_b, 1), shift_rep(left_a, -1)
+    up, down, near, hot_other = lax.optimization_barrier((up, down, near, hot_other))
+    right_a, left_b = call(
         pass_on_kernel,
-        [chunk] * 2,
+        [pair] * 2,
         [SMEM] + [VMEM] * 4,
-        [hot_ids, up, down, right, left],
-    )
-    from_left, from_right = shift_rep(right, 1), shift_rep(left, -1)
+        [hot_ids, up, down, right_a, left_b],
+    )
+    from_left_a, from_right_b = shift_rep(right_a, 1), shift_rep(left_b, -1)
     for bits in (2, 1):
         near = jnp.concatenate([near, cross_z(near, bits)], axis=0)
     (mine,) = call(
         settle_kernel,
         [chunk],
-        [SMEM] + [VMEM] * 3,
-        [hot_ids, from_left, from_right, mine],
-    )
+        [SMEM] + [VMEM] * 5,
+        [hot_ids, from_left_a, from_left_b, from_right_a, from_right_b, mine],
+    )
+    own_quarter, near = lax.optimization_barrier((mine, near))
     asked = [near] + [cross_x(near, bits) for bits in range(1, N_X)]
-    hot_other = swap_core(hot_ids)
-
-    of_left, of_right = shift_rep(mine, 1), shift_rep(mine, -1)
+
+    of_left, of_right, swapped = shift_rep(mine, 1), shift_rep(mine, -1), swap_core(own_quarter)
+    of_left, of_right, swapped = lax.optimization_barrier((of_left, of_right, swapped))
     far_a, far_b = shift_rep(of_left[:, :PAIR], 1), shift_rep(of_right[:, PAIR:], -1)
     far_a, far_b, *asked = lax.optimization_barrier((far_a, far_b, *asked))
     keys = [mine, of_left, of_right, far_a, far_b]
-    keys = keys + [swap_core(k) for k in keys]
+    keys = keys + [swapped] + [swap_core(k) for k in keys[1:]]
 
     rows = near.shape[0]
     parts = []

time: 109 us -> 116 us (1.064)
  starting transfers between devices: 44.2 us -> 48.4 us
  waiting for transfers between devices: 39.2 us -> 42.6 us
    ppermute x8 -> x10, waiting for transfers between devices: 18.3 us -> 21.8 us  [shift_rep(): return lax.ppermute(a, 'rep', [(i, (i + by) % N_REP) for i in range(N_REP)])]
    ppermute x10, starting transfers between devices: 23.2 us -> 25.6 us  [cross_z(): return lax.ppermute(a, 'z', [(i, i ^ bits) for i in range(N_Z)])]
    ppermute x8 -> x10, starting transfers between devices: 13.5 us -> 15.2 us  [shift_rep(): return lax.ppermute(a, 'rep', [(i, (i + by) % N_REP) for i in range(N_REP)])]
    ppermute x6, waiting for transfers between devices: 9.57 us -> 8.18 us  [cross_x(): return lax.ppermute(a, 'x', [(i, i ^ bits) for i in range(N_X)])]
    ppermute x10, waiting for transfers between devices: 9.78 us -> 11.1 us  [cross_z(): return lax.ppermute(a, 'z', [(i, i ^ bits) for i in range(N_Z)])]
  transfers between devices with their start and end apart: 30 -> 32, of which waited for: 14 -> 14; matrix products, arithmetic and copies ran while one was open for 0% -> 0% of each run, Pallas kernels for 15% -> 14%
where the time goes in v7:
time: 116 us
  starting transfers between devices  48.4 us (42%)
  waiting for transfers between devices  42.6 us (37%)
  Pallas kernels  23.9 us (21%)
    ppermute x10, starting transfers between devices, cross_z(): return lax.ppermute(a, 'z', [(i, i ^ bits) for i in range(N_Z)])  25.6 us
    pallas_call x10, Pallas kernels, call(): pl.pallas_call(kernel, out_shape=tuple((jax.ShapeDtypeStruct(*o) for o in...  23.9 us
    ppermute x10, waiting for transfers between devices, shift_rep(): return lax.ppermute(a, 'rep', [(i, (i + by) % N_REP) for i in range(N_REP)])  21.8 us
    ppermute x10, starting transfers between devices, shift_rep(): return lax.ppermute(a, 'rep', [(i, (i + by) % N_REP) for i in range(N_REP)])  15.2 us
    ppermute x10, waiting for transfers between devices, cross_z(): return lax.ppermute(a, 'z', [(i, i ^ bits) for i in range(N_Z)])  11.1 us
    ppermute x6, waiting for transfers between devices, cross_x(): return lax.ppermute(a, 'x', [(i, i ^ bits) for i in range(N_X)])  8.18 us
    ppermute x6, starting transfers between devices, cross_x(): return lax.ppermute(a, 'x', [(i, i ^ bits) for i in range(N_X)])  6.47 us
  transfers between devices with their start and end apart: 32, of which 14 were waited for; matrix products, arithmetic and copies ran while one was open for 0% of the time, Pallas kernels for 14%

profile of v7, /device:TPU:6, one launch (start us, length us, event | category | flops | bytes accessed | tf_op | source)
XLA Modules:
  0.0 116.1 jit_solution(5782484300273062195)
XLA Ops:
  0.7 1.7 %shard_map.46 = (bf16[576,256]{1,0:T(8,128)(2,1)S(1)}, bf16[576,256]{1,0:T(8,128)(2,1)S(1)}) custom-call(s32[2]{0:T(128)S(1)} %copy-done, bf16[576,4096]{1,0:T(8,128)(2,1)} %bitcast.4), custom_call_target="tpu_custom_call" | custom-call | tf_op jit(solution)/shard_map/pallas_call | solution.py:275
  2.5 1.7 %collective-permute-start = (bf16[576,256]{1,0:T(8,128)(2,1)S(1)}, bf16[576,256]{1,0:T(8,128)(2,1)S(1)}, u32[]{:S(2)}, u32[]{:S(2)}) collective-permute-start(bf16[576,256]{1,0:T(8,128)(2,1)S(1)} %get-tuple-element.48), channel_id=1, source_target_pairs={{0,1},{1,2},{2,3},{3,0},{4,5},{5,6},{6,7},{7,4},{8,9},{9,10},{10,1... | collective-permute-start | bytes 884744 | tf_op jit(solution)/shard_map/ppermute | solution.py:43
  4.1 1.7 %collective-permute-start.1 = (bf16[576,256]{1,0:T(8,128)(2,1)S(1)}, bf16[576,256]{1,0:T(8,128)(2,1)S(1)}, u32[]{:S(2)}, u32[]{:S(2)}) collective-permute-start(bf16[576,256]{1,0:T(8,128)(2,1)S(1)} %get-tuple-element.49), channel_id=1, source_target_pairs={{0,3},{1,0},{2,1},{3,2},{4,7},{5,4},{6,5},{7,6},{8,11},{9,8},{10,9... | collective-permute-start | bytes 884744 | tf_op jit(solution)/shard_map/ppermute | solution.py:43
  5.9 7.3 %collective-permute-start.2 = (bf16[32,576]{1,0:T(8,128)(2,1)S(1)}, bf16[32,576]{1,0:T(8,128)(2,1)S(1)}, u32[]{:S(2)}, u32[]{:S(2)}) collective-permute-start(bf16[32,576]{1,0:T(8,128)(2,1)S(1)} %bitcast.6), channel_id=1, source_target_pairs={{0,32},{8,40},{16,48},{24,56},{32,0},{40,8},{48,16},{56,24},{1,33}... | collective-permute-start | bytes 110600 | tf_op jit(solution)/shard_map/ppermute | solution.py:55
  13.2 2.1 %collective-permute-done.2 = bf16[32,576]{1,0:T(8,128)(2,1)S(1)} collective-permute-done((bf16[32,576]{1,0:T(8,128)(2,1)S(1)}, bf16[32,576]{1,0:T(8,128)(2,1)S(1)}, u32[]{:S(2)}, u32[]{:S(2)}) %collective-permute-start.2) | collective-permute-done | bytes 36896 | tf_op jit(solution)/shard_map/ppermute | solution.py:55
  15.3 2.0 %collective-permute-start.10 = (bf16[64,576]{1,0:T(8,128)(2,1)S(1)}, bf16[64,576]{1,0:T(8,128)(2,1)S(1)}, u32[]{:S(2)}, u32[]{:S(2)}) collective-permute-start(bf16[64,576]{1,0:T(8,128)(2,1)S(1)} %pad_maximum_fusion.2), channel_id=1, source_target_pairs={{0,16},{8,24},{16,0},{24,8},{32,48},{40,56},{48,32},{56,40},{1,17}... | collective-permute-start | bytes 221192 | tf_op jit(solution)/shard_map/ppermute | solution.py:55
  17.3 2.2 %shard_map.47 = (bf16[576,256]{1,0:T(8,128)(2,1)S(1)}, bf16[576,256]{1,0:T(8,128)(2,1)S(1)}, bf16[576,256]{1,0:T(8,128)(2,1)S(1)}, bf16[576,256]{1,0:T(8,128)(2,1)S(1)}, bf16[576,512]{1,0:T(8,128)(2,1)S(1)}) custom-call(s32[2]{0:T(128)S(1)} %copy-done.1, bf16[576,4096]{1,0:T(8,128)(2,1)} %bitcast.5), custom_call_target="tpu_custom_call" | custom-call | tf_op jit(solution)/shard_map/pallas_call | solution.py:275
  20.0 2.9 %collective-permute-start.6 = (bf16[576,256]{1,0:T(8,128)(2,1)S(1)}, bf16[576,256]{1,0:T(8,128)(2,1)S(1)}, u32[]{:S(2)}, u32[]{:S(2)}) collective-permute-start(bf16[576,256]{1,0:T(8,128)(2,1)S(1)} %get-tuple-element.56), channel_id=1, source_target_pairs={{0,3},{1,0},{2,1},{3,2},{4,7},{5,4},{6,5},{7,6},{8,11},{9,8},{10,9... | collective-permute-start | bytes 884744 | tf_op jit(solution)/shard_map/ppermute | solution.py:43
  23.7 3.2 %collective-permute-start.7 = (bf16[576,256]{1,0:T(8,128)(2,1)S(1)}, bf16[576,256]{1,0:T(8,128)(2,1)S(1)}, u32[]{:S(2)}, u32[]{:S(2)}) collective-permute-start(bf16[576,256]{1,0:T(8,128)(2,1)S(1)} %get-tuple-element.57), channel_id=1, source_target_pairs={{0,3},{1,0},{2,1},{3,2},{4,7},{5,4},{6,5},{7,6},{8,11},{9,8},{10,9... | collective-permute-start | bytes 884744 | tf_op jit(solution)/shard_map/ppermute | solution.py:43
  26.9 2.0 %collective-permute-start.11 = (bf16[128,576]{1,0:T(8,128)(2,1)S(1)}, bf16[128,576]{1,0:T(8,128)(2,1)S(1)}, u32[]{:S(2)}, u32[]{:S(2)}) collective-permute-start(bf16[128,576]{1,0:T(8,128)(2,1)S(1)} %pad_maximum_fusion.1), channel_id=1, source_target_pairs={{0,8},{8,0},{16,24},{24,16},{32,40},{40,32},{48,56},{56,48},{1,9},... | collective-permute-start | bytes 442376 | tf_op jit(solution)/shard_map/ppermute | solution.py:55
  28.9 3.4 %collective-permute-done.11 = bf16[128,576]{1,0:T(8,128)(2,1)S(1)} collective-permute-done((bf16[128,576]{1,0:T(8,128)(2,1)S(1)}, bf16[128,576]{1,0:T(8,128)(2,1)S(1)}, u32[]{:S(2)}, u32[]{:S(2)}) %collective-permute-start.11) | collective-permute-done | bytes 147488 | tf_op jit(solution)/shard_map/ppermute | solution.py:55
  32.4 2.1 %collective-permute-done.4.left_a = bf16[576,256]{1,0:T(8,128)(2,1)S(1)} collective-permute-done((bf16[576,256]{1,0:T(8,128)(2,1)S(1)}, bf16[576,256]{1,0:T(8,128)(2,1)S(1)}, u32[]{:S(2)}, u32[]{:S(2)}) %collective-permute-start.4) | collective-permute-done | bytes 294944 | tf_op jit(solution)/shard_map/ppermute | solution.py:43
  35.3 3.0 %collective-permute-start.9 = (bf16[576,512]{1,0:T(8,128)(2,1)S(1)}, bf16[576,512]{1,0:T(8,128)(2,1)S(1)}, u32[]{:S(2)}, u32[]{:S(2)}) collective-permute-start(bf16[576,512]{1,0:T(8,128)(2,1)S(1)} %shard_map.49.refs_0_), channel_id=1, source_target_pairs={{0,3},{1,0},{2,1},{3,2},{4,7},{5,4},{6,5},{7,6},{8,11},{9,8},{10,9... | collective-permute-start | bytes 1769480 | tf_op jit(solution)/shard_map/ppermute | solution.py:43
  38.8 2.4 %collective-permute-start.16 = (bf16[256,576]{1,0:T(8,128)(2,1)S(1)}, bf16[256,576]{1,0:T(8,128)(2,1)S(1)}, u32[]{:S(2)}, u32[]{:S(2)}) collective-permute-start(bf16[256,576]{1,0:T(8,128)(2,1)S(1)} %pad_maximum_fusion.q_ref), channel_id=1, source_target_pairs={{0,128},{64,192},{128,0},{192,64},{1,129},{65,193},{129,1},{193,65... | collective-permute-start | bytes 884744 | tf_op jit(solution)/shard_map/ppermute | solution.py:51
  42.4 9.1 %collective-permute-done.9.refs_2_ = bf16[576,512]{1,0:T(8,128)(2,1)S(1)} collective-permute-done((bf16[576,512]{1,0:T(8,128)(2,1)S(1)}, bf16[576,512]{1,0:T(8,128)(2,1)S(1)}, u32[]{:S(2)}, u32[]{:S(2)}) %collective-permute-start.9) | collective-permute-done | bytes 589856 | tf_op jit(solution)/shard_map/ppermute | solution.py:43
  51.5 3.4 %collective-permute-done.8.refs_1_ = bf16[576,512]{1,0:T(8,128)(2,1)S(1)} collective-permute-done((bf16[576,512]{1,0:T(8,128)(2,1)S(1)}, bf16[576,512]{1,0:T(8,128)(2,1)S(1)}, u32[]{:S(2)}, u32[]{:S(2)}) %collective-permute-start.8) | collective-permute-done | bytes 589856 | tf_op jit(solution)/shard_map/ppermute | solution.py:43
  55.5 1.7 %collective-permute-start.13 = (bf16[576,256]{1,0:T(8,128)(2,1)S(1)}, bf16[576,256]{1,0:T(8,128)(2,1)S(1)}, u32[]{:S(2)}, u32[]{:S(2)}) collective-permute-start(bf16[576,256]{1,0:T(8,128)(2,1)S(1)} %slice.6), channel_id=1, source_target_pairs={{0,1},{1,2},{2,3},{3,0},{4,5},{5,6},{6,7},{7,4},{8,9},{9,10},{10,1... | collective-permute-start | bytes 884744 | tf_op jit(solution)/shard_map/ppermute | solution.py:43
  57.8 5.7 %collective-permute-done.14.refs_4_ = bf16[576,256]{1,0:T(8,128)(2,1)S(1)} collective-permute-done((bf16[576,256]{1,0:T(8,128)(2,1)S(1)}, bf16[576,256]{1,0:T(8,128)(2,1)S(1)}, u32[]{:S(2)}, u32[]{:S(2)}) %collective-permute-start.14) | collective-permute-done | bytes 294944 | tf_op jit(solution)/shard_map/ppermute | solution.py:43
  63.5 1.5 %collective-permute-done.13.refs_3_ = bf16[576,256]{1,0:T(8,128)(2,1)S(1)} collective-permute-done((bf16[576,256]{1,0:T(8,128)(2,1)S(1)}, bf16[576,256]{1,0:T(8,128)(2,1)S(1)}, u32[]{:S(2)}, u32[]{:S(2)}) %collective-permute-start.13) | collective-permute-done | bytes 294944 | tf_op jit(solution)/shard_map/ppermute | solution.py:43
  67.0 4.3 %shard_map.50 = bf16[264,512]{1,0:T(8,128)(2,1)S(1)} custom-call(bf16[256,576]{1,0:T(8,128)(2,1)S(1)} %collective-permute-done.16.q_ref, s32[16]{0:T(128)S(1)} %copy-done.2, s32[2]{0:T(128)S(1)} %copy-done.1, s32[2]{0:T(128)S(1)} %collective-permute-done.3.hot_other_ref, bf16[576,512]{1,0:T(8,128)(2,1)S(1)} %shard_map.49.refs_0_, ...), custom_call_target="tpu_custom_call" | custom-call | tf_op jit(solution)/shard_map/pallas_call | solution.py:275
  71.3 1.5 %collective-permute-start.22 = (bf16[264,512]{1,0:T(8,128)(2,1)S(1)}, bf16[264,512]{1,0:T(8,128)(2,1)S(1)}, u32[]{:S(2)}, u32[]{:S(2)}) collective-permute-start(bf16[264,512]{1,0:T(8,128)(2,1)S(1)} %shard_map.50), channel_id=1, source_target_pairs={{0,128},{64,192},{128,0},{192,64},{1,129},{65,193},{129,1},{193,65... | collective-permute-start | bytes 811016 | tf_op jit(solution)/shard_map/ppermute | solution.py:51
  72.8 4.3 %shard_map.51 = bf16[264,512]{1,0:T(8,128)(2,1)S(1)} custom-call(bf16[256,576]{1,0:T(8,128)(2,1)S(1)} %collective-permute-done.15.q_ref, s32[16]{0:T(128)S(1)} %copy-done.2, s32[2]{0:T(128)S(1)} %copy-done.1, s32[2]{0:T(128)S(1)} %collective-permute-done.3.hot_other_ref, bf16[576,512]{1,0:T(8,128)(2,1)S(1)} %shard_map.49.refs_0_, ...), custom_call_target="tpu_custom_call" | custom-call | tf_op jit(solution)/shard_map/pallas_call | solution.py:275
  77.4 4.0 %collective-permute-done.22.refs_0_ = bf16[264,512]{1,0:T(8,128)(2,1)S(1)} collective-permute-done((bf16[264,512]{1,0:T(8,128)(2,1)S(1)}, bf16[264,512]{1,0:T(8,128)(2,1)S(1)}, u32[]{:S(2)}, u32[]{:S(2)}) %collective-permute-start.22) | collective-permute-done | bytes 270368 | tf_op jit(solution)/shard_map/ppermute | solution.py:51
  81.4 4.3 %shard_map.52 = bf16[264,512]{1,0:T(8,128)(2,1)S(1)} custom-call(bf16[256,576]{1,0:T(8,128)(2,1)S(1)} %collective-permute-done.17.q_ref, s32[16]{0:T(128)S(1)} %copy-done.2, s32[2]{0:T(128)S(1)} %copy-done.1, s32[2]{0:T(128)S(1)} %collective-permute-done.3.hot_other_ref, bf16[576,512]{1,0:T(8,128)(2,1)S(1)} %shard_map.49.refs_0_, ...), custom_call_target="tpu_custom_call" | custom-call | tf_op jit(solution)/shard_map/pallas_call | solution.py:275
  86.3 4.3 %shard_map.53.refs_3_ = bf16[264,512]{1,0:T(8,128)(2,1)S(1)} custom-call(bf16[256,576]{1,0:T(8,128)(2,1)S(1)} %pad_maximum_fusion.q_ref, s32[16]{0:T(128)S(1)} %copy-done.2, s32[2]{0:T(128)S(1)} %copy-done.1, s32[2]{0:T(128)S(1)} %collective-permute-done.3.hot_other_ref, bf16[576,512]{1,0:T(8,128)(2,1)S(1)} %shard_map.49.refs_0_, ...), custom_call_target="tpu_custom_call" | custom-call | tf_op jit(solution)/shard_map/pallas_call | solution.py:275
  90.5 4.2 %collective-permute-done.24.refs_2_ = bf16[264,512]{1,0:T(8,128)(2,1)S(1)} collective-permute-done((bf16[264,512]{1,0:T(8,128)(2,1)S(1)}, bf16[264,512]{1,0:T(8,128)(2,1)S(1)}, u32[]{:S(2)}, u32[]{:S(2)}) %collective-permute-start.24) | collective-permute-done | bytes 270368 | tf_op jit(solution)/shard_map/ppermute | solution.py:51
  95.3 5.2 %collective-permute-start.25 = (bf16[32,640]{1,0:T(8,128)(2,1)S(1)}, bf16[32,640]{1,0:T(8,128)(2,1)S(1)}, u32[]{:S(2)}, u32[]{:S(2)}) collective-permute-start(bf16[32,640]{1,0:T(8,128)(2,1)S(1)} %get-tuple-element.84), channel_id=1, source_target_pairs={{0,32},{8,40},{16,48},{24,56},{32,0},{40,8},{48,16},{56,24},{1,33}... | collective-permute-start | bytes 122888 | tf_op jit(solution)/shard_map/ppermute | solution.py:55
  101.9 1.6 %collective-permute-start.28 = (bf16[32,640]{1,0:T(8,128)(2,1)S(1)}, bf16[32,640]{1,0:T(8,128)(2,1)S(1)}, u32[]{:S(2)}, u32[]{:S(2)}) collective-permute-start(bf16[32,640]{1,0:T(8,128)(2,1)S(1)} %get-tuple-element.87), channel_id=1, source_target_pairs={{0,8},{8,0},{16,24},{24,16},{32,40},{40,32},{48,56},{56,48},{1,9},... | collective-permute-start | bytes 122888 | tf_op jit(solution)/shard_map/ppermute | solution.py:55
  103.5 4.0 %collective-permute-start.29 = (bf16[32,640]{1,0:T(8,128)(2,1)S(1)}, bf16[32,640]{1,0:T(8,128)(2,1)S(1)}, u32[]{:S(2)}, u32[]{:S(2)}) collective-permute-start(bf16[32,640]{1,0:T(8,128)(2,1)S(1)} %get-tuple-element.88), channel_id=1, source_target_pairs={{0,40},{8,32},{16,56},{24,48},{32,8},{40,0},{48,24},{56,16},{1,41}... | collective-permute-start | bytes 122888 | tf_op jit(solution)/shard_map/ppermute | solution.py:55
  107.5 2.1 %collective-permute-start.30 = (bf16[32,640]{1,0:T(8,128)(2,1)S(1)}, bf16[32,640]{1,0:T(8,128)(2,1)S(1)}, u32[]{:S(2)}, u32[]{:S(2)}) collective-permute-start(bf16[32,640]{1,0:T(8,128)(2,1)S(1)} %get-tuple-element.89), channel_id=1, source_target_pairs={{0,24},{8,16},{16,8},{24,0},{32,56},{40,48},{48,40},{56,32},{1,25}... | collective-permute-start | bytes 122888 | tf_op jit(solution)/shard_map/ppermute | solution.py:55
  110.5 2.8 %collective-permute-done.30.refs_6_ = bf16[32,640]{1,0:T(8,128)(2,1)S(1)} collective-permute-done((bf16[32,640]{1,0:T(8,128)(2,1)S(1)}, bf16[32,640]{1,0:T(8,128)(2,1)S(1)}, u32[]{:S(2)}, u32[]{:S(2)}) %collective-permute-start.30) | collective-permute-done | bytes 40992 | tf_op jit(solution)/shard_map/ppermute | solution.py:55
  113.3 1.9 %collective-permute-done.31.refs_7_ = bf16[32,640]{1,0:T(8,128)(2,1)S(1)} collective-permute-done((bf16[32,640]{1,0:T(8,128)(2,1)S(1)}, bf16[32,640]{1,0:T(8,128)(2,1)S(1)}, u32[]{:S(2)}, u32[]{:S(2)}) %collective-permute-start.31) | collective-permute-done | bytes 40992 | tf_op jit(solution)/shard_map/ppermute | solution.py:55
  (57 shorter events, 12.5 us)
Async XLA Ops:
  2.5 12.8 %collective-permute-start = (bf16[576,256]{1,0:T(8,128)(2,1)S(1)}, bf16[576,256]{1,0:T(8,128)(2,1)S(1)}, u32[]{:S(2)}, u32[]{:S(2)}) collective-permute-start(bf16[576,256]{1,0:T(8,128)(2,1)S(1)} %get-tuple-element.48), channel_id=1, source_target_pairs={{0,1},{1,2},{2,3},{3,0},{4,5},{5,6},{6,7},{7,4},{8,9},{9,10},{10,1... | collective-permute-start | bytes 884744 | tf_op jit(solution)/shard_map/ppermute | solution.py:43
  4.1 11.2 %collective-permute-start.1 = (bf16[576,256]{1,0:T(8,128)(2,1)S(1)}, bf16[576,256]{1,0:T(8,128)(2,1)S(1)}, u32[]{:S(2)}, u32[]{:S(2)}) collective-permute-start(bf16[576,256]{1,0:T(8,128)(2,1)S(1)} %get-tuple-element.49), channel_id=1, source_target_pairs={{0,3},{1,0},{2,1},{3,2},{4,7},{5,4},{6,5},{7,6},{8,11},{9,8},{10,9... | collective-permute-start | bytes 884744 | tf_op jit(solution)/shard_map/ppermute | solution.py:43
  5.9 9.3 %collective-permute-start.2 = (bf16[32,576]{1,0:T(8,128)(2,1)S(1)}, bf16[32,576]{1,0:T(8,128)(2,1)S(1)}, u32[]{:S(2)}, u32[]{:S(2)}) collective-permute-start(bf16[32,576]{1,0:T(8,128)(2,1)S(1)} %bitcast.6), channel_id=1, source_target_pairs={{0,32},{8,40},{16,48},{24,56},{32,0},{40,8},{48,16},{56,24},{1,33}... | collective-permute-start | bytes 110600 | tf_op jit(solution)/shard_map/ppermute | solution.py:55
  13.2 2.1 %collective-permute-start.3 = (s32[2]{0:T(128)S(1)}, s32[2]{0:T(128)S(1)}, u32[]{:S(2)}, u32[]{:S(2)}) collective-permute-start(s32[2]{0:T(128)S(1)} %copy-done.1), channel_id=1, source_target_pairs={{0,4},{4,0},{1,5},{5,1},{2,6},{6,2},{3,7},{7,3},{8,12},{12,8},{9,1... | collective-permute-start | bytes 32 | tf_op jit(solution)/shard_map/ppermute | solution.py:47
  15.3 11.6 %collective-permute-start.10 = (bf16[64,576]{1,0:T(8,128)(2,1)S(1)}, bf16[64,576]{1,0:T(8,128)(2,1)S(1)}, u32[]{:S(2)}, u32[]{:S(2)}) collective-permute-start(bf16[64,576]{1,0:T(8,128)(2,1)S(1)} %pad_maximum_fusion.2), channel_id=1, source_target_pairs={{0,16},{8,24},{16,0},{24,8},{32,48},{40,56},{48,32},{56,40},{1,17}... | collective-permute-start | bytes 221192 | tf_op jit(solution)/shard_map/ppermute | solution.py:55
  19.6 12.8 %collective-permute-start.5 = (bf16[576,256]{1,0:T(8,128)(2,1)S(1)}, bf16[576,256]{1,0:T(8,128)(2,1)S(1)}, u32[]{:S(2)}, u32[]{:S(2)}) collective-permute-start(bf16[576,256]{1,0:T(8,128)(2,1)S(1)} %get-tuple-element.55), channel_id=1, source_target_pairs={{0,1},{1,2},{2,3},{3,0},{4,5},{5,6},{6,7},{7,4},{8,9},{9,10},{10,1... | collective-permute-start | bytes 884744 | tf_op jit(solution)/shard_map/ppermute | solution.py:43
  20.0 12.3 %collective-permute-start.6 = (bf16[576,256]{1,0:T(8,128)(2,1)S(1)}, bf16[576,256]{1,0:T(8,128)(2,1)S(1)}, u32[]{:S(2)}, u32[]{:S(2)}) collective-permute-start(bf16[576,256]{1,0:T(8,128)(2,1)S(1)} %get-tuple-element.56), channel_id=1, source_target_pairs={{0,3},{1,0},{2,1},{3,2},{4,7},{5,4},{6,5},{7,6},{8,11},{9,8},{10,9... | collective-permute-start | bytes 884744 | tf_op jit(solution)/shard_map/ppermute | solution.py:43
  23.6 10.9 %collective-permute-start.4 = (bf16[576,256]{1,0:T(8,128)(2,1)S(1)}, bf16[576,256]{1,0:T(8,128)(2,1)S(1)}, u32[]{:S(2)}, u32[]{:S(2)}) collective-permute-start(bf16[576,256]{1,0:T(8,128)(2,1)S(1)} %get-tuple-element.54), channel_id=1, source_target_pairs={{0,1},{1,2},{2,3},{3,0},{4,5},{5,6},{6,7},{7,4},{8,9},{9,10},{10,1... | collective-permute-start | bytes 884744 | tf_op jit(solution)/shard_map/ppermute | solution.py:43
  23.7 10.8 %collective-permute-start.7 = (bf16[576,256]{1,0:T(8,128)(2,1)S(1)}, bf16[576,256]{1,0:T(8,128)(2,1)S(1)}, u32[]{:S(2)}, u32[]{:S(2)}) collective-permute-start(bf16[576,256]{1,0:T(8,128)(2,1)S(1)} %get-tuple-element.57), channel_id=1, source_target_pairs={{0,3},{1,0},{2,1},{3,2},{4,7},{5,4},{6,5},{7,6},{8,11},{9,8},{10,9... | collective-permute-start | bytes 884744 | tf_op jit(solution)/shard_map/ppermute | solution.py:43
  26.9 5.4 %collective-permute-start.11 = (bf16[128,576]{1,0:T(8,128)(2,1)S(1)}, bf16[128,576]{1,0:T(8,128)(2,1)S(1)}, u32[]{:S(2)}, u32[]{:S(2)}) collective-permute-start(bf16[128,576]{1,0:T(8,128)(2,1)S(1)} %pad_maximum_fusion.1), channel_id=1, source_target_pairs={{0,8},{8,0},{16,24},{24,16},{32,40},{40,32},{48,56},{56,48},{1,9},... | collective-permute-start | bytes 442376 | tf_op jit(solution)/shard_map/ppermute | solution.py:55
  35.2 6.0 %collective-permute-start.12 = (bf16[576,512]{1,0:T(8,128)(2,1)S(1)}, bf16[576,512]{1,0:T(8,128)(2,1)S(1)}, u32[]{:S(2)}, u32[]{:S(2)}) collective-permute-start(bf16[576,512]{1,0:T(8,128)(2,1)S(1)} %shard_map.49.refs_0_), channel_id=1, source_target_pairs={{0,4},{4,0},{1,5},{5,1},{2,6},{6,2},{3,7},{7,3},{8,12},{12,8},{9,1... | collective-permute-start | bytes 1769480 | tf_op jit(solution)/shard_map/ppermute | solution.py:47
  35.3 16.2 %collective-permute-start.9 = (bf16[576,512]{1,0:T(8,128)(2,1)S(1)}, bf16[576,512]{1,0:T(8,128)(2,1)S(1)}, u32[]{:S(2)}, u32[]{:S(2)}) collective-permute-start(bf16[576,512]{1,0:T(8,128)(2,1)S(1)} %shard_map.49.refs_0_), channel_id=1, source_target_pairs={{0,3},{1,0},{2,1},{3,2},{4,7},{5,4},{6,5},{7,6},{8,11},{9,8},{10,9... | collective-permute-start | bytes 1769480 | tf_op jit(solution)/shard_map/ppermute | solution.py:43
  38.3 16.6 %collective-permute-start.8 = (bf16[576,512]{1,0:T(8,128)(2,1)S(1)}, bf16[576,512]{1,0:T(8,128)(2,1)S(1)}, u32[]{:S(2)}, u32[]{:S(2)}) collective-permute-start(bf16[576,512]{1,0:T(8,128)(2,1)S(1)} %shard_map.49.refs_0_), channel_id=1, source_target_pairs={{0,1},{1,2},{2,3},{3,0},{4,5},{5,6},{6,7},{7,4},{8,9},{9,10},{10,1... | collective-permute-start | bytes 1769480 | tf_op jit(solution)/shard_map/ppermute | solution.py:43
  38.3 18.9 %collective-permute-start.17 = (bf16[256,576]{1,0:T(8,128)(2,1)S(1)}, bf16[256,576]{1,0:T(8,128)(2,1)S(1)}, u32[]{:S(2)}, u32[]{:S(2)}) collective-permute-start(bf16[256,576]{1,0:T(8,128)(2,1)S(1)} %pad_maximum_fusion.q_ref), channel_id=1, source_target_pairs={{0,192},{64,128},{128,64},{192,0},{1,193},{65,129},{129,65},{193,1... | collective-permute-start | bytes 884744 | tf_op jit(solution)/shard_map/ppermute | solution.py:51
  38.8 18.5 %collective-permute-start.16 = (bf16[256,576]{1,0:T(8,128)(2,1)S(1)}, bf16[256,576]{1,0:T(8,128)(2,1)S(1)}, u32[]{:S(2)}, u32[]{:S(2)}) collective-permute-start(bf16[256,576]{1,0:T(8,128)(2,1)S(1)} %pad_maximum_fusion.q_ref), channel_id=1, source_target_pairs={{0,128},{64,192},{128,0},{192,64},{1,129},{65,193},{129,1},{193,65... | collective-permute-start | bytes 884744 | tf_op jit(solution)/shard_map/ppermute | solution.py:51
  41.2 16.5 %collective-permute-start.15 = (bf16[256,576]{1,0:T(8,128)(2,1)S(1)}, bf16[256,576]{1,0:T(8,128)(2,1)S(1)}, u32[]{:S(2)}, u32[]{:S(2)}) collective-permute-start(bf16[256,576]{1,0:T(8,128)(2,1)S(1)} %pad_maximum_fusion.q_ref), channel_id=1, source_target_pairs={{0,64},{64,0},{128,192},{192,128},{1,65},{65,1},{129,193},{193,129... | collective-permute-start | bytes 884744 | tf_op jit(solution)/shard_map/ppermute | solution.py:51
  55.0 8.5 %collective-permute-start.14 = (bf16[576,256]{1,0:T(8,128)(2,1)S(1)}, bf16[576,256]{1,0:T(8,128)(2,1)S(1)}, u32[]{:S(2)}, u32[]{:S(2)}) collective-permute-start(bf16[576,256]{1,0:T(8,128)(2,1)S(1)} %slice.7), channel_id=1, source_target_pairs={{0,3},{1,0},{2,1},{3,2},{4,7},{5,4},{6,5},{7,6},{8,11},{9,8},{10,9... | collective-permute-start | bytes 884744 | tf_op jit(solution)/shard_map/ppermute | solution.py:43
  55.5 9.5 %collective-permute-start.13 = (bf16[576,256]{1,0:T(8,128)(2,1)S(1)}, bf16[576,256]{1,0:T(8,128)(2,1)S(1)}, u32[]{:S(2)}, u32[]{:S(2)}) collective-permute-start(bf16[576,256]{1,0:T(8,128)(2,1)S(1)} %slice.6), channel_id=1, source_target_pairs={{0,1},{1,2},{2,3},{3,0},{4,5},{5,6},{6,7},{7,4},{8,9},{9,10},{10,1... | collective-permute-start | bytes 884744 | tf_op jit(solution)/shard_map/ppermute | solution.py:43
  57.3 9.7 %collective-permute-start.18 = (bf16[576,512]{1,0:T(8,128)(2,1)S(1)}, bf16[576,512]{1,0:T(8,128)(2,1)S(1)}, u32[]{:S(2)}, u32[]{:S(2)}) collective-permute-start(bf16[576,512]{1,0:T(8,128)(2,1)S(1)} %collective-permute-done.8.refs_1_), channel_id=1, source_target_pairs={{0,4},{4,0},{1,5},{5,1},{2,6},{6,2},{3,7},{7,3},{8,12},{12,8},{9,1... | collective-permute-start | bytes 1769480 | tf_op jit(solution)/shard_map/ppermute | solution.py:47
  57.3 9.7 %collective-permute-start.19 = (bf16[576,512]{1,0:T(8,128)(2,1)S(1)}, bf16[576,512]{1,0:T(8,128)(2,1)S(1)}, u32[]{:S(2)}, u32[]{:S(2)}) collective-permute-start(bf16[576,512]{1,0:T(8,128)(2,1)S(1)} %collective-permute-done.9.refs_2_), channel_id=1, source_target_pairs={{0,4},{4,0},{1,5},{5,1},{2,6},{6,2},{3,7},{7,3},{8,12},{12,8},{9,1... | collective-permute-start | bytes 1769480 | tf_op jit(solution)/shard_map/ppermute | solution.py:47
  65.0 1.6 %collective-permute-start.20 = (bf16[576,256]{1,0:T(8,128)(2,1)S(1)}, bf16[576,256]{1,0:T(8,128)(2,1)S(1)}, u32[]{:S(2)}, u32[]{:S(2)}) collective-permute-start(bf16[576,256]{1,0:T(8,128)(2,1)S(1)} %collective-permute-done.13.refs_3_), channel_id=1, source_target_pairs={{0,4},{4,0},{1,5},{5,1},{2,6},{6,2},{3,7},{7,3},{8,12},{12,8},{9,1... | collective-permute-start | bytes 884744 | tf_op jit(solution)/shard_map/ppermute | solution.py:47
  65.0 2.0 %collective-permute-start.21 = (bf16[576,256]{1,0:T(8,128)(2,1)S(1)}, bf16[576,256]{1,0:T(8,128)(2,1)S(1)}, u32[]{:S(2)}, u32[]{:S(2)}) collective-permute-start(bf16[576,256]{1,0:T(8,128)(2,1)S(1)} %collective-permute-done.14.refs_4_), channel_id=1, source_target_pairs={{0,4},{4,0},{1,5},{5,1},{2,6},{6,2},{3,7},{7,3},{8,12},{12,8},{9,1... | collective-permute-start | bytes 884744 | tf_op jit(solution)/shard_map/ppermute | solution.py:47
  71.3 10.1 %collective-permute-start.22 = (bf16[264,512]{1,0:T(8,128)(2,1)S(1)}, bf16[264,512]{1,0:T(8,128)(2,1)S(1)}, u32[]{:S(2)}, u32[]{:S(2)}) collective-permute-start(bf16[264,512]{1,0:T(8,128)(2,1)S(1)} %shard_map.50), channel_id=1, source_target_pairs={{0,128},{64,192},{128,0},{192,64},{1,129},{65,193},{129,1},{193,65... | collective-permute-start | bytes 811016 | tf_op jit(solution)/shard_map/ppermute | solution.py:51
  77.1 9.2 %collective-permute-start.23 = (bf16[264,512]{1,0:T(8,128)(2,1)S(1)}, bf16[264,512]{1,0:T(8,128)(2,1)S(1)}, u32[]{:S(2)}, u32[]{:S(2)}) collective-permute-start(bf16[264,512]{1,0:T(8,128)(2,1)S(1)} %shard_map.51), channel_id=1, source_target_pairs={{0,64},{64,0},{128,192},{192,128},{1,65},{65,1},{129,193},{193,129... | collective-permute-start | bytes 811016 | tf_op jit(solution)/shard_map/ppermute | solution.py:51
  85.7 9.0 %collective-permute-start.24 = (bf16[264,512]{1,0:T(8,128)(2,1)S(1)}, bf16[264,512]{1,0:T(8,128)(2,1)S(1)}, u32[]{:S(2)}, u32[]{:S(2)}) collective-permute-start(bf16[264,512]{1,0:T(8,128)(2,1)S(1)} %shard_map.52), channel_id=1, source_target_pairs={{0,192},{64,128},{128,64},{192,0},{1,193},{65,129},{129,65},{193,1... | collective-permute-start | bytes 811016 | tf_op jit(solution)/shard_map/ppermute | solution.py:51
  95.3 12.2 %collective-permute-start.25 = (bf16[32,640]{1,0:T(8,128)(2,1)S(1)}, bf16[32,640]{1,0:T(8,128)(2,1)S(1)}, u32[]{:S(2)}, u32[]{:S(2)}) collective-permute-start(bf16[32,640]{1,0:T(8,128)(2,1)S(1)} %get-tuple-element.84), channel_id=1, source_target_pairs={{0,32},{8,40},{16,48},{24,56},{32,0},{40,8},{48,16},{56,24},{1,33}... | collective-permute-start | bytes 122888 | tf_op jit(solution)/shard_map/ppermute | solution.py:55
  100.4 9.1 %collective-permute-start.26 = (bf16[32,640]{1,0:T(8,128)(2,1)S(1)}, bf16[32,640]{1,0:T(8,128)(2,1)S(1)}, u32[]{:S(2)}, u32[]{:S(2)}) collective-permute-start(bf16[32,640]{1,0:T(8,128)(2,1)S(1)} %get-tuple-element.85), channel_id=1, source_target_pairs={{0,16},{8,24},{16,0},{24,8},{32,48},{40,56},{48,32},{56,40},{1,17}... | collective-permute-start | bytes 122888 | tf_op jit(solution)/shard_map/ppermute | solution.py:55
  101.9 7.7 %collective-permute-start.27 = (bf16[32,640]{1,0:T(8,128)(2,1)S(1)}, bf16[32,640]{1,0:T(8,128)(2,1)S(1)}, u32[]{:S(2)}, u32[]{:S(2)}) collective-permute-start(bf16[32,640]{1,0:T(8,128)(2,1)S(1)} %get-tuple-element.86), channel_id=1, source_target_pairs={{0,48},{8,56},{16,32},{24,40},{32,16},{40,24},{48,0},{56,8},{1,49}... | collective-permute-start | bytes 122888 | tf_op jit(solution)/shard_map/ppermute | solution.py:55
  101.9 7.7 %collective-permute-start.28 = (bf16[32,640]{1,0:T(8,128)(2,1)S(1)}, bf16[32,640]{1,0:T(8,128)(2,1)S(1)}, u32[]{:S(2)}, u32[]{:S(2)}) collective-permute-start(bf16[32,640]{1,0:T(8,128)(2,1)S(1)} %get-tuple-element.87), channel_id=1, source_target_pairs={{0,8},{8,0},{16,24},{24,16},{32,40},{40,32},{48,56},{56,48},{1,9},... | collective-permute-start | bytes 122888 | tf_op jit(solution)/shard_map/ppermute | solution.py:55
  103.5 7.1 %collective-permute-start.29 = (bf16[32,640]{1,0:T(8,128)(2,1)S(1)}, bf16[32,640]{1,0:T(8,128)(2,1)S(1)}, u32[]{:S(2)}, u32[]{:S(2)}) collective-permute-start(bf16[32,640]{1,0:T(8,128)(2,1)S(1)} %get-tuple-element.88), channel_id=1, source_target_pairs={{0,40},{8,32},{16,56},{24,48},{32,8},{40,0},{48,24},{56,16},{1,41}... | collective-permute-start | bytes 122888 | tf_op jit(solution)/shard_map/ppermute | solution.py:55
  107.5 5.8 %collective-permute-start.30 = (bf16[32,640]{1,0:T(8,128)(2,1)S(1)}, bf16[32,640]{1,0:T(8,128)(2,1)S(1)}, u32[]{:S(2)}, u32[]{:S(2)}) collective-permute-start(bf16[32,640]{1,0:T(8,128)(2,1)S(1)} %get-tuple-element.89), channel_id=1, source_target_pairs={{0,24},{8,16},{16,8},{24,0},{32,56},{40,48},{48,40},{56,32},{1,25}... | collective-permute-start | bytes 122888 | tf_op jit(solution)/shard_map/ppermute | solution.py:55
  109.6 5.7 %collective-permute-start.31 = (bf16[32,640]{1,0:T(8,128)(2,1)S(1)}, bf16[32,640]{1,0:T(8,128)(2,1)S(1)}, u32[]{:S(2)}, u32[]{:S(2)}) collective-permute-start(bf16[32,640]{1,0:T(8,128)(2,1)S(1)} %get-tuple-element.90), channel_id=1, source_target_pairs={{0,56},{8,48},{16,40},{24,32},{32,24},{40,16},{48,8},{56,0},{1,57}... | collective-permute-start | bytes 122888 | tf_op jit(solution)/shard_map/ppermute | solution.py:55
  (4 other events, 70.7 us)

commit v8 on v7

--- a/solution.py
+++ b/solution.py
@@ -324,15 +324,13 @@
         [SMEM] + [VMEM] * 5,
         [hot_ids, from_left_a, from_left_b, from_right_a, from_right_b, mine],
     )
-    own_quarter, near = lax.optimization_barrier((mine, near))
     asked = [near] + [cross_x(near, bits) for bits in range(1, N_X)]
 
-    of_left, of_right, swapped = shift_rep(mine, 1), shift_rep(mine, -1), swap_core(own_quarter)
-    of_left, of_right, swapped = lax.optimization_barrier((of_left, of_right, swapped))
+    of_left, of_right = shift_rep(mine, 1), shift_rep(mine, -1)
     far_a, far_b = shift_rep(of_left[:, :PAIR], 1), shift_rep(of_right[:, PAIR:], -1)
     far_a, far_b, *asked = lax.optimization_barrier((far_a, far_b, *asked))
     keys = [mine, of_left, of_right, far_a, far_b]
-    keys = keys + [swapped] + [swap_core(k) for k in keys[1:]]
+    keys = keys + [swap_core(k) for k in keys]
 
     rows = near.shape[0]
     parts = []

time: 116 us -> 108 us (0.931)
  waiting for transfers between devices: 42.6 us -> 35.8 us
  starting transfers between devices: 48.4 us -> 47.2 us
    ppermute x10, waiting for transfers between devices: 21.8 us -> 17.8 us  [shift_rep(): return lax.ppermute(a, 'rep', [(i, (i + by) % N_REP) for i in range(N_REP)])]
    ppermute x10, waiting for transfers between devices: 11.1 us -> 7.34 us  [cross_z(): return lax.ppermute(a, 'z', [(i, i ^ bits) for i in range(N_Z)])]
    ppermute x10, starting transfers between devices: 25.6 us -> 22.5 us  [cross_z(): return lax.ppermute(a, 'z', [(i, i ^ bits) for i in range(N_Z)])]
    ppermute x10, starting transfers between devices: 15.2 us -> 17 us  [shift_rep(): return lax.ppermute(a, 'rep', [(i, (i + by) % N_REP) for i in range(N_REP)])]
  transfers between devices with their start and end apart: 32 -> 32, of which waited for: 14 -> 13; matrix products, arithmetic and copies ran while one was open for 0% -> 0% of each run, Pallas kernels for 14% -> 15%
where the time goes in v8:
time: 108 us
  starting transfers between devices  47.2 us (44%)
  waiting for transfers between devices  35.8 us (33%)
  Pallas kernels  23.9 us (22%)
    pallas_call x10, Pallas kernels, call(): pl.pallas_call(kernel, out_shape=tuple((jax.ShapeDtypeStruct(*o) for o in...  23.9 us
    ppermute x10, starting transfers between devices, cross_z(): return lax.ppermute(a, 'z', [(i, i ^ bits) for i in range(N_Z)])  22.5 us
    ppermute x10, waiting for transfers between devices, shift_rep(): return lax.ppermute(a, 'rep', [(i, (i + by) % N_REP) for i in range(N_REP)])  17.8 us
    ppermute x10, starting transfers between devices, shift_rep(): return lax.ppermute(a, 'rep', [(i, (i + by) % N_REP) for i in range(N_REP)])  17 us
    ppermute x6, waiting for transfers between devices, cross_x(): return lax.ppermute(a, 'x', [(i, i ^ bits) for i in range(N_X)])  9.11 us
    ppermute x10, waiting for transfers between devices, cross_z(): return lax.ppermute(a, 'z', [(i, i ^ bits) for i in range(N_Z)])  7.34 us
    ppermute x6, starting transfers between devices, cross_x(): return lax.ppermute(a, 'x', [(i, i ^ bits) for i in range(N_X)])  6.6 us
  transfers between devices with their start and end apart: 32, of which 13 were waited for; matrix products, arithmetic and copies ran while one was open for 0% of the time, Pallas kernels for 15%

profile of v8, /device:TPU:6, one launch (start us, length us, event | category | flops | bytes accessed | tf_op | source)
XLA Modules:
  0.0 108.0 jit_solution(875681732234454527)
XLA Ops:
  0.7 1.7 %shard_map.46 = (bf16[576,256]{1,0:T(8,128)(2,1)S(1)}, bf16[576,256]{1,0:T(8,128)(2,1)S(1)}) custom-call(s32[2]{0:T(128)S(1)} %copy-done, bf16[576,4096]{1,0:T(8,128)(2,1)} %bitcast.4), custom_call_target="tpu_custom_call" | custom-call | tf_op jit(solution)/shard_map/pallas_call | solution.py:275
  2.5 1.7 %collective-permute-start = (bf16[576,256]{1,0:T(8,128)(2,1)S(1)}, bf16[576,256]{1,0:T(8,128)(2,1)S(1)}, u32[]{:S(2)}, u32[]{:S(2)}) collective-permute-start(bf16[576,256]{1,0:T(8,128)(2,1)S(1)} %get-tuple-element.43), channel_id=1, source_target_pairs={{0,1},{1,2},{2,3},{3,0},{4,5},{5,6},{6,7},{7,4},{8,9},{9,10},{10,1... | collective-permute-start | bytes 884744 | tf_op jit(solution)/shard_map/ppermute | solution.py:43
  4.1 1.7 %collective-permute-start.1 = (bf16[576,256]{1,0:T(8,128)(2,1)S(1)}, bf16[576,256]{1,0:T(8,128)(2,1)S(1)}, u32[]{:S(2)}, u32[]{:S(2)}) collective-permute-start(bf16[576,256]{1,0:T(8,128)(2,1)S(1)} %get-tuple-element.44), channel_id=1, source_target_pairs={{0,3},{1,0},{2,1},{3,2},{4,7},{5,4},{6,5},{7,6},{8,11},{9,8},{10,9... | collective-permute-start | bytes 884744 | tf_op jit(solution)/shard_map/ppermute | solution.py:43
  5.9 7.3 %collective-permute-start.2 = (bf16[32,576]{1,0:T(8,128)(2,1)S(1)}, bf16[32,576]{1,0:T(8,128)(2,1)S(1)}, u32[]{:S(2)}, u32[]{:S(2)}) collective-permute-start(bf16[32,576]{1,0:T(8,128)(2,1)S(1)} %bitcast.6), channel_id=1, source_target_pairs={{0,32},{8,40},{16,48},{24,56},{32,0},{40,8},{48,16},{56,24},{1,33}... | collective-permute-start | bytes 110600 | tf_op jit(solution)/shard_map/ppermute | solution.py:55
  13.2 2.2 %shard_map.47 = (bf16[576,256]{1,0:T(8,128)(2,1)S(1)}, bf16[576,256]{1,0:T(8,128)(2,1)S(1)}, bf16[576,256]{1,0:T(8,128)(2,1)S(1)}, bf16[576,256]{1,0:T(8,128)(2,1)S(1)}, bf16[576,512]{1,0:T(8,128)(2,1)S(1)}) custom-call(s32[2]{0:T(128)S(1)} %copy-done.1, bf16[576,4096]{1,0:T(8,128)(2,1)} %bitcast.5), custom_call_target="tpu_custom_call" | custom-call | tf_op jit(solution)/shard_map/pallas_call | solution.py:275
  15.9 2.9 %collective-permute-start.6 = (bf16[576,256]{1,0:T(8,128)(2,1)S(1)}, bf16[576,256]{1,0:T(8,128)(2,1)S(1)}, u32[]{:S(2)}, u32[]{:S(2)}) collective-permute-start(bf16[576,256]{1,0:T(8,128)(2,1)S(1)} %get-tuple-element.51), channel_id=1, source_target_pairs={{0,3},{1,0},{2,1},{3,2},{4,7},{5,4},{6,5},{7,6},{8,11},{9,8},{10,9... | collective-permute-start | bytes 884744 | tf_op jit(solution)/shard_map/ppermute | solution.py:43
  19.6 3.2 %collective-permute-start.7 = (bf16[576,256]{1,0:T(8,128)(2,1)S(1)}, bf16[576,256]{1,0:T(8,128)(2,1)S(1)}, u32[]{:S(2)}, u32[]{:S(2)}) collective-permute-start(bf16[576,256]{1,0:T(8,128)(2,1)S(1)} %get-tuple-element.52), channel_id=1, source_target_pairs={{0,3},{1,0},{2,1},{3,2},{4,7},{5,4},{6,5},{7,6},{8,11},{9,8},{10,9... | collective-permute-start | bytes 884744 | tf_op jit(solution)/shard_map/ppermute | solution.py:43
  22.8 1.5 %collective-permute-start.12 = (bf16[64,576]{1,0:T(8,128)(2,1)S(1)}, bf16[64,576]{1,0:T(8,128)(2,1)S(1)}, u32[]{:S(2)}, u32[]{:S(2)}) collective-permute-start(bf16[64,576]{1,0:T(8,128)(2,1)S(1)} %pad_maximum_fusion.1), channel_id=1, source_target_pairs={{0,16},{8,24},{16,0},{24,8},{32,48},{40,56},{48,32},{56,40},{1,17}... | collective-permute-start | bytes 221192 | tf_op jit(solution)/shard_map/ppermute | solution.py:55
  24.3 4.9 %collective-permute-done.12 = bf16[64,576]{1,0:T(8,128)(2,1)S(1)} collective-permute-done((bf16[64,576]{1,0:T(8,128)(2,1)S(1)}, bf16[64,576]{1,0:T(8,128)(2,1)S(1)}, u32[]{:S(2)}, u32[]{:S(2)}) %collective-permute-start.12) | collective-permute-done | bytes 73760 | tf_op jit(solution)/shard_map/ppermute | solution.py:55
  29.4 3.1 %collective-permute-done.4.left_a = bf16[576,256]{1,0:T(8,128)(2,1)S(1)} collective-permute-done((bf16[576,256]{1,0:T(8,128)(2,1)S(1)}, bf16[576,256]{1,0:T(8,128)(2,1)S(1)}, u32[]{:S(2)}, u32[]{:S(2)}) %collective-permute-start.4) | collective-permute-done | bytes 294944 | tf_op jit(solution)/shard_map/ppermute | solution.py:43
  33.2 3.0 %collective-permute-start.10 = (bf16[576,512]{1,0:T(8,128)(2,1)S(1)}, bf16[576,512]{1,0:T(8,128)(2,1)S(1)}, u32[]{:S(2)}, u32[]{:S(2)}) collective-permute-start(bf16[576,512]{1,0:T(8,128)(2,1)S(1)} %shard_map.49.refs_0_), channel_id=1, source_target_pairs={{0,3},{1,0},{2,1},{3,2},{4,7},{5,4},{6,5},{7,6},{8,11},{9,8},{10,9... | collective-permute-start | bytes 1769480 | tf_op jit(solution)/shard_map/ppermute | solution.py:43
  36.9 2.4 %collective-permute-start.15 = (bf16[256,576]{1,0:T(8,128)(2,1)S(1)}, bf16[256,576]{1,0:T(8,128)(2,1)S(1)}, u32[]{:S(2)}, u32[]{:S(2)}) collective-permute-start(bf16[256,576]{1,0:T(8,128)(2,1)S(1)} %constant_dynamic-update-slice_fusion.q_ref), channel_id=1, source_target_pairs={{0,128},{64,192},{128,0},{192,64},{1,129},{65,193},{129,1},{193,65... | collective-permute-start | bytes 884744 | tf_op jit(solution)/shard_map/ppermute | solution.py:51
  39.3 1.2 %collective-permute-start.14 = (bf16[256,576]{1,0:T(8,128)(2,1)S(1)}, bf16[256,576]{1,0:T(8,128)(2,1)S(1)}, u32[]{:S(2)}, u32[]{:S(2)}) collective-permute-start(bf16[256,576]{1,0:T(8,128)(2,1)S(1)} %constant_dynamic-update-slice_fusion.q_ref), channel_id=1, source_target_pairs={{0,64},{64,0},{128,192},{192,128},{1,65},{65,1},{129,193},{193,129... | collective-permute-start | bytes 884744 | tf_op jit(solution)/shard_map/ppermute | solution.py:51
  40.5 7.9 %collective-permute-done.10.refs_2_ = bf16[576,512]{1,0:T(8,128)(2,1)S(1)} collective-permute-done((bf16[576,512]{1,0:T(8,128)(2,1)S(1)}, bf16[576,512]{1,0:T(8,128)(2,1)S(1)}, u32[]{:S(2)}, u32[]{:S(2)}) %collective-permute-start.10) | collective-permute-done | bytes 589856 | tf_op jit(solution)/shard_map/ppermute | solution.py:43
  48.4 3.8 %collective-permute-start.11 = (bf16[576,256]{1,0:T(8,128)(2,1)S(1)}, bf16[576,256]{1,0:T(8,128)(2,1)S(1)}, u32[]{:S(2)}, u32[]{:S(2)}) collective-permute-start(bf16[576,256]{1,0:T(8,128)(2,1)S(1)} %slice.9), channel_id=1, source_target_pairs={{0,3},{1,0},{2,1},{3,2},{4,7},{5,4},{6,5},{7,6},{8,11},{9,8},{10,9... | collective-permute-start | bytes 884744 | tf_op jit(solution)/shard_map/ppermute | solution.py:43
  54.0 3.1 %collective-permute-done.11.refs_4_ = bf16[576,256]{1,0:T(8,128)(2,1)S(1)} collective-permute-done((bf16[576,256]{1,0:T(8,128)(2,1)S(1)}, bf16[576,256]{1,0:T(8,128)(2,1)S(1)}, u32[]{:S(2)}, u32[]{:S(2)}) %collective-permute-start.11) | collective-permute-done | bytes 294944 | tf_op jit(solution)/shard_map/ppermute | solution.py:43
  57.1 3.7 %collective-permute-done.9.refs_3_ = bf16[576,256]{1,0:T(8,128)(2,1)S(1)} collective-permute-done((bf16[576,256]{1,0:T(8,128)(2,1)S(1)}, bf16[576,256]{1,0:T(8,128)(2,1)S(1)}, u32[]{:S(2)}, u32[]{:S(2)}) %collective-permute-start.9) | collective-permute-done | bytes 294944 | tf_op jit(solution)/shard_map/ppermute | solution.py:43
  61.3 1.1 collective-permute-done.20.refs_8_
  62.8 4.3 %shard_map.50 = bf16[264,512]{1,0:T(8,128)(2,1)S(1)} custom-call(bf16[256,576]{1,0:T(8,128)(2,1)S(1)} %collective-permute-done.15.q_ref, s32[16]{0:T(128)S(1)} %copy-done.2, s32[2]{0:T(128)S(1)} %copy-done.1, s32[2]{0:T(128)S(1)} %collective-permute-done.3.hot_other_ref, bf16[576,512]{1,0:T(8,128)(2,1)S(1)} %shard_map.49.refs_0_, ...), custom_call_target="tpu_custom_call" | custom-call | tf_op jit(solution)/shard_map/pallas_call | solution.py:275
  67.1 1.5 %collective-permute-start.22 = (bf16[264,512]{1,0:T(8,128)(2,1)S(1)}, bf16[264,512]{1,0:T(8,128)(2,1)S(1)}, u32[]{:S(2)}, u32[]{:S(2)}) collective-permute-start(bf16[264,512]{1,0:T(8,128)(2,1)S(1)} %shard_map.50), channel_id=1, source_target_pairs={{0,128},{64,192},{128,0},{192,64},{1,129},{65,193},{129,1},{193,65... | collective-permute-start | bytes 811016 | tf_op jit(solution)/shard_map/ppermute | solution.py:51
  68.6 4.3 %shard_map.51 = bf16[264,512]{1,0:T(8,128)(2,1)S(1)} custom-call(bf16[256,576]{1,0:T(8,128)(2,1)S(1)} %collective-permute-done.14.q_ref, s32[16]{0:T(128)S(1)} %copy-done.2, s32[2]{0:T(128)S(1)} %copy-done.1, s32[2]{0:T(128)S(1)} %collective-permute-done.3.hot_other_ref, bf16[576,512]{1,0:T(8,128)(2,1)S(1)} %shard_map.49.refs_0_, ...), custom_call_target="tpu_custom_call" | custom-call | tf_op jit(solution)/shard_map/pallas_call | solution.py:275
  73.2 4.0 %collective-permute-done.22.refs_0_ = bf16[264,512]{1,0:T(8,128)(2,1)S(1)} collective-permute-done((bf16[264,512]{1,0:T(8,128)(2,1)S(1)}, bf16[264,512]{1,0:T(8,128)(2,1)S(1)}, u32[]{:S(2)}, u32[]{:S(2)}) %collective-permute-start.22) | collective-permute-done | bytes 270368 | tf_op jit(solution)/shard_map/ppermute | solution.py:51
  77.2 4.3 %shard_map.52 = bf16[264,512]{1,0:T(8,128)(2,1)S(1)} custom-call(bf16[256,576]{1,0:T(8,128)(2,1)S(1)} %collective-permute-done.16.q_ref, s32[16]{0:T(128)S(1)} %copy-done.2, s32[2]{0:T(128)S(1)} %copy-done.1, s32[2]{0:T(128)S(1)} %collective-permute-done.3.hot_other_ref, bf16[576,512]{1,0:T(8,128)(2,1)S(1)} %shard_map.49.refs_0_, ...), custom_call_target="tpu_custom_call" | custom-call | tf_op jit(solution)/shard_map/pallas_call | solution.py:275
  82.1 4.3 %shard_map.53.refs_3_ = bf16[264,512]{1,0:T(8,128)(2,1)S(1)} custom-call(bf16[256,576]{1,0:T(8,128)(2,1)S(1)} %constant_dynamic-update-slice_fusion.q_ref, s32[16]{0:T(128)S(1)} %copy-done.2, s32[2]{0:T(128)S(1)} %copy-done.1, s32[2]{0:T(128)S(1)} %collective-permute-done.3.hot_other_ref, bf16[576,512]{1,0:T(8,128)(2,1)S(1)} %shard_map.49.refs_0_, ...), custom_call_target="tpu_custom_call" | custom-call | tf_op jit(solution)/shard_map/pallas_call | solution.py:275
  86.3 4.1 %collective-permute-done.24.refs_2_ = bf16[264,512]{1,0:T(8,128)(2,1)S(1)} collective-permute-done((bf16[264,512]{1,0:T(8,128)(2,1)S(1)}, bf16[264,512]{1,0:T(8,128)(2,1)S(1)}, u32[]{:S(2)}, u32[]{:S(2)}) %collective-permute-start.24) | collective-permute-done | bytes 270368 | tf_op jit(solution)/shard_map/ppermute | solution.py:51
  91.1 1.6 %collective-permute-start.26 = (bf16[32,640]{1,0:T(8,128)(2,1)S(1)}, bf16[32,640]{1,0:T(8,128)(2,1)S(1)}, u32[]{:S(2)}, u32[]{:S(2)}) collective-permute-start(bf16[32,640]{1,0:T(8,128)(2,1)S(1)} %get-tuple-element.75), channel_id=1, source_target_pairs={{0,16},{8,24},{16,0},{24,8},{32,48},{40,56},{48,32},{56,40},{1,17}... | collective-permute-start | bytes 122888 | tf_op jit(solution)/shard_map/ppermute | solution.py:55
  92.7 4.9 %collective-permute-start.27 = (bf16[32,640]{1,0:T(8,128)(2,1)S(1)}, bf16[32,640]{1,0:T(8,128)(2,1)S(1)}, u32[]{:S(2)}, u32[]{:S(2)}) collective-permute-start(bf16[32,640]{1,0:T(8,128)(2,1)S(1)} %get-tuple-element.76), channel_id=1, source_target_pairs={{0,48},{8,56},{16,32},{24,40},{32,16},{40,24},{48,0},{56,8},{1,49}... | collective-permute-start | bytes 122888 | tf_op jit(solution)/shard_map/ppermute | solution.py:55
  97.6 1.0 collective-permute-start.28
  99.1 1.9 %collective-permute-start.30 = (bf16[32,640]{1,0:T(8,128)(2,1)S(1)}, bf16[32,640]{1,0:T(8,128)(2,1)S(1)}, u32[]{:S(2)}, u32[]{:S(2)}) collective-permute-start(bf16[32,640]{1,0:T(8,128)(2,1)S(1)} %get-tuple-element.79), channel_id=1, source_target_pairs={{0,24},{8,16},{16,8},{24,0},{32,56},{40,48},{48,40},{56,32},{1,25}... | collective-permute-start | bytes 122888 | tf_op jit(solution)/shard_map/ppermute | solution.py:55
  101.0 3.7 %collective-permute-start.31 = (bf16[32,640]{1,0:T(8,128)(2,1)S(1)}, bf16[32,640]{1,0:T(8,128)(2,1)S(1)}, u32[]{:S(2)}, u32[]{:S(2)}) collective-permute-start(bf16[32,640]{1,0:T(8,128)(2,1)S(1)} %get-tuple-element.80), channel_id=1, source_target_pairs={{0,56},{8,48},{16,40},{24,32},{32,24},{40,16},{48,8},{56,0},{1,57}... | collective-permute-start | bytes 122888 | tf_op jit(solution)/shard_map/ppermute | solution.py:55
  104.7 1.0 collective-permute-done.29.refs_5_
  105.6 1.4 %collective-permute-done.31.refs_7_ = bf16[32,640]{1,0:T(8,128)(2,1)S(1)} collective-permute-done((bf16[32,640]{1,0:T(8,128)(2,1)S(1)}, bf16[32,640]{1,0:T(8,128)(2,1)S(1)}, u32[]{:S(2)}, u32[]{:S(2)}) %collective-permute-start.31) | collective-permute-done | bytes 40992 | tf_op jit(solution)/shard_map/ppermute | solution.py:55
  (59 shorter events, 9.3 us)
Async XLA Ops:
  2.5 16.3 %collective-permute-start = (bf16[576,256]{1,0:T(8,128)(2,1)S(1)}, bf16[576,256]{1,0:T(8,128)(2,1)S(1)}, u32[]{:S(2)}, u32[]{:S(2)}) collective-permute-start(bf16[576,256]{1,0:T(8,128)(2,1)S(1)} %get-tuple-element.43), channel_id=1, source_target_pairs={{0,1},{1,2},{2,3},{3,0},{4,5},{5,6},{6,7},{7,4},{8,9},{9,10},{10,1... | collective-permute-start | bytes 884744 | tf_op jit(solution)/shard_map/ppermute | solution.py:43
  4.1 14.7 %collective-permute-start.1 = (bf16[576,256]{1,0:T(8,128)(2,1)S(1)}, bf16[576,256]{1,0:T(8,128)(2,1)S(1)}, u32[]{:S(2)}, u32[]{:S(2)}) collective-permute-start(bf16[576,256]{1,0:T(8,128)(2,1)S(1)} %get-tuple-element.44), channel_id=1, source_target_pairs={{0,3},{1,0},{2,1},{3,2},{4,7},{5,4},{6,5},{7,6},{8,11},{9,8},{10,9... | collective-permute-start | bytes 884744 | tf_op jit(solution)/shard_map/ppermute | solution.py:43
  5.9 10.0 %collective-permute-start.2 = (bf16[32,576]{1,0:T(8,128)(2,1)S(1)}, bf16[32,576]{1,0:T(8,128)(2,1)S(1)}, u32[]{:S(2)}, u32[]{:S(2)}) collective-permute-start(bf16[32,576]{1,0:T(8,128)(2,1)S(1)} %bitcast.6), channel_id=1, source_target_pairs={{0,32},{8,40},{16,48},{24,56},{32,0},{40,8},{48,16},{56,24},{1,33}... | collective-permute-start | bytes 110600 | tf_op jit(solution)/shard_map/ppermute | solution.py:55
  13.2 5.6 %collective-permute-start.3 = (s32[2]{0:T(128)S(1)}, s32[2]{0:T(128)S(1)}, u32[]{:S(2)}, u32[]{:S(2)}) collective-permute-start(s32[2]{0:T(128)S(1)} %copy-done.1), channel_id=1, source_target_pairs={{0,4},{4,0},{1,5},{5,1},{2,6},{6,2},{3,7},{7,3},{8,12},{12,8},{9,1... | collective-permute-start | bytes 32 | tf_op jit(solution)/shard_map/ppermute | solution.py:47
  15.4 13.9 %collective-permute-start.5 = (bf16[576,256]{1,0:T(8,128)(2,1)S(1)}, bf16[576,256]{1,0:T(8,128)(2,1)S(1)}, u32[]{:S(2)}, u32[]{:S(2)}) collective-permute-start(bf16[576,256]{1,0:T(8,128)(2,1)S(1)} %get-tuple-element.50), channel_id=1, source_target_pairs={{0,1},{1,2},{2,3},{3,0},{4,5},{5,6},{6,7},{7,4},{8,9},{9,10},{10,1... | collective-permute-start | bytes 884744 | tf_op jit(solution)/shard_map/ppermute | solution.py:43
  15.9 13.5 %collective-permute-start.6 = (bf16[576,256]{1,0:T(8,128)(2,1)S(1)}, bf16[576,256]{1,0:T(8,128)(2,1)S(1)}, u32[]{:S(2)}, u32[]{:S(2)}) collective-permute-start(bf16[576,256]{1,0:T(8,128)(2,1)S(1)} %get-tuple-element.51), channel_id=1, source_target_pairs={{0,3},{1,0},{2,1},{3,2},{4,7},{5,4},{6,5},{7,6},{8,11},{9,8},{10,9... | collective-permute-start | bytes 884744 | tf_op jit(solution)/shard_map/ppermute | solution.py:43
  19.5 13.0 %collective-permute-start.4 = (bf16[576,256]{1,0:T(8,128)(2,1)S(1)}, bf16[576,256]{1,0:T(8,128)(2,1)S(1)}, u32[]{:S(2)}, u32[]{:S(2)}) collective-permute-start(bf16[576,256]{1,0:T(8,128)(2,1)S(1)} %get-tuple-element.49), channel_id=1, source_target_pairs={{0,1},{1,2},{2,3},{3,0},{4,5},{5,6},{6,7},{7,4},{8,9},{9,10},{10,1... | collective-permute-start | bytes 884744 | tf_op jit(solution)/shard_map/ppermute | solution.py:43
  19.6 12.9 %collective-permute-start.7 = (bf16[576,256]{1,0:T(8,128)(2,1)S(1)}, bf16[576,256]{1,0:T(8,128)(2,1)S(1)}, u32[]{:S(2)}, u32[]{:S(2)}) collective-permute-start(bf16[576,256]{1,0:T(8,128)(2,1)S(1)} %get-tuple-element.52), channel_id=1, source_target_pairs={{0,3},{1,0},{2,1},{3,2},{4,7},{5,4},{6,5},{7,6},{8,11},{9,8},{10,9... | collective-permute-start | bytes 884744 | tf_op jit(solution)/shard_map/ppermute | solution.py:43
  22.8 6.4 %collective-permute-start.12 = (bf16[64,576]{1,0:T(8,128)(2,1)S(1)}, bf16[64,576]{1,0:T(8,128)(2,1)S(1)}, u32[]{:S(2)}, u32[]{:S(2)}) collective-permute-start(bf16[64,576]{1,0:T(8,128)(2,1)S(1)} %pad_maximum_fusion.1), channel_id=1, source_target_pairs={{0,16},{8,24},{16,0},{24,8},{32,48},{40,56},{48,32},{56,40},{1,17}... | collective-permute-start | bytes 221192 | tf_op jit(solution)/shard_map/ppermute | solution.py:55
  29.2 7.0 %collective-permute-start.13 = (bf16[128,576]{1,0:T(8,128)(2,1)S(1)}, bf16[128,576]{1,0:T(8,128)(2,1)S(1)}, u32[]{:S(2)}, u32[]{:S(2)}) collective-permute-start(bf16[128,576]{1,0:T(8,128)(2,1)S(1)} %pad_maximum_fusion), channel_id=1, source_target_pairs={{0,8},{8,0},{16,24},{24,16},{32,40},{40,32},{48,56},{56,48},{1,9},... | collective-permute-start | bytes 442376 | tf_op jit(solution)/shard_map/ppermute | solution.py:55
  33.2 15.2 %collective-permute-start.10 = (bf16[576,512]{1,0:T(8,128)(2,1)S(1)}, bf16[576,512]{1,0:T(8,128)(2,1)S(1)}, u32[]{:S(2)}, u32[]{:S(2)}) collective-permute-start(bf16[576,512]{1,0:T(8,128)(2,1)S(1)} %shard_map.49.refs_0_), channel_id=1, source_target_pairs={{0,3},{1,0},{2,1},{3,2},{4,7},{5,4},{6,5},{7,6},{8,11},{9,8},{10,9... | collective-permute-start | bytes 1769480 | tf_op jit(solution)/shard_map/ppermute | solution.py:43
  36.2 16.0 %collective-permute-start.8 = (bf16[576,512]{1,0:T(8,128)(2,1)S(1)}, bf16[576,512]{1,0:T(8,128)(2,1)S(1)}, u32[]{:S(2)}, u32[]{:S(2)}) collective-permute-start(bf16[576,512]{1,0:T(8,128)(2,1)S(1)} %shard_map.49.refs_0_), channel_id=1, source_target_pairs={{0,1},{1,2},{2,3},{3,0},{4,5},{5,6},{6,7},{7,4},{8,9},{9,10},{10,1... | collective-permute-start | bytes 1769480 | tf_op jit(solution)/shard_map/ppermute | solution.py:43
  36.3 17.1 %collective-permute-start.16 = (bf16[256,576]{1,0:T(8,128)(2,1)S(1)}, bf16[256,576]{1,0:T(8,128)(2,1)S(1)}, u32[]{:S(2)}, u32[]{:S(2)}) collective-permute-start(bf16[256,576]{1,0:T(8,128)(2,1)S(1)} %constant_dynamic-update-slice_fusion.q_ref), channel_id=1, source_target_pairs={{0,192},{64,128},{128,64},{192,0},{1,193},{65,129},{129,65},{193,1... | collective-permute-start | bytes 884744 | tf_op jit(solution)/shard_map/ppermute | solution.py:51
  36.9 16.5 %collective-permute-start.15 = (bf16[256,576]{1,0:T(8,128)(2,1)S(1)}, bf16[256,576]{1,0:T(8,128)(2,1)S(1)}, u32[]{:S(2)}, u32[]{:S(2)}) collective-permute-start(bf16[256,576]{1,0:T(8,128)(2,1)S(1)} %constant_dynamic-update-slice_fusion.q_ref), channel_id=1, source_target_pairs={{0,128},{64,192},{128,0},{192,64},{1,129},{65,193},{129,1},{193,65... | collective-permute-start | bytes 884744 | tf_op jit(solution)/shard_map/ppermute | solution.py:51
  39.3 14.7 %collective-permute-start.14 = (bf16[256,576]{1,0:T(8,128)(2,1)S(1)}, bf16[256,576]{1,0:T(8,128)(2,1)S(1)}, u32[]{:S(2)}, u32[]{:S(2)}) collective-permute-start(bf16[256,576]{1,0:T(8,128)(2,1)S(1)} %constant_dynamic-update-slice_fusion.q_ref), channel_id=1, source_target_pairs={{0,64},{64,0},{128,192},{192,128},{1,65},{65,1},{129,193},{193,129... | collective-permute-start | bytes 884744 | tf_op jit(solution)/shard_map/ppermute | solution.py:51
  48.4 8.7 %collective-permute-start.11 = (bf16[576,256]{1,0:T(8,128)(2,1)S(1)}, bf16[576,256]{1,0:T(8,128)(2,1)S(1)}, u32[]{:S(2)}, u32[]{:S(2)}) collective-permute-start(bf16[576,256]{1,0:T(8,128)(2,1)S(1)} %slice.9), channel_id=1, source_target_pairs={{0,3},{1,0},{2,1},{3,2},{4,7},{5,4},{6,5},{7,6},{8,11},{9,8},{10,9... | collective-permute-start | bytes 884744 | tf_op jit(solution)/shard_map/ppermute | solution.py:43
  52.2 8.6 %collective-permute-start.9 = (bf16[576,256]{1,0:T(8,128)(2,1)S(1)}, bf16[576,256]{1,0:T(8,128)(2,1)S(1)}, u32[]{:S(2)}, u32[]{:S(2)}) collective-permute-start(bf16[576,256]{1,0:T(8,128)(2,1)S(1)} %slice.8), channel_id=1, source_target_pairs={{0,1},{1,2},{2,3},{3,0},{4,5},{5,6},{6,7},{7,4},{8,9},{9,10},{10,1... | collective-permute-start | bytes 884744 | tf_op jit(solution)/shard_map/ppermute | solution.py:43
  53.4 7.9 %collective-permute-start.17 = (bf16[576,512]{1,0:T(8,128)(2,1)S(1)}, bf16[576,512]{1,0:T(8,128)(2,1)S(1)}, u32[]{:S(2)}, u32[]{:S(2)}) collective-permute-start(bf16[576,512]{1,0:T(8,128)(2,1)S(1)} %shard_map.49.refs_0_), channel_id=1, source_target_pairs={{0,4},{4,0},{1,5},{5,1},{2,6},{6,2},{3,7},{7,3},{8,12},{12,8},{9,1... | collective-permute-start | bytes 1769480 | tf_op jit(solution)/shard_map/ppermute | solution.py:47
  53.4 7.9 %collective-permute-start.19 = (bf16[576,512]{1,0:T(8,128)(2,1)S(1)}, bf16[576,512]{1,0:T(8,128)(2,1)S(1)}, u32[]{:S(2)}, u32[]{:S(2)}) collective-permute-start(bf16[576,512]{1,0:T(8,128)(2,1)S(1)} %collective-permute-done.10.refs_2_), channel_id=1, source_target_pairs={{0,4},{4,0},{1,5},{5,1},{2,6},{6,2},{3,7},{7,3},{8,12},{12,8},{9,1... | collective-permute-start | bytes 1769480 | tf_op jit(solution)/shard_map/ppermute | solution.py:47
  54.0 8.8 %collective-permute-start.18 = (bf16[576,512]{1,0:T(8,128)(2,1)S(1)}, bf16[576,512]{1,0:T(8,128)(2,1)S(1)}, u32[]{:S(2)}, u32[]{:S(2)}) collective-permute-start(bf16[576,512]{1,0:T(8,128)(2,1)S(1)} %collective-permute-done.8.refs_1_), channel_id=1, source_target_pairs={{0,4},{4,0},{1,5},{5,1},{2,6},{6,2},{3,7},{7,3},{8,12},{12,8},{9,1... | collective-permute-start | bytes 1769480 | tf_op jit(solution)/shard_map/ppermute | solution.py:47
  60.8 1.6 %collective-permute-start.20 = (bf16[576,256]{1,0:T(8,128)(2,1)S(1)}, bf16[576,256]{1,0:T(8,128)(2,1)S(1)}, u32[]{:S(2)}, u32[]{:S(2)}) collective-permute-start(bf16[576,256]{1,0:T(8,128)(2,1)S(1)} %collective-permute-done.9.refs_3_), channel_id=1, source_target_pairs={{0,4},{4,0},{1,5},{5,1},{2,6},{6,2},{3,7},{7,3},{8,12},{12,8},{9,1... | collective-permute-start | bytes 884744 | tf_op jit(solution)/shard_map/ppermute | solution.py:47
  60.8 2.0 %collective-permute-start.21 = (bf16[576,256]{1,0:T(8,128)(2,1)S(1)}, bf16[576,256]{1,0:T(8,128)(2,1)S(1)}, u32[]{:S(2)}, u32[]{:S(2)}) collective-permute-start(bf16[576,256]{1,0:T(8,128)(2,1)S(1)} %collective-permute-done.11.refs_4_), channel_id=1, source_target_pairs={{0,4},{4,0},{1,5},{5,1},{2,6},{6,2},{3,7},{7,3},{8,12},{12,8},{9,1... | collective-permute-start | bytes 884744 | tf_op jit(solution)/shard_map/ppermute | solution.py:47
  67.1 10.1 %collective-permute-start.22 = (bf16[264,512]{1,0:T(8,128)(2,1)S(1)}, bf16[264,512]{1,0:T(8,128)(2,1)S(1)}, u32[]{:S(2)}, u32[]{:S(2)}) collective-permute-start(bf16[264,512]{1,0:T(8,128)(2,1)S(1)} %shard_map.50), channel_id=1, source_target_pairs={{0,128},{64,192},{128,0},{192,64},{1,129},{65,193},{129,1},{193,65... | collective-permute-start | bytes 811016 | tf_op jit(solution)/shard_map/ppermute | solution.py:51
  72.9 9.2 %collective-permute-start.23 = (bf16[264,512]{1,0:T(8,128)(2,1)S(1)}, bf16[264,512]{1,0:T(8,128)(2,1)S(1)}, u32[]{:S(2)}, u32[]{:S(2)}) collective-permute-start(bf16[264,512]{1,0:T(8,128)(2,1)S(1)} %shard_map.51), channel_id=1, source_target_pairs={{0,64},{64,0},{128,192},{192,128},{1,65},{65,1},{129,193},{193,129... | collective-permute-start | bytes 811016 | tf_op jit(solution)/shard_map/ppermute | solution.py:51
  81.5 9.0 %collective-permute-start.24 = (bf16[264,512]{1,0:T(8,128)(2,1)S(1)}, bf16[264,512]{1,0:T(8,128)(2,1)S(1)}, u32[]{:S(2)}, u32[]{:S(2)}) collective-permute-start(bf16[264,512]{1,0:T(8,128)(2,1)S(1)} %shard_map.52), channel_id=1, source_target_pairs={{0,192},{64,128},{128,64},{192,0},{1,193},{65,129},{129,65},{193,1... | collective-permute-start | bytes 811016 | tf_op jit(solution)/shard_map/ppermute | solution.py:51
  91.0 8.1 %collective-permute-start.25 = (bf16[32,640]{1,0:T(8,128)(2,1)S(1)}, bf16[32,640]{1,0:T(8,128)(2,1)S(1)}, u32[]{:S(2)}, u32[]{:S(2)}) collective-permute-start(bf16[32,640]{1,0:T(8,128)(2,1)S(1)} %get-tuple-element.74), channel_id=1, source_target_pairs={{0,32},{8,40},{16,48},{24,56},{32,0},{40,8},{48,16},{56,24},{1,33}... | collective-permute-start | bytes 122888 | tf_op jit(solution)/shard_map/ppermute | solution.py:55
  91.1 9.9 %collective-permute-start.26 = (bf16[32,640]{1,0:T(8,128)(2,1)S(1)}, bf16[32,640]{1,0:T(8,128)(2,1)S(1)}, u32[]{:S(2)}, u32[]{:S(2)}) collective-permute-start(bf16[32,640]{1,0:T(8,128)(2,1)S(1)} %get-tuple-element.75), channel_id=1, source_target_pairs={{0,16},{8,24},{16,0},{24,8},{32,48},{40,56},{48,32},{56,40},{1,17}... | collective-permute-start | bytes 122888 | tf_op jit(solution)/shard_map/ppermute | solution.py:55
  92.7 12.0 %collective-permute-start.27 = (bf16[32,640]{1,0:T(8,128)(2,1)S(1)}, bf16[32,640]{1,0:T(8,128)(2,1)S(1)}, u32[]{:S(2)}, u32[]{:S(2)}) collective-permute-start(bf16[32,640]{1,0:T(8,128)(2,1)S(1)} %get-tuple-element.76), channel_id=1, source_target_pairs={{0,48},{8,56},{16,32},{24,40},{32,16},{40,24},{48,0},{56,8},{1,49}... | collective-permute-start | bytes 122888 | tf_op jit(solution)/shard_map/ppermute | solution.py:55
  97.6 7.1 %collective-permute-start.28 = (bf16[32,640]{1,0:T(8,128)(2,1)S(1)}, bf16[32,640]{1,0:T(8,128)(2,1)S(1)}, u32[]{:S(2)}, u32[]{:S(2)}) collective-permute-start(bf16[32,640]{1,0:T(8,128)(2,1)S(1)} %get-tuple-element.77), channel_id=1, source_target_pairs={{0,8},{8,0},{16,24},{24,16},{32,40},{40,32},{48,56},{56,48},{1,9},... | collective-permute-start | bytes 122888 | tf_op jit(solution)/shard_map/ppermute | solution.py:55
  98.6 7.0 %collective-permute-start.29 = (bf16[32,640]{1,0:T(8,128)(2,1)S(1)}, bf16[32,640]{1,0:T(8,128)(2,1)S(1)}, u32[]{:S(2)}, u32[]{:S(2)}) collective-permute-start(bf16[32,640]{1,0:T(8,128)(2,1)S(1)} %get-tuple-element.78), channel_id=1, source_target_pairs={{0,40},{8,32},{16,56},{24,48},{32,8},{40,0},{48,24},{56,16},{1,41}... | collective-permute-start | bytes 122888 | tf_op jit(solution)/shard_map/ppermute | solution.py:55
  99.1 6.6 %collective-permute-start.30 = (bf16[32,640]{1,0:T(8,128)(2,1)S(1)}, bf16[32,640]{1,0:T(8,128)(2,1)S(1)}, u32[]{:S(2)}, u32[]{:S(2)}) collective-permute-start(bf16[32,640]{1,0:T(8,128)(2,1)S(1)} %get-tuple-element.79), channel_id=1, source_target_pairs={{0,24},{8,16},{16,8},{24,0},{32,56},{40,48},{48,40},{56,32},{1,25}... | collective-permute-start | bytes 122888 | tf_op jit(solution)/shard_map/ppermute | solution.py:55
  101.0 6.1 %collective-permute-start.31 = (bf16[32,640]{1,0:T(8,128)(2,1)S(1)}, bf16[32,640]{1,0:T(8,128)(2,1)S(1)}, u32[]{:S(2)}, u32[]{:S(2)}) collective-permute-start(bf16[32,640]{1,0:T(8,128)(2,1)S(1)} %get-tuple-element.80), channel_id=1, source_target_pairs={{0,56},{8,48},{16,40},{24,32},{32,24},{40,16},{48,8},{56,0},{1,57}... | collective-permute-start | bytes 122888 | tf_op jit(solution)/shard_map/ppermute | solution.py:55
  (4 other events, 75.9 us)

commit v9 on v8

--- a/solution.py
+++ b/solution.py
@@ -25,8 +25,9 @@
 PAIR = HOT_GRP * HALF
 CHUNK = 2 * PAIR
 NEVER = -1e30
+N_FAR = N_Z // 2
 STAT_ROWS = 8
-Z_ORDER = (0, 4, 2, 6, 1, 5, 3, 7)
+Z_ORDER = (0, 4, 2, 6)
 SCALE = QK**-0.5
 LOG2_E = 1.4426950408889634
 N_FAR = N_Z // 2
@@ -49,6 +50,14 @@
 
 def cross_x(a, bits):
     return lax.ppermute(a, "x", [(i, i ^ bits) for i in range(N_X)])
+
+
+def cross_xz(a, bits_x, bits_z):
+    pairs = []
+    for x in range(N_X):
+        for z in range(N_Z):
+            pairs.append((x * N_Z + z, (x ^ bits_x) * N_Z + (z ^ bits_z)))
+    return lax.ppermute(a, ("x", "z"), pairs)
 
 
 def cross_z(a, bits):
@@ -185,10 +194,11 @@
 
 def attend_kernel(q_ref, len_ref, hot_ref, hot_other_ref, *refs):
     n = len(PLACES)
-    key_refs, o_ref = refs[:-1], refs[-1]
+    key_refs, outs = refs[: N_C * n], refs[N_C * n :]
     q = q_ref[...]
     lens = visible_lengths(len_ref, q.shape[0])
     parts = []
+    all_scores = []
     for other, hot in enumerate((hot_ref, hot_other_ref)):
         keys = key_refs[other * n : (other + 1) * n]
         scores = []
@@ -196,6 +206,10 @@
             numbers = row_numbers(hot, other, *place)
             s = jnp.dot(q, k_ref[...], preferred_element_type=f32)
             scores.append(jnp.where(numbers < lens, s, NEVER))
+        all_scores.append(scores)
+    for other in range(2):
+        keys = key_refs[other * n : (other + 1) * n]
+        scores = all_scores[other]
         peak = functools.reduce(jnp.maximum, [fold(jnp.maximum, s) for s in scores])
         peak = peak.max(axis=1, keepdims=True)
         total = 0.0
@@ -215,18 +229,25 @@
         numer = numer + v * f
         total = total + t * f
     o = (numer * (1.0 / jnp.maximum(total, 1.0))).astype(bf16)
-    rows = q.shape[0]
-    lanes = lax.broadcasted_iota(jnp.int32, (rows, 128), 1)
+    lanes = lax.broadcasted_iota(jnp.int32, (q.shape[0], 128), 1)
     stats = jnp.where(lanes == 0, top * SCALE, total).T[:2, :]
-    terms = three_terms(stats[0:1]) + three_terms(stats[1:2])
-    terms = [t.astype(f32) for t in terms] + [jnp.zeros((STAT_ROWS - 6, rows), f32)]
-    o_ref[:rows, :] = o
-    o_ref[rows:, :rows] = jnp.concatenate(terms, axis=0).astype(bf16)
-    o_ref[rows:, rows:] = jnp.zeros((STAT_ROWS, LAT - rows), bf16)
+    rows = o.shape[0] // 2
+    for flip, o_ref in enumerate(outs):
+        o_ref[:rows, :] = o[flip * rows : (flip + 1) * rows]
+        mine = stats[:, flip * rows : (flip + 1) * rows]
+        terms = three_terms(mine[0:1]) + three_terms(mine[1:2])
+        terms = [t.astype(f32) for t in terms] + [jnp.zeros((STAT_ROWS - 6, rows), f32)]
+        o_ref[rows:, :rows] = jnp.concatenate(terms, axis=0).astype(bf16)
+        o_ref[rows:, rows:] = jnp.zeros((STAT_ROWS, LAT - rows), bf16)
 
 
 def merge_kernel(*refs):
-    parts, outs = refs[:N_X], refs[N_X:]
+    n_in = N_X * 2
+    parts, sends, (own_ref, stat_ref) = (
+        refs[:n_in],
+        refs[n_in : n_in + N_FAR - 1],
+        refs[n_in + N_FAR - 1 :],
+    )
     rows = parts[0].shape[0] - STAT_ROWS
     tops, totals = [], []
     for p in parts:
@@ -240,32 +261,40 @@
     table = [w * inv for w in weights] + [top, total]
     table.append(jnp.zeros((128 - len(table), rows), f32))
     table = jnp.concatenate(table, axis=0).T
-    n = rows // N_Z
+    n = rows // N_FAR
     lane = lax.broadcasted_iota(jnp.int32, (n, 128), 1)
-    for i, ref in enumerate(outs):
-        at = slice(i * n, (i + 1) * n)
+    for far in range(N_FAR):
+        at = slice(far * n, (far + 1) * n)
         acc = 0.0
-        for j, p in enumerate(parts):
-            acc = acc + p[at, :].astype(f32) * table[at, j : j + 1]
-        ref[:, :LAT] = acc.astype(ref.dtype)
-        packed = jnp.zeros((n, 128), f32)
-        terms = three_terms(table[at, N_X : N_X + 1])
-        terms += three_terms(table[at, N_X + 1 : N_X + 2])
-        for j, term in enumerate(terms):
-            packed = jnp.where(lane == j, term.astype(f32), packed)
-        ref[:, LAT:] = packed.astype(ref.dtype)
-
-
-def finish_kernel(*refs):
-    parts, out_ref = [r[...].astype(f32) for r in refs[:-1]], refs[-1]
-    tops, totals = [], []
+        for i, p in enumerate(parts):
+            acc = acc + p[at, :].astype(f32) * table[at, i : i + 1]
+        if far:
+            ref = sends[far - 1]
+            ref[:, :LAT] = acc.astype(bf16)
+            packed = jnp.zeros((n, 128), f32)
+            terms = three_terms(table[at, n_in : n_in + 1])
+            terms += three_terms(table[at, n_in + 1 : n_in + 2])
+            for i, term in enumerate(terms):
+                packed = jnp.where(lane == i, term.astype(f32), packed)
+            ref[:, LAT:] = packed.astype(bf16)
+        else:
+            own_ref[...] = acc
+            stat_ref[...] = table[at]
+
+
+def finish_kernel(own_ref, stat_ref, *refs):
+    parts, out_ref = refs[:-1], refs[-1]
+    n_in = N_X * 2
+    tops, totals, values = [stat_ref[:, n_in : n_in + 1]], [stat_ref[:, n_in + 1 : n_in + 2]], [own_ref[...]]
     for p in parts:
-        s = p[:, LAT:]
+        s = p[:, LAT:].astype(f32)
         tops.append(s[:, 0:1] + s[:, 1:2] + s[:, 2:3])
         totals.append(s[:, 3:4] + s[:, 4:5] + s[:, 5:6])
+        values.append(p[:, :LAT].astype(f32))
     top = functools.reduce(jnp.maximum, tops)
     weights = [t * jnp.exp(m - top) for m, t in zip(tops, totals)]
-    o = sum(p[:, :LAT] * w for p, w in zip(parts, weights)) / sum(weights)
+    total = sum(weights)
+    o = sum(v * w for v, w in zip(values, weights)) / total
     count = out_ref.shape[0]
     for head in range(o.shape[0] // count):
         out_ref[:, head * LAT : (head + 1) * LAT] = o[head * count : (head + 1) * count].astype(bf16)
@@ -332,33 +361,40 @@
     keys = [mine, of_left, of_right, far_a, far_b]
     keys = keys + [swap_core(k) for k in keys]
 
-    rows = near.shape[0]
+    rows = near.shape[0] // 2
+    part = ((rows + STAT_ROWS, LAT), bf16)
     parts = []
     for i, hop in enumerate((2, 1, 3, 0)):
         if i > 1:
-            lengths, parts[i - 2] = lax.optimization_barrier((lengths, parts[i - 2]))
-        (o,) = call(
+            lengths, *sent = lax.optimization_barrier((lengths, *parts[2 * i - 4 : 2 * i - 2]))
+            parts[2 * i - 4 : 2 * i - 2] = sent
+        same, flipped = call(
             attend_kernel,
-            [((rows + STAT_ROWS, LAT), bf16)],
+            [part, part],
             [VMEM, SMEM, SMEM, SMEM] + [VMEM] * len(keys),
             [asked[hop], lengths, hot_ids, hot_other, *keys],
         )
-        lengths, o = lax.optimization_barrier((lengths, o))
-        parts.append(cross_x(o, hop) if hop else o)
+        lengths, same, flipped = lax.optimization_barrier((lengths, same, flipped))
+        if hop == 0:
+            flipped, *sent = lax.optimization_barrier((flipped, *parts[2 * i - 2 :]))
+            parts[2 * i - 2 :] = sent
+        parts.append(cross_xz(flipped, hop, 1))
+        parts.append(cross_xz(same, hop, 0) if hop else same)
 
     n = own.shape[0]
-    ours, *sends = call(
+    message = ((n, LAT + 128), bf16)
+    *sends, ours, stat = call(
         merge_kernel,
-        [((n, LAT + 128), f32 if i == 0 else bf16) for i in range(N_Z)],
-        [VMEM] * N_X,
+        [message] * (N_FAR - 1) + [((n, LAT), f32), ((n, 128), f32)],
+        [VMEM] * len(parts),
         parts,
     )
     sends = [cross_z(s, bits) for s, bits in zip(sends, Z_ORDER[1:])]
     (out,) = call(
         finish_kernel,
         [((count, n // count * LAT), bf16)],
-        [VMEM] * N_Z,
-        [ours, *sends],
+        [VMEM] * (2 + len(sends)),
+        [ours, stat, *sends],
     )
     return out
 

time: 108 us -> 109 us (level)
  waiting for transfers between devices: 35.8 us -> 38.4 us
  starting transfers between devices: 47.2 us -> 46.1 us
    ppermute x0 -> x7, waiting for transfers between devices: none -> 10.8 us  [cross_xz(): return lax.ppermute(a, ('x', 'z'), pairs)]
    ppermute x0 -> x7, starting transfers between devices: none -> 8.29 us  [cross_xz(): return lax.ppermute(a, ('x', 'z'), pairs)]
    ppermute x6 -> x3, waiting for transfers between devices: 9.11 us -> 0.99 us  [cross_x(): return lax.ppermute(a, 'x', [(i, i ^ bits) for i in range(N_X)])]
    ppermute x10 -> x6, starting transfers between devices: 22.5 us -> 15.6 us  [cross_z(): return lax.ppermute(a, 'z', [(i, i ^ bits) for i in range(N_Z)])]
    ppermute x6 -> x3, starting transfers between devices: 6.6 us -> 4.18 us  [cross_x(): return lax.ppermute(a, 'x', [(i, i ^ bits) for i in range(N_X)])]
    ppermute x10 -> x6, waiting for transfers between devices: 7.34 us -> 7.34 us  [cross_z(): return lax.ppermute(a, 'z', [(i, i ^ bits) for i in range(N_Z)])]
  transfers between devices with their start and end apart: 32 -> 32, of which waited for: 13 -> 15; matrix products, arithmetic and copies ran while one was open for 0% -> 0% of each run, Pallas kernels for 15% -> 15%
where the time goes in v9:
time: 109 us
  starting transfers between devices  46.1 us (42%)
  waiting for transfers between devices  38.4 us (35%)
  Pallas kernels  23.2 us (21%)
    pallas_call x10, Pallas kernels, call(): pl.pallas_call(kernel, out_shape=tuple((jax.ShapeDtypeStruct(*o) for o in...  23.2 us
    ppermute x10, waiting for transfers between devices, shift_rep(): return lax.ppermute(a, 'rep', [(i, (i + by) % N_REP) for i in range(N_REP)])  17.7 us
    ppermute x10, starting transfers between devices, shift_rep(): return lax.ppermute(a, 'rep', [(i, (i + by) % N_REP) for i in range(N_REP)])  17 us
    ppermute x6, starting transfers between devices, cross_z(): return lax.ppermute(a, 'z', [(i, i ^ bits) for i in range(N_Z)])  15.6 us
    ppermute x7, waiting for transfers between devices, cross_xz(): return lax.ppermute(a, ('x', 'z'), pairs)  10.8 us
    ppermute x7, starting transfers between devices, cross_xz(): return lax.ppermute(a, ('x', 'z'), pairs)  8.29 us
    ppermute x6, waiting for transfers between devices, cross_z(): return lax.ppermute(a, 'z', [(i, i ^ bits) for i in range(N_Z)])  7.34 us
    ppermute x3, starting transfers between devices, cross_x(): return lax.ppermute(a, 'x', [(i, i ^ bits) for i in range(N_X)])  4.18 us
  transfers between devices with their start and end apart: 32, of which 15 were waited for; matrix products, arithmetic and copies ran while one was open for 0% of the time, Pallas kernels for 15%

profile of v9, /device:TPU:6, one launch (start us, length us, event | category | flops | bytes accessed | tf_op | source)
XLA Modules:
  0.0 108.9 jit_solution(2176360103970604531)
XLA Ops:
  0.7 1.7 %shard_map.46 = (bf16[576,256]{1,0:T(8,128)(2,1)S(1)}, bf16[576,256]{1,0:T(8,128)(2,1)S(1)}) custom-call(s32[2]{0:T(128)S(1)} %copy-done, bf16[576,4096]{1,0:T(8,128)(2,1)} %bitcast.4), custom_call_target="tpu_custom_call" | custom-call | tf_op jit(solution)/shard_map/pallas_call | solution.py:304
  2.5 1.7 %collective-permute-start = (bf16[576,256]{1,0:T(8,128)(2,1)S(1)}, bf16[576,256]{1,0:T(8,128)(2,1)S(1)}, u32[]{:S(2)}, u32[]{:S(2)}) collective-permute-start(bf16[576,256]{1,0:T(8,128)(2,1)S(1)} %get-tuple-element.57), channel_id=1, source_target_pairs={{0,1},{1,2},{2,3},{3,0},{4,5},{5,6},{6,7},{7,4},{8,9},{9,10},{10,1... | collective-permute-start | bytes 884744 | tf_op jit(solution)/shard_map/ppermute | solution.py:44
  4.1 1.7 %collective-permute-start.1 = (bf16[576,256]{1,0:T(8,128)(2,1)S(1)}, bf16[576,256]{1,0:T(8,128)(2,1)S(1)}, u32[]{:S(2)}, u32[]{:S(2)}) collective-permute-start(bf16[576,256]{1,0:T(8,128)(2,1)S(1)} %get-tuple-element.58), channel_id=1, source_target_pairs={{0,3},{1,0},{2,1},{3,2},{4,7},{5,4},{6,5},{7,6},{8,11},{9,8},{10,9... | collective-permute-start | bytes 884744 | tf_op jit(solution)/shard_map/ppermute | solution.py:44
  5.9 7.3 %collective-permute-start.2 = (bf16[32,576]{1,0:T(8,128)(2,1)S(1)}, bf16[32,576]{1,0:T(8,128)(2,1)S(1)}, u32[]{:S(2)}, u32[]{:S(2)}) collective-permute-start(bf16[32,576]{1,0:T(8,128)(2,1)S(1)} %bitcast.6), channel_id=1, source_target_pairs={{0,32},{8,40},{16,48},{24,56},{32,0},{40,8},{48,16},{56,24},{1,33}... | collective-permute-start | bytes 110600 | tf_op jit(solution)/shard_map/ppermute | solution.py:64
  13.2 2.2 %shard_map.47 = (bf16[576,256]{1,0:T(8,128)(2,1)S(1)}, bf16[576,256]{1,0:T(8,128)(2,1)S(1)}, bf16[576,256]{1,0:T(8,128)(2,1)S(1)}, bf16[576,256]{1,0:T(8,128)(2,1)S(1)}, bf16[576,512]{1,0:T(8,128)(2,1)S(1)}) custom-call(s32[2]{0:T(128)S(1)} %copy-done.1, bf16[576,4096]{1,0:T(8,128)(2,1)} %bitcast.5), custom_call_target="tpu_custom_call" | custom-call | tf_op jit(solution)/shard_map/pallas_call | solution.py:304
  15.9 2.9 %collective-permute-start.6 = (bf16[576,256]{1,0:T(8,128)(2,1)S(1)}, bf16[576,256]{1,0:T(8,128)(2,1)S(1)}, u32[]{:S(2)}, u32[]{:S(2)}) collective-permute-start(bf16[576,256]{1,0:T(8,128)(2,1)S(1)} %get-tuple-element.65), channel_id=1, source_target_pairs={{0,3},{1,0},{2,1},{3,2},{4,7},{5,4},{6,5},{7,6},{8,11},{9,8},{10,9... | collective-permute-start | bytes 884744 | tf_op jit(solution)/shard_map/ppermute | solution.py:44
  19.6 3.2 %collective-permute-start.7 = (bf16[576,256]{1,0:T(8,128)(2,1)S(1)}, bf16[576,256]{1,0:T(8,128)(2,1)S(1)}, u32[]{:S(2)}, u32[]{:S(2)}) collective-permute-start(bf16[576,256]{1,0:T(8,128)(2,1)S(1)} %get-tuple-element.66), channel_id=1, source_target_pairs={{0,3},{1,0},{2,1},{3,2},{4,7},{5,4},{6,5},{7,6},{8,11},{9,8},{10,9... | collective-permute-start | bytes 884744 | tf_op jit(solution)/shard_map/ppermute | solution.py:44
  22.8 1.5 %collective-permute-start.12 = (bf16[64,576]{1,0:T(8,128)(2,1)S(1)}, bf16[64,576]{1,0:T(8,128)(2,1)S(1)}, u32[]{:S(2)}, u32[]{:S(2)}) collective-permute-start(bf16[64,576]{1,0:T(8,128)(2,1)S(1)} %pad_maximum_fusion.1), channel_id=1, source_target_pairs={{0,16},{8,24},{16,0},{24,8},{32,48},{40,56},{48,32},{56,40},{1,17}... | collective-permute-start | bytes 221192 | tf_op jit(solution)/shard_map/ppermute | solution.py:64
  24.3 4.9 %collective-permute-done.12 = bf16[64,576]{1,0:T(8,128)(2,1)S(1)} collective-permute-done((bf16[64,576]{1,0:T(8,128)(2,1)S(1)}, bf16[64,576]{1,0:T(8,128)(2,1)S(1)}, u32[]{:S(2)}, u32[]{:S(2)}) %collective-permute-start.12) | collective-permute-done | bytes 73760 | tf_op jit(solution)/shard_map/ppermute | solution.py:64
  29.5 3.0 %collective-permute-done.4.left_a = bf16[576,256]{1,0:T(8,128)(2,1)S(1)} collective-permute-done((bf16[576,256]{1,0:T(8,128)(2,1)S(1)}, bf16[576,256]{1,0:T(8,128)(2,1)S(1)}, u32[]{:S(2)}, u32[]{:S(2)}) %collective-permute-start.4) | collective-permute-done | bytes 294944 | tf_op jit(solution)/shard_map/ppermute | solution.py:44
  33.2 3.0 %collective-permute-start.10 = (bf16[576,512]{1,0:T(8,128)(2,1)S(1)}, bf16[576,512]{1,0:T(8,128)(2,1)S(1)}, u32[]{:S(2)}, u32[]{:S(2)}) collective-permute-start(bf16[576,512]{1,0:T(8,128)(2,1)S(1)} %shard_map.49.refs_0_), channel_id=1, source_target_pairs={{0,3},{1,0},{2,1},{3,2},{4,7},{5,4},{6,5},{7,6},{8,11},{9,8},{10,9... | collective-permute-start | bytes 1769480 | tf_op jit(solution)/shard_map/ppermute | solution.py:44
  36.9 2.4 %collective-permute-start.15 = (bf16[256,576]{1,0:T(8,128)(2,1)S(1)}, bf16[256,576]{1,0:T(8,128)(2,1)S(1)}, u32[]{:S(2)}, u32[]{:S(2)}) collective-permute-start(bf16[256,576]{1,0:T(8,128)(2,1)S(1)} %constant_dynamic-update-slice_fusion.q_ref), channel_id=1, source_target_pairs={{0,128},{64,192},{128,0},{192,64},{1,129},{65,193},{129,1},{193,65... | collective-permute-start | bytes 884744 | tf_op jit(solution)/shard_map/ppermute | solution.py:52
  39.3 1.2 %collective-permute-start.14 = (bf16[256,576]{1,0:T(8,128)(2,1)S(1)}, bf16[256,576]{1,0:T(8,128)(2,1)S(1)}, u32[]{:S(2)}, u32[]{:S(2)}) collective-permute-start(bf16[256,576]{1,0:T(8,128)(2,1)S(1)} %constant_dynamic-update-slice_fusion.q_ref), channel_id=1, source_target_pairs={{0,64},{64,0},{128,192},{192,128},{1,65},{65,1},{129,193},{193,129... | collective-permute-start | bytes 884744 | tf_op jit(solution)/shard_map/ppermute | solution.py:52
  40.5 7.9 %collective-permute-done.10.refs_2_ = bf16[576,512]{1,0:T(8,128)(2,1)S(1)} collective-permute-done((bf16[576,512]{1,0:T(8,128)(2,1)S(1)}, bf16[576,512]{1,0:T(8,128)(2,1)S(1)}, u32[]{:S(2)}, u32[]{:S(2)}) %collective-permute-start.10) | collective-permute-done | bytes 589856 | tf_op jit(solution)/shard_map/ppermute | solution.py:44
  48.4 3.8 %collective-permute-start.11 = (bf16[576,256]{1,0:T(8,128)(2,1)S(1)}, bf16[576,256]{1,0:T(8,128)(2,1)S(1)}, u32[]{:S(2)}, u32[]{:S(2)}) collective-permute-start(bf16[576,256]{1,0:T(8,128)(2,1)S(1)} %slice.9), channel_id=1, source_target_pairs={{0,3},{1,0},{2,1},{3,2},{4,7},{5,4},{6,5},{7,6},{8,11},{9,8},{10,9... | collective-permute-start | bytes 884744 | tf_op jit(solution)/shard_map/ppermute | solution.py:44
  54.0 3.1 %collective-permute-done.11.refs_4_ = bf16[576,256]{1,0:T(8,128)(2,1)S(1)} collective-permute-done((bf16[576,256]{1,0:T(8,128)(2,1)S(1)}, bf16[576,256]{1,0:T(8,128)(2,1)S(1)}, u32[]{:S(2)}, u32[]{:S(2)}) %collective-permute-start.11) | collective-permute-done | bytes 294944 | tf_op jit(solution)/shard_map/ppermute | solution.py:44
  57.1 3.7 %collective-permute-done.9.refs_3_ = bf16[576,256]{1,0:T(8,128)(2,1)S(1)} collective-permute-done((bf16[576,256]{1,0:T(8,128)(2,1)S(1)}, bf16[576,256]{1,0:T(8,128)(2,1)S(1)}, u32[]{:S(2)}, u32[]{:S(2)}) %collective-permute-start.9) | collective-permute-done | bytes 294944 | tf_op jit(solution)/shard_map/ppermute | solution.py:44
  62.8 4.1 %shard_map.50 = (bf16[136,512]{1,0:T(8,128)(2,1)S(1)}, bf16[136,512]{1,0:T(8,128)(2,1)S(1)}) custom-call(bf16[256,576]{1,0:T(8,128)(2,1)S(1)} %collective-permute-done.15.q_ref, s32[16]{0:T(128)S(1)} %copy-done.2, s32[2]{0:T(128)S(1)} %copy-done.1, s32[2]{0:T(128)S(1)} %collective-permute-done.3.hot_other_ref, bf16[576,512]{1,0:T(8,128)(2,1)S(1)} %shard_map.49.refs_0_, ...), custom_call_target="tpu_custom_call" | custom-call | tf_op jit(solution)/shard_map/pallas_call | solution.py:304
  66.9 1.9 %collective-permute-start.22 = (bf16[136,512]{1,0:T(8,128)(2,1)S(1)}, bf16[136,512]{1,0:T(8,128)(2,1)S(1)}, u32[]{:S(2)}, u32[]{:S(2)}) collective-permute-start(bf16[136,512]{1,0:T(8,128)(2,1)S(1)} %get-tuple-element.80), channel_id=1, source_target_pairs={{0,136},{8,128},{16,152},{24,144},{32,168},{40,160},{48,184},{56,1... | collective-permute-start | bytes 417800 | tf_op jit(solution)/shard_map/ppermute | solution.py:60
  68.8 2.0 %collective-permute-start.23 = (bf16[136,512]{1,0:T(8,128)(2,1)S(1)}, bf16[136,512]{1,0:T(8,128)(2,1)S(1)}, u32[]{:S(2)}, u32[]{:S(2)}) collective-permute-start(bf16[136,512]{1,0:T(8,128)(2,1)S(1)} %get-tuple-element.81), channel_id=1, source_target_pairs={{0,128},{8,136},{16,144},{24,152},{32,160},{40,168},{48,176},{56,1... | collective-permute-start | bytes 417800 | tf_op jit(solution)/shard_map/ppermute | solution.py:60
  70.8 4.1 %shard_map.51 = (bf16[136,512]{1,0:T(8,128)(2,1)S(1)}, bf16[136,512]{1,0:T(8,128)(2,1)S(1)}) custom-call(bf16[256,576]{1,0:T(8,128)(2,1)S(1)} %collective-permute-done.14.q_ref, s32[16]{0:T(128)S(1)} %copy-done.2, s32[2]{0:T(128)S(1)} %copy-done.1, s32[2]{0:T(128)S(1)} %collective-permute-done.3.hot_other_ref, bf16[576,512]{1,0:T(8,128)(2,1)S(1)} %shard_map.49.refs_0_, ...), custom_call_target="tpu_custom_call" | custom-call | tf_op jit(solution)/shard_map/pallas_call | solution.py:304
  74.9 1.5 %collective-permute-start.24 = (bf16[136,512]{1,0:T(8,128)(2,1)S(1)}, bf16[136,512]{1,0:T(8,128)(2,1)S(1)}, u32[]{:S(2)}, u32[]{:S(2)}) collective-permute-start(bf16[136,512]{1,0:T(8,128)(2,1)S(1)} %get-tuple-element.89), channel_id=1, source_target_pairs={{0,72},{8,64},{16,88},{24,80},{32,104},{40,96},{48,120},{56,112},{... | collective-permute-start | bytes 417800 | tf_op jit(solution)/shard_map/ppermute | solution.py:60
  76.4 1.2 %collective-permute-start.25 = (bf16[136,512]{1,0:T(8,128)(2,1)S(1)}, bf16[136,512]{1,0:T(8,128)(2,1)S(1)}, u32[]{:S(2)}, u32[]{:S(2)}) collective-permute-start(bf16[136,512]{1,0:T(8,128)(2,1)S(1)} %get-tuple-element.90), channel_id=1, source_target_pairs={{0,64},{8,72},{16,80},{24,88},{32,96},{40,104},{48,112},{56,120},{... | collective-permute-start | bytes 417800 | tf_op jit(solution)/shard_map/ppermute | solution.py:60
  77.6 3.4 %collective-permute-done.23.refs_1_ = bf16[136,512]{1,0:T(8,128)(2,1)S(1)} collective-permute-done((bf16[136,512]{1,0:T(8,128)(2,1)S(1)}, bf16[136,512]{1,0:T(8,128)(2,1)S(1)}, u32[]{:S(2)}, u32[]{:S(2)}) %collective-permute-start.23) | collective-permute-done | bytes 139296 | tf_op jit(solution)/shard_map/ppermute | solution.py:60
  81.1 4.1 %shard_map.52 = (bf16[136,512]{1,0:T(8,128)(2,1)S(1)}, bf16[136,512]{1,0:T(8,128)(2,1)S(1)}) custom-call(bf16[256,576]{1,0:T(8,128)(2,1)S(1)} %collective-permute-done.16.q_ref, s32[16]{0:T(128)S(1)} %copy-done.2, s32[2]{0:T(128)S(1)} %copy-done.1, s32[2]{0:T(128)S(1)} %collective-permute-done.3.hot_other_ref, bf16[576,512]{1,0:T(8,128)(2,1)S(1)} %shard_map.49.refs_0_, ...), custom_call_target="tpu_custom_call" | custom-call | tf_op jit(solution)/shard_map/pallas_call | solution.py:304
  85.8 4.1 %shard_map.53 = (bf16[136,512]{1,0:T(8,128)(2,1)S(1)}, bf16[136,512]{1,0:T(8,128)(2,1)S(1)}) custom-call(bf16[256,576]{1,0:T(8,128)(2,1)S(1)} %constant_dynamic-update-slice_fusion.q_ref, s32[16]{0:T(128)S(1)} %copy-done.2, s32[2]{0:T(128)S(1)} %copy-done.1, s32[2]{0:T(128)S(1)} %collective-permute-done.3.hot_other_ref, ...), custom_call_target="tpu_custom_call" | custom-call | tf_op jit(solution)/shard_map/pallas_call | solution.py:304
  89.9 2.6 %collective-permute-done.26.refs_4_ = bf16[136,512]{1,0:T(8,128)(2,1)S(1)} collective-permute-done((bf16[136,512]{1,0:T(8,128)(2,1)S(1)}, bf16[136,512]{1,0:T(8,128)(2,1)S(1)}, u32[]{:S(2)}, u32[]{:S(2)}) %collective-permute-start.26) | collective-permute-done | bytes 139296 | tf_op jit(solution)/shard_map/ppermute | solution.py:60
  94.2 4.2 %collective-permute-done.28.refs_6_ = bf16[136,512]{1,0:T(8,128)(2,1)S(1)} collective-permute-done((bf16[136,512]{1,0:T(8,128)(2,1)S(1)}, bf16[136,512]{1,0:T(8,128)(2,1)S(1)}, u32[]{:S(2)}, u32[]{:S(2)}) %collective-permute-start.28) | collective-permute-done | bytes 139296 | tf_op jit(solution)/shard_map/ppermute | solution.py:60
  98.9 2.4 %collective-permute-start.30 = (bf16[32,640]{1,0:T(8,128)(2,1)S(1)}, bf16[32,640]{1,0:T(8,128)(2,1)S(1)}, u32[]{:S(2)}, u32[]{:S(2)}) collective-permute-start(bf16[32,640]{1,0:T(8,128)(2,1)S(1)} %get-tuple-element.107), channel_id=1, source_target_pairs={{0,16},{8,24},{16,0},{24,8},{32,48},{40,56},{48,32},{56,40},{1,17}... | collective-permute-start | bytes 122888 | tf_op jit(solution)/shard_map/ppermute | solution.py:64
  101.3 4.1 %collective-permute-start.31 = (bf16[32,640]{1,0:T(8,128)(2,1)S(1)}, bf16[32,640]{1,0:T(8,128)(2,1)S(1)}, u32[]{:S(2)}, u32[]{:S(2)}) collective-permute-start(bf16[32,640]{1,0:T(8,128)(2,1)S(1)} %get-tuple-element.108), channel_id=1, source_target_pairs={{0,48},{8,56},{16,32},{24,40},{32,16},{40,24},{48,0},{56,8},{1,49}... | collective-permute-start | bytes 122888 | tf_op jit(solution)/shard_map/ppermute | solution.py:64
  105.4 1.4 %collective-permute-done.29.refs_0_ = bf16[32,640]{1,0:T(8,128)(2,1)S(1)} collective-permute-done((bf16[32,640]{1,0:T(8,128)(2,1)S(1)}, bf16[32,640]{1,0:T(8,128)(2,1)S(1)}, u32[]{:S(2)}, u32[]{:S(2)}) %collective-permute-start.29) | collective-permute-done | bytes 40992 | tf_op jit(solution)/shard_map/ppermute | solution.py:64
  107.8 1.1 shard_map.55
  (59 shorter events, 11.3 us)
Async XLA Ops:
  2.5 16.3 %collective-permute-start = (bf16[576,256]{1,0:T(8,128)(2,1)S(1)}, bf16[576,256]{1,0:T(8,128)(2,1)S(1)}, u32[]{:S(2)}, u32[]{:S(2)}) collective-permute-start(bf16[576,256]{1,0:T(8,128)(2,1)S(1)} %get-tuple-element.57), channel_id=1, source_target_pairs={{0,1},{1,2},{2,3},{3,0},{4,5},{5,6},{6,7},{7,4},{8,9},{9,10},{10,1... | collective-permute-start | bytes 884744 | tf_op jit(solution)/shard_map/ppermute | solution.py:44
  4.1 14.7 %collective-permute-start.1 = (bf16[576,256]{1,0:T(8,128)(2,1)S(1)}, bf16[576,256]{1,0:T(8,128)(2,1)S(1)}, u32[]{:S(2)}, u32[]{:S(2)}) collective-permute-start(bf16[576,256]{1,0:T(8,128)(2,1)S(1)} %get-tuple-element.58), channel_id=1, source_target_pairs={{0,3},{1,0},{2,1},{3,2},{4,7},{5,4},{6,5},{7,6},{8,11},{9,8},{10,9... | collective-permute-start | bytes 884744 | tf_op jit(solution)/shard_map/ppermute | solution.py:44
  5.9 10.0 %collective-permute-start.2 = (bf16[32,576]{1,0:T(8,128)(2,1)S(1)}, bf16[32,576]{1,0:T(8,128)(2,1)S(1)}, u32[]{:S(2)}, u32[]{:S(2)}) collective-permute-start(bf16[32,576]{1,0:T(8,128)(2,1)S(1)} %bitcast.6), channel_id=1, source_target_pairs={{0,32},{8,40},{16,48},{24,56},{32,0},{40,8},{48,16},{56,24},{1,33}... | collective-permute-start | bytes 110600 | tf_op jit(solution)/shard_map/ppermute | solution.py:64
  13.2 5.6 %collective-permute-start.3 = (s32[2]{0:T(128)S(1)}, s32[2]{0:T(128)S(1)}, u32[]{:S(2)}, u32[]{:S(2)}) collective-permute-start(s32[2]{0:T(128)S(1)} %copy-done.1), channel_id=1, source_target_pairs={{0,4},{4,0},{1,5},{5,1},{2,6},{6,2},{3,7},{7,3},{8,12},{12,8},{9,1... | collective-permute-start | bytes 32 | tf_op jit(solution)/shard_map/ppermute | solution.py:48
  15.4 14.0 %collective-permute-start.5 = (bf16[576,256]{1,0:T(8,128)(2,1)S(1)}, bf16[576,256]{1,0:T(8,128)(2,1)S(1)}, u32[]{:S(2)}, u32[]{:S(2)}) collective-permute-start(bf16[576,256]{1,0:T(8,128)(2,1)S(1)} %get-tuple-element.64), channel_id=1, source_target_pairs={{0,1},{1,2},{2,3},{3,0},{4,5},{5,6},{6,7},{7,4},{8,9},{9,10},{10,1... | collective-permute-start | bytes 884744 | tf_op jit(solution)/shard_map/ppermute | solution.py:44
  15.9 13.6 %collective-permute-start.6 = (bf16[576,256]{1,0:T(8,128)(2,1)S(1)}, bf16[576,256]{1,0:T(8,128)(2,1)S(1)}, u32[]{:S(2)}, u32[]{:S(2)}) collective-permute-start(bf16[576,256]{1,0:T(8,128)(2,1)S(1)} %get-tuple-element.65), channel_id=1, source_target_pairs={{0,3},{1,0},{2,1},{3,2},{4,7},{5,4},{6,5},{7,6},{8,11},{9,8},{10,9... | collective-permute-start | bytes 884744 | tf_op jit(solution)/shard_map/ppermute | solution.py:44
  19.5 13.0 %collective-permute-start.4 = (bf16[576,256]{1,0:T(8,128)(2,1)S(1)}, bf16[576,256]{1,0:T(8,128)(2,1)S(1)}, u32[]{:S(2)}, u32[]{:S(2)}) collective-permute-start(bf16[576,256]{1,0:T(8,128)(2,1)S(1)} %get-tuple-element.63), channel_id=1, source_target_pairs={{0,1},{1,2},{2,3},{3,0},{4,5},{5,6},{6,7},{7,4},{8,9},{9,10},{10,1... | collective-permute-start | bytes 884744 | tf_op jit(solution)/shard_map/ppermute | solution.py:44
  19.6 12.9 %collective-permute-start.7 = (bf16[576,256]{1,0:T(8,128)(2,1)S(1)}, bf16[576,256]{1,0:T(8,128)(2,1)S(1)}, u32[]{:S(2)}, u32[]{:S(2)}) collective-permute-start(bf16[576,256]{1,0:T(8,128)(2,1)S(1)} %get-tuple-element.66), channel_id=1, source_target_pairs={{0,3},{1,0},{2,1},{3,2},{4,7},{5,4},{6,5},{7,6},{8,11},{9,8},{10,9... | collective-permute-start | bytes 884744 | tf_op jit(solution)/shard_map/ppermute | solution.py:44
  22.8 6.4 %collective-permute-start.12 = (bf16[64,576]{1,0:T(8,128)(2,1)S(1)}, bf16[64,576]{1,0:T(8,128)(2,1)S(1)}, u32[]{:S(2)}, u32[]{:S(2)}) collective-permute-start(bf16[64,576]{1,0:T(8,128)(2,1)S(1)} %pad_maximum_fusion.1), channel_id=1, source_target_pairs={{0,16},{8,24},{16,0},{24,8},{32,48},{40,56},{48,32},{56,40},{1,17}... | collective-permute-start | bytes 221192 | tf_op jit(solution)/shard_map/ppermute | solution.py:64
  29.2 7.0 %collective-permute-start.13 = (bf16[128,576]{1,0:T(8,128)(2,1)S(1)}, bf16[128,576]{1,0:T(8,128)(2,1)S(1)}, u32[]{:S(2)}, u32[]{:S(2)}) collective-permute-start(bf16[128,576]{1,0:T(8,128)(2,1)S(1)} %pad_maximum_fusion), channel_id=1, source_target_pairs={{0,8},{8,0},{16,24},{24,16},{32,40},{40,32},{48,56},{56,48},{1,9},... | collective-permute-start | bytes 442376 | tf_op jit(solution)/shard_map/ppermute | solution.py:64
  33.2 15.2 %collective-permute-start.10 = (bf16[576,512]{1,0:T(8,128)(2,1)S(1)}, bf16[576,512]{1,0:T(8,128)(2,1)S(1)}, u32[]{:S(2)}, u32[]{:S(2)}) collective-permute-start(bf16[576,512]{1,0:T(8,128)(2,1)S(1)} %shard_map.49.refs_0_), channel_id=1, source_target_pairs={{0,3},{1,0},{2,1},{3,2},{4,7},{5,4},{6,5},{7,6},{8,11},{9,8},{10,9... | collective-permute-start | bytes 1769480 | tf_op jit(solution)/shard_map/ppermute | solution.py:44
  36.2 16.0 %collective-permute-start.8 = (bf16[576,512]{1,0:T(8,128)(2,1)S(1)}, bf16[576,512]{1,0:T(8,128)(2,1)S(1)}, u32[]{:S(2)}, u32[]{:S(2)}) collective-permute-start(bf16[576,512]{1,0:T(8,128)(2,1)S(1)} %shard_map.49.refs_0_), channel_id=1, source_target_pairs={{0,1},{1,2},{2,3},{3,0},{4,5},{5,6},{6,7},{7,4},{8,9},{9,10},{10,1... | collective-permute-start | bytes 1769480 | tf_op jit(solution)/shard_map/ppermute | solution.py:44
  36.3 17.1 %collective-permute-start.16 = (bf16[256,576]{1,0:T(8,128)(2,1)S(1)}, bf16[256,576]{1,0:T(8,128)(2,1)S(1)}, u32[]{:S(2)}, u32[]{:S(2)}) collective-permute-start(bf16[256,576]{1,0:T(8,128)(2,1)S(1)} %constant_dynamic-update-slice_fusion.q_ref), channel_id=1, source_target_pairs={{0,192},{64,128},{128,64},{192,0},{1,193},{65,129},{129,65},{193,1... | collective-permute-start | bytes 884744 | tf_op jit(solution)/shard_map/ppermute | solution.py:52
  36.9 16.5 %collective-permute-start.15 = (bf16[256,576]{1,0:T(8,128)(2,1)S(1)}, bf16[256,576]{1,0:T(8,128)(2,1)S(1)}, u32[]{:S(2)}, u32[]{:S(2)}) collective-permute-start(bf16[256,576]{1,0:T(8,128)(2,1)S(1)} %constant_dynamic-update-slice_fusion.q_ref), channel_id=1, source_target_pairs={{0,128},{64,192},{128,0},{192,64},{1,129},{65,193},{129,1},{193,65... | collective-permute-start | bytes 884744 | tf_op jit(solution)/shard_map/ppermute | solution.py:52
  39.3 14.7 %collective-permute-start.14 = (bf16[256,576]{1,0:T(8,128)(2,1)S(1)}, bf16[256,576]{1,0:T(8,128)(2,1)S(1)}, u32[]{:S(2)}, u32[]{:S(2)}) collective-permute-start(bf16[256,576]{1,0:T(8,128)(2,1)S(1)} %constant_dynamic-update-slice_fusion.q_ref), channel_id=1, source_target_pairs={{0,64},{64,0},{128,192},{192,128},{1,65},{65,1},{129,193},{193,129... | collective-permute-start | bytes 884744 | tf_op jit(solution)/shard_map/ppermute | solution.py:52
  48.4 8.7 %collective-permute-start.11 = (bf16[576,256]{1,0:T(8,128)(2,1)S(1)}, bf16[576,256]{1,0:T(8,128)(2,1)S(1)}, u32[]{:S(2)}, u32[]{:S(2)}) collective-permute-start(bf16[576,256]{1,0:T(8,128)(2,1)S(1)} %slice.9), channel_id=1, source_target_pairs={{0,3},{1,0},{2,1},{3,2},{4,7},{5,4},{6,5},{7,6},{8,11},{9,8},{10,9... | collective-permute-start | bytes 884744 | tf_op jit(solution)/shard_map/ppermute | solution.py:44
  52.2 8.6 %collective-permute-start.9 = (bf16[576,256]{1,0:T(8,128)(2,1)S(1)}, bf16[576,256]{1,0:T(8,128)(2,1)S(1)}, u32[]{:S(2)}, u32[]{:S(2)}) collective-permute-start(bf16[576,256]{1,0:T(8,128)(2,1)S(1)} %slice.8), channel_id=1, source_target_pairs={{0,1},{1,2},{2,3},{3,0},{4,5},{5,6},{6,7},{7,4},{8,9},{9,10},{10,1... | collective-permute-start | bytes 884744 | tf_op jit(solution)/shard_map/ppermute | solution.py:44
  53.4 7.9 %collective-permute-start.17 = (bf16[576,512]{1,0:T(8,128)(2,1)S(1)}, bf16[576,512]{1,0:T(8,128)(2,1)S(1)}, u32[]{:S(2)}, u32[]{:S(2)}) collective-permute-start(bf16[576,512]{1,0:T(8,128)(2,1)S(1)} %shard_map.49.refs_0_), channel_id=1, source_target_pairs={{0,4},{4,0},{1,5},{5,1},{2,6},{6,2},{3,7},{7,3},{8,12},{12,8},{9,1... | collective-permute-start | bytes 1769480 | tf_op jit(solution)/shard_map/ppermute | solution.py:48
  53.4 7.9 %collective-permute-start.19 = (bf16[576,512]{1,0:T(8,128)(2,1)S(1)}, bf16[576,512]{1,0:T(8,128)(2,1)S(1)}, u32[]{:S(2)}, u32[]{:S(2)}) collective-permute-start(bf16[576,512]{1,0:T(8,128)(2,1)S(1)} %collective-permute-done.10.refs_2_), channel_id=1, source_target_pairs={{0,4},{4,0},{1,5},{5,1},{2,6},{6,2},{3,7},{7,3},{8,12},{12,8},{9,1... | collective-permute-start | bytes 1769480 | tf_op jit(solution)/shard_map/ppermute | solution.py:48
  54.0 8.8 %collective-permute-start.18 = (bf16[576,512]{1,0:T(8,128)(2,1)S(1)}, bf16[576,512]{1,0:T(8,128)(2,1)S(1)}, u32[]{:S(2)}, u32[]{:S(2)}) collective-permute-start(bf16[576,512]{1,0:T(8,128)(2,1)S(1)} %collective-permute-done.8.refs_1_), channel_id=1, source_target_pairs={{0,4},{4,0},{1,5},{5,1},{2,6},{6,2},{3,7},{7,3},{8,12},{12,8},{9,1... | collective-permute-start | bytes 1769480 | tf_op jit(solution)/shard_map/ppermute | solution.py:48
  60.8 1.6 %collective-permute-start.20 = (bf16[576,256]{1,0:T(8,128)(2,1)S(1)}, bf16[576,256]{1,0:T(8,128)(2,1)S(1)}, u32[]{:S(2)}, u32[]{:S(2)}) collective-permute-start(bf16[576,256]{1,0:T(8,128)(2,1)S(1)} %collective-permute-done.9.refs_3_), channel_id=1, source_target_pairs={{0,4},{4,0},{1,5},{5,1},{2,6},{6,2},{3,7},{7,3},{8,12},{12,8},{9,1... | collective-permute-start | bytes 884744 | tf_op jit(solution)/shard_map/ppermute | solution.py:48
  60.8 2.0 %collective-permute-start.21 = (bf16[576,256]{1,0:T(8,128)(2,1)S(1)}, bf16[576,256]{1,0:T(8,128)(2,1)S(1)}, u32[]{:S(2)}, u32[]{:S(2)}) collective-permute-start(bf16[576,256]{1,0:T(8,128)(2,1)S(1)} %collective-permute-done.11.refs_4_), channel_id=1, source_target_pairs={{0,4},{4,0},{1,5},{5,1},{2,6},{6,2},{3,7},{7,3},{8,12},{12,8},{9,1... | collective-permute-start | bytes 884744 | tf_op jit(solution)/shard_map/ppermute | solution.py:48
  66.9 10.7 %collective-permute-start.22 = (bf16[136,512]{1,0:T(8,128)(2,1)S(1)}, bf16[136,512]{1,0:T(8,128)(2,1)S(1)}, u32[]{:S(2)}, u32[]{:S(2)}) collective-permute-start(bf16[136,512]{1,0:T(8,128)(2,1)S(1)} %get-tuple-element.80), channel_id=1, source_target_pairs={{0,136},{8,128},{16,152},{24,144},{32,168},{40,160},{48,184},{56,1... | collective-permute-start | bytes 417800 | tf_op jit(solution)/shard_map/ppermute | solution.py:60
  68.8 12.2 %collective-permute-start.23 = (bf16[136,512]{1,0:T(8,128)(2,1)S(1)}, bf16[136,512]{1,0:T(8,128)(2,1)S(1)}, u32[]{:S(2)}, u32[]{:S(2)}) collective-permute-start(bf16[136,512]{1,0:T(8,128)(2,1)S(1)} %get-tuple-element.81), channel_id=1, source_target_pairs={{0,128},{8,136},{16,144},{24,152},{32,160},{40,168},{48,176},{56,1... | collective-permute-start | bytes 417800 | tf_op jit(solution)/shard_map/ppermute | solution.py:60
  74.9 10.9 %collective-permute-start.24 = (bf16[136,512]{1,0:T(8,128)(2,1)S(1)}, bf16[136,512]{1,0:T(8,128)(2,1)S(1)}, u32[]{:S(2)}, u32[]{:S(2)}) collective-permute-start(bf16[136,512]{1,0:T(8,128)(2,1)S(1)} %get-tuple-element.89), channel_id=1, source_target_pairs={{0,72},{8,64},{16,88},{24,80},{32,104},{40,96},{48,120},{56,112},{... | collective-permute-start | bytes 417800 | tf_op jit(solution)/shard_map/ppermute | solution.py:60
  76.4 9.4 %collective-permute-start.25 = (bf16[136,512]{1,0:T(8,128)(2,1)S(1)}, bf16[136,512]{1,0:T(8,128)(2,1)S(1)}, u32[]{:S(2)}, u32[]{:S(2)}) collective-permute-start(bf16[136,512]{1,0:T(8,128)(2,1)S(1)} %get-tuple-element.90), channel_id=1, source_target_pairs={{0,64},{8,72},{16,80},{24,88},{32,96},{40,104},{48,112},{56,120},{... | collective-permute-start | bytes 417800 | tf_op jit(solution)/shard_map/ppermute | solution.py:60
  85.2 7.4 %collective-permute-start.26 = (bf16[136,512]{1,0:T(8,128)(2,1)S(1)}, bf16[136,512]{1,0:T(8,128)(2,1)S(1)}, u32[]{:S(2)}, u32[]{:S(2)}) collective-permute-start(bf16[136,512]{1,0:T(8,128)(2,1)S(1)} %get-tuple-element.98), channel_id=1, source_target_pairs={{0,200},{8,192},{16,216},{24,208},{32,232},{40,224},{48,248},{56,2... | collective-permute-start | bytes 417800 | tf_op jit(solution)/shard_map/ppermute | solution.py:60
  85.3 7.8 %collective-permute-start.27 = (bf16[136,512]{1,0:T(8,128)(2,1)S(1)}, bf16[136,512]{1,0:T(8,128)(2,1)S(1)}, u32[]{:S(2)}, u32[]{:S(2)}) collective-permute-start(bf16[136,512]{1,0:T(8,128)(2,1)S(1)} %get-tuple-element.99), channel_id=1, source_target_pairs={{0,192},{8,200},{16,208},{24,216},{32,224},{40,232},{48,240},{56,2... | collective-permute-start | bytes 417800 | tf_op jit(solution)/shard_map/ppermute | solution.py:60
  93.1 5.2 %collective-permute-start.28 = (bf16[136,512]{1,0:T(8,128)(2,1)S(1)}, bf16[136,512]{1,0:T(8,128)(2,1)S(1)}, u32[]{:S(2)}, u32[]{:S(2)}) collective-permute-start(bf16[136,512]{1,0:T(8,128)(2,1)S(1)} %get-tuple-element.102), channel_id=1, source_target_pairs={{0,8},{8,0},{16,24},{24,16},{32,40},{40,32},{48,56},{56,48},{64,72... | collective-permute-start | bytes 417800 | tf_op jit(solution)/shard_map/ppermute | solution.py:60
  98.8 8.0 %collective-permute-start.29 = (bf16[32,640]{1,0:T(8,128)(2,1)S(1)}, bf16[32,640]{1,0:T(8,128)(2,1)S(1)}, u32[]{:S(2)}, u32[]{:S(2)}) collective-permute-start(bf16[32,640]{1,0:T(8,128)(2,1)S(1)} %get-tuple-element.106), channel_id=1, source_target_pairs={{0,32},{8,40},{16,48},{24,56},{32,0},{40,8},{48,16},{56,24},{1,33}... | collective-permute-start | bytes 122888 | tf_op jit(solution)/shard_map/ppermute | solution.py:64
  98.9 7.9 %collective-permute-start.30 = (bf16[32,640]{1,0:T(8,128)(2,1)S(1)}, bf16[32,640]{1,0:T(8,128)(2,1)S(1)}, u32[]{:S(2)}, u32[]{:S(2)}) collective-permute-start(bf16[32,640]{1,0:T(8,128)(2,1)S(1)} %get-tuple-element.107), channel_id=1, source_target_pairs={{0,16},{8,24},{16,0},{24,8},{32,48},{40,56},{48,32},{56,40},{1,17}... | collective-permute-start | bytes 122888 | tf_op jit(solution)/shard_map/ppermute | solution.py:64
  101.3 6.6 %collective-permute-start.31 = (bf16[32,640]{1,0:T(8,128)(2,1)S(1)}, bf16[32,640]{1,0:T(8,128)(2,1)S(1)}, u32[]{:S(2)}, u32[]{:S(2)}) collective-permute-start(bf16[32,640]{1,0:T(8,128)(2,1)S(1)} %get-tuple-element.108), channel_id=1, source_target_pairs={{0,48},{8,56},{16,32},{24,40},{32,16},{40,24},{48,0},{56,8},{1,49}... | collective-permute-start | bytes 122888 | tf_op jit(solution)/shard_map/ppermute | solution.py:64
  (4 other events, 75.9 us)

commit v10 on v8

--- a/solution.py
+++ b/solution.py
@@ -189,6 +189,7 @@
     q = q_ref[...]
     lens = visible_lengths(len_ref, q.shape[0])
     parts = []
+    all_scores = []
     for other, hot in enumerate((hot_ref, hot_other_ref)):
         keys = key_refs[other * n : (other + 1) * n]
         scores = []
@@ -196,6 +197,10 @@
             numbers = row_numbers(hot, other, *place)
             s = jnp.dot(q, k_ref[...], preferred_element_type=f32)
             scores.append(jnp.where(numbers < lens, s, NEVER))
+        all_scores.append(scores)
+    for other in range(2):
+        keys = key_refs[other * n : (other + 1) * n]
+        scores = all_scores[other]
         peak = functools.reduce(jnp.maximum, [fold(jnp.maximum, s) for s in scores])
         peak = peak.max(axis=1, keepdims=True)
         total = 0.0
@@ -334,7 +339,7 @@
 
     rows = near.shape[0]
     parts = []
-    for i, hop in enumerate((2, 1, 3, 0)):
+    for i, hop in enumerate((1, 3, 2, 0)):
         if i > 1:
             lengths, parts[i - 2] = lax.optimization_barrier((lengths, parts[i - 2]))
         (o,) = call(

time: 108 us -> 107 us (level)
  waiting for transfers between devices: 35.8 us -> 33.5 us
  starting transfers between devices: 47.2 us -> 48.6 us
    ppermute x6, waiting for transfers between devices: 9.11 us -> 6.87 us  [cross_x(): return lax.ppermute(a, 'x', [(i, i ^ bits) for i in range(N_X)])]
    ppermute x6, starting transfers between devices: 6.6 us -> 8.01 us  [cross_x(): return lax.ppermute(a, 'x', [(i, i ^ bits) for i in range(N_X)])]
  transfers between devices with their start and end apart: 32 -> 32, of which waited for: 13 -> 14; matrix products, arithmetic and copies ran while one was open for 0% -> 0% of each run, Pallas kernels for 15% -> 15%
where the time goes in v10:
time: 107 us; the launch traced here: 106 us
  starting transfers between devices  48.6 us (45%)
  waiting for transfers between devices  33.5 us (31%)
  Pallas kernels  23.2 us (22%)
    pallas_call x10, Pallas kernels, call(): pl.pallas_call(kernel, out_shape=tuple((jax.ShapeDtypeStruct(*o) for o in...  23.2 us
    ppermute x10, starting transfers between devices, cross_z(): return lax.ppermute(a, 'z', [(i, i ^ bits) for i in range(N_Z)])  22.5 us
    ppermute x10, waiting for transfers between devices, shift_rep(): return lax.ppermute(a, 'rep', [(i, (i + by) % N_REP) for i in range(N_REP)])  17.8 us
    ppermute x10, starting transfers between devices, shift_rep(): return lax.ppermute(a, 'rep', [(i, (i + by) % N_REP) for i in range(N_REP)])  17 us
    ppermute x6, starting transfers between devices, cross_x(): return lax.ppermute(a, 'x', [(i, i ^ bits) for i in range(N_X)])  8.01 us
    ppermute x10, waiting for transfers between devices, cross_z(): return lax.ppermute(a, 'z', [(i, i ^ bits) for i in range(N_Z)])  7.34 us
    ppermute x6, waiting for transfers between devices, cross_x(): return lax.ppermute(a, 'x', [(i, i ^ bits) for i in range(N_X)])  6.87 us
  transfers between devices with their start and end apart: 32, of which 14 were waited for; matrix products, arithmetic and copies ran while one was open for 0% of the time, Pallas kernels for 15%

profile of v10, /device:TPU:6, one launch (start us, length us, event | category | flops | bytes accessed | tf_op | source)
XLA Modules:
  0.0 106.4 jit_solution(9478595892632032022)
XLA Ops:
  0.7 1.7 %shard_map.46 = (bf16[576,256]{1,0:T(8,128)(2,1)S(1)}, bf16[576,256]{1,0:T(8,128)(2,1)S(1)}) custom-call(s32[2]{0:T(128)S(1)} %copy-done, bf16[576,4096]{1,0:T(8,128)(2,1)} %bitcast.4), custom_call_target="tpu_custom_call" | custom-call | tf_op jit(solution)/shard_map/pallas_call | solution.py:280
  2.5 1.7 %collective-permute-start = (bf16[576,256]{1,0:T(8,128)(2,1)S(1)}, bf16[576,256]{1,0:T(8,128)(2,1)S(1)}, u32[]{:S(2)}, u32[]{:S(2)}) collective-permute-start(bf16[576,256]{1,0:T(8,128)(2,1)S(1)} %get-tuple-element.43), channel_id=1, source_target_pairs={{0,1},{1,2},{2,3},{3,0},{4,5},{5,6},{6,7},{7,4},{8,9},{9,10},{10,1... | collective-permute-start | bytes 884744 | tf_op jit(solution)/shard_map/ppermute | solution.py:43
  4.1 1.7 %collective-permute-start.1 = (bf16[576,256]{1,0:T(8,128)(2,1)S(1)}, bf16[576,256]{1,0:T(8,128)(2,1)S(1)}, u32[]{:S(2)}, u32[]{:S(2)}) collective-permute-start(bf16[576,256]{1,0:T(8,128)(2,1)S(1)} %get-tuple-element.44), channel_id=1, source_target_pairs={{0,3},{1,0},{2,1},{3,2},{4,7},{5,4},{6,5},{7,6},{8,11},{9,8},{10,9... | collective-permute-start | bytes 884744 | tf_op jit(solution)/shard_map/ppermute | solution.py:43
  5.9 7.3 %collective-permute-start.2 = (bf16[32,576]{1,0:T(8,128)(2,1)S(1)}, bf16[32,576]{1,0:T(8,128)(2,1)S(1)}, u32[]{:S(2)}, u32[]{:S(2)}) collective-permute-start(bf16[32,576]{1,0:T(8,128)(2,1)S(1)} %bitcast.6), channel_id=1, source_target_pairs={{0,32},{8,40},{16,48},{24,56},{32,0},{40,8},{48,16},{56,24},{1,33}... | collective-permute-start | bytes 110600 | tf_op jit(solution)/shard_map/ppermute | solution.py:55
  13.2 2.2 %shard_map.47 = (bf16[576,256]{1,0:T(8,128)(2,1)S(1)}, bf16[576,256]{1,0:T(8,128)(2,1)S(1)}, bf16[576,256]{1,0:T(8,128)(2,1)S(1)}, bf16[576,256]{1,0:T(8,128)(2,1)S(1)}, bf16[576,512]{1,0:T(8,128)(2,1)S(1)}) custom-call(s32[2]{0:T(128)S(1)} %copy-done.1, bf16[576,4096]{1,0:T(8,128)(2,1)} %bitcast.5), custom_call_target="tpu_custom_call" | custom-call | tf_op jit(solution)/shard_map/pallas_call | solution.py:280
  15.9 2.9 %collective-permute-start.6 = (bf16[576,256]{1,0:T(8,128)(2,1)S(1)}, bf16[576,256]{1,0:T(8,128)(2,1)S(1)}, u32[]{:S(2)}, u32[]{:S(2)}) collective-permute-start(bf16[576,256]{1,0:T(8,128)(2,1)S(1)} %get-tuple-element.51), channel_id=1, source_target_pairs={{0,3},{1,0},{2,1},{3,2},{4,7},{5,4},{6,5},{7,6},{8,11},{9,8},{10,9... | collective-permute-start | bytes 884744 | tf_op jit(solution)/shard_map/ppermute | solution.py:43
  19.6 3.2 %collective-permute-start.7 = (bf16[576,256]{1,0:T(8,128)(2,1)S(1)}, bf16[576,256]{1,0:T(8,128)(2,1)S(1)}, u32[]{:S(2)}, u32[]{:S(2)}) collective-permute-start(bf16[576,256]{1,0:T(8,128)(2,1)S(1)} %get-tuple-element.52), channel_id=1, source_target_pairs={{0,3},{1,0},{2,1},{3,2},{4,7},{5,4},{6,5},{7,6},{8,11},{9,8},{10,9... | collective-permute-start | bytes 884744 | tf_op jit(solution)/shard_map/ppermute | solution.py:43
  22.8 1.5 %collective-permute-start.12 = (bf16[64,576]{1,0:T(8,128)(2,1)S(1)}, bf16[64,576]{1,0:T(8,128)(2,1)S(1)}, u32[]{:S(2)}, u32[]{:S(2)}) collective-permute-start(bf16[64,576]{1,0:T(8,128)(2,1)S(1)} %pad_maximum_fusion.1), channel_id=1, source_target_pairs={{0,16},{8,24},{16,0},{24,8},{32,48},{40,56},{48,32},{56,40},{1,17}... | collective-permute-start | bytes 221192 | tf_op jit(solution)/shard_map/ppermute | solution.py:55
  24.3 4.9 %collective-permute-done.12 = bf16[64,576]{1,0:T(8,128)(2,1)S(1)} collective-permute-done((bf16[64,576]{1,0:T(8,128)(2,1)S(1)}, bf16[64,576]{1,0:T(8,128)(2,1)S(1)}, u32[]{:S(2)}, u32[]{:S(2)}) %collective-permute-start.12) | collective-permute-done | bytes 73760 | tf_op jit(solution)/shard_map/ppermute | solution.py:55
  29.4 3.1 %collective-permute-done.4.left_a = bf16[576,256]{1,0:T(8,128)(2,1)S(1)} collective-permute-done((bf16[576,256]{1,0:T(8,128)(2,1)S(1)}, bf16[576,256]{1,0:T(8,128)(2,1)S(1)}, u32[]{:S(2)}, u32[]{:S(2)}) %collective-permute-start.4) | collective-permute-done | bytes 294944 | tf_op jit(solution)/shard_map/ppermute | solution.py:43
  33.2 3.0 %collective-permute-start.10 = (bf16[576,512]{1,0:T(8,128)(2,1)S(1)}, bf16[576,512]{1,0:T(8,128)(2,1)S(1)}, u32[]{:S(2)}, u32[]{:S(2)}) collective-permute-start(bf16[576,512]{1,0:T(8,128)(2,1)S(1)} %shard_map.49.refs_0_), channel_id=1, source_target_pairs={{0,3},{1,0},{2,1},{3,2},{4,7},{5,4},{6,5},{7,6},{8,11},{9,8},{10,9... | collective-permute-start | bytes 1769480 | tf_op jit(solution)/shard_map/ppermute | solution.py:43
  36.9 2.4 %collective-permute-start.15 = (bf16[256,576]{1,0:T(8,128)(2,1)S(1)}, bf16[256,576]{1,0:T(8,128)(2,1)S(1)}, u32[]{:S(2)}, u32[]{:S(2)}) collective-permute-start(bf16[256,576]{1,0:T(8,128)(2,1)S(1)} %constant_dynamic-update-slice_fusion.q_ref), channel_id=1, source_target_pairs={{0,128},{64,192},{128,0},{192,64},{1,129},{65,193},{129,1},{193,65... | collective-permute-start | bytes 884744 | tf_op jit(solution)/shard_map/ppermute | solution.py:51
  39.3 1.2 %collective-permute-start.14 = (bf16[256,576]{1,0:T(8,128)(2,1)S(1)}, bf16[256,576]{1,0:T(8,128)(2,1)S(1)}, u32[]{:S(2)}, u32[]{:S(2)}) collective-permute-start(bf16[256,576]{1,0:T(8,128)(2,1)S(1)} %constant_dynamic-update-slice_fusion.q_ref), channel_id=1, source_target_pairs={{0,64},{64,0},{128,192},{192,128},{1,65},{65,1},{129,193},{193,129... | collective-permute-start | bytes 884744 | tf_op jit(solution)/shard_map/ppermute | solution.py:51
  40.5 7.9 %collective-permute-done.10.refs_2_ = bf16[576,512]{1,0:T(8,128)(2,1)S(1)} collective-permute-done((bf16[576,512]{1,0:T(8,128)(2,1)S(1)}, bf16[576,512]{1,0:T(8,128)(2,1)S(1)}, u32[]{:S(2)}, u32[]{:S(2)}) %collective-permute-start.10) | collective-permute-done | bytes 589856 | tf_op jit(solution)/shard_map/ppermute | solution.py:43
  48.4 3.8 %collective-permute-start.11 = (bf16[576,256]{1,0:T(8,128)(2,1)S(1)}, bf16[576,256]{1,0:T(8,128)(2,1)S(1)}, u32[]{:S(2)}, u32[]{:S(2)}) collective-permute-start(bf16[576,256]{1,0:T(8,128)(2,1)S(1)} %slice.9), channel_id=1, source_target_pairs={{0,3},{1,0},{2,1},{3,2},{4,7},{5,4},{6,5},{7,6},{8,11},{9,8},{10,9... | collective-permute-start | bytes 884744 | tf_op jit(solution)/shard_map/ppermute | solution.py:43
  54.0 3.1 %collective-permute-done.11.refs_4_ = bf16[576,256]{1,0:T(8,128)(2,1)S(1)} collective-permute-done((bf16[576,256]{1,0:T(8,128)(2,1)S(1)}, bf16[576,256]{1,0:T(8,128)(2,1)S(1)}, u32[]{:S(2)}, u32[]{:S(2)}) %collective-permute-start.11) | collective-permute-done | bytes 294944 | tf_op jit(solution)/shard_map/ppermute | solution.py:43
  57.1 3.7 %collective-permute-done.9.refs_3_ = bf16[576,256]{1,0:T(8,128)(2,1)S(1)} collective-permute-done((bf16[576,256]{1,0:T(8,128)(2,1)S(1)}, bf16[576,256]{1,0:T(8,128)(2,1)S(1)}, u32[]{:S(2)}, u32[]{:S(2)}) %collective-permute-start.9) | collective-permute-done | bytes 294944 | tf_op jit(solution)/shard_map/ppermute | solution.py:43
  61.3 1.1 %collective-permute-done.20.refs_8_ = bf16[576,256]{1,0:T(8,128)(2,1)S(1)} collective-permute-done((bf16[576,256]{1,0:T(8,128)(2,1)S(1)}, bf16[576,256]{1,0:T(8,128)(2,1)S(1)}, u32[]{:S(2)}, u32[]{:S(2)}) %collective-permute-start.20) | collective-permute-done | bytes 294944 | tf_op jit(solution)/shard_map/ppermute | solution.py:47
  62.8 4.1 %shard_map.50 = bf16[264,512]{1,0:T(8,128)(2,1)S(1)} custom-call(bf16[256,576]{1,0:T(8,128)(2,1)S(1)} %collective-permute-done.14.q_ref, s32[16]{0:T(128)S(1)} %copy-done.2, s32[2]{0:T(128)S(1)} %copy-done.1, s32[2]{0:T(128)S(1)} %collective-permute-done.3.hot_other_ref, bf16[576,512]{1,0:T(8,128)(2,1)S(1)} %shard_map.49.refs_0_, ...), custom_call_target="tpu_custom_call" | custom-call | tf_op jit(solution)/shard_map/pallas_call | solution.py:280
  67.8 4.1 %shard_map.51 = bf16[264,512]{1,0:T(8,128)(2,1)S(1)} custom-call(bf16[256,576]{1,0:T(8,128)(2,1)S(1)} %collective-permute-done.16.q_ref, s32[16]{0:T(128)S(1)} %copy-done.2, s32[2]{0:T(128)S(1)} %copy-done.1, s32[2]{0:T(128)S(1)} %collective-permute-done.3.hot_other_ref, bf16[576,512]{1,0:T(8,128)(2,1)S(1)} %shard_map.49.refs_0_, ...), custom_call_target="tpu_custom_call" | custom-call | tf_op jit(solution)/shard_map/pallas_call | solution.py:280
  71.9 1.5 %collective-permute-start.23 = (bf16[264,512]{1,0:T(8,128)(2,1)S(1)}, bf16[264,512]{1,0:T(8,128)(2,1)S(1)}, u32[]{:S(2)}, u32[]{:S(2)}) collective-permute-start(bf16[264,512]{1,0:T(8,128)(2,1)S(1)} %shard_map.51), channel_id=1, source_target_pairs={{0,192},{64,128},{128,64},{192,0},{1,193},{65,129},{129,65},{193,1... | collective-permute-start | bytes 811016 | tf_op jit(solution)/shard_map/ppermute | solution.py:51
  73.3 2.2 %collective-permute-done.22.refs_0_ = bf16[264,512]{1,0:T(8,128)(2,1)S(1)} collective-permute-done((bf16[264,512]{1,0:T(8,128)(2,1)S(1)}, bf16[264,512]{1,0:T(8,128)(2,1)S(1)}, u32[]{:S(2)}, u32[]{:S(2)}) %collective-permute-start.22) | collective-permute-done | bytes 270368 | tf_op jit(solution)/shard_map/ppermute | solution.py:51
  75.5 4.1 %shard_map.52 = bf16[264,512]{1,0:T(8,128)(2,1)S(1)} custom-call(bf16[256,576]{1,0:T(8,128)(2,1)S(1)} %collective-permute-done.15.q_ref, s32[16]{0:T(128)S(1)} %copy-done.2, s32[2]{0:T(128)S(1)} %copy-done.1, s32[2]{0:T(128)S(1)} %collective-permute-done.3.hot_other_ref, bf16[576,512]{1,0:T(8,128)(2,1)S(1)} %shard_map.49.refs_0_, ...), custom_call_target="tpu_custom_call" | custom-call | tf_op jit(solution)/shard_map/pallas_call | solution.py:280
  79.6 1.5 %collective-permute-start.24 = (bf16[264,512]{1,0:T(8,128)(2,1)S(1)}, bf16[264,512]{1,0:T(8,128)(2,1)S(1)}, u32[]{:S(2)}, u32[]{:S(2)}) collective-permute-start(bf16[264,512]{1,0:T(8,128)(2,1)S(1)} %shard_map.52), channel_id=1, source_target_pairs={{0,128},{64,192},{128,0},{192,64},{1,129},{65,193},{129,1},{193,65... | collective-permute-start | bytes 811016 | tf_op jit(solution)/shard_map/ppermute | solution.py:51
  81.7 4.1 %shard_map.53.refs_3_ = bf16[264,512]{1,0:T(8,128)(2,1)S(1)} custom-call(bf16[256,576]{1,0:T(8,128)(2,1)S(1)} %constant_dynamic-update-slice_fusion.q_ref, s32[16]{0:T(128)S(1)} %copy-done.2, s32[2]{0:T(128)S(1)} %copy-done.1, s32[2]{0:T(128)S(1)} %collective-permute-done.3.hot_other_ref, bf16[576,512]{1,0:T(8,128)(2,1)S(1)} %shard_map.49.refs_0_, ...), custom_call_target="tpu_custom_call" | custom-call | tf_op jit(solution)/shard_map/pallas_call | solution.py:280
  85.7 3.1 %collective-permute-done.24.refs_2_ = bf16[264,512]{1,0:T(8,128)(2,1)S(1)} collective-permute-done((bf16[264,512]{1,0:T(8,128)(2,1)S(1)}, bf16[264,512]{1,0:T(8,128)(2,1)S(1)}, u32[]{:S(2)}, u32[]{:S(2)}) %collective-permute-start.24) | collective-permute-done | bytes 270368 | tf_op jit(solution)/shard_map/ppermute | solution.py:51
  89.5 1.6 %collective-permute-start.26 = (bf16[32,640]{1,0:T(8,128)(2,1)S(1)}, bf16[32,640]{1,0:T(8,128)(2,1)S(1)}, u32[]{:S(2)}, u32[]{:S(2)}) collective-permute-start(bf16[32,640]{1,0:T(8,128)(2,1)S(1)} %get-tuple-element.75), channel_id=1, source_target_pairs={{0,16},{8,24},{16,0},{24,8},{32,48},{40,56},{48,32},{56,40},{1,17}... | collective-permute-start | bytes 122888 | tf_op jit(solution)/shard_map/ppermute | solution.py:55
  91.1 4.9 %collective-permute-start.27 = (bf16[32,640]{1,0:T(8,128)(2,1)S(1)}, bf16[32,640]{1,0:T(8,128)(2,1)S(1)}, u32[]{:S(2)}, u32[]{:S(2)}) collective-permute-start(bf16[32,640]{1,0:T(8,128)(2,1)S(1)} %get-tuple-element.76), channel_id=1, source_target_pairs={{0,48},{8,56},{16,32},{24,40},{32,16},{40,24},{48,0},{56,8},{1,49}... | collective-permute-start | bytes 122888 | tf_op jit(solution)/shard_map/ppermute | solution.py:55
  96.0 1.0 collective-permute-start.28
  97.5 1.9 %collective-permute-start.30 = (bf16[32,640]{1,0:T(8,128)(2,1)S(1)}, bf16[32,640]{1,0:T(8,128)(2,1)S(1)}, u32[]{:S(2)}, u32[]{:S(2)}) collective-permute-start(bf16[32,640]{1,0:T(8,128)(2,1)S(1)} %get-tuple-element.79), channel_id=1, source_target_pairs={{0,24},{8,16},{16,8},{24,0},{32,56},{40,48},{48,40},{56,32},{1,25}... | collective-permute-start | bytes 122888 | tf_op jit(solution)/shard_map/ppermute | solution.py:55
  99.4 3.7 %collective-permute-start.31 = (bf16[32,640]{1,0:T(8,128)(2,1)S(1)}, bf16[32,640]{1,0:T(8,128)(2,1)S(1)}, u32[]{:S(2)}, u32[]{:S(2)}) collective-permute-start(bf16[32,640]{1,0:T(8,128)(2,1)S(1)} %get-tuple-element.80), channel_id=1, source_target_pairs={{0,56},{8,48},{16,40},{24,32},{32,24},{40,16},{48,8},{56,0},{1,57}... | collective-permute-start | bytes 122888 | tf_op jit(solution)/shard_map/ppermute | solution.py:55
  104.1 1.4 %collective-permute-done.31.refs_7_ = bf16[32,640]{1,0:T(8,128)(2,1)S(1)} collective-permute-done((bf16[32,640]{1,0:T(8,128)(2,1)S(1)}, bf16[32,640]{1,0:T(8,128)(2,1)S(1)}, u32[]{:S(2)}, u32[]{:S(2)}) %collective-permute-start.31) | collective-permute-done | bytes 40992 | tf_op jit(solution)/shard_map/ppermute | solution.py:55
  (59 shorter events, 10.8 us)
Async XLA Ops:
  2.5 16.3 %collective-permute-start = (bf16[576,256]{1,0:T(8,128)(2,1)S(1)}, bf16[576,256]{1,0:T(8,128)(2,1)S(1)}, u32[]{:S(2)}, u32[]{:S(2)}) collective-permute-start(bf16[576,256]{1,0:T(8,128)(2,1)S(1)} %get-tuple-element.43), channel_id=1, source_target_pairs={{0,1},{1,2},{2,3},{3,0},{4,5},{5,6},{6,7},{7,4},{8,9},{9,10},{10,1... | collective-permute-start | bytes 884744 | tf_op jit(solution)/shard_map/ppermute | solution.py:43
  4.1 14.7 %collective-permute-start.1 = (bf16[576,256]{1,0:T(8,128)(2,1)S(1)}, bf16[576,256]{1,0:T(8,128)(2,1)S(1)}, u32[]{:S(2)}, u32[]{:S(2)}) collective-permute-start(bf16[576,256]{1,0:T(8,128)(2,1)S(1)} %get-tuple-element.44), channel_id=1, source_target_pairs={{0,3},{1,0},{2,1},{3,2},{4,7},{5,4},{6,5},{7,6},{8,11},{9,8},{10,9... | collective-permute-start | bytes 884744 | tf_op jit(solution)/shard_map/ppermute | solution.py:43
  5.9 10.0 %collective-permute-start.2 = (bf16[32,576]{1,0:T(8,128)(2,1)S(1)}, bf16[32,576]{1,0:T(8,128)(2,1)S(1)}, u32[]{:S(2)}, u32[]{:S(2)}) collective-permute-start(bf16[32,576]{1,0:T(8,128)(2,1)S(1)} %bitcast.6), channel_id=1, source_target_pairs={{0,32},{8,40},{16,48},{24,56},{32,0},{40,8},{48,16},{56,24},{1,33}... | collective-permute-start | bytes 110600 | tf_op jit(solution)/shard_map/ppermute | solution.py:55
  13.2 5.6 %collective-permute-start.3 = (s32[2]{0:T(128)S(1)}, s32[2]{0:T(128)S(1)}, u32[]{:S(2)}, u32[]{:S(2)}) collective-permute-start(s32[2]{0:T(128)S(1)} %copy-done.1), channel_id=1, source_target_pairs={{0,4},{4,0},{1,5},{5,1},{2,6},{6,2},{3,7},{7,3},{8,12},{12,8},{9,1... | collective-permute-start | bytes 32 | tf_op jit(solution)/shard_map/ppermute | solution.py:47
  15.4 13.9 %collective-permute-start.5 = (bf16[576,256]{1,0:T(8,128)(2,1)S(1)}, bf16[576,256]{1,0:T(8,128)(2,1)S(1)}, u32[]{:S(2)}, u32[]{:S(2)}) collective-permute-start(bf16[576,256]{1,0:T(8,128)(2,1)S(1)} %get-tuple-element.50), channel_id=1, source_target_pairs={{0,1},{1,2},{2,3},{3,0},{4,5},{5,6},{6,7},{7,4},{8,9},{9,10},{10,1... | collective-permute-start | bytes 884744 | tf_op jit(solution)/shard_map/ppermute | solution.py:43
  15.9 13.5 %collective-permute-start.6 = (bf16[576,256]{1,0:T(8,128)(2,1)S(1)}, bf16[576,256]{1,0:T(8,128)(2,1)S(1)}, u32[]{:S(2)}, u32[]{:S(2)}) collective-permute-start(bf16[576,256]{1,0:T(8,128)(2,1)S(1)} %get-tuple-element.51), channel_id=1, source_target_pairs={{0,3},{1,0},{2,1},{3,2},{4,7},{5,4},{6,5},{7,6},{8,11},{9,8},{10,9... | collective-permute-start | bytes 884744 | tf_op jit(solution)/shard_map/ppermute | solution.py:43
  19.5 13.0 %collective-permute-start.4 = (bf16[576,256]{1,0:T(8,128)(2,1)S(1)}, bf16[576,256]{1,0:T(8,128)(2,1)S(1)}, u32[]{:S(2)}, u32[]{:S(2)}) collective-permute-start(bf16[576,256]{1,0:T(8,128)(2,1)S(1)} %get-tuple-element.49), channel_id=1, source_target_pairs={{0,1},{1,2},{2,3},{3,0},{4,5},{5,6},{6,7},{7,4},{8,9},{9,10},{10,1... | collective-permute-start | bytes 884744 | tf_op jit(solution)/shard_map/ppermute | solution.py:43
  19.6 12.9 %collective-permute-start.7 = (bf16[576,256]{1,0:T(8,128)(2,1)S(1)}, bf16[576,256]{1,0:T(8,128)(2,1)S(1)}, u32[]{:S(2)}, u32[]{:S(2)}) collective-permute-start(bf16[576,256]{1,0:T(8,128)(2,1)S(1)} %get-tuple-element.52), channel_id=1, source_target_pairs={{0,3},{1,0},{2,1},{3,2},{4,7},{5,4},{6,5},{7,6},{8,11},{9,8},{10,9... | collective-permute-start | bytes 884744 | tf_op jit(solution)/shard_map/ppermute | solution.py:43
  22.8 6.4 %collective-permute-start.12 = (bf16[64,576]{1,0:T(8,128)(2,1)S(1)}, bf16[64,576]{1,0:T(8,128)(2,1)S(1)}, u32[]{:S(2)}, u32[]{:S(2)}) collective-permute-start(bf16[64,576]{1,0:T(8,128)(2,1)S(1)} %pad_maximum_fusion.1), channel_id=1, source_target_pairs={{0,16},{8,24},{16,0},{24,8},{32,48},{40,56},{48,32},{56,40},{1,17}... | collective-permute-start | bytes 221192 | tf_op jit(solution)/shard_map/ppermute | solution.py:55
  29.2 7.0 %collective-permute-start.13 = (bf16[128,576]{1,0:T(8,128)(2,1)S(1)}, bf16[128,576]{1,0:T(8,128)(2,1)S(1)}, u32[]{:S(2)}, u32[]{:S(2)}) collective-permute-start(bf16[128,576]{1,0:T(8,128)(2,1)S(1)} %pad_maximum_fusion), channel_id=1, source_target_pairs={{0,8},{8,0},{16,24},{24,16},{32,40},{40,32},{48,56},{56,48},{1,9},... | collective-permute-start | bytes 442376 | tf_op jit(solution)/shard_map/ppermute | solution.py:55
  33.2 15.2 %collective-permute-start.10 = (bf16[576,512]{1,0:T(8,128)(2,1)S(1)}, bf16[576,512]{1,0:T(8,128)(2,1)S(1)}, u32[]{:S(2)}, u32[]{:S(2)}) collective-permute-start(bf16[576,512]{1,0:T(8,128)(2,1)S(1)} %shard_map.49.refs_0_), channel_id=1, source_target_pairs={{0,3},{1,0},{2,1},{3,2},{4,7},{5,4},{6,5},{7,6},{8,11},{9,8},{10,9... | collective-permute-start | bytes 1769480 | tf_op jit(solution)/shard_map/ppermute | solution.py:43
  36.2 16.0 %collective-permute-start.8 = (bf16[576,512]{1,0:T(8,128)(2,1)S(1)}, bf16[576,512]{1,0:T(8,128)(2,1)S(1)}, u32[]{:S(2)}, u32[]{:S(2)}) collective-permute-start(bf16[576,512]{1,0:T(8,128)(2,1)S(1)} %shard_map.49.refs_0_), channel_id=1, source_target_pairs={{0,1},{1,2},{2,3},{3,0},{4,5},{5,6},{6,7},{7,4},{8,9},{9,10},{10,1... | collective-permute-start | bytes 1769480 | tf_op jit(solution)/shard_map/ppermute | solution.py:43
  36.3 17.1 %collective-permute-start.16 = (bf16[256,576]{1,0:T(8,128)(2,1)S(1)}, bf16[256,576]{1,0:T(8,128)(2,1)S(1)}, u32[]{:S(2)}, u32[]{:S(2)}) collective-permute-start(bf16[256,576]{1,0:T(8,128)(2,1)S(1)} %constant_dynamic-update-slice_fusion.q_ref), channel_id=1, source_target_pairs={{0,192},{64,128},{128,64},{192,0},{1,193},{65,129},{129,65},{193,1... | collective-permute-start | bytes 884744 | tf_op jit(solution)/shard_map/ppermute | solution.py:51
  36.9 16.5 %collective-permute-start.15 = (bf16[256,576]{1,0:T(8,128)(2,1)S(1)}, bf16[256,576]{1,0:T(8,128)(2,1)S(1)}, u32[]{:S(2)}, u32[]{:S(2)}) collective-permute-start(bf16[256,576]{1,0:T(8,128)(2,1)S(1)} %constant_dynamic-update-slice_fusion.q_ref), channel_id=1, source_target_pairs={{0,128},{64,192},{128,0},{192,64},{1,129},{65,193},{129,1},{193,65... | collective-permute-start | bytes 884744 | tf_op jit(solution)/shard_map/ppermute | solution.py:51
  39.3 14.7 %collective-permute-start.14 = (bf16[256,576]{1,0:T(8,128)(2,1)S(1)}, bf16[256,576]{1,0:T(8,128)(2,1)S(1)}, u32[]{:S(2)}, u32[]{:S(2)}) collective-permute-start(bf16[256,576]{1,0:T(8,128)(2,1)S(1)} %constant_dynamic-update-slice_fusion.q_ref), channel_id=1, source_target_pairs={{0,64},{64,0},{128,192},{192,128},{1,65},{65,1},{129,193},{193,129... | collective-permute-start | bytes 884744 | tf_op jit(solution)/shard_map/ppermute | solution.py:51
  48.4 8.7 %collective-permute-start.11 = (bf16[576,256]{1,0:T(8,128)(2,1)S(1)}, bf16[576,256]{1,0:T(8,128)(2,1)S(1)}, u32[]{:S(2)}, u32[]{:S(2)}) collective-permute-start(bf16[576,256]{1,0:T(8,128)(2,1)S(1)} %slice.9), channel_id=1, source_target_pairs={{0,3},{1,0},{2,1},{3,2},{4,7},{5,4},{6,5},{7,6},{8,11},{9,8},{10,9... | collective-permute-start | bytes 884744 | tf_op jit(solution)/shard_map/ppermute | solution.py:43
  52.2 8.6 %collective-permute-start.9 = (bf16[576,256]{1,0:T(8,128)(2,1)S(1)}, bf16[576,256]{1,0:T(8,128)(2,1)S(1)}, u32[]{:S(2)}, u32[]{:S(2)}) collective-permute-start(bf16[576,256]{1,0:T(8,128)(2,1)S(1)} %slice.8), channel_id=1, source_target_pairs={{0,1},{1,2},{2,3},{3,0},{4,5},{5,6},{6,7},{7,4},{8,9},{9,10},{10,1... | collective-permute-start | bytes 884744 | tf_op jit(solution)/shard_map/ppermute | solution.py:43
  53.4 7.9 %collective-permute-start.17 = (bf16[576,512]{1,0:T(8,128)(2,1)S(1)}, bf16[576,512]{1,0:T(8,128)(2,1)S(1)}, u32[]{:S(2)}, u32[]{:S(2)}) collective-permute-start(bf16[576,512]{1,0:T(8,128)(2,1)S(1)} %shard_map.49.refs_0_), channel_id=1, source_target_pairs={{0,4},{4,0},{1,5},{5,1},{2,6},{6,2},{3,7},{7,3},{8,12},{12,8},{9,1... | collective-permute-start | bytes 1769480 | tf_op jit(solution)/shard_map/ppermute | solution.py:47
  53.4 7.9 %collective-permute-start.19 = (bf16[576,512]{1,0:T(8,128)(2,1)S(1)}, bf16[576,512]{1,0:T(8,128)(2,1)S(1)}, u32[]{:S(2)}, u32[]{:S(2)}) collective-permute-start(bf16[576,512]{1,0:T(8,128)(2,1)S(1)} %collective-permute-done.10.refs_2_), channel_id=1, source_target_pairs={{0,4},{4,0},{1,5},{5,1},{2,6},{6,2},{3,7},{7,3},{8,12},{12,8},{9,1... | collective-permute-start | bytes 1769480 | tf_op jit(solution)/shard_map/ppermute | solution.py:47
  54.0 8.8 %collective-permute-start.18 = (bf16[576,512]{1,0:T(8,128)(2,1)S(1)}, bf16[576,512]{1,0:T(8,128)(2,1)S(1)}, u32[]{:S(2)}, u32[]{:S(2)}) collective-permute-start(bf16[576,512]{1,0:T(8,128)(2,1)S(1)} %collective-permute-done.8.refs_1_), channel_id=1, source_target_pairs={{0,4},{4,0},{1,5},{5,1},{2,6},{6,2},{3,7},{7,3},{8,12},{12,8},{9,1... | collective-permute-start | bytes 1769480 | tf_op jit(solution)/shard_map/ppermute | solution.py:47
  60.8 1.6 %collective-permute-start.20 = (bf16[576,256]{1,0:T(8,128)(2,1)S(1)}, bf16[576,256]{1,0:T(8,128)(2,1)S(1)}, u32[]{:S(2)}, u32[]{:S(2)}) collective-permute-start(bf16[576,256]{1,0:T(8,128)(2,1)S(1)} %collective-permute-done.9.refs_3_), channel_id=1, source_target_pairs={{0,4},{4,0},{1,5},{5,1},{2,6},{6,2},{3,7},{7,3},{8,12},{12,8},{9,1... | collective-permute-start | bytes 884744 | tf_op jit(solution)/shard_map/ppermute | solution.py:47
  60.8 2.0 %collective-permute-start.21 = (bf16[576,256]{1,0:T(8,128)(2,1)S(1)}, bf16[576,256]{1,0:T(8,128)(2,1)S(1)}, u32[]{:S(2)}, u32[]{:S(2)}) collective-permute-start(bf16[576,256]{1,0:T(8,128)(2,1)S(1)} %collective-permute-done.11.refs_4_), channel_id=1, source_target_pairs={{0,4},{4,0},{1,5},{5,1},{2,6},{6,2},{3,7},{7,3},{8,12},{12,8},{9,1... | collective-permute-start | bytes 884744 | tf_op jit(solution)/shard_map/ppermute | solution.py:47
  66.9 8.6 %collective-permute-start.22 = (bf16[264,512]{1,0:T(8,128)(2,1)S(1)}, bf16[264,512]{1,0:T(8,128)(2,1)S(1)}, u32[]{:S(2)}, u32[]{:S(2)}) collective-permute-start(bf16[264,512]{1,0:T(8,128)(2,1)S(1)} %shard_map.50), channel_id=1, source_target_pairs={{0,64},{64,0},{128,192},{192,128},{1,65},{65,1},{129,193},{193,129... | collective-permute-start | bytes 811016 | tf_op jit(solution)/shard_map/ppermute | solution.py:51
  71.9 9.8 %collective-permute-start.23 = (bf16[264,512]{1,0:T(8,128)(2,1)S(1)}, bf16[264,512]{1,0:T(8,128)(2,1)S(1)}, u32[]{:S(2)}, u32[]{:S(2)}) collective-permute-start(bf16[264,512]{1,0:T(8,128)(2,1)S(1)} %shard_map.51), channel_id=1, source_target_pairs={{0,192},{64,128},{128,64},{192,0},{1,193},{65,129},{129,65},{193,1... | collective-permute-start | bytes 811016 | tf_op jit(solution)/shard_map/ppermute | solution.py:51
  79.6 9.3 %collective-permute-start.24 = (bf16[264,512]{1,0:T(8,128)(2,1)S(1)}, bf16[264,512]{1,0:T(8,128)(2,1)S(1)}, u32[]{:S(2)}, u32[]{:S(2)}) collective-permute-start(bf16[264,512]{1,0:T(8,128)(2,1)S(1)} %shard_map.52), channel_id=1, source_target_pairs={{0,128},{64,192},{128,0},{192,64},{1,129},{65,193},{129,1},{193,65... | collective-permute-start | bytes 811016 | tf_op jit(solution)/shard_map/ppermute | solution.py:51
  89.4 8.1 %collective-permute-start.25 = (bf16[32,640]{1,0:T(8,128)(2,1)S(1)}, bf16[32,640]{1,0:T(8,128)(2,1)S(1)}, u32[]{:S(2)}, u32[]{:S(2)}) collective-permute-start(bf16[32,640]{1,0:T(8,128)(2,1)S(1)} %get-tuple-element.74), channel_id=1, source_target_pairs={{0,32},{8,40},{16,48},{24,56},{32,0},{40,8},{48,16},{56,24},{1,33}... | collective-permute-start | bytes 122888 | tf_op jit(solution)/shard_map/ppermute | solution.py:55
  89.5 9.9 %collective-permute-start.26 = (bf16[32,640]{1,0:T(8,128)(2,1)S(1)}, bf16[32,640]{1,0:T(8,128)(2,1)S(1)}, u32[]{:S(2)}, u32[]{:S(2)}) collective-permute-start(bf16[32,640]{1,0:T(8,128)(2,1)S(1)} %get-tuple-element.75), channel_id=1, source_target_pairs={{0,16},{8,24},{16,0},{24,8},{32,48},{40,56},{48,32},{56,40},{1,17}... | collective-permute-start | bytes 122888 | tf_op jit(solution)/shard_map/ppermute | solution.py:55
  91.1 12.0 %collective-permute-start.27 = (bf16[32,640]{1,0:T(8,128)(2,1)S(1)}, bf16[32,640]{1,0:T(8,128)(2,1)S(1)}, u32[]{:S(2)}, u32[]{:S(2)}) collective-permute-start(bf16[32,640]{1,0:T(8,128)(2,1)S(1)} %get-tuple-element.76), channel_id=1, source_target_pairs={{0,48},{8,56},{16,32},{24,40},{32,16},{40,24},{48,0},{56,8},{1,49}... | collective-permute-start | bytes 122888 | tf_op jit(solution)/shard_map/ppermute | solution.py:55
  96.0 7.1 %collective-permute-start.28 = (bf16[32,640]{1,0:T(8,128)(2,1)S(1)}, bf16[32,640]{1,0:T(8,128)(2,1)S(1)}, u32[]{:S(2)}, u32[]{:S(2)}) collective-permute-start(bf16[32,640]{1,0:T(8,128)(2,1)S(1)} %get-tuple-element.77), channel_id=1, source_target_pairs={{0,8},{8,0},{16,24},{24,16},{32,40},{40,32},{48,56},{56,48},{1,9},... | collective-permute-start | bytes 122888 | tf_op jit(solution)/shard_map/ppermute | solution.py:55
  97.1 7.0 %collective-permute-start.29 = (bf16[32,640]{1,0:T(8,128)(2,1)S(1)}, bf16[32,640]{1,0:T(8,128)(2,1)S(1)}, u32[]{:S(2)}, u32[]{:S(2)}) collective-permute-start(bf16[32,640]{1,0:T(8,128)(2,1)S(1)} %get-tuple-element.78), channel_id=1, source_target_pairs={{0,40},{8,32},{16,56},{24,48},{32,8},{40,0},{48,24},{56,16},{1,41}... | collective-permute-start | bytes 122888 | tf_op jit(solution)/shard_map/ppermute | solution.py:55
  97.5 6.6 %collective-permute-start.30 = (bf16[32,640]{1,0:T(8,128)(2,1)S(1)}, bf16[32,640]{1,0:T(8,128)(2,1)S(1)}, u32[]{:S(2)}, u32[]{:S(2)}) collective-permute-start(bf16[32,640]{1,0:T(8,128)(2,1)S(1)} %get-tuple-element.79), channel_id=1, source_target_pairs={{0,24},{8,16},{16,8},{24,0},{32,56},{40,48},{48,40},{56,32},{1,25}... | collective-permute-start | bytes 122888 | tf_op jit(solution)/shard_map/ppermute | solution.py:55
  99.4 6.1 %collective-permute-start.31 = (bf16[32,640]{1,0:T(8,128)(2,1)S(1)}, bf16[32,640]{1,0:T(8,128)(2,1)S(1)}, u32[]{:S(2)}, u32[]{:S(2)}) collective-permute-start(bf16[32,640]{1,0:T(8,128)(2,1)S(1)} %get-tuple-element.80), channel_id=1, source_target_pairs={{0,56},{8,48},{16,40},{24,32},{32,24},{40,16},{48,8},{56,0},{1,57}... | collective-permute-start | bytes 122888 | tf_op jit(solution)/shard_map/ppermute | solution.py:55
  (4 other events, 75.9 us)

commit v11 on v6

--- a/solution.py
+++ b/solution.py
@@ -29,6 +29,7 @@
 Z_ORDER = (0, 4, 2, 6, 1, 5, 3, 7)
 SCALE = QK**-0.5
 LOG2_E = 1.4426950408889634
+N_FAR = N_Z // 2
 f32 = jnp.float32
 bf16 = jnp.bfloat16
 
@@ -81,16 +82,17 @@
     run_copies(copies)
 
 
-def own_cut_kernel(hot_ref, lat_ref, right_ref, left_ref, mine_ref, sems):
+def own_cut_kernel(hot_ref, lat_ref, right_a, right_b, left_a, left_b, mine_ref, sems):
     rank = lax.axis_index("rep")
     copies = []
-    for hop, dst in ((1, right_ref), (3, left_ref), (0, mine_ref)):
-        for half in range(2):
+    for hop, halves in ((1, (right_a, right_b)), (3, (left_a, left_b)), (0, (mine_ref, mine_ref))):
+        for half, dst in enumerate(halves):
             for slot in range(HOT_GRP):
+                to = slot * HALF + (half * PAIR if hop == 0 else 0)
                 copies.append(
                     pltpu.make_async_copy(
                         lat_ref.at[:, column(hot_ref, slot, (rank + hop) % N_REP, half)],
-                        dst.at[:, pl.ds(half * PAIR + slot * HALF, HALF)],
+                        dst.at[:, pl.ds(to, HALF)],
                         sems.at[len(copies)],
                     )
                 )
@@ -99,25 +101,22 @@
 
 def pass_on_kernel(hot_ref, from_left, from_right, right_in, left_in, right_ref, left_ref):
     rank = lax.axis_index("rep")
-    right_ref[:, PAIR:] = right_in[:, PAIR:]
-    left_ref[:, :PAIR] = left_in[:, :PAIR]
     for slot in range(HOT_GRP):
         a = slice(slot * HALF, (slot + 1) * HALF)
-        b = slice(PAIR + slot * HALF, PAIR + (slot + 1) * HALF)
         here = hot_ref[slot] // PER_DEV == rank
 
         @pl.when(here)
         def _():
             right_ref[:, a] = right_in[:, a]
-            left_ref[:, b] = left_in[:, b]
+            left_ref[:, a] = left_in[:, a]
 
         @pl.when(jnp.logical_not(here))
         def _():
             right_ref[:, a] = from_left[:, a]
-            left_ref[:, b] = from_right[:, a]
-
-
-def settle_kernel(hot_ref, from_left, from_right, mine_in, mine_ref):
+            left_ref[:, a] = from_right[:, a]
+
+
+def settle_kernel(hot_ref, left_a, left_b, right_a, right_b, mine_in, mine_ref):
     rank = lax.axis_index("rep")
     for slot in range(HOT_GRP):
         a = slice(slot * HALF, (slot + 1) * HALF)
@@ -131,19 +130,19 @@
 
         @pl.when(away >= 2)
         def _():
-            mine_ref[:, a] = from_left[:, a]
+            mine_ref[:, a] = left_a[:, a]
 
         @pl.when(away == 1)
         def _():
-            mine_ref[:, a] = from_right[:, a]
+            mine_ref[:, a] = right_a[:, a]
 
         @pl.when(away == 3)
         def _():
-            mine_ref[:, b] = from_left[:, b]
+            mine_ref[:, b] = left_b[:, a]
 
         @pl.when((away == 1) | (away == 2))
         def _():
-            mine_ref[:, b] = from_right[:, b]
+            mine_ref[:, b] = right_b[:, a]
 
 
 def three_terms(v):
@@ -321,42 +320,39 @@
         mib=50,
         scratch_shapes=[pltpu.SemaphoreType.DMA((4,))],
     )
+    up, down = shift_rep(up, 1), shift_rep(down, -1)
     own = queries.reshape(count, -1, WIDTH).transpose(1, 0, 2).reshape(-1, WIDTH)
     near = jnp.concatenate([own, cross_z(own, 4)], axis=0)
-    up, down, near = lax.optimization_barrier((up, down, near))
-    up, down = shift_rep(up, 1), shift_rep(down, -1)
-    near = jnp.concatenate([near, cross_z(near, 2)], axis=0)
-    right, left, mine = call(
+    hot_other = swap_core(hot_ids)
+    right_a, right_b, left_a, left_b, mine = call(
         own_cut_kernel,
-        [chunk] * 3,
+        [pair] * 4 + [chunk],
         [SMEM, ANY],
         [hot_ids, by_column],
         mib=50,
         scratch_shapes=[pltpu.SemaphoreType.DMA((12,))],
     )
-    up, down, near = lax.optimization_barrier((up, down, near))
-    right, left = call(
+    from_left_b, from_right_a = shift_rep(right_b, 1), shift_rep(left_a, -1)
+    up, down, near, hot_other = lax.optimization_barrier((up, down, near, hot_other))
+    right_a, left_b = call(
         pass_on_kernel,
-        [chunk] * 2,
+        [pair] * 2,
         [SMEM] + [VMEM] * 4,
-        [hot_ids, up, down, right, left],
-    )
-    from_left, from_right = shift_rep(right, 1), shift_rep(left, -1)
-    near = jnp.concatenate([near, cross_z(near, 1)], axis=0)
-    asked = [near] + [cross_x(near, bits) for bits in range(1, N_X)]
-    from_left, from_right, asked[1], asked[3] = lax.optimization_barrier(
-        (from_left, from_right, asked[1], asked[3])
-    )
+        [hot_ids, up, down, right_a, left_b],
+    )
+    from_left_a, from_right_b = shift_rep(right_a, 1), shift_rep(left_b, -1)
+    for bits in (2, 1):
+        near = jnp.concatenate([near, cross_z(near, bits)], axis=0)
     (mine,) = call(
         settle_kernel,
         [chunk],
-        [SMEM] + [VMEM] * 3,
-        [hot_ids, from_left, from_right, mine],
-    )
-    hot_other = swap_core(hot_ids)
+        [SMEM] + [VMEM] * 5,
+        [hot_ids, from_left_a, from_left_b, from_right_a, from_right_b, mine],
+    )
+    asked = [near] + [cross_x(near, bits) for bits in range(1, N_X)]
 
     of_left, of_right = shift_rep(mine, 1), shift_rep(mine, -1)
-    of_left, of_right, asked[2] = lax.optimization_barrier((of_left, of_right, asked[2]))
+    of_left, of_right, *asked = lax.optimization_barrier((of_left, of_right, *asked))
     far_a, far_b = shift_rep(of_left[:, :PAIR], 1), shift_rep(of_right[:, PAIR:], -1)
     keys = [mine, of_left, of_right]
     swapped = [swap_core(k) for k in keys]

time: 111 us -> 111 us (level)
  starting transfers between devices: 42.5 us -> 47.7 us
  waiting for transfers between devices: 41 us -> 37.5 us
    ppermute x8 -> x10, starting transfers between devices: 10.8 us -> 16 us  [shift_rep(): return lax.ppermute(a, 'rep', [(i, (i + by) % N_REP) for i in range(N_REP)])]
    ppermute x10, waiting for transfers between devices: 10.6 us -> 7.34 us  [cross_z(): return lax.ppermute(a, 'z', [(i, i ^ bits) for i in range(N_Z)])]
    ppermute x6, starting transfers between devices: 6.68 us -> 8.02 us  [cross_x(): return lax.ppermute(a, 'x', [(i, i ^ bits) for i in range(N_X)])]
    ppermute x10, starting transfers between devices: 23.9 us -> 22.6 us  [cross_z(): return lax.ppermute(a, 'z', [(i, i ^ bits) for i in range(N_Z)])]
    ppermute x8 -> x10, waiting for transfers between devices: 6.18 us -> 6.72 us  [shift_rep(): return lax.ppermute(a, 'rep', [(i, (i + by) % N_REP) for i in range(N_REP)])]
  transfers between devices with their start and end apart: 30 -> 32, of which waited for: 18 -> 13; matrix products, arithmetic and copies ran while one was open for 0% -> 0% of each run, Pallas kernels for 17% -> 17%
where the time goes in v11:
time: 111 us
  starting transfers between devices  47.7 us (43%)
  waiting for transfers between devices  37.5 us (34%)
  Pallas kernels  24.3 us (22%)
    pallas_call x12, Pallas kernels, call(): pl.pallas_call(kernel, out_shape=tuple((jax.ShapeDtypeStruct(*o) for o in...  24.3 us
    ppermute x10, starting transfers between devices, cross_z(): return lax.ppermute(a, 'z', [(i, i ^ bits) for i in range(N_Z)])  22.6 us
    ppermute x6, waiting for transfers between devices, cross_x(): return lax.ppermute(a, 'x', [(i, i ^ bits) for i in range(N_X)])  22 us
    ppermute x10, starting transfers between devices, shift_rep(): return lax.ppermute(a, 'rep', [(i, (i + by) % N_REP) for i in range(N_REP)])  16 us
    ppermute x6, starting transfers between devices, cross_x(): return lax.ppermute(a, 'x', [(i, i ^ bits) for i in range(N_X)])  8.02 us
    ppermute x10, waiting for transfers between devices, cross_z(): return lax.ppermute(a, 'z', [(i, i ^ bits) for i in range(N_Z)])  7.34 us
    ppermute x10, waiting for transfers between devices, shift_rep(): return lax.ppermute(a, 'rep', [(i, (i + by) % N_REP) for i in range(N_REP)])  6.72 us
  transfers between devices with their start and end apart: 32, of which 13 were waited for; matrix products, arithmetic and copies ran while one was open for 0% of the time, Pallas kernels for 17%

profile of v11, /device:TPU:6, one launch (start us, length us, event | category | flops | bytes accessed | tf_op | source)
XLA Modules:
  0.0 110.7 jit_solution(10739434295960080001)
XLA Ops:
  0.7 1.7 %shard_map.46 = (bf16[576,256]{1,0:T(8,128)(2,1)S(1)}, bf16[576,256]{1,0:T(8,128)(2,1)S(1)}) custom-call(s32[2]{0:T(128)S(1)} %copy-done, bf16[576,4096]{1,0:T(8,128)(2,1)} %bitcast.4), custom_call_target="tpu_custom_call" | custom-call | tf_op jit(solution)/shard_map/pallas_call | solution.py:300
  2.4 1.7 %collective-permute-start = (bf16[576,256]{1,0:T(8,128)(2,1)S(1)}, bf16[576,256]{1,0:T(8,128)(2,1)S(1)}, u32[]{:S(2)}, u32[]{:S(2)}) collective-permute-start(bf16[576,256]{1,0:T(8,128)(2,1)S(1)} %get-tuple-element.84), channel_id=1, source_target_pairs={{0,1},{1,2},{2,3},{3,0},{4,5},{5,6},{6,7},{7,4},{8,9},{9,10},{10,1... | collective-permute-start | bytes 884744 | tf_op jit(solution)/shard_map/ppermute | solution.py:43
  4.0 1.7 %collective-permute-start.1 = (bf16[576,256]{1,0:T(8,128)(2,1)S(1)}, bf16[576,256]{1,0:T(8,128)(2,1)S(1)}, u32[]{:S(2)}, u32[]{:S(2)}) collective-permute-start(bf16[576,256]{1,0:T(8,128)(2,1)S(1)} %get-tuple-element.85), channel_id=1, source_target_pairs={{0,3},{1,0},{2,1},{3,2},{4,7},{5,4},{6,5},{7,6},{8,11},{9,8},{10,9... | collective-permute-start | bytes 884744 | tf_op jit(solution)/shard_map/ppermute | solution.py:43
  5.8 7.3 %collective-permute-start.2 = (bf16[32,576]{1,0:T(8,128)(2,1)S(1)}, bf16[32,576]{1,0:T(8,128)(2,1)S(1)}, u32[]{:S(2)}, u32[]{:S(2)}) collective-permute-start(bf16[32,576]{1,0:T(8,128)(2,1)S(1)} %bitcast.6), channel_id=1, source_target_pairs={{0,32},{8,40},{16,48},{24,56},{32,0},{40,8},{48,16},{56,24},{1,33}... | collective-permute-start | bytes 110600 | tf_op jit(solution)/shard_map/ppermute | solution.py:55
  13.1 2.2 %shard_map.47 = (bf16[576,256]{1,0:T(8,128)(2,1)S(1)}, bf16[576,256]{1,0:T(8,128)(2,1)S(1)}, bf16[576,256]{1,0:T(8,128)(2,1)S(1)}, bf16[576,256]{1,0:T(8,128)(2,1)S(1)}, bf16[576,512]{1,0:T(8,128)(2,1)S(1)}) custom-call(s32[2]{0:T(128)S(1)} %copy-done.1, bf16[576,4096]{1,0:T(8,128)(2,1)} %bitcast.5), custom_call_target="tpu_custom_call" | custom-call | tf_op jit(solution)/shard_map/pallas_call | solution.py:300
  15.8 2.9 %collective-permute-start.6 = (bf16[576,256]{1,0:T(8,128)(2,1)S(1)}, bf16[576,256]{1,0:T(8,128)(2,1)S(1)}, u32[]{:S(2)}, u32[]{:S(2)}) collective-permute-start(bf16[576,256]{1,0:T(8,128)(2,1)S(1)} %get-tuple-element.92), channel_id=1, source_target_pairs={{0,3},{1,0},{2,1},{3,2},{4,7},{5,4},{6,5},{7,6},{8,11},{9,8},{10,9... | collective-permute-start | bytes 884744 | tf_op jit(solution)/shard_map/ppermute | solution.py:43
  19.5 3.2 %collective-permute-start.7 = (bf16[576,256]{1,0:T(8,128)(2,1)S(1)}, bf16[576,256]{1,0:T(8,128)(2,1)S(1)}, u32[]{:S(2)}, u32[]{:S(2)}) collective-permute-start(bf16[576,256]{1,0:T(8,128)(2,1)S(1)} %get-tuple-element.93), channel_id=1, source_target_pairs={{0,3},{1,0},{2,1},{3,2},{4,7},{5,4},{6,5},{7,6},{8,11},{9,8},{10,9... | collective-permute-start | bytes 884744 | tf_op jit(solution)/shard_map/ppermute | solution.py:43
  22.7 1.5 %collective-permute-start.10 = (bf16[64,576]{1,0:T(8,128)(2,1)S(1)}, bf16[64,576]{1,0:T(8,128)(2,1)S(1)}, u32[]{:S(2)}, u32[]{:S(2)}) collective-permute-start(bf16[64,576]{1,0:T(8,128)(2,1)S(1)} %pad_maximum_fusion.1), channel_id=1, source_target_pairs={{0,16},{8,24},{16,0},{24,8},{32,48},{40,56},{48,32},{56,40},{1,17}... | collective-permute-start | bytes 221192 | tf_op jit(solution)/shard_map/ppermute | solution.py:55
  24.2 4.9 %collective-permute-done.10 = bf16[64,576]{1,0:T(8,128)(2,1)S(1)} collective-permute-done((bf16[64,576]{1,0:T(8,128)(2,1)S(1)}, bf16[64,576]{1,0:T(8,128)(2,1)S(1)}, u32[]{:S(2)}, u32[]{:S(2)}) %collective-permute-start.10) | collective-permute-done | bytes 73760 | tf_op jit(solution)/shard_map/ppermute | solution.py:55
  29.4 3.0 %collective-permute-done.4.left_a = bf16[576,256]{1,0:T(8,128)(2,1)S(1)} collective-permute-done((bf16[576,256]{1,0:T(8,128)(2,1)S(1)}, bf16[576,256]{1,0:T(8,128)(2,1)S(1)}, u32[]{:S(2)}, u32[]{:S(2)}) %collective-permute-start.4) | collective-permute-done | bytes 294944 | tf_op jit(solution)/shard_map/ppermute | solution.py:43
  33.1 3.0 %collective-permute-start.9 = (bf16[576,512]{1,0:T(8,128)(2,1)S(1)}, bf16[576,512]{1,0:T(8,128)(2,1)S(1)}, u32[]{:S(2)}, u32[]{:S(2)}) collective-permute-start(bf16[576,512]{1,0:T(8,128)(2,1)S(1)} %shard_map.49.refs_4_.refs_7_), channel_id=1, source_target_pairs={{0,3},{1,0},{2,1},{3,2},{4,7},{5,4},{6,5},{7,6},{8,11},{9,8},{10,9... | collective-permute-start | bytes 1769480 | tf_op jit(solution)/shard_map/ppermute | solution.py:43
  36.8 2.4 %collective-permute-start.13 = (bf16[256,576]{1,0:T(8,128)(2,1)S(1)}, bf16[256,576]{1,0:T(8,128)(2,1)S(1)}, u32[]{:S(2)}, u32[]{:S(2)}) collective-permute-start(bf16[256,576]{1,0:T(8,128)(2,1)S(1)} %constant_dynamic-update-slice_fusion.refs_0_.q_ref), channel_id=1, source_target_pairs={{0,128},{64,192},{128,0},{192,64},{1,129},{65,193},{129,1},{193,65... | collective-permute-start | bytes 884744 | tf_op jit(solution)/shard_map/ppermute | solution.py:51
  39.2 1.2 %collective-permute-start.12 = (bf16[256,576]{1,0:T(8,128)(2,1)S(1)}, bf16[256,576]{1,0:T(8,128)(2,1)S(1)}, u32[]{:S(2)}, u32[]{:S(2)}) collective-permute-start(bf16[256,576]{1,0:T(8,128)(2,1)S(1)} %constant_dynamic-update-slice_fusion.refs_0_.q_ref), channel_id=1, source_target_pairs={{0,64},{64,0},{128,192},{192,128},{1,65},{65,1},{129,193},{193,129... | collective-permute-start | bytes 884744 | tf_op jit(solution)/shard_map/ppermute | solution.py:51
  40.4 12.9 %collective-permute-done.14.refs_3_.q_ref = bf16[256,576]{1,0:T(8,128)(2,1)S(1)} collective-permute-done((bf16[256,576]{1,0:T(8,128)(2,1)S(1)}, bf16[256,576]{1,0:T(8,128)(2,1)S(1)}, u32[]{:S(2)}, u32[]{:S(2)}) %collective-permute-start.14) | collective-permute-done | bytes 294944 | tf_op jit(solution)/shard_map/ppermute | solution.py:51
  54.5 3.0 %collective-permute-start.19 = (bf16[576,256]{1,0:T(8,128)(2,1)S(1)}, bf16[576,256]{1,0:T(8,128)(2,1)S(1)}, u32[]{:S(2)}, u32[]{:S(2)}) collective-permute-start(bf16[576,256]{1,0:T(8,128)(2,1)S(1)} %slice.7), channel_id=1, source_target_pairs={{0,3},{1,0},{2,1},{3,2},{4,7},{5,4},{6,5},{7,6},{8,11},{9,8},{10,9... | collective-permute-start | bytes 884744 | tf_op jit(solution)/shard_map/ppermute | solution.py:43
  57.5 3.2 %shard_map.50 = (f32[256,1536]{1,0:T(8,128)S(1)}, f32[256,128]{1,0:T(8,128)S(1)}, f32[256,1536]{1,0:T(8,128)S(1)}, f32[256,128]{1,0:T(8,128)S(1)}, f32[256,1536]...) custom-call(s32[16]{0:T(128)S(1)} %copy-done.2, s32[2]{0:T(128)S(1)} %copy-done.1, ...), custom_call_target="tpu_custom_call" | custom-call | tf_op jit(solution)/shard_map/pallas_call | solution.py:300
  60.7 3.2 %shard_map.51 = (f32[256,1536]{1,0:T(8,128)S(1)}, f32[256,128]{1,0:T(8,128)S(1)}, f32[256,1536]{1,0:T(8,128)S(1)}, f32[256,128]{1,0:T(8,128)S(1)}, f32[256,1536]...) custom-call(s32[16]{0:T(128)S(1)} %copy-done.2, ...), custom_call_target="tpu_custom_call" | custom-call | tf_op jit(solution)/shard_map/pallas_call | solution.py:300
  64.2 3.4 %collective-permute-done.18.refs_10_ = bf16[576,256]{1,0:T(8,128)(2,1)S(1)} collective-permute-done((bf16[576,256]{1,0:T(8,128)(2,1)S(1)}, bf16[576,256]{1,0:T(8,128)(2,1)S(1)}, u32[]{:S(2)}, u32[]{:S(2)}) %collective-permute-start.18) | collective-permute-done | bytes 294944 | tf_op jit(solution)/shard_map/ppermute | solution.py:43
  68.1 1.1 collective-permute-done.20.refs_15_
  69.6 2.8 %shard_map.52 = bf16[264,512]{1,0:T(8,128)(2,1)S(1)} custom-call(bf16[256,576]{1,0:T(8,128)(2,1)S(1)} %collective-permute-done.12.refs_1_.q_ref, f32[256,1536]{1,0:T(8,128)S(1)} %get-tuple-element.126.refs_0_, f32[256,128]{1,0:T(8,128)S(1)} %get-tuple-element.127.refs_1_, f32[256,1536]{1,0:T(8,128)S(1)} %get-tuple-element.128.refs_2_, ...), custom_call_target="tpu_custom_call" | custom-call | tf_op jit(solution)/shard_map/pallas_call | solution.py:300
  73.3 2.8 %shard_map.53 = bf16[264,512]{1,0:T(8,128)(2,1)S(1)} custom-call(bf16[256,576]{1,0:T(8,128)(2,1)S(1)} %collective-permute-done.14.refs_3_.q_ref, f32[256,1536]{1,0:T(8,128)S(1)} %get-tuple-element.133.refs_0_, f32[256,128]{1,0:T(8,128)S(1)} %get-tuple-element.134.refs_1_, f32[256,1536]{1,0:T(8,128)S(1)} %get-tuple-element.135.refs_2_, ...), custom_call_target="tpu_custom_call" | custom-call | tf_op jit(solution)/shard_map/pallas_call | solution.py:300
  76.1 1.4 %collective-permute-start.23 = (bf16[264,512]{1,0:T(8,128)(2,1)S(1)}, bf16[264,512]{1,0:T(8,128)(2,1)S(1)}, u32[]{:S(2)}, u32[]{:S(2)}) collective-permute-start(bf16[264,512]{1,0:T(8,128)(2,1)S(1)} %shard_map.53), channel_id=1, source_target_pairs={{0,192},{64,128},{128,64},{192,0},{1,193},{65,129},{129,65},{193,1... | collective-permute-start | bytes 811016 | tf_op jit(solution)/shard_map/ppermute | solution.py:51
  77.6 3.5 %collective-permute-done.22.refs_0_ = bf16[264,512]{1,0:T(8,128)(2,1)S(1)} collective-permute-done((bf16[264,512]{1,0:T(8,128)(2,1)S(1)}, bf16[264,512]{1,0:T(8,128)(2,1)S(1)}, u32[]{:S(2)}, u32[]{:S(2)}) %collective-permute-start.22) | collective-permute-done | bytes 270368 | tf_op jit(solution)/shard_map/ppermute | solution.py:51
  81.0 2.8 %shard_map.54 = bf16[264,512]{1,0:T(8,128)(2,1)S(1)} custom-call(bf16[256,576]{1,0:T(8,128)(2,1)S(1)} %collective-permute-done.13.refs_2_.q_ref, f32[256,1536]{1,0:T(8,128)S(1)} %get-tuple-element.141.refs_0_, f32[256,128]{1,0:T(8,128)S(1)} %get-tuple-element.142.refs_1_, f32[256,1536]{1,0:T(8,128)S(1)} %get-tuple-element.143.refs_2_, ...), custom_call_target="tpu_custom_call" | custom-call | tf_op jit(solution)/shard_map/pallas_call | solution.py:300
  83.8 1.5 %collective-permute-start.24 = (bf16[264,512]{1,0:T(8,128)(2,1)S(1)}, bf16[264,512]{1,0:T(8,128)(2,1)S(1)}, u32[]{:S(2)}, u32[]{:S(2)}) collective-permute-start(bf16[264,512]{1,0:T(8,128)(2,1)S(1)} %shard_map.54), channel_id=1, source_target_pairs={{0,128},{64,192},{128,0},{192,64},{1,129},{65,193},{129,1},{193,65... | collective-permute-start | bytes 811016 | tf_op jit(solution)/shard_map/ppermute | solution.py:51
  85.9 2.8 %shard_map.55.refs_3_ = bf16[264,512]{1,0:T(8,128)(2,1)S(1)} custom-call(bf16[256,576]{1,0:T(8,128)(2,1)S(1)} %constant_dynamic-update-slice_fusion.refs_0_.q_ref, f32[256,1536]{1,0:T(8,128)S(1)} %get-tuple-element.150.refs_0_, f32[256,128]{1,0:T(8,128)S(1)} %get-tuple-element.151.refs_1_, f32[256,1536]{1,0:T(8,128)S(1)} %get-tuple-element.152.refs_2_, ...), custom_call_target="tpu_custom_call" | custom-call | tf_op jit(solution)/shard_map/pallas_call | solution.py:300
  88.7 4.4 %collective-permute-done.24.refs_2_ = bf16[264,512]{1,0:T(8,128)(2,1)S(1)} collective-permute-done((bf16[264,512]{1,0:T(8,128)(2,1)S(1)}, bf16[264,512]{1,0:T(8,128)(2,1)S(1)}, u32[]{:S(2)}, u32[]{:S(2)}) %collective-permute-start.24) | collective-permute-done | bytes 270368 | tf_op jit(solution)/shard_map/ppermute | solution.py:51
  93.8 1.6 %collective-permute-start.26 = (bf16[32,640]{1,0:T(8,128)(2,1)S(1)}, bf16[32,640]{1,0:T(8,128)(2,1)S(1)}, u32[]{:S(2)}, u32[]{:S(2)}) collective-permute-start(bf16[32,640]{1,0:T(8,128)(2,1)S(1)} %get-tuple-element.157), channel_id=1, source_target_pairs={{0,16},{8,24},{16,0},{24,8},{32,48},{40,56},{48,32},{56,40},{1,17}... | collective-permute-start | bytes 122888 | tf_op jit(solution)/shard_map/ppermute | solution.py:55
  95.3 4.9 %collective-permute-start.27 = (bf16[32,640]{1,0:T(8,128)(2,1)S(1)}, bf16[32,640]{1,0:T(8,128)(2,1)S(1)}, u32[]{:S(2)}, u32[]{:S(2)}) collective-permute-start(bf16[32,640]{1,0:T(8,128)(2,1)S(1)} %get-tuple-element.158), channel_id=1, source_target_pairs={{0,48},{8,56},{16,32},{24,40},{32,16},{40,24},{48,0},{56,8},{1,49}... | collective-permute-start | bytes 122888 | tf_op jit(solution)/shard_map/ppermute | solution.py:55
  101.7 1.9 %collective-permute-start.30 = (bf16[32,640]{1,0:T(8,128)(2,1)S(1)}, bf16[32,640]{1,0:T(8,128)(2,1)S(1)}, u32[]{:S(2)}, u32[]{:S(2)}) collective-permute-start(bf16[32,640]{1,0:T(8,128)(2,1)S(1)} %get-tuple-element.161), channel_id=1, source_target_pairs={{0,24},{8,16},{16,8},{24,0},{32,56},{40,48},{48,40},{56,32},{1,25}... | collective-permute-start | bytes 122888 | tf_op jit(solution)/shard_map/ppermute | solution.py:55
  103.6 3.7 %collective-permute-start.31 = (bf16[32,640]{1,0:T(8,128)(2,1)S(1)}, bf16[32,640]{1,0:T(8,128)(2,1)S(1)}, u32[]{:S(2)}, u32[]{:S(2)}) collective-permute-start(bf16[32,640]{1,0:T(8,128)(2,1)S(1)} %get-tuple-element.162), channel_id=1, source_target_pairs={{0,56},{8,48},{16,40},{24,32},{32,24},{40,16},{48,8},{56,0},{1,57}... | collective-permute-start | bytes 122888 | tf_op jit(solution)/shard_map/ppermute | solution.py:55
  108.2 1.5 %collective-permute-done.31.refs_7_ = bf16[32,640]{1,0:T(8,128)(2,1)S(1)} collective-permute-done((bf16[32,640]{1,0:T(8,128)(2,1)S(1)}, bf16[32,640]{1,0:T(8,128)(2,1)S(1)}, u32[]{:S(2)}, u32[]{:S(2)}) %collective-permute-start.31) | collective-permute-done | bytes 40992 | tf_op jit(solution)/shard_map/ppermute | solution.py:55
  (61 shorter events, 11.5 us)
Async XLA Ops:
  2.4 16.3 %collective-permute-start = (bf16[576,256]{1,0:T(8,128)(2,1)S(1)}, bf16[576,256]{1,0:T(8,128)(2,1)S(1)}, u32[]{:S(2)}, u32[]{:S(2)}) collective-permute-start(bf16[576,256]{1,0:T(8,128)(2,1)S(1)} %get-tuple-element.84), channel_id=1, source_target_pairs={{0,1},{1,2},{2,3},{3,0},{4,5},{5,6},{6,7},{7,4},{8,9},{9,10},{10,1... | collective-permute-start | bytes 884744 | tf_op jit(solution)/shard_map/ppermute | solution.py:43
  4.0 14.7 %collective-permute-start.1 = (bf16[576,256]{1,0:T(8,128)(2,1)S(1)}, bf16[576,256]{1,0:T(8,128)(2,1)S(1)}, u32[]{:S(2)}, u32[]{:S(2)}) collective-permute-start(bf16[576,256]{1,0:T(8,128)(2,1)S(1)} %get-tuple-element.85), channel_id=1, source_target_pairs={{0,3},{1,0},{2,1},{3,2},{4,7},{5,4},{6,5},{7,6},{8,11},{9,8},{10,9... | collective-permute-start | bytes 884744 | tf_op jit(solution)/shard_map/ppermute | solution.py:43
  5.8 10.0 %collective-permute-start.2 = (bf16[32,576]{1,0:T(8,128)(2,1)S(1)}, bf16[32,576]{1,0:T(8,128)(2,1)S(1)}, u32[]{:S(2)}, u32[]{:S(2)}) collective-permute-start(bf16[32,576]{1,0:T(8,128)(2,1)S(1)} %bitcast.6), channel_id=1, source_target_pairs={{0,32},{8,40},{16,48},{24,56},{32,0},{40,8},{48,16},{56,24},{1,33}... | collective-permute-start | bytes 110600 | tf_op jit(solution)/shard_map/ppermute | solution.py:55
  13.1 5.6 %collective-permute-start.3 = (s32[2]{0:T(128)S(1)}, s32[2]{0:T(128)S(1)}, u32[]{:S(2)}, u32[]{:S(2)}) collective-permute-start(s32[2]{0:T(128)S(1)} %copy-done.1), channel_id=1, source_target_pairs={{0,4},{4,0},{1,5},{5,1},{2,6},{6,2},{3,7},{7,3},{8,12},{12,8},{9,1... | collective-permute-start | bytes 32 | tf_op jit(solution)/shard_map/ppermute | solution.py:47
  15.4 14.0 %collective-permute-start.5 = (bf16[576,256]{1,0:T(8,128)(2,1)S(1)}, bf16[576,256]{1,0:T(8,128)(2,1)S(1)}, u32[]{:S(2)}, u32[]{:S(2)}) collective-permute-start(bf16[576,256]{1,0:T(8,128)(2,1)S(1)} %get-tuple-element.91), channel_id=1, source_target_pairs={{0,1},{1,2},{2,3},{3,0},{4,5},{5,6},{6,7},{7,4},{8,9},{9,10},{10,1... | collective-permute-start | bytes 884744 | tf_op jit(solution)/shard_map/ppermute | solution.py:43
  15.8 13.6 %collective-permute-start.6 = (bf16[576,256]{1,0:T(8,128)(2,1)S(1)}, bf16[576,256]{1,0:T(8,128)(2,1)S(1)}, u32[]{:S(2)}, u32[]{:S(2)}) collective-permute-start(bf16[576,256]{1,0:T(8,128)(2,1)S(1)} %get-tuple-element.92), channel_id=1, source_target_pairs={{0,3},{1,0},{2,1},{3,2},{4,7},{5,4},{6,5},{7,6},{8,11},{9,8},{10,9... | collective-permute-start | bytes 884744 | tf_op jit(solution)/shard_map/ppermute | solution.py:43
  19.4 13.0 %collective-permute-start.4 = (bf16[576,256]{1,0:T(8,128)(2,1)S(1)}, bf16[576,256]{1,0:T(8,128)(2,1)S(1)}, u32[]{:S(2)}, u32[]{:S(2)}) collective-permute-start(bf16[576,256]{1,0:T(8,128)(2,1)S(1)} %get-tuple-element.90), channel_id=1, source_target_pairs={{0,1},{1,2},{2,3},{3,0},{4,5},{5,6},{6,7},{7,4},{8,9},{9,10},{10,1... | collective-permute-start | bytes 884744 | tf_op jit(solution)/shard_map/ppermute | solution.py:43
  19.5 12.9 %collective-permute-start.7 = (bf16[576,256]{1,0:T(8,128)(2,1)S(1)}, bf16[576,256]{1,0:T(8,128)(2,1)S(1)}, u32[]{:S(2)}, u32[]{:S(2)}) collective-permute-start(bf16[576,256]{1,0:T(8,128)(2,1)S(1)} %get-tuple-element.93), channel_id=1, source_target_pairs={{0,3},{1,0},{2,1},{3,2},{4,7},{5,4},{6,5},{7,6},{8,11},{9,8},{10,9... | collective-permute-start | bytes 884744 | tf_op jit(solution)/shard_map/ppermute | solution.py:43
  22.7 6.4 %collective-permute-start.10 = (bf16[64,576]{1,0:T(8,128)(2,1)S(1)}, bf16[64,576]{1,0:T(8,128)(2,1)S(1)}, u32[]{:S(2)}, u32[]{:S(2)}) collective-permute-start(bf16[64,576]{1,0:T(8,128)(2,1)S(1)} %pad_maximum_fusion.1), channel_id=1, source_target_pairs={{0,16},{8,24},{16,0},{24,8},{32,48},{40,56},{48,32},{56,40},{1,17}... | collective-permute-start | bytes 221192 | tf_op jit(solution)/shard_map/ppermute | solution.py:55
  29.1 7.0 %collective-permute-start.11 = (bf16[128,576]{1,0:T(8,128)(2,1)S(1)}, bf16[128,576]{1,0:T(8,128)(2,1)S(1)}, u32[]{:S(2)}, u32[]{:S(2)}) collective-permute-start(bf16[128,576]{1,0:T(8,128)(2,1)S(1)} %pad_maximum_fusion), channel_id=1, source_target_pairs={{0,8},{8,0},{16,24},{24,16},{32,40},{40,32},{48,56},{56,48},{1,9},... | collective-permute-start | bytes 442376 | tf_op jit(solution)/shard_map/ppermute | solution.py:55
  33.1 20.8 %collective-permute-start.9 = (bf16[576,512]{1,0:T(8,128)(2,1)S(1)}, bf16[576,512]{1,0:T(8,128)(2,1)S(1)}, u32[]{:S(2)}, u32[]{:S(2)}) collective-permute-start(bf16[576,512]{1,0:T(8,128)(2,1)S(1)} %shard_map.49.refs_4_.refs_7_), channel_id=1, source_target_pairs={{0,3},{1,0},{2,1},{3,2},{4,7},{5,4},{6,5},{7,6},{8,11},{9,8},{10,9... | collective-permute-start | bytes 1769480 | tf_op jit(solution)/shard_map/ppermute | solution.py:43
  36.1 17.8 %collective-permute-start.8 = (bf16[576,512]{1,0:T(8,128)(2,1)S(1)}, bf16[576,512]{1,0:T(8,128)(2,1)S(1)}, u32[]{:S(2)}, u32[]{:S(2)}) collective-permute-start(bf16[576,512]{1,0:T(8,128)(2,1)S(1)} %shard_map.49.refs_4_.refs_7_), channel_id=1, source_target_pairs={{0,1},{1,2},{2,3},{3,0},{4,5},{5,6},{6,7},{7,4},{8,9},{9,10},{10,1... | collective-permute-start | bytes 1769480 | tf_op jit(solution)/shard_map/ppermute | solution.py:43
  36.2 17.1 %collective-permute-start.14 = (bf16[256,576]{1,0:T(8,128)(2,1)S(1)}, bf16[256,576]{1,0:T(8,128)(2,1)S(1)}, u32[]{:S(2)}, u32[]{:S(2)}) collective-permute-start(bf16[256,576]{1,0:T(8,128)(2,1)S(1)} %constant_dynamic-update-slice_fusion.refs_0_.q_ref), channel_id=1, source_target_pairs={{0,192},{64,128},{128,64},{192,0},{1,193},{65,129},{129,65},{193,1... | collective-permute-start | bytes 884744 | tf_op jit(solution)/shard_map/ppermute | solution.py:51
  36.8 16.5 %collective-permute-start.13 = (bf16[256,576]{1,0:T(8,128)(2,1)S(1)}, bf16[256,576]{1,0:T(8,128)(2,1)S(1)}, u32[]{:S(2)}, u32[]{:S(2)}) collective-permute-start(bf16[256,576]{1,0:T(8,128)(2,1)S(1)} %constant_dynamic-update-slice_fusion.refs_0_.q_ref), channel_id=1, source_target_pairs={{0,128},{64,192},{128,0},{192,64},{1,129},{65,193},{129,1},{193,65... | collective-permute-start | bytes 884744 | tf_op jit(solution)/shard_map/ppermute | solution.py:51
  39.2 14.7 %collective-permute-start.12 = (bf16[256,576]{1,0:T(8,128)(2,1)S(1)}, bf16[256,576]{1,0:T(8,128)(2,1)S(1)}, u32[]{:S(2)}, u32[]{:S(2)}) collective-permute-start(bf16[256,576]{1,0:T(8,128)(2,1)S(1)} %constant_dynamic-update-slice_fusion.refs_0_.q_ref), channel_id=1, source_target_pairs={{0,64},{64,0},{128,192},{192,128},{1,65},{65,1},{129,193},{193,129... | collective-permute-start | bytes 884744 | tf_op jit(solution)/shard_map/ppermute | solution.py:51
  53.3 4.2 %collective-permute-start.15 = (bf16[576,512]{1,0:T(8,128)(2,1)S(1)}, bf16[576,512]{1,0:T(8,128)(2,1)S(1)}, u32[]{:S(2)}, u32[]{:S(2)}) collective-permute-start(bf16[576,512]{1,0:T(8,128)(2,1)S(1)} %shard_map.49.refs_4_.refs_7_), channel_id=1, source_target_pairs={{0,4},{4,0},{1,5},{5,1},{2,6},{6,2},{3,7},{7,3},{8,12},{12,8},{9,1... | collective-permute-start | bytes 1769480 | tf_op jit(solution)/shard_map/ppermute | solution.py:47
  53.9 3.6 %collective-permute-start.16 = (bf16[576,512]{1,0:T(8,128)(2,1)S(1)}, bf16[576,512]{1,0:T(8,128)(2,1)S(1)}, u32[]{:S(2)}, u32[]{:S(2)}) collective-permute-start(bf16[576,512]{1,0:T(8,128)(2,1)S(1)} %collective-permute-done.8.refs_5_.refs_8_), channel_id=1, source_target_pairs={{0,4},{4,0},{1,5},{5,1},{2,6},{6,2},{3,7},{7,3},{8,12},{12,8},{9,1... | collective-permute-start | bytes 1769480 | tf_op jit(solution)/shard_map/ppermute | solution.py:47
  53.9 3.6 %collective-permute-start.17 = (bf16[576,512]{1,0:T(8,128)(2,1)S(1)}, bf16[576,512]{1,0:T(8,128)(2,1)S(1)}, u32[]{:S(2)}, u32[]{:S(2)}) collective-permute-start(bf16[576,512]{1,0:T(8,128)(2,1)S(1)} %collective-permute-done.9.refs_6_.refs_9_), channel_id=1, source_target_pairs={{0,4},{4,0},{1,5},{5,1},{2,6},{6,2},{3,7},{7,3},{8,12},{12,8},{9,1... | collective-permute-start | bytes 1769480 | tf_op jit(solution)/shard_map/ppermute | solution.py:47
  54.5 9.7 %collective-permute-start.19 = (bf16[576,256]{1,0:T(8,128)(2,1)S(1)}, bf16[576,256]{1,0:T(8,128)(2,1)S(1)}, u32[]{:S(2)}, u32[]{:S(2)}) collective-permute-start(bf16[576,256]{1,0:T(8,128)(2,1)S(1)} %slice.7), channel_id=1, source_target_pairs={{0,3},{1,0},{2,1},{3,2},{4,7},{5,4},{6,5},{7,6},{8,11},{9,8},{10,9... | collective-permute-start | bytes 884744 | tf_op jit(solution)/shard_map/ppermute | solution.py:43
  57.5 10.1 %collective-permute-start.18 = (bf16[576,256]{1,0:T(8,128)(2,1)S(1)}, bf16[576,256]{1,0:T(8,128)(2,1)S(1)}, u32[]{:S(2)}, u32[]{:S(2)}) collective-permute-start(bf16[576,256]{1,0:T(8,128)(2,1)S(1)} %slice.6), channel_id=1, source_target_pairs={{0,1},{1,2},{2,3},{3,0},{4,5},{5,6},{6,7},{7,4},{8,9},{9,10},{10,1... | collective-permute-start | bytes 884744 | tf_op jit(solution)/shard_map/ppermute | solution.py:43
  67.6 1.6 %collective-permute-start.20 = (bf16[576,256]{1,0:T(8,128)(2,1)S(1)}, bf16[576,256]{1,0:T(8,128)(2,1)S(1)}, u32[]{:S(2)}, u32[]{:S(2)}) collective-permute-start(bf16[576,256]{1,0:T(8,128)(2,1)S(1)} %collective-permute-done.18.refs_10_), channel_id=1, source_target_pairs={{0,4},{4,0},{1,5},{5,1},{2,6},{6,2},{3,7},{7,3},{8,12},{12,8},{9,1... | collective-permute-start | bytes 884744 | tf_op jit(solution)/shard_map/ppermute | solution.py:47
  67.6 2.0 %collective-permute-start.21 = (bf16[576,256]{1,0:T(8,128)(2,1)S(1)}, bf16[576,256]{1,0:T(8,128)(2,1)S(1)}, u32[]{:S(2)}, u32[]{:S(2)}) collective-permute-start(bf16[576,256]{1,0:T(8,128)(2,1)S(1)} %collective-permute-done.19.refs_11_), channel_id=1, source_target_pairs={{0,4},{4,0},{1,5},{5,1},{2,6},{6,2},{3,7},{7,3},{8,12},{12,8},{9,1... | collective-permute-start | bytes 884744 | tf_op jit(solution)/shard_map/ppermute | solution.py:47
  72.4 8.6 %collective-permute-start.22 = (bf16[264,512]{1,0:T(8,128)(2,1)S(1)}, bf16[264,512]{1,0:T(8,128)(2,1)S(1)}, u32[]{:S(2)}, u32[]{:S(2)}) collective-permute-start(bf16[264,512]{1,0:T(8,128)(2,1)S(1)} %shard_map.52), channel_id=1, source_target_pairs={{0,64},{64,0},{128,192},{192,128},{1,65},{65,1},{129,193},{193,129... | collective-permute-start | bytes 811016 | tf_op jit(solution)/shard_map/ppermute | solution.py:51
  76.1 9.8 %collective-permute-start.23 = (bf16[264,512]{1,0:T(8,128)(2,1)S(1)}, bf16[264,512]{1,0:T(8,128)(2,1)S(1)}, u32[]{:S(2)}, u32[]{:S(2)}) collective-permute-start(bf16[264,512]{1,0:T(8,128)(2,1)S(1)} %shard_map.53), channel_id=1, source_target_pairs={{0,192},{64,128},{128,64},{192,0},{1,193},{65,129},{129,65},{193,1... | collective-permute-start | bytes 811016 | tf_op jit(solution)/shard_map/ppermute | solution.py:51
  83.8 9.3 %collective-permute-start.24 = (bf16[264,512]{1,0:T(8,128)(2,1)S(1)}, bf16[264,512]{1,0:T(8,128)(2,1)S(1)}, u32[]{:S(2)}, u32[]{:S(2)}) collective-permute-start(bf16[264,512]{1,0:T(8,128)(2,1)S(1)} %shard_map.54), channel_id=1, source_target_pairs={{0,128},{64,192},{128,0},{192,64},{1,129},{65,193},{129,1},{193,65... | collective-permute-start | bytes 811016 | tf_op jit(solution)/shard_map/ppermute | solution.py:51
  93.7 8.1 %collective-permute-start.25 = (bf16[32,640]{1,0:T(8,128)(2,1)S(1)}, bf16[32,640]{1,0:T(8,128)(2,1)S(1)}, u32[]{:S(2)}, u32[]{:S(2)}) collective-permute-start(bf16[32,640]{1,0:T(8,128)(2,1)S(1)} %get-tuple-element.156), channel_id=1, source_target_pairs={{0,32},{8,40},{16,48},{24,56},{32,0},{40,8},{48,16},{56,24},{1,33}... | collective-permute-start | bytes 122888 | tf_op jit(solution)/shard_map/ppermute | solution.py:55
  93.8 9.8 %collective-permute-start.26 = (bf16[32,640]{1,0:T(8,128)(2,1)S(1)}, bf16[32,640]{1,0:T(8,128)(2,1)S(1)}, u32[]{:S(2)}, u32[]{:S(2)}) collective-permute-start(bf16[32,640]{1,0:T(8,128)(2,1)S(1)} %get-tuple-element.157), channel_id=1, source_target_pairs={{0,16},{8,24},{16,0},{24,8},{32,48},{40,56},{48,32},{56,40},{1,17}... | collective-permute-start | bytes 122888 | tf_op jit(solution)/shard_map/ppermute | solution.py:55
  95.3 12.0 %collective-permute-start.27 = (bf16[32,640]{1,0:T(8,128)(2,1)S(1)}, bf16[32,640]{1,0:T(8,128)(2,1)S(1)}, u32[]{:S(2)}, u32[]{:S(2)}) collective-permute-start(bf16[32,640]{1,0:T(8,128)(2,1)S(1)} %get-tuple-element.158), channel_id=1, source_target_pairs={{0,48},{8,56},{16,32},{24,40},{32,16},{40,24},{48,0},{56,8},{1,49}... | collective-permute-start | bytes 122888 | tf_op jit(solution)/shard_map/ppermute | solution.py:55
  100.3 7.1 %collective-permute-start.28 = (bf16[32,640]{1,0:T(8,128)(2,1)S(1)}, bf16[32,640]{1,0:T(8,128)(2,1)S(1)}, u32[]{:S(2)}, u32[]{:S(2)}) collective-permute-start(bf16[32,640]{1,0:T(8,128)(2,1)S(1)} %get-tuple-element.159), channel_id=1, source_target_pairs={{0,8},{8,0},{16,24},{24,16},{32,40},{40,32},{48,56},{56,48},{1,9},... | collective-permute-start | bytes 122888 | tf_op jit(solution)/shard_map/ppermute | solution.py:55
  101.2 7.0 %collective-permute-start.29 = (bf16[32,640]{1,0:T(8,128)(2,1)S(1)}, bf16[32,640]{1,0:T(8,128)(2,1)S(1)}, u32[]{:S(2)}, u32[]{:S(2)}) collective-permute-start(bf16[32,640]{1,0:T(8,128)(2,1)S(1)} %get-tuple-element.160), channel_id=1, source_target_pairs={{0,40},{8,32},{16,56},{24,48},{32,8},{40,0},{48,24},{56,16},{1,41}... | collective-permute-start | bytes 122888 | tf_op jit(solution)/shard_map/ppermute | solution.py:55
  101.7 6.5 %collective-permute-start.30 = (bf16[32,640]{1,0:T(8,128)(2,1)S(1)}, bf16[32,640]{1,0:T(8,128)(2,1)S(1)}, u32[]{:S(2)}, u32[]{:S(2)}) collective-permute-start(bf16[32,640]{1,0:T(8,128)(2,1)S(1)} %get-tuple-element.161), channel_id=1, source_target_pairs={{0,24},{8,16},{16,8},{24,0},{32,56},{40,48},{48,40},{56,32},{1,25}... | collective-permute-start | bytes 122888 | tf_op jit(solution)/shard_map/ppermute | solution.py:55
  103.6 6.1 %collective-permute-start.31 = (bf16[32,640]{1,0:T(8,128)(2,1)S(1)}, bf16[32,640]{1,0:T(8,128)(2,1)S(1)}, u32[]{:S(2)}, u32[]{:S(2)}) collective-permute-start(bf16[32,640]{1,0:T(8,128)(2,1)S(1)} %get-tuple-element.162), channel_id=1, source_target_pairs={{0,56},{8,48},{16,40},{24,32},{32,24},{40,16},{48,8},{56,0},{1,57}... | collective-permute-start | bytes 122888 | tf_op jit(solution)/shard_map/ppermute | solution.py:55
  (4 other events, 43.3 us)
